TPU v7x, 32 devices: a whole 2x2x4 slice. The times are simulated.
32 devices in a mesh: seq: 8 (over z, core), tp: 4 (over y, x).
Axes of the slice: x: 2, y: 2, z: 4, core: 2. Of those that a mesh axis runs over, the one named last changes fastest.
Arguments:
- layer_in: bfloat16 [4096, 2048], P('seq'), may hold values from -6 to 6
- positions: int32 [4096], P('seq'), may hold values from 0 to 2047, as said below
- seq_ids: int32 [4096], P('seq'), may hold values from 0 to 1, as said below
- norm1_gain: float32 [2048], replicated, may hold values from 0.5 to 1.5
- norm2_gain: float32 [2048], replicated, may hold values from 0.5 to 1.5
- w_query: float32 [2048, 2048], P('seq', 'tp'), may hold values from -0.125 to 0.125
- w_key: float32 [2048, 2048], P('seq', 'tp'), may hold values from -0.125 to 0.125
- w_value: float32 [2048, 2048], P('seq', 'tp'), may hold values from -0.125 to 0.125
- w_out: float32 [2048, 2048], P('tp', 'seq'), may hold values from -4 to 4
- w_gate: float32 [2048, 8192], P('seq', 'tp'), may hold values from -0.125 to 0.125
- w_up: float32 [2048, 8192], P('seq', 'tp'), may hold values from -0.125 to 0.125
- w_down: float32 [8192, 2048], P('tp', 'seq'), may hold values from -0.0625 to 0.0625
- out_grad: bfloat16 [4096, 2048], P('seq'), may hold values from -6 to 6
Outputs:
- layer_out: bfloat16 [4096, 2048], P('seq')
- in_grad: float32 [4096, 2048], P('seq')
- grad_norm1: float32 [2048], P('seq')
- grad_norm2: float32 [2048], P('seq')
- grad_w_query: float32 [2048, 2048], P('seq', 'tp')
- grad_w_key: float32 [2048, 2048], P('seq', 'tp')
- grad_w_value: float32 [2048, 2048], P('seq', 'tp')
- grad_w_out: float32 [2048, 2048], P('tp', 'seq')
- grad_w_gate: float32 [2048, 8192], P('seq', 'tp')
- grad_w_up: float32 [2048, 8192], P('seq', 'tp')
- grad_w_down: float32 [8192, 2048], P('tp', 'seq')
Inputs may be any that keep to these rules, and one draw needn't show every extreme that they name: The shard of 512 rows at index r of seq holds, in an order that varies from shard to shard, four blocks of 128 consecutive positions: for each of the two sequences its blocks number r and 15 - r. Each position of each sequence appears once. `seq_ids`: the sequence of each row, constant over each block of 128 rows described for positions; each shard holds two such blocks of each sequence, and each sequence has 2048 rows.
All inputs are finite; a program needn't handle non-finite values.
Results may differ from a plain program's by a relative error of at most 0.024.
Values may be sent and summed in bfloat16 or wider, within the bound.
No kernel may reach another device: no remote copies, remote signals or barrier semaphores. Data moves between devices by JAX's collectives and lax.ppermute only.
A program may use at most 192 MiB of HBM per device.

v0:
```python
import math

import jax
import jax.numpy as jnp
from jax import lax
from jax.sharding import PartitionSpec as P

HD = 128


EPSILON = 1e-06


def angles(places):
    half_width = HD // 2
    frequency = jnp.power(
        jnp.float32(10000.0), -jnp.arange(half_width, dtype=jnp.float32) / half_width
    )
    phase_angle = places.astype(jnp.float32)[:, None] * frequency[None, :]
    return (jnp.cos(phase_angle)[:, None, :], jnp.sin(phase_angle)[:, None, :])


def rotate(heads, rot_cos, rot_sin):
    half_width = heads.shape[-1] // 2
    front_half = heads[..., :half_width]
    back_half = heads[..., half_width:]
    return jnp.concatenate(
        [front_half * rot_cos - back_half * rot_sin, back_half * rot_cos + front_half * rot_sin],
        axis=-1,
    )


def rotate_back(grads, rot_cos, rot_sin):
    half_width = grads.shape[-1] // 2
    front_half = grads[..., :half_width]
    back_half = grads[..., half_width:]
    return jnp.concatenate(
        [front_half * rot_cos + back_half * rot_sin, back_half * rot_cos - front_half * rot_sin],
        axis=-1,
    )


def matrix(left, right):
    return jnp.dot(left, right, preferred_element_type=jnp.float32)


def inner_rows(left, right):
    return lax.dot_general(
        left, right, (((0,), (0,)), ((), ())), preferred_element_type=jnp.float32
    )


def outer_cols(left, right):
    return lax.dot_general(
        left, right, (((1,), (1,)), ((), ())), preferred_element_type=jnp.float32
    )


def arrange(values, order):
    blocks = values.reshape((4, values.shape[0] // 4) + values.shape[1:])
    return blocks[order].reshape(values.shape)


def regroup(values, shard_rows):
    count = values.shape[0] // shard_rows
    half_rows = shard_rows // 2
    split_form = values.reshape((count, 2, half_rows) + values.shape[1:])
    return jnp.swapaxes(split_form, 0, 1).reshape((2, count * half_rows) + values.shape[1:])


def unsplit(values):
    return values.reshape((values.shape[0] * values.shape[1],) + values.shape[2:])


def split_scores(query_split, key_split, qpos_split, kpos_split, score_scale, score_bias):
    raw = (
        jnp.einsum("sqhd,skhd->shqk", query_split, key_split, preferred_element_type=jnp.float32)
        * score_scale
        + score_bias
    )
    allowed = (kpos_split[:, None, :] <= qpos_split[:, :, None])[:, None]
    return (jax.nn.sigmoid(raw), allowed)


def split_attend(
    query_split, key_split, value_split, qpos_split, kpos_split, score_scale, score_bias
):
    sig, allowed = split_scores(
        query_split, key_split, qpos_split, kpos_split, score_scale, score_bias
    )
    attn_weights = jnp.where(allowed, sig, 0.0).astype(jnp.bfloat16)
    return unsplit(
        jnp.einsum("shqk,skhd->sqhd", attn_weights, value_split, preferred_element_type=jnp.float32)
    )


def split_grads(
    query_split, key_split, value_split, grad_split, qpos_split, kpos_split, score_scale, score_bias
):
    sig, allowed = split_scores(
        query_split, key_split, qpos_split, kpos_split, score_scale, score_bias
    )
    attn_weights = jnp.where(allowed, sig, 0.0).astype(jnp.bfloat16)
    grad_prob = jnp.einsum(
        "sqhd,skhd->shqk", grad_split, value_split, preferred_element_type=jnp.float32
    )
    grad_score = jnp.where(allowed, grad_prob * sig * (1.0 - sig), 0.0).astype(jnp.bfloat16)
    return (attn_weights, grad_score)


def on_device(
    layer_in,
    positions,
    seq_ids,
    norm1_gain,
    norm2_gain,
    w_query,
    w_key,
    w_value,
    w_out,
    w_gate,
    w_up,
    w_down,
    out_grad,
):
    row_count = layer_in.shape[0]
    shard_count = lax.axis_size("seq")
    score_bias = -math.log(shard_count * row_count // 2)
    score_scale = 1.0 / math.sqrt(HD)
    block_seq = seq_ids.reshape(4, row_count // 4)[:, 0]
    order = jnp.argsort(block_seq, stable=True)
    inverse = jnp.argsort(order, stable=True)
    pos_sorted = arrange(positions, order)
    seq_sorted = arrange(seq_ids, order)
    every_pos, every_seq = (
        lax.all_gather(pos_sorted, "seq", axis=0, tiled=True),
        lax.all_gather(seq_sorted, "seq", axis=0, tiled=True),
    )
    query_full, key_full, value_full, out_full, gate_full, up_full, down_full = (
        lax.all_gather(w_query.astype(jnp.bfloat16), "seq", axis=0, tiled=True),
        lax.all_gather(w_key.astype(jnp.bfloat16), "seq", axis=0, tiled=True),
        lax.all_gather(w_value.astype(jnp.bfloat16), "seq", axis=0, tiled=True),
        lax.all_gather(w_out.astype(jnp.bfloat16), "seq", axis=1, tiled=True),
        lax.all_gather(w_gate.astype(jnp.bfloat16), "seq", axis=0, tiled=True),
        lax.all_gather(w_up.astype(jnp.bfloat16), "seq", axis=0, tiled=True),
        lax.all_gather(w_down.astype(jnp.bfloat16), "seq", axis=1, tiled=True),
    )
    head_cols = query_full.shape[1]
    head_count = head_cols // HD
    rot_cos, rot_sin = angles(positions)
    inputs = layer_in.astype(jnp.float32)
    scale_one = lax.rsqrt(jnp.mean(inputs * inputs, axis=-1, keepdims=True) + EPSILON)
    normed_one = (inputs * scale_one * norm1_gain).astype(jnp.bfloat16)
    query_heads = rotate(
        matrix(normed_one, query_full).reshape(row_count, head_count, HD), rot_cos, rot_sin
    ).astype(jnp.bfloat16)
    key_heads = rotate(
        matrix(normed_one, key_full).reshape(row_count, head_count, HD), rot_cos, rot_sin
    ).astype(jnp.bfloat16)
    value_rows = matrix(normed_one, value_full).astype(jnp.bfloat16)
    query_sorted = arrange(query_heads, order)
    key_rows = arrange(key_heads.reshape(row_count, head_cols), order)
    value_sorted = arrange(value_rows, order)
    query_split = regroup(query_sorted, row_count)
    qpos_split = regroup(pos_sorted, row_count)
    zero_out = jnp.zeros((row_count, head_count, HD), jnp.float32)
    key_block = lax.all_gather(key_rows, "seq", axis=0, tiled=True)
    value_block = lax.all_gather(value_sorted, "seq", axis=0, tiled=True)
    piece_rows = key_block.shape[0]
    key_pos = every_pos
    key_heads_piece = key_block.reshape(piece_rows, head_count, HD)
    value_heads_piece = value_block.reshape(piece_rows, head_count, HD)
    term = split_attend(
        query_split,
        regroup(key_heads_piece, row_count),
        regroup(value_heads_piece, row_count),
        qpos_split,
        regroup(key_pos, row_count),
        score_scale,
        score_bias,
    )
    mixed_heads = arrange(term, inverse).reshape(row_count, head_cols).astype(jnp.bfloat16)
    residual = inputs + lax.psum(matrix(mixed_heads, out_full), "tp")
    scale_two = lax.rsqrt(jnp.mean(residual * residual, axis=-1, keepdims=True) + EPSILON)
    normed_two = (residual * scale_two * norm2_gain).astype(jnp.bfloat16)
    gate = matrix(normed_two, gate_full)
    up_proj = matrix(normed_two, up_full)
    gate_sig = jax.nn.sigmoid(gate)
    hidden = (gate * gate_sig * up_proj).astype(jnp.bfloat16)
    layer_out = (
        residual
        + lax.psum(matrix(hidden, down_full).astype(jnp.bfloat16), "tp").astype(jnp.float32)
    ).astype(jnp.bfloat16)
    query_full, key_full, value_full, out_full, gate_full, up_full, down_full = (
        lax.all_gather(w_query.astype(jnp.bfloat16), "seq", axis=0, tiled=True),
        lax.all_gather(w_key.astype(jnp.bfloat16), "seq", axis=0, tiled=True),
        lax.all_gather(w_value.astype(jnp.bfloat16), "seq", axis=0, tiled=True),
        lax.all_gather(w_out.astype(jnp.bfloat16), "seq", axis=1, tiled=True),
        lax.all_gather(w_gate.astype(jnp.bfloat16), "seq", axis=0, tiled=True),
        lax.all_gather(w_up.astype(jnp.bfloat16), "seq", axis=0, tiled=True),
        lax.all_gather(w_down.astype(jnp.bfloat16), "seq", axis=1, tiled=True),
    )
    grad_w_down = inner_rows(hidden, out_grad)
    grad_hidden = outer_cols(out_grad, down_full)
    grad_gate = (grad_hidden * up_proj * gate_sig * (1.0 + gate * (1.0 - gate_sig))).astype(
        jnp.bfloat16
    )
    grad_up = (grad_hidden * gate * gate_sig).astype(jnp.bfloat16)
    grad_w_gate = inner_rows(normed_two, grad_gate)
    grad_w_up = inner_rows(normed_two, grad_up)
    grad_normed_two = lax.psum(
        (outer_cols(grad_gate, gate_full) + outer_cols(grad_up, up_full)).astype(jnp.bfloat16), "tp"
    ).astype(jnp.float32)
    gain_two = jnp.sum(grad_normed_two * residual * scale_two, axis=0)
    effect_two = grad_normed_two * norm2_gain
    grad_resid = (
        out_grad.astype(jnp.float32)
        + scale_two * effect_two
        - residual
        * (scale_two * scale_two * scale_two)
        * jnp.mean(effect_two * residual, axis=-1, keepdims=True)
    )
    grad_resid_low = grad_resid.astype(jnp.bfloat16)
    grad_w_out = inner_rows(mixed_heads, grad_resid_low)
    grad_mixed = (
        outer_cols(grad_resid_low, out_full).astype(jnp.bfloat16).reshape(row_count, head_count, HD)
    )
    grad_sorted = arrange(grad_mixed, order)
    grad_split = regroup(grad_sorted, row_count)
    all_keys, all_values = (
        lax.all_gather(key_rows, "seq", axis=0, tiled=True),
        lax.all_gather(value_sorted, "seq", axis=0, tiled=True),
    )
    key_stack = all_keys.reshape(shard_count, row_count, head_count, HD)
    value_stack = all_values.reshape(shard_count, row_count, head_count, HD)
    kpos_stack = every_pos.reshape(shard_count, row_count)

    def back_step(grad_query, blocks):
        key_block, value_block, key_pos = blocks
        key_split = regroup(key_block, row_count)
        attn_weights, grad_score = split_grads(
            query_split,
            key_split,
            regroup(value_block, row_count),
            grad_split,
            qpos_split,
            regroup(key_pos, row_count),
            score_scale,
            score_bias,
        )
        grad_query = (
            grad_query
            + unsplit(
                jnp.einsum(
                    "shqk,skhd->sqhd", grad_score, key_split, preferred_element_type=jnp.float32
                )
            )
            * score_scale
        )
        key_term = (
            jnp.einsum(
                "shqk,sqhd->skhd", grad_score, query_split, preferred_element_type=jnp.float32
            )
            * score_scale
        )
        value_term = jnp.einsum(
            "shqk,sqhd->skhd", attn_weights, grad_split, preferred_element_type=jnp.float32
        )
        half_rows = row_count // 2
        key_back = jnp.swapaxes(key_term.reshape(2, 1, half_rows, head_cols), 0, 1).reshape(
            row_count, head_cols
        )
        value_back = jnp.swapaxes(value_term.reshape(2, 1, half_rows, head_cols), 0, 1).reshape(
            row_count, head_cols
        )
        return (grad_query, (key_back, value_back))

    grad_query, term_stack = lax.scan(back_step, zero_out, (key_stack, value_stack, kpos_stack))
    key_terms = term_stack[0].reshape(shard_count * row_count, head_cols)
    value_terms = term_stack[1].reshape(shard_count * row_count, head_cols)
    key_sum, value_sum = (
        lax.psum_scatter(
            key_terms.astype(jnp.bfloat16), "seq", scatter_dimension=0, tiled=True
        ).astype(jnp.float32),
        lax.psum_scatter(
            value_terms.astype(jnp.bfloat16), "seq", scatter_dimension=0, tiled=True
        ).astype(jnp.float32),
    )
    grad_query = arrange(grad_query, inverse)
    key_sum = arrange(key_sum, inverse)
    value_sum = arrange(value_sum, inverse)
    grad_query_lin = (
        rotate_back(grad_query, rot_cos, rot_sin).reshape(row_count, head_cols).astype(jnp.bfloat16)
    )
    grad_key_lin = (
        rotate_back(key_sum.reshape(row_count, head_count, HD), rot_cos, rot_sin)
        .reshape(row_count, head_cols)
        .astype(jnp.bfloat16)
    )
    grad_value_low = value_sum.astype(jnp.bfloat16)
    grad_w_query = inner_rows(normed_one, grad_query_lin)
    grad_w_key = inner_rows(normed_one, grad_key_lin)
    grad_w_value = inner_rows(normed_one, grad_value_low)
    grad_normed_one = lax.psum(
        (
            outer_cols(grad_query_lin, query_full)
            + outer_cols(grad_key_lin, key_full)
            + outer_cols(grad_value_low, value_full)
        ).astype(jnp.bfloat16),
        "tp",
    ).astype(jnp.float32)
    gain_one = jnp.sum(grad_normed_one * inputs * scale_one, axis=0)
    effect_one = grad_normed_one * norm1_gain
    in_grad = (
        grad_resid
        + scale_one * effect_one
        - inputs
        * (scale_one * scale_one * scale_one)
        * jnp.mean(effect_one * inputs, axis=-1, keepdims=True)
    )
    summed = (
        lax.psum_scatter(
            grad_w_query.astype(jnp.bfloat16), "seq", scatter_dimension=0, tiled=True
        ).astype(jnp.float32),
        lax.psum_scatter(
            grad_w_key.astype(jnp.bfloat16), "seq", scatter_dimension=0, tiled=True
        ).astype(jnp.float32),
        lax.psum_scatter(
            grad_w_value.astype(jnp.bfloat16), "seq", scatter_dimension=0, tiled=True
        ).astype(jnp.float32),
        lax.psum_scatter(
            grad_w_out.astype(jnp.bfloat16), "seq", scatter_dimension=1, tiled=True
        ).astype(jnp.float32),
        lax.psum_scatter(
            grad_w_gate.astype(jnp.bfloat16), "seq", scatter_dimension=0, tiled=True
        ).astype(jnp.float32),
        lax.psum_scatter(
            grad_w_up.astype(jnp.bfloat16), "seq", scatter_dimension=0, tiled=True
        ).astype(jnp.float32),
        lax.psum_scatter(
            grad_w_down.astype(jnp.bfloat16), "seq", scatter_dimension=1, tiled=True
        ).astype(jnp.float32),
        lax.psum_scatter(
            gain_one.astype(jnp.bfloat16), "seq", scatter_dimension=0, tiled=True
        ).astype(jnp.float32),
        lax.psum_scatter(
            gain_two.astype(jnp.bfloat16), "seq", scatter_dimension=0, tiled=True
        ).astype(jnp.float32),
    )
    return (
        layer_out,
        in_grad,
        summed[7],
        summed[8],
        summed[0],
        summed[1],
        summed[2],
        summed[3],
        summed[4],
        summed[5],
        summed[6],
    )


def solution(mesh):
    in_specs = (
        P("seq", None),
        P("seq"),
        P("seq"),
        P(),
        P(),
        P("seq", "tp"),
        P("seq", "tp"),
        P("seq", "tp"),
        P("tp", "seq"),
        P("seq", "tp"),
        P("seq", "tp"),
        P("tp", "seq"),
        P("seq", None),
    )
    out_specs = (
        P("seq", None),
        P("seq", None),
        P("seq"),
        P("seq"),
        P("seq", "tp"),
        P("seq", "tp"),
        P("seq", "tp"),
        P("tp", "seq"),
        P("seq", "tp"),
        P("seq", "tp"),
        P("tp", "seq"),
    )
    return jax.shard_map(
        on_device, mesh=mesh, in_specs=in_specs, out_specs=out_specs, check_vma=False
    )
```

profile of v0, /device:TPU:0, one launch (start us, length us, event | category | flops | bytes accessed | tf_op | source)
XLA Modules:
  0.0 1521.6 jit_solution(15668812939216227215)
XLA Ops:
  16.8 25.2 %all-gather.17.cloned.1.call-done = bf16[2048,512]{1,0:T(8,128)(2,1)} async-done(((bf16[256,512]{1,0:T(8,128)(2,1)}), bf16[2048,512]{1,0:T(8,128)(2,1)}) %all-gather.17.cloned.1.call-update) | async-done | bytes 2097168 | tf_op jit(solution)/shard_map/all_gather | solution.py:141
  42.0 3.0 fusion.50
  45.0 27.8 %all-gather.15.cloned.1.call-done = bf16[2048,512]{1,0:T(8,128)(2,1)} async-done(((bf16[256,512]{1,0:T(8,128)(2,1)}), bf16[2048,512]{1,0:T(8,128)(2,1)}) %all-gather.15.cloned.1.call-update) | async-done | bytes 2097168 | tf_op jit(solution)/shard_map/all_gather | solution.py:140
  72.8 3.0 fusion.52
  79.1 24.5 %all-gather.11.cloned.1.call-done = bf16[2048,512]{1,0:T(8,128)(2,1)} async-done(((bf16[256,512]{1,0:T(8,128)(2,1)}), bf16[2048,512]{1,0:T(8,128)(2,1)}) %all-gather.11.cloned.1.call-update) | async-done | bytes 2097168 | tf_op jit(solution)/shard_map/all_gather | solution.py:142
  103.7 3.7 convolution_convert_fusion.9
  112.5 13.1 all-gather
  131.7 20.8 %all-gather.19.cloned.1.call-done = bf16[4096,512]{0,1:T(8,128)(2,1)} async-done(((bf16[512,512]{0,1:T(8,128)(2,1)}), bf16[4096,512]{0,1:T(8,128)(2,1)}) %all-gather.19.cloned.1.call-update) | async-done | bytes 4194320 | tf_op jit(solution)/shard_map/all_gather | solution.py:167
  152.5 7.8 reshape.326
  160.3 11.8 copy.119
  172.1 5.2 copy.100
  177.3 23.1 %all-gather.13.cloned.1.call-done = bf16[4096,512]{0,1:T(8,128)(2,1)} async-done(((bf16[512,512]{0,1:T(8,128)(2,1)}), bf16[4096,512]{0,1:T(8,128)(2,1)}) %all-gather.13.cloned.1.call-update) | async-done | bytes 4194320 | tf_op jit(solution)/shard_map/all_gather | solution.py:168
  200.4 7.8 reshape.324
  208.2 11.8 copy.117
  220.0 6.1 copy.93
  226.1 7.4 reshape.215
  233.6 10.7 fusion.33
  248.5 5.0 fusion.37
  256.4 2.9 convert_element_type.200
  262.5 93.8 %all-reduce.8.cloned.1.call-done = f32[512,2048]{1,0:T(8,128)} async-done(((f32[512,2048]{1,0:T(8,128)}), f32[512,2048]{1,0:T(8,128)}) %all-reduce.8.cloned.1.call-update) | async-done | bytes 4194320 | tf_op jit(solution)/shard_map/psum | solution.py:183
  361.5 79.1 %all-gather.23.cloned.1.call-done = bf16[2048,2048]{1,0:T(8,128)(2,1)} async-done(((bf16[256,2048]{1,0:T(8,128)(2,1)}), bf16[2048,2048]{1,0:T(8,128)(2,1)}) %all-gather.23.cloned.1.call-update) | async-done | bytes 8388624 | tf_op jit(solution)/shard_map/all_gather | solution.py:144
  440.6 9.4 fusion.56
  450.0 73.5 %all-gather.25.cloned.1.call-done = bf16[2048,2048]{1,0:T(8,128)(2,1)} async-done(((bf16[256,2048]{1,0:T(8,128)(2,1)}), bf16[2048,2048]{1,0:T(8,128)(2,1)}) %all-gather.25.cloned.1.call-update) | async-done | bytes 8388624 | tf_op jit(solution)/shard_map/all_gather | solution.py:145
  523.5 9.4 fusion.57
  532.9 73.7 %all-gather.27.cloned.1.call-done = bf16[2048,2048]{1,0:T(8,128)(2,1)} async-done(((bf16[2048,256]{1,0:T(8,128)(2,1)}), bf16[2048,2048]{1,0:T(8,128)(2,1)}) %all-gather.27.cloned.1.call-update) | async-done | bytes 8388624 | tf_op jit(solution)/shard_map/all_gather | solution.py:146
  606.7 11.8 multiply_convert_fusion
  618.5 8.5 fusion.58
  627.0 5.8 add_convert_fusion.1
  633.8 6.3 copy.125
  640.1 8.1 copy.106
  648.2 6.4 copy.126
  654.6 8.0 copy.107
  662.6 38.2 %all-reduce.10.cloned.1.call-done = bf16[512,2048]{1,0:T(8,128)(2,1)} async-done(((bf16[512,2048]{1,0:T(8,128)(2,1)}), bf16[512,2048]{1,0:T(8,128)(2,1)}) %all-reduce.10.cloned.1.call-update) | async-done | bytes 2097168 | tf_op jit(solution)/shard_map/psum | solution.py:211
  700.8 4.3 fusion.23
  711.9 172.8 %while.16 = (s32[]{:T(128)}, f32[512,4,128]{2,0,1:T(8,128)}, bf16[8,512,512]{2,1,0:T(8,128)(2,1)}, bf16[8,512,512]{2,1,0:T(8,128)(2,1)}, bf16[8,512,4,128]{3,1,2...) while((s32[]{:T(128)}, f32[512,4,128]{2,0,1:T(8,128)}, ...), condition=%wide.wide.region_9.10_spmd.clone, body=%wide.wide.region_8.9_spmd.clone.sunk | while | flops 678297600 | bytes 37630664 | solution.py:278
  713.7 3.1 add_divide_fusion.4
  734.3 3.1 add_divide_fusion.4
  756.0 3.1 add_divide_fusion.4
  777.7 3.1 add_divide_fusion.4
  799.5 3.1 add_divide_fusion.4
  821.2 3.1 add_divide_fusion.4
  843.0 3.1 add_divide_fusion.4
  864.7 3.1 add_divide_fusion.4
  885.7 4.8 convolution_convert_fusion.3
  892.1 42.8 %reduce-scatter.10.cloned.1.call-done = bf16[512,512]{1,0:T(8,128)(2,1)} async-done(((bf16[4096,512]{1,0:T(8,128)(2,1)}), bf16[512,512]{1,0:T(8,128)(2,1)}) %reduce-scatter.10.cloned.1.call-update) | async-done | bytes 524304 | tf_op jit(solution)/shard_map/reduce_scatter | solution.py:282
  945.5 2.8 convolution_convert_fusion.6
  948.4 2.8 convolution_convert_fusion.5
  951.2 34.1 %reduce-scatter.12.cloned.1.call-done = bf16[512,512]{1,0:T(8,128)(2,1)} async-done(((bf16[4096,512]{1,0:T(8,128)(2,1)}), bf16[512,512]{1,0:T(8,128)(2,1)}) %reduce-scatter.12.cloned.1.call-update) | async-done | bytes 524304 | tf_op jit(solution)/shard_map/reduce_scatter | solution.py:285
  987.8 3.7 convolution_convert_fusion.4
  992.0 10.0 convolution_convert_fusion.7
  1008.0 10.1 convolution_convert_fusion.2
  1018.3 10.1 convolution_convert_fusion.1
  1028.5 10.1 convolution_convert_fusion
  1042.3 16.5 %reduce-scatter.14.cloned.1.call-done = bf16[256,512]{1,0:T(8,128)(2,1)} async-done(((bf16[2048,512]{1,0:T(8,128)(2,1)}), bf16[256,512]{1,0:T(8,128)(2,1)}) %reduce-scatter.14.cloned.1.call-update) | async-done | bytes 262160 | tf_op jit(solution)/shard_map/reduce_scatter | solution.py:322
  1060.5 34.8 %reduce-scatter.16.cloned.1.call-done = bf16[256,512]{1,0:T(8,128)(2,1)} async-done(((bf16[2048,512]{1,0:T(8,128)(2,1)}), bf16[256,512]{1,0:T(8,128)(2,1)}) %reduce-scatter.16.cloned.1.call-update) | async-done | bytes 262160 | tf_op jit(solution)/shard_map/reduce_scatter | solution.py:325
  1097.2 34.9 %reduce-scatter.18.cloned.1.call-done = bf16[256,512]{1,0:T(8,128)(2,1)} async-done(((bf16[2048,512]{1,0:T(8,128)(2,1)}), bf16[256,512]{1,0:T(8,128)(2,1)}) %reduce-scatter.18.cloned.1.call-update) | async-done | bytes 262160 | tf_op jit(solution)/shard_map/reduce_scatter | solution.py:328
  1133.9 105.0 %all-reduce.12.cloned.1.call-done = (bf16[512,2048]{1,0:T(8,128)(2,1)}, bf16[512,2048]{1,0:T(8,128)(2,1)}) async-done(((bf16[512,2048]{1,0:T(8,128)(2,1)}, bf16[512,2048]{1,0:T(8,128)(2,1)}), (bf16[512,2048]{1,0:T(8,128)(2,1)}, bf16[512,2048]{1,0:T(8,128)(2,1)})) %all-reduce.12.cloned.1.call-update) | async-done | bytes 4194320 | tf_op jit(solution)/shard_map/psum | solution.py:192
  1238.8 3.2 fusion.30
  1242.0 17.2 %all-reduce.2 = (bf16[2048]{0:T(1024)(128)(2,1)S(1)}, bf16[2048]{0:T(1024)(128)(2,1)S(1)}) all-reduce(bf16[2048]{0:T(1024)(128)(2,1)S(1)} %get-tuple-element.137, bf16[2048]{0:T(1024)(128)(2,1)S(1)} %get-tuple-element.135), channel_id=4, replica_groups=mesh['seq'=8,'tp'=4] {'seq'}, use_global_device_ids=true, to_apply=%region_15.16.clone | all-reduce | flops 4096 | bytes 16384
  1260.5 5.1 add_convert_fusion.2
  1265.6 3.2 fusion.18
  1268.8 62.6 %reduce-scatter.22.cloned.1.call-done = bf16[256,2048]{1,0:T(8,128)(2,1)} async-done(((bf16[2048,2048]{1,0:T(8,128)(2,1)}), bf16[256,2048]{1,0:T(8,128)(2,1)}) %reduce-scatter.22.cloned.1.call-update) | async-done | bytes 1048592 | tf_op jit(solution)/shard_map/reduce_scatter | solution.py:334
  1334.2 87.3 %reduce-scatter.24.cloned.1.call-done = bf16[256,2048]{1,0:T(8,128)(2,1)} async-done(((bf16[2048,2048]{1,0:T(8,128)(2,1)}), bf16[256,2048]{1,0:T(8,128)(2,1)}) %reduce-scatter.24.cloned.1.call-update) | async-done | bytes 1048592 | tf_op jit(solution)/shard_map/reduce_scatter | solution.py:337
  1424.2 87.6 %reduce-scatter.26.cloned.1.call-done = bf16[2048,256]{1,0:T(8,128)(2,1)} async-done(((bf16[2048,2048]{1,0:T(8,128)(2,1)}), bf16[2048,256]{1,0:T(8,128)(2,1)}) %reduce-scatter.26.cloned.1.call-update) | async-done | bytes 1048592 | tf_op jit(solution)/shard_map/reduce_scatter | solution.py:340
  (370 shorter events, 234.6 us)
Async XLA Ops:
  7.2 8.0 copy-start.5
  7.2 34.9 %copy-start.29 = (f32[2048]{0:T(1024)S(1)}, f32[2048]{0:T(1024)}, u32[]{:S(2)}) copy-start(f32[2048]{0:T(1024)} %param.18) | copy-start | bytes 24580
  7.2 34.8 %all-gather.17.cloned.1.call-start = ((), (), s32[]{:S(2)}) async-start(), calls=%async_computation.12 | async-start | bytes 2359296 | tf_op jit(solution)/shard_map/all_gather | solution.py:141
  9.2 63.7 %all-gather.15.cloned.1.call-start = ((), (), s32[]{:S(2)}) async-start(), calls=%async_computation.11 | async-start | bytes 2359296 | tf_op jit(solution)/shard_map/all_gather | solution.py:140
  11.0 92.6 %all-gather.11.cloned.1.call-start = ((), (), s32[]{:S(2)}) async-start(), calls=%async_computation.9 | async-start | bytes 2359296 | tf_op jit(solution)/shard_map/all_gather | solution.py:142
  12.9 139.6 %all-gather.19.cloned.1.call-start = ((), (), s32[]{:S(2)}) async-start(), calls=%async_computation.13 | async-start | bytes 4718592 | tf_op jit(solution)/shard_map/all_gather | solution.py:167
  16.2 87.4 %copy-start.31 = (f32[512]{0:T(512)}, f32[512]{0:T(512)S(1)}, u32[]{:S(2)}) copy-start(f32[512]{0:T(512)S(1)} %get-tuple-element.187) | copy-start | bytes 6148
  16.8 59.0 %copy-start.20 = (f32[512,64]{0,1:T(8,128)}, f32[512,64]{0,1:T(8,128)S(1)}, u32[]{:S(2)}) copy-start(f32[512,64]{0,1:T(8,128)S(1)} %get-tuple-element.184) | copy-start | bytes 393220
  16.8 59.0 %copy-start.22 = (f32[512,64]{0,1:T(8,128)}, f32[512,64]{0,1:T(8,128)S(1)}, u32[]{:S(2)}) copy-start(f32[512,64]{0,1:T(8,128)S(1)} %get-tuple-element.185) | copy-start | bytes 393220
  79.1 32.9 %copy-start.26 = (s32[512]{0:T(512)S(1)}, s32[512]{0:T(512)}, u32[]{:S(2)}) copy-start(s32[512]{0:T(512)} %param.16) | copy-start | bytes 6148
  79.1 121.3 %all-gather.13.cloned.1.call-start = ((), (), s32[]{:S(2)}) async-start(), calls=%async_computation.10 | async-start | bytes 4718592 | tf_op jit(solution)/shard_map/all_gather | solution.py:168
  107.3 20.8 %copy-start.25 = (bf16[512,4,64]{0,2,1:T(8,128)(2,1)S(1)}, bf16[512,4,64]{0,2,1:T(8,128)(2,1)}, u32[]{:S(2)}) copy-start(bf16[512,4,64]{0,2,1:T(8,128)(2,1)} %get-tuple-element.174) | copy-start | bytes 786436
  107.3 21.1 %copy-start.24 = (bf16[512,4,64]{0,2,1:T(8,128)(2,1)S(1)}, bf16[512,4,64]{0,2,1:T(8,128)(2,1)}, u32[]{:S(2)}) copy-start(bf16[512,4,64]{0,2,1:T(8,128)(2,1)} %get-tuple-element.175) | copy-start | bytes 786436
  110.1 138.4 %all-gather.21.cloned.1.call-start = ((), (), s32[]{:S(2)}) async-start(), calls=%async_computation.14 | async-start | bytes 2359296 | tf_op jit(solution)/shard_map/all_gather | solution.py:143
  111.9 244.4 %all-reduce.8.cloned.1.call-start = ((), (), s32[]{:S(2)}) async-start(), calls=%async_computation.15 | async-start | bytes 8388608 | tf_op jit(solution)/shard_map/psum | solution.py:183
  112.5 520.4 %copy-start.28 = (s32[4,128]{1,0:T(4,128)}, s32[4,128]{1,0:T(4,128)S(1)}, u32[]{:S(2)}) copy-start(s32[4,128]{1,0:T(4,128)S(1)} %gather_fusion.1) | copy-start | bytes 6148
  248.4 5.1 copy-start.18
  253.5 187.1 %all-gather.23.cloned.1.call-start = ((), (), s32[]{:S(2)}) async-start(), calls=%async_computation.16 | async-start | bytes 9437184 | tf_op jit(solution)/shard_map/all_gather | solution.py:144
  256.3 267.2 %all-gather.25.cloned.1.call-start = ((), (), s32[]{:S(2)}) async-start(), calls=%async_computation.17 | async-start | bytes 9437184 | tf_op jit(solution)/shard_map/all_gather | solution.py:145
  259.3 347.4 %all-gather.27.cloned.1.call-start = ((), (), s32[]{:S(2)}) async-start(), calls=%async_computation.18 | async-start | bytes 9437184 | tf_op jit(solution)/shard_map/all_gather | solution.py:146
  262.0 99.1 %copy-start.27 = (f32[2048]{0:T(1024)S(1)}, f32[2048]{0:T(1024)}, u32[]{:S(2)}) copy-start(f32[2048]{0:T(1024)} %param.19) | copy-start | bytes 24580
  262.1 438.8 %all-reduce.10.cloned.1.call-start = ((), (), s32[]{:S(2)}) async-start(), calls=%async_computation.19 | async-start | bytes 4194304 | tf_op jit(solution)/shard_map/psum | solution.py:211
  359.1 2.0 copy-start
  361.5 162.0 %copy-start.12 = (bf16[512,2048]{1,0:T(8,128)(2,1)}, bf16[512,2048]{1,0:T(8,128)(2,1)S(1)}, u32[]{:S(2)}) copy-start(bf16[512,2048]{1,0:T(8,128)(2,1)S(1)} %multiply_convert_fusion.3) | copy-start | bytes 6291460
  618.5 8.5 copy-start.37
  618.5 8.5 copy-start.36
  618.5 8.5 copy-start.34
  632.8 302.1 %reduce-scatter.10.cloned.1.call-start = ((), (), s32[]{:S(2)}) async-start(), calls=%async_computation.20 | async-start | bytes 4718592 | tf_op jit(solution)/shard_map/reduce_scatter | solution.py:282
  654.6 50.6 %copy-start.15 = (bf16[512,2048]{1,0:T(8,128)(2,1)S(1)}, bf16[512,2048]{1,0:T(8,128)(2,1)}, u32[]{:S(2)}) copy-start(bf16[512,2048]{1,0:T(8,128)(2,1)} %param.27) | copy-start | bytes 6291460
  700.8 4.4 copy-start.1
  700.8 4.7 copy-start.9
  705.6 3.3 copy-start.14
  706.8 2.0 copy-start.7
  727.8 2.7 copy-start.3
  748.3 2.7 copy-start.3
  770.1 2.7 copy-start.3
  791.8 2.7 copy-start.3
  813.6 2.7 copy-start.3
  835.3 2.7 copy-start.3
  857.0 2.7 copy-start.3
  878.8 2.8 copy-start.3
  884.7 1.1 copy-start.19
  884.7 100.7 %reduce-scatter.12.cloned.1.call-start = ((), (), s32[]{:S(2)}) async-start(), calls=%async_computation.21 | async-start | bytes 4718592 | tf_op jit(solution)/shard_map/reduce_scatter | solution.py:285
  885.5 5.2 copy-start.4
  885.5 155.0 %reduce-scatter.20.cloned.1.call-start = ((), (), s32[]{:S(2)}) async-start(), calls=%async_computation.25 | async-start | bytes 2359296 | tf_op jit(solution)/shard_map/reduce_scatter | solution.py:331
  890.6 168.2 %reduce-scatter.14.cloned.1.call-start = ((), (), s32[]{:S(2)}) async-start(), calls=%async_computation.22 | async-start | bytes 2359296 | tf_op jit(solution)/shard_map/reduce_scatter | solution.py:322
  937.0 6.8 copy-start.21
  937.1 6.8 copy-start.23
  939.0 6.5 copy-start.6
  939.0 6.5 copy-start.30
  939.0 6.5 copy-start.32
  948.3 147.1 %reduce-scatter.16.cloned.1.call-start = ((), (), s32[]{:S(2)}) async-start(), calls=%async_computation.23 | async-start | bytes 2359296 | tf_op jit(solution)/shard_map/reduce_scatter | solution.py:325
  951.2 180.9 %reduce-scatter.18.cloned.1.call-start = ((), (), s32[]{:S(2)}) async-start(), calls=%async_computation.24 | async-start | bytes 2359296 | tf_op jit(solution)/shard_map/reduce_scatter | solution.py:328
  991.5 247.3 %all-reduce.12.cloned.1.call-start = ((), (), s32[]{:S(2)}) async-start(), calls=%async_computation.29 | async-start | bytes 8388608 | tf_op jit(solution)/shard_map/psum | solution.py:192
  992.0 10.0 copy-start.16
  1002.0 1.6 copy-start.17
  1003.6 1.6 copy-start.11
  1003.6 1.7 copy-start.13
  1007.9 323.5 %reduce-scatter.22.cloned.1.call-start = ((), (), s32[]{:S(2)}) async-start(), calls=%async_computation.26 | async-start | bytes 9437184 | tf_op jit(solution)/shard_map/reduce_scatter | solution.py:334
  1018.1 403.4 %reduce-scatter.24.cloned.1.call-start = ((), (), s32[]{:S(2)}) async-start(), calls=%async_computation.27 | async-start | bytes 9437184 | tf_op jit(solution)/shard_map/reduce_scatter | solution.py:337
  1028.4 483.4 %reduce-scatter.26.cloned.1.call-start = ((), (), s32[]{:S(2)}) async-start(), calls=%async_computation.28 | async-start | bytes 9437184 | tf_op jit(solution)/shard_map/reduce_scatter | solution.py:340
  1260.4 5.1 copy-start.8
  1260.4 5.1 copy-start.10
  1260.4 5.1 copy-start.33
  (9 other events, 7.0 us)
Sparse Core Ops, SparseCore 0:
  10.2 31.7 all-gather.16
  44.2 28.5 all-gather.14
  75.0 28.5 all-gather.10
  105.7 46.7 all-gather.18
  154.5 45.8 all-gather.12
  202.4 29.5 all-gather.20
  253.6 102.5 all-reduce.7
  358.5 82.0 all-gather.22
  442.9 80.5 all-gather.24
  525.6 81.0 all-gather.26
  632.9 67.8 all-reduce.9
  884.8 50.0 reduce-scatter.9
  937.2 48.1 reduce-scatter.11
  987.5 33.9 reduce-scatter.19
  1024.3 34.4 reduce-scatter.13
  1060.9 34.4 reduce-scatter.15
  1097.5 34.5 reduce-scatter.17
  1136.0 102.7 all-reduce.11
  1241.2 90.1 reduce-scatter.21
  1333.6 87.7 reduce-scatter.23
  1423.9 87.9 reduce-scatter.25
where the time goes:
time: 1530 us; the launch traced here: 1520 us
  waiting for transfers between devices  986 us (64%)
  local copies, waits for them, and re-layouts  209 us (14%)
  matrix products  195 us (13%)
  other arithmetic  81.9 us (5%)
  blocking collectives  30.2 us (2%)
  between operations  15.9 us (1%)
    psum x1, waiting for transfers between devices, on_device(): lax.psum(matrix(hidden, down_full).astype(jnp.bfloat16), 'tp')  105 us
    psum x1, waiting for transfers between devices, on_device(): residual = inputs + lax.psum(matrix(mixed_heads, out_full), 'tp')  93.8 us
    reduce_scatter x1, waiting for transfers between devices, on_device(): lax.psum_scatter(grad_w_down.astype(jnp.bfloat16), 'seq', scatter_dimensi...  87.6 us
    reduce_scatter x1, waiting for transfers between devices, on_device(): lax.psum_scatter(grad_w_up.astype(jnp.bfloat16), 'seq', scatter_dimension...  87.3 us
    all_gather x1, waiting for transfers between devices, on_device(): lax.all_gather(w_gate.astype(jnp.bfloat16), 'seq', axis=0, tiled=True)  79.1 us
    all_gather x1, waiting for transfers between devices, on_device(): lax.all_gather(w_down.astype(jnp.bfloat16), 'seq', axis=1, tiled=True)  73.7 us
    all_gather x1, waiting for transfers between devices, on_device(): lax.all_gather(w_up.astype(jnp.bfloat16), 'seq', axis=0, tiled=True)  73.5 us
    reduce_scatter x1, waiting for transfers between devices, on_device(): lax.psum_scatter(grad_w_gate.astype(jnp.bfloat16), 'seq', scatter_dimensi...  62.6 us
  transfers between devices with their start and end apart: 21, of which 19 were waited for; matrix products, arithmetic and copies ran while one was open for 17% of the time, Pallas kernels for 0%

commit v1 on v0

v1 whole, which is shorter than its diff:
```python
import functools
import math

import jax
import jax.numpy as jnp
from jax import lax
from jax.experimental import pallas as pl
from jax.experimental.pallas import tpu as pltpu
from jax.sharding import Mesh
from jax.sharding import PartitionSpec as P

HD = 128
EPSILON = 1e-06
LOG2E = 1.4426950408889634
BF = jnp.bfloat16
F32 = jnp.float32


def dot_nt(left, right):
    return lax.dot_general(left, right, (((1,), (1,)), ((), ())), preferred_element_type=F32)


def dot_nn(left, right):
    return lax.dot_general(left, right, (((1,), (0,)), ((), ())), preferred_element_type=F32)


def dot_tn(left, right):
    return lax.dot_general(left, right, (((0,), (0,)), ((), ())), preferred_element_type=F32)


def attend_kernel(
    tab_ref, qkv_ref, cos_ref, sin_ref, out_ref, q_ref, k_ref, v_ref, acc_ref, *, chunk, tile, bias2
):
    groups, rows, _ = qkv_ref.shape
    per_group = rows // chunk
    length = groups * rows
    for j in range(length // chunk):
        g, s = divmod(j, per_group)
        here = pl.ds(s * chunk, chunk)
        there = pl.ds(pl.multiple_of(tab_ref[j] * chunk, chunk), chunk)
        cos = cos_ref[there, :]
        sin = sin_ref[there, :]
        q = qkv_ref[g, here, 0:HD].astype(F32)
        k = qkv_ref[g, here, HD : 2 * HD].astype(F32)
        q_ref[there, :] = (q * cos - pltpu.roll(q, HD // 2, 1) * sin).astype(BF)
        k_ref[there, :] = (k * cos - pltpu.roll(k, HD // 2, 1) * sin).astype(BF)
        v_ref[there, :] = qkv_ref[g, here, 2 * HD : 3 * HD]
    slope = -LOG2E / math.sqrt(HD)

    def part(i, j, masked):
        qs = q_ref[pl.ds(i * tile, tile), :]
        ks = k_ref[pl.ds(j * tile, tile), :]
        vs = v_ref[pl.ds(j * tile, tile), :]
        sig = 1.0 / (1.0 + jnp.exp2(dot_nt(qs, ks) * slope + bias2))
        if masked:
            row = lax.broadcasted_iota(jnp.int32, (tile, tile), 0)
            col = lax.broadcasted_iota(jnp.int32, (tile, tile), 1)
            sig = jnp.where(col <= row, sig, 0.0)
        return dot_nn(sig.astype(BF), vs)

    def query(i, carry):
        own = pl.ds(pl.multiple_of(i * tile, tile), tile)
        acc_ref[own, :] = part(i, i, True)

        def key(j, carry):
            acc_ref[own, :] += part(i, j, False)
            return carry

        lax.fori_loop(0, i, key, 0)
        return carry

    lax.fori_loop(0, length // tile, query, 0)
    for j in range(length // chunk):
        g, s = divmod(j, per_group)
        there = pl.ds(pl.multiple_of(tab_ref[j] * chunk, chunk), chunk)
        out_ref[g, pl.ds(s * chunk, chunk), :] = acc_ref[there, :].astype(BF)


def attend_back_kernel(
    tab_ref,
    grad_ref,
    q_ref,
    k_ref,
    v_ref,
    cos_ref,
    sin_ref,
    out_ref,
    do_ref,
    dq_ref,
    dk_ref,
    dv_ref,
    *,
    chunk,
    tile,
    bias2,
):
    groups, rows, _ = grad_ref.shape
    per_group = rows // chunk
    length = groups * rows
    for j in range(length // chunk):
        g, s = divmod(j, per_group)
        there = pl.ds(pl.multiple_of(tab_ref[j] * chunk, chunk), chunk)
        do_ref[there, :] = grad_ref[g, pl.ds(s * chunk, chunk), :]
    slope = -LOG2E / math.sqrt(HD)
    scale = 1.0 / math.sqrt(HD)

    def part(i, j, masked):
        qi = pl.ds(pl.multiple_of(i * tile, tile), tile)
        kj = pl.ds(pl.multiple_of(j * tile, tile), tile)
        qs, ks, vs, dos = q_ref[qi, :], k_ref[kj, :], v_ref[kj, :], do_ref[qi, :]
        sig = 1.0 / (1.0 + jnp.exp2(dot_nt(ks, qs) * slope + bias2))
        dsc = dot_nt(vs, dos) * sig * (1.0 - sig)
        if masked:
            row = lax.broadcasted_iota(jnp.int32, (tile, tile), 0)
            col = lax.broadcasted_iota(jnp.int32, (tile, tile), 1)
            sig = jnp.where(row <= col, sig, 0.0)
            dsc = jnp.where(row <= col, dsc, 0.0)
        dsc = dsc.astype(BF)
        dv = dot_nn(sig.astype(BF), dos)
        dk = dot_nn(dsc, qs)
        dq = dot_tn(dsc, ks)
        if masked:
            dq_ref[qi, :] = dq
            dk_ref[kj, :] = dk
            dv_ref[kj, :] = dv
        else:
            dq_ref[qi, :] += dq
            dk_ref[kj, :] += dk
            dv_ref[kj, :] += dv

    def query(i, carry):
        part(i, i, True)

        def key(j, carry):
            part(i, j, False)
            return carry

        lax.fori_loop(0, i, key, 0)
        return carry

    lax.fori_loop(0, length // tile, query, 0)
    for j in range(length // chunk):
        g, s = divmod(j, per_group)
        here = pl.ds(s * chunk, chunk)
        there = pl.ds(pl.multiple_of(tab_ref[j] * chunk, chunk), chunk)
        cos = cos_ref[there, :] * scale
        sin = sin_ref[there, :] * scale
        dq = dq_ref[there, :]
        dk = dk_ref[there, :]
        out_ref[g, here, 0:HD] = (dq * cos + pltpu.roll(dq, HD // 2, 1) * sin).astype(BF)
        out_ref[g, here, HD : 2 * HD] = (dk * cos + pltpu.roll(dk, HD // 2, 1) * sin).astype(BF)
        out_ref[g, here, 2 * HD : 3 * HD] = dv_ref[there, :].astype(BF)


def attend(table, qkv, cos, sin, chunk, length):
    groups, rows, _ = qkv.shape
    tile = min(512, length)
    full = jax.ShapeDtypeStruct((length, HD), BF)
    vm = pl.BlockSpec(memory_space=pltpu.VMEM)
    return pl.pallas_call(
        functools.partial(attend_kernel, chunk=chunk, tile=tile, bias2=math.log2(length)),
        out_shape=(jax.ShapeDtypeStruct((groups, rows, HD), BF), full, full, full),
        in_specs=[pl.BlockSpec(memory_space=pltpu.SMEM), vm, vm, vm],
        out_specs=(vm, vm, vm, vm),
        scratch_shapes=[pltpu.VMEM((length, HD), F32)],
        compiler_params=pltpu.CompilerParams(vmem_limit_bytes=40 << 20),
        cost_estimate=pl.CostEstimate(
            flops=2 * length * length * HD,
            transcendentals=length * length,
            bytes_accessed=length * HD * 24,
        ),
        name="attend",
    )(table, qkv, cos, sin)


def attend_back(table, grad, q, k, v, cos, sin, chunk, length):
    groups, rows, _ = grad.shape
    tile = min(512, length)
    vm = pl.BlockSpec(memory_space=pltpu.VMEM)
    return pl.pallas_call(
        functools.partial(attend_back_kernel, chunk=chunk, tile=tile, bias2=math.log2(length)),
        out_shape=jax.ShapeDtypeStruct((groups, rows, 3 * HD), BF),
        in_specs=[pl.BlockSpec(memory_space=pltpu.SMEM)] + [vm] * 6,
        out_specs=vm,
        scratch_shapes=[pltpu.VMEM((length, HD), BF)] + [pltpu.VMEM((length, HD), F32)] * 3,
        compiler_params=pltpu.CompilerParams(vmem_limit_bytes=40 << 20),
        cost_estimate=pl.CostEstimate(
            flops=5 * length * length * HD,
            transcendentals=length * length,
            bytes_accessed=length * HD * 24,
        ),
        name="attend_back",
    )(table, grad, q, k, v, cos, sin)


def build(z_size, tp_size):
    shards = 2 * z_size
    ring = list(range(0, 1)) + list(range(1, z_size, 2)) + list(range(z_size - 2, 0, -2))
    place = [ring.index(z) for z in range(z_size)]
    forward = [(ring[i], ring[(i + 1) % z_size]) for i in range(z_size)]
    backward = [(b, a) for a, b in forward]
    half_ring = z_size // 2
    offsets = [0]
    for k in range(1, half_ring):
        offsets += [-k, k]
    offsets += [half_ring]
    holder = [[ring[(place[z] + off) % z_size] for off in offsets] for z in range(z_size)]
    swap_core = [(0, 1), (1, 0)]

    def gather_ring(x):
        chunks = [x]
        ahead = back = x
        for _ in range(1, half_ring):
            ahead = lax.ppermute(ahead, "z", forward)
            back = lax.ppermute(back, "z", backward)
            chunks += [ahead, back]
        mid = x.shape[0] // 2
        one = lax.ppermute(ahead[:mid], "z", forward)
        two = lax.ppermute(back[mid:], "z", backward)
        return jnp.concatenate(chunks + [one, two], axis=0)

    def scatter_ring(parts):
        mid = parts.shape[1] // 2
        last = len(offsets) - 1
        one = lax.ppermute(parts[last, :mid].astype(BF), "z", forward)
        two = lax.ppermute(parts[last, mid:].astype(BF), "z", backward)
        for k in range(half_ring - 1, 0, -1):
            fwd, bwd = parts[offsets.index(k)], parts[offsets.index(-k)]
            if k == half_ring - 1:
                fwd = jnp.concatenate([fwd[:mid] + one.astype(F32), fwd[mid:]], axis=0)
                bwd = jnp.concatenate([bwd[:mid], bwd[mid:] + two.astype(F32)], axis=0)
            else:
                fwd = fwd + one.astype(F32)
                bwd = bwd + two.astype(F32)
            one = lax.ppermute(fwd.astype(BF), "z", forward)
            two = lax.ppermute(bwd.astype(BF), "z", backward)
        return parts[0] + one.astype(F32) + two.astype(F32)

    def gather_tp(x):
        if tp_size != 4:
            return lax.all_gather(x, "tp", axis=0)
        index = lax.axis_index("tp")
        over_x = [(0, 1), (1, 0), (2, 3), (3, 2)]
        over_y = [(0, 2), (2, 0), (1, 3), (3, 1)]
        mid = x.shape[0] // 2
        near_x = lax.ppermute(x, "tp", over_x)
        near_y = lax.ppermute(x, "tp", over_y)
        far = jnp.concatenate(
            [lax.ppermute(near_y[:mid], "tp", over_x), lax.ppermute(near_x[mid:], "tp", over_y)]
        )
        return jnp.take(
            jnp.stack([x, near_x, near_y, far]),
            jnp.bitwise_xor(jnp.arange(4, dtype=jnp.int32), index),
            axis=0,
            mode="clip",
        )

    def on_device(
        layer_in,
        positions,
        seq_ids,
        norm1_gain,
        norm2_gain,
        w_query,
        w_key,
        w_value,
        w_out,
        w_gate,
        w_up,
        w_down,
        out_grad,
    ):
        z, core, tp = lax.axis_index("z"), lax.axis_index("core"), lax.axis_index("tp")
        rows, width = layer_in.shape
        block = rows // 4
        own = rows // tp_size
        group = own * z_size
        length = rows * shards // 2
        k_rows = width // shards
        heads = w_query.shape[1] * tp_size // HD
        heads_here = heads // z_size
        plain = w_query.shape[1] == z_size * HD and heads_here == tp_size

        def permute(x):
            lead = x.shape[:-1]
            return jnp.swapaxes(x.reshape(lead + (z_size, 2, k_rows)), -3, -2).reshape(x.shape)

        def restore(x):
            lead = x.shape[:-1]
            return jnp.swapaxes(x.reshape(lead + (2, z_size, k_rows)), -3, -2).reshape(x.shape)

        key = seq_ids.reshape(4, block)[:, 0] * (4 * length) + positions.reshape(4, block)[:, 0]
        rank = jnp.sum((key[None, :] < key[:, None]).astype(jnp.int32), axis=1)
        source_core = tp // (tp_size // 2)
        offset = (tp % (tp_size // 2)) * own

        def piece(x, seq):
            wanted = 2 * seq + offset // block
            start = jnp.sum(jnp.where(rank == wanted, jnp.arange(4, dtype=jnp.int32), 0)) * block
            return lax.dynamic_slice(x, (start + offset % block, 0), (own, width))

        both_self = jnp.stack([piece(layer_in, core), piece(out_grad, core)])
        both_other = jnp.stack([piece(layer_in, 1 - core), piece(out_grad, 1 - core)])
        both_other = lax.ppermute(both_other, "core", swap_core)
        both = permute(jnp.where(core == source_core, both_self, both_other))
        x_own = both[0].astype(F32)
        gy_own = both[1]
        gain1 = permute(norm1_gain)
        gain2 = permute(norm2_gain)
        scale1 = lax.rsqrt(jnp.mean(x_own * x_own, axis=-1, keepdims=True) + EPSILON)
        xn1 = gather_ring((x_own * scale1 * gain1).astype(BF))

        def exchange(w, split, concat):
            return lax.all_to_all(w, "z", split_axis=split, concat_axis=concat, tiled=True)

        def gather_rows(w):
            return lax.all_gather(w, ("core", "tp"), axis=0, tiled=False).reshape(
                (2, tp_size) + w.shape
            )

        def gather_cols(w):
            return lax.all_gather(w, ("tp", "core"), axis=0, tiled=False).reshape(
                tp_size, 2 * w.shape[0], w.shape[1]
            )

        if plain:
            qkv_low = jnp.stack([w_query, w_key, w_value], axis=1).astype(BF)
            qkv_low = qkv_low.reshape(k_rows, 3, z_size, HD).swapaxes(1, 2)
            qkv_low = exchange(qkv_low.reshape(k_rows, z_size * 3 * HD), 1, 0)
            qkv_w = gather_cols(qkv_low)
            out_w = gather_rows(exchange(w_out.astype(BF), 0, 1))
            out_w = out_w.reshape(2, tp_size * HD, width // 2)
        else:
            first = z * heads_here * HD

            def whole(w, cols):
                w = lax.all_gather(w.astype(BF), "tp", axis=cols, tiled=True)
                return lax.all_gather(w, ("z", "core"), axis=1 - cols, tiled=True)

            def columns(w):
                w = lax.dynamic_slice(whole(w, 1), (0, first), (width, heads_here * HD))
                return permute(w.T).reshape(heads_here, HD, width).swapaxes(1, 2)

            qkv_w = jnp.concatenate([columns(w_query), columns(w_key), columns(w_value)], axis=2)
            out_w = lax.dynamic_slice(whole(w_out, 0), (first, 0), (heads_here * HD, width))
            out_w = permute(out_w).reshape(heads_here * HD, 2, width // 2).swapaxes(0, 1)
        gate_w = gather_cols(exchange(w_gate.astype(BF), 1, 0))
        up_w = gather_cols(exchange(w_up.astype(BF), 1, 0))
        down_w = gather_rows(exchange(w_down.astype(BF), 0, 1))

        half = HD // 2
        frequency = jnp.power(F32(10000.0), -jnp.arange(half, dtype=F32) / half)
        phase = jnp.arange(length, dtype=jnp.int32).astype(F32)[:, None] * frequency[None, :]
        rot_cos, rot_sin = jnp.cos(phase), jnp.sin(phase)
        cos = jnp.concatenate([rot_cos, rot_cos], axis=1)
        sin = jnp.concatenate([rot_sin, -rot_sin], axis=1)
        t_all = jnp.arange(tp_size, dtype=jnp.int32)[:, None]
        z_all = jnp.asarray(holder, jnp.int32)[z][None, :]
        off_all = (t_all % (tp_size // 2)) * own
        shard_all = 2 * z_all + t_all // (tp_size // 2)
        block_all = jnp.where(off_all < block, shard_all, 2 * shards - 1 - shard_all)
        table = ((block_all * block + off_all % block) // own).reshape(-1)

        def to_heads(x):
            if heads_here == tp_size:
                return lax.all_to_all(x, "tp", split_axis=0, concat_axis=0, tiled=True)
            every = lax.all_gather(x, "tp", axis=0)
            return lax.dynamic_index_in_dim(
                every, tp * heads_here // tp_size, axis=1, keepdims=False
            )

        def to_tokens(x):
            if heads_here == tp_size:
                return lax.all_to_all(x, "tp", split_axis=0, concat_axis=0, tiled=True)
            every = lax.all_gather(x, "tp", axis=0)[:: tp_size // heads_here]
            return lax.dynamic_index_in_dim(every, tp, axis=1, keepdims=False)

        qkv = jnp.einsum("mk,tkn->tmn", xn1, qkv_w, preferred_element_type=F32).astype(BF)
        heads_out, q, k, v = attend(table, to_heads(qkv), cos, sin, own, length)
        mixed = jnp.swapaxes(to_tokens(heads_out), 0, 1).reshape(group, heads_here * HD)
        attn = jnp.einsum("mh,chd->mcd", mixed, out_w, preferred_element_type=F32)
        hres = x_own + scatter_ring(attn.reshape(z_size, own, width))

        scale2 = lax.rsqrt(jnp.mean(hres * hres, axis=-1, keepdims=True) + EPSILON)
        gy = gather_ring(gy_own)
        xn2 = gather_ring((hres * scale2 * gain2).astype(BF))
        dhid = jnp.einsum(
            "mcd,ctfd->tmf",
            gy.reshape(group, 2, width // 2),
            down_w,
            preferred_element_type=F32,
        )
        gate = jnp.einsum("mk,tkn->tmn", xn2, gate_w, preferred_element_type=F32)
        up = jnp.einsum("mk,tkn->tmn", xn2, up_w, preferred_element_type=F32)
        sig = jax.nn.sigmoid(gate)
        hid = (gate * sig * up).astype(BF)
        dgate = (dhid * up * sig * (1.0 + gate * (1.0 - sig))).astype(BF)
        dup = (dhid * gate * sig).astype(BF)
        dxn2 = jnp.einsum("tmn,tkn->mk", dgate, gate_w, preferred_element_type=F32) + jnp.einsum(
            "tmn,tkn->mk", dup, up_w, preferred_element_type=F32
        )
        dxn2 = scatter_ring(dxn2.reshape(z_size, own, width))
        ffn = jnp.einsum("tmf,ctfd->mcd", hid, down_w, preferred_element_type=F32)
        layer_own = hres + scatter_ring(ffn.reshape(z_size, own, width))

        def reduce_cols(part, out_cols):
            part = part.astype(BF).reshape(2 * tp_size, width // 2, part.shape[2])
            part = lax.psum_scatter(part, ("tp", "core"), scatter_dimension=0, tiled=False)
            return exchange(part, 0, 1)

        def reduce_rows(part):
            part = part.astype(BF).reshape((2 * tp_size,) + part.shape[2:])
            part = lax.psum_scatter(part, ("core", "tp"), scatter_dimension=0, tiled=False)
            return exchange(part, 1, 0)

        g_down = reduce_rows(
            jnp.einsum(
                "tmf,mcd->ctfd",
                hid,
                gy.reshape(group, 2, width // 2),
                preferred_element_type=F32,
            )
        ).astype(F32)
        g_gate = reduce_cols(
            jnp.einsum("mk,tmn->tkn", xn2, dgate, preferred_element_type=F32), None
        ).astype(F32)
        g_up = reduce_cols(
            jnp.einsum("mk,tmn->tkn", xn2, dup, preferred_element_type=F32), None
        ).astype(F32)

        gain2_part = jnp.sum(dxn2 * hres * scale2, axis=0)
        e2 = dxn2 * gain2
        dres = (
            gy_own.astype(F32)
            + scale2 * e2
            - hres
            * (scale2 * scale2 * scale2)
            * jnp.mean(e2 * hres, axis=-1, keepdims=True)
        )
        dres_all = gather_ring(dres.astype(BF))
        dres_split = dres_all.reshape(group, 2, width // 2)
        dmix = jnp.einsum("mcd,chd->mh", dres_split, out_w, preferred_element_type=F32).astype(BF)
        dmix = jnp.swapaxes(dmix.reshape(group, heads_here, HD), 0, 1)
        dqkv = to_tokens(attend_back(table, to_heads(dmix), q, k, v, cos, sin, own, length))
        dxn1 = jnp.einsum("tmn,tkn->mk", dqkv, qkv_w, preferred_element_type=F32)
        dxn1 = scatter_ring(dxn1.reshape(z_size, own, width))
        g_out = jnp.einsum("mh,mcd->chd", mixed, dres_split, preferred_element_type=F32)
        g_qkv = jnp.einsum("mk,tmn->tkn", xn1, dqkv, preferred_element_type=F32)
        if plain:
            g_out = reduce_rows(g_out.reshape(2, tp_size, HD, width // 2)).astype(F32)
            g_qkv = reduce_cols(g_qkv, None).reshape(k_rows, z_size, 3, HD)
            g_query, g_key, g_value = (
                g_qkv[:, :, i].reshape(k_rows, z_size * HD).astype(F32) for i in range(3)
            )
        else:

            def spread(part, cols):
                if cols:
                    out = lax.dynamic_update_slice(
                        jnp.zeros((width, heads * HD), BF), part.astype(BF), (0, first)
                    )
                else:
                    out = lax.dynamic_update_slice(
                        jnp.zeros((heads * HD, width), BF), part.astype(BF), (first, 0)
                    )
                out = lax.psum_scatter(
                    out, ("z", "core"), scatter_dimension=0 if cols else 1, tiled=True
                )
                return lax.psum_scatter(
                    out, "tp", scatter_dimension=1 if cols else 0, tiled=True
                ).astype(F32)

            def back_columns(i):
                part = g_qkv[:, :, i * HD : (i + 1) * HD].swapaxes(1, 2)
                return spread(restore(part).reshape(heads_here * HD, width).T, True)

            g_query, g_key, g_value = back_columns(0), back_columns(1), back_columns(2)
            g_out = jnp.swapaxes(g_out, 0, 1).reshape(heads_here * HD, width)
            g_out = spread(restore(g_out), False)
        gain1_part = jnp.sum(dxn1 * x_own * scale1, axis=0)
        e1 = dxn1 * gain1
        in_own = (
            dres
            + scale1 * e1
            - x_own
            * (scale1 * scale1 * scale1)
            * jnp.mean(e1 * x_own, axis=-1, keepdims=True)
        )

        gains = restore(jnp.stack([gain1_part, gain2_part])).reshape(2, shards, 1, k_rows)
        gains = jnp.broadcast_to(gains, (2, shards, tp_size, k_rows)).reshape(
            2, shards * tp_size, k_rows
        )
        gains = lax.all_to_all(
            gains, ("z", "core", "tp"), split_axis=1, concat_axis=1, tiled=True
        )
        gains = jnp.sum(gains, axis=1)

        def spread_rows(x):
            every = gather_tp(restore(x.astype(BF))).reshape(2, rows // 2, width)
            kept = lax.dynamic_index_in_dim(every, core, axis=0, keepdims=False)
            sent = lax.dynamic_index_in_dim(every, 1 - core, axis=0, keepdims=False)
            came = lax.ppermute(sent, "core", swap_core)
            first_seq = jnp.where(core == 0, kept, came)
            second_seq = jnp.where(core == 0, came, kept)
            blocks = jnp.concatenate([first_seq, second_seq]).reshape(4, block, width)
            return jnp.take(blocks, rank, axis=0, mode="clip").reshape(rows, width)

        layer_out = spread_rows(layer_own)
        in_grad = spread_rows(in_own).astype(F32)
        return (
            layer_out,
            in_grad,
            gains[0],
            gains[1],
            g_query,
            g_key,
            g_value,
            g_out,
            g_gate,
            g_up,
            g_down,
        )

    return on_device


def solution(mesh):
    tp_size = mesh.shape["tp"]
    z_size = mesh.shape["seq"] // 2
    split = Mesh(mesh.devices.reshape(z_size, 2, tp_size), ("z", "core", "tp"))
    seq = ("z", "core")
    in_specs = (
        P(seq, None),
        P(seq),
        P(seq),
        P(),
        P(),
        P(seq, "tp"),
        P(seq, "tp"),
        P(seq, "tp"),
        P("tp", seq),
        P(seq, "tp"),
        P(seq, "tp"),
        P("tp", seq),
        P(seq, None),
    )
    out_specs = (
        P(seq, None),
        P(seq, None),
        P(seq),
        P(seq),
        P(seq, "tp"),
        P(seq, "tp"),
        P(seq, "tp"),
        P("tp", seq),
        P(seq, "tp"),
        P(seq, "tp"),
        P("tp", seq),
    )
    return jax.shard_map(
        build(z_size, tp_size), mesh=split, in_specs=in_specs, out_specs=out_specs, check_vma=False
    )
```

time: 1530 us -> 941 us (0.62)
  waiting for transfers between devices: 986 us -> 352 us
  blocking collectives: 30.2 us -> 134 us
  starting transfers between devices: 2.07 us -> 89 us
  matrix products: 195 us -> 122 us
  local copies, waits for them, and re-layouts: 209 us -> 147 us
  other arithmetic: 81.9 us -> 50.3 us
  Pallas kernels: 0 us -> 18.5 us
    all_gather x9 -> x5, waiting for transfers between devices: 348 us -> 0.05 us  [the longest x3 0.02 us: gather_cols(): lax.all_gather(w, ('tp', 'core'), axis=0, tiled=False)]
    reduce_scatter x9 -> x5, waiting for transfers between devices: 401 us -> 96.6 us  [the longest x2 60.4 us: reduce_rows(): lax.psum_scatter(part, ('core', 'tp'), scatter_dimension=0, tiled=False)]
    psum x3 -> x0, waiting for transfers between devices: 237 us -> none  [the longest x1 105 us: on_device(): lax.psum(matrix(hidden, down_full).astype(jnp.bfloat16), 'tp')]
    ppermute x0 -> x43, waiting for transfers between devices: none -> 189 us  [the longest x4 57.3 us: gather_ring(): ahead = lax.ppermute(ahead, 'z', forward)]
    all_to_all x0 -> x6, blocking collectives: none -> 134 us  [the longest x4 93.1 us: exchange(): lax.all_to_all(w, 'z', split_axis=split, concat_axis=concat, tiled=True)]
    dot_general x62 -> x15, matrix products: 195 us -> 122 us  [the longest x1 14.4 us: on_device(): jnp.einsum('mcd,ctfd->tmf', gy.reshape(group, 2, width // 2), down_w, pre...]
    all_to_all x0 -> x9, waiting for transfers between devices: none -> 66.1 us  [the longest x6 32 us: exchange(): lax.all_to_all(w, 'z', split_axis=split, concat_axis=concat, tiled=True)]
    ppermute x0 -> x43, starting transfers between devices: none -> 53.1 us  [the longest x4 12.4 us: gather_ring(): two = lax.ppermute(back[mid:], 'z', backward)]
  transfers between devices with their start and end apart: 21 -> 62, of which waited for: 19 -> 32; matrix products, arithmetic and copies ran while one was open for 17% -> 28% of each run, Pallas kernels for 0% -> 2%
where the time goes in v1:
time: 941 us; the launch traced here: 930 us
  waiting for transfers between devices  352 us (37%)
  local copies, waits for them, and re-layouts  147 us (16%)
  blocking collectives  134 us (14%)
  matrix products  122 us (13%)
  starting transfers between devices  89 us (9%)
  other arithmetic  50.3 us (5%)
  Pallas kernels  18.5 us (2%)
  between operations  17.1 us (2%)
    all_to_all x4, blocking collectives, exchange(): lax.all_to_all(w, 'z', split_axis=split, concat_axis=concat, tiled=True)  93.1 us
    reduce_scatter x2, waiting for transfers between devices, reduce_rows(): lax.psum_scatter(part, ('core', 'tp'), scatter_dimension=0, tiled=False)  60.4 us
    ppermute x4, waiting for transfers between devices, gather_ring(): ahead = lax.ppermute(ahead, 'z', forward)  57.3 us
    reduce_scatter x3, waiting for transfers between devices, reduce_cols(): lax.psum_scatter(part, ('tp', 'core'), scatter_dimension=0, tiled=False)  36.2 us
    unnamed x106, local copies, waits for them, and re-layouts  33.8 us
    all_to_all x6, waiting for transfers between devices, exchange(): lax.all_to_all(w, 'z', split_axis=split, concat_axis=concat, tiled=True)  32 us
    convert_element_type x3, local copies, waits for them, and re-layouts, reduce_cols(): part = part.astype(BF).reshape(2 * tp_size, width // 2, part.shape[2])  31.7 us
    ppermute x4, waiting for transfers between devices, scatter_ring(): one = lax.ppermute(fwd.astype(BF), 'z', forward)  30.8 us
  transfers between devices with their start and end apart: 62, of which 32 were waited for; matrix products, arithmetic and copies ran while one was open for 28% of the time, Pallas kernels for 2%

profile of v1, /device:TPU:0, one launch (start us, length us, event | category | flops | bytes accessed | tf_op | source)
XLA Modules:
  0.0 930.3 jit_solution(10895087735502146765)
XLA Ops:
  10.0 26.2 %all_to_all.173 = bf16[256,4,384]{0,2,1:T(8,128)(2,1)S(1)} all-to-all(bf16[256,4,384]{0,2,1:T(8,128)(2,1)S(1)} %bitcast.359), channel_id=1, replica_groups=mesh['z'=4,'core'=2,'tp'=4] {'z'}, dimensions={1} | all-to-all | bytes 1572864 | tf_op jit(solution)/shard_map/all_to_all | solution.py:314
  38.7 10.9 %all_to_all.174 = bf16[4,128,256]{2,1,0:T(8,128)(2,1)S(1)} all-to-all(bf16[4,128,256]{2,1,0:T(8,128)(2,1)S(1)} %bitcast.382), channel_id=1, replica_groups=mesh['z'=4,'core'=2,'tp'=4] {'z'}, dimensions={0} | all-to-all | bytes 524288 | tf_op jit(solution)/shard_map/all_to_all | solution.py:314
  51.9 27.9 %all_to_all.175 = bf16[256,4,512]{2,0,1:T(8,128)(2,1)} all-to-all(bf16[256,4,512]{2,0,1:T(8,128)(2,1)S(1)} %copy.459), channel_id=1, replica_groups=mesh['z'=4,'core'=2,'tp'=4] {'z'}, dimensions={1} | all-to-all | bytes 2097152 | tf_op jit(solution)/shard_map/all_to_all | solution.py:314
  82.2 28.0 %all_to_all.176 = bf16[256,4,512]{2,0,1:T(8,128)(2,1)} all-to-all(bf16[256,4,512]{2,0,1:T(8,128)(2,1)S(1)} %copy.457), channel_id=1, replica_groups=mesh['z'=4,'core'=2,'tp'=4] {'z'}, dimensions={1} | all-to-all | bytes 2097152 | tf_op jit(solution)/shard_map/all_to_all | solution.py:314
  112.9 3.5 all-to-all-start.6
  125.0 16.2 %all-to-all-done.6 = bf16[4,512,256]{2,1,0:T(8,128)(2,1)S(1)} async-done(((bf16[4,512,256]{2,1,0:T(8,128)(2,1)}), bf16[4,512,256]{2,1,0:T(8,128)(2,1)S(1)}, u32[]{:S(2)}, u32[]{:S(2)}) %all-to-all-start.6) | async-done | bytes 1048608 | tf_op jit(solution)/shard_map/all_to_all | solution.py:314
  150.7 22.9 %collective-permute-done.1 = bf16[128,2048]{1,0:T(8,128)(2,1)S(1)} collective-permute-done((bf16[128,2048]{1,0:T(8,128)(2,1)S(1)}, bf16[128,2048]{1,0:T(8,128)(2,1)S(1)}, u32[]{:S(2)}, u32[]{:S(2)}) %collective-permute-start.1) | collective-permute-done | bytes 524320 | tf_op jit(solution)/shard_map/ppermute | solution.py:214
  176.8 11.5 %collective-permute-done.3 = bf16[64,2048]{1,0:T(8,128)(2,1)S(1)} collective-permute-done((bf16[64,2048]{1,0:T(8,128)(2,1)S(1)}, bf16[64,2048]{1,0:T(8,128)(2,1)S(1)}, u32[]{:S(2)}, u32[]{:S(2)}) %collective-permute-start.3) | collective-permute-done | bytes 262176 | tf_op jit(solution)/shard_map/ppermute | solution.py:218
  188.4 8.0 fusion.36
  196.4 3.9 all-to-all-start.1
  200.7 3.7 multiply_sine_fusion
  212.3 24.5 %all-to-all-done.1.qkv_ref = bf16[4,512,384]{2,1,0:T(8,128)(2,1)S(1)} async-done(((bf16[4,512,384]{2,1,0:T(8,128)(2,1)}), bf16[4,512,384]{2,1,0:T(8,128)(2,1)S(1)}, u32[]{:S(2)}, u32[]{:S(2)}) %all-to-all-start.1) | async-done | bytes 1572896 | tf_op jit(solution)/shard_map/all_to_all | solution.py:366
  238.1 7.7 attend.1
  247.3 3.5 all-to-all-start.2
  260.1 4.0 all-to-all-done.2
  264.3 4.9 fusion.65
  274.0 4.5 reshape.438
  285.1 6.3 collective-permute-done.5
  291.6 6.2 collective-permute-done.7
  302.9 9.2 collective-permute-done.6
  312.1 9.1 collective-permute-done.8
  329.7 12.7 %collective-permute-done.9 = bf16[128,2048]{1,0:T(8,128)(2,1)S(1)} collective-permute-done((bf16[128,2048]{1,0:T(8,128)(2,1)S(1)}, bf16[128,2048]{1,0:T(8,128)(2,1)S(1)}, u32[]{:S(2)}, u32[]{:S(2)}) %collective-permute-start.9) | collective-permute-done | bytes 524320 | tf_op jit(solution)/shard_map/ppermute | solution.py:214
  347.6 5.0 collective-permute-done.11
  354.0 10.5 %fusion.21 = f32[512,4,512]{2,0,1:T(8,128)} fusion(bf16[4,2048,512]{2,1,0:T(8,128)(2,1)} %bitcast.417, bf16[512,2048]{1,0:T(8,128)(2,1)} %constant_dynamic-update-slice_fusion.5), kind=kOutput, calls=%fused_computation.43 | convolution fusion | flops 4294967296 | bytes 14680064 | tf_op jit(solution)/shard_map/mk,tkn->tmn/dot_general | solution.py:394
  364.6 10.5 %fusion.23 = f32[512,4,512]{2,0,1:T(8,128)} fusion(bf16[4,2048,512]{2,1,0:T(8,128)(2,1)} %bitcast.419, bf16[512,2048]{1,0:T(8,128)(2,1)} %constant_dynamic-update-slice_fusion.5), kind=kOutput, calls=%fused_computation.45 | convolution fusion | flops 4294967296 | bytes 14680064 | tf_op jit(solution)/shard_map/mk,tkn->tmn/dot_general | solution.py:393
  375.1 14.4 %fusion.4 = (bf16[4,512,512]{2,1,0:T(8,128)(2,1)}, bf16[4,512,512]{2,1,0:T(8,128)(2,1)}, bf16[4,512,512]{2,1,0:T(8,128)(2,1)S(1)}) fusion(f32[512,4,512]{2,0,1:T(8,128)} %fusion.23, f32[512,4,512]{2,0,1:T(8,128)} %fusion.21, bf16[2,4,512,1024]{3,2,1,0:T(8,128)(2,1)} %bitcast.421, bf16[512,2,1024]{2,0,1:T(8,128)(2,1)} %bitcast_dynamic-update-slice_fusion.2), kind=kOutput, calls=%fused_computation.14 | convolution fusion | flops 4311744512 | bytes 25165824 | tf_op jit(solution)/shard_map/mcd,ctfd->tmf/dot_general | solution.py:387
  389.5 10.5 %fusion.67 = (bf16[512,2,1024]{2,0,1:T(8,128)(2,1)S(1)}, f32[512,2,1024]{2,0,1:T(8,128)}) fusion(bf16[2,4,512,1024]{3,2,1,0:T(8,128)(2,1)} %bitcast.422, bf16[4,512,512]{2,1,0:T(8,128)(2,1)S(1)} %get-tuple-element.113), kind=kOutput, calls=%fused_computation.206 | convolution fusion | flops 4296015872 | bytes 16777216 | tf_op jit(solution)/shard_map/tmf,ctfd->mcd/dot_general | solution.py:403
  404.2 4.5 reshape.439
  414.3 7.0 fusion.69
  421.2 7.7 fusion.66
  435.3 10.7 %collective-permute-done.26 = bf16[64,2048]{1,0:T(8,128)(2,1)S(1)} collective-permute-done((bf16[64,2048]{1,0:T(8,128)(2,1)S(1)}, bf16[64,2048]{1,0:T(8,128)(2,1)S(1)}, u32[]{:S(2)}, u32[]{:S(2)}) %collective-permute-start.26) | collective-permute-done | bytes 262176 | tf_op jit(solution)/shard_map/ppermute | solution.py:225
  450.7 4.9 collective-permute-done.14
  455.6 8.0 collective-permute-done.16
  463.6 7.4 collective-permute-done.27
  471.0 5.1 collective-permute-done.29
  483.0 21.7 %collective-permute-done.30 = bf16[128,2048]{1,0:T(8,128)(2,1)S(1)} collective-permute-done((bf16[128,2048]{1,0:T(8,128)(2,1)S(1)}, bf16[128,2048]{1,0:T(8,128)(2,1)S(1)}, u32[]{:S(2)}, u32[]{:S(2)}) %collective-permute-start.30) | collective-permute-done | bytes 524320 | tf_op jit(solution)/shard_map/ppermute | solution.py:214
  507.9 7.9 collective-permute-done.32
  518.7 4.3 fusion.42
  525.2 17.0 %all_to_all.177.grad_ref = bf16[4,512,128]{2,1,0:T(8,128)(2,1)S(1)} all-to-all(bf16[4,512,128]{2,1,0:T(8,128)(2,1)} %bitcast.373), channel_id=1, replica_groups=mesh['z'=4,'core'=2,'tp'=4] {'tp'}, dimensions={0} | all-to-all | bytes 1048576 | tf_op jit(solution)/shard_map/all_to_all | solution.py:366
  543.3 10.8 %attend_back.1 = bf16[4,512,384]{2,1,0:T(8,128)(2,1)S(1)} custom-call(s32[16]{0:T(128)S(1)} %and_select_fusion.tab_ref, bf16[4,512,128]{2,1,0:T(8,128)(2,1)S(1)} %all_to_all.177.grad_ref, bf16[2048,128]{1,0:T(8,128)(2,1)S(1)} %get-tuple-element.16.q_ref, bf16[2048,128]{1,0:T(8,128)(2,1)S(1)} %copy-done.3, bf16[2048,128]{1,0:T(8,128)(2,1)S(1)} %copy-done.5, ...), custom_call_target="tpu_custom_call" | custom-call | flops 2684354560 | bytes 6291456 | tf_op jit(solution)/shard_map/attend_back/pallas_call | solution.py:180
  554.1 23.9 %all_to_all.178 = bf16[4,512,384]{2,1,0:T(8,128)(2,1)S(1)} all-to-all(bf16[4,512,384]{2,1,0:T(8,128)(2,1)S(1)} %attend_back.1), channel_id=1, replica_groups=mesh['z'=4,'core'=2,'tp'=4] {'tp'}, dimensions={0} | all-to-all | bytes 3145728 | tf_op jit(solution)/shard_map/all_to_all | solution.py:374
  578.0 5.4 convert_bitcast_fusion.2
  583.4 8.6 copy.483
  592.0 10.8 %convert_bitcast_fusion.1 = bf16[4,2048,512]{1,2,0:T(8,128)(2,1)} fusion(bf16[4,512,512]{2,1,0:T(8,128)(2,1)} %get-tuple-element.112, bf16[512,2048]{1,0:T(8,128)(2,1)} %constant_dynamic-update-slice_fusion.5), kind=kOutput, calls=%fused_computation.5 | convolution fusion | flops 4299161600 | bytes 12582912 | tf_op jit(solution)/shard_map/mk,tmn->tkn/dot_general | solution.py:425
  602.9 11.6 %copy.488 = bf16[4,2048,512]{2,1,0:T(8,128)(2,1)} copy(bf16[4,2048,512]{1,2,0:T(8,128)(2,1)} %convert_bitcast_fusion.1) | data formatting | bytes 16777216 | tf_op jit(solution)/shard_map/convert_element_type | solution.py:407
  615.0 10.1 %convert_bitcast_fusion = bf16[4,2048,512]{1,2,0:T(8,128)(2,1)} fusion(bf16[4,512,512]{2,1,0:T(8,128)(2,1)} %get-tuple-element.111, bf16[512,2048]{1,0:T(8,128)(2,1)} %constant_dynamic-update-slice_fusion.5), kind=kOutput, calls=%fused_computation.4 | convolution fusion | flops 4299161600 | bytes 12582912 | tf_op jit(solution)/shard_map/mk,tmn->tkn/dot_general | solution.py:428
  625.1 11.5 %copy.491 = bf16[4,2048,512]{2,1,0:T(8,128)(2,1)} copy(bf16[4,2048,512]{1,2,0:T(8,128)(2,1)} %convert_bitcast_fusion) | data formatting | bytes 16777216 | tf_op jit(solution)/shard_map/convert_element_type | solution.py:407
  636.7 10.2 %convolution_convert_fusion = bf16[2,1024,4,512]{3,1,2,0:T(8,128)(2,1)} fusion(bf16[512,2,1024]{2,0,1:T(8,128)(2,1)} %bitcast_dynamic-update-slice_fusion.2, bf16[4,512,512]{2,1,0:T(8,128)(2,1)} %copy-done.37), kind=kOutput, calls=%fused_computation.7 | convolution fusion | flops 4299161600 | bytes 12582912 | tf_op jit(solution)/shard_map/tmf,mcd->ctfd/dot_general | solution.py:417
  646.9 5.6 fusion.68
  655.6 7.8 collective-permute-done.34
  671.5 9.4 %collective-permute-done.35 = bf16[128,2048]{1,0:T(8,128)(2,1)} collective-permute-done((bf16[128,2048]{1,0:T(8,128)(2,1)}, bf16[128,2048]{1,0:T(8,128)(2,1)}, u32[]{:S(2)}, u32[]{:S(2)}) %collective-permute-start.35) | collective-permute-done | bytes 524320 | tf_op jit(solution)/shard_map/ppermute | solution.py:235
  680.9 7.7 collective-permute-done.37
  696.2 5.6 all-to-all-done.9
  709.7 4.3 all-to-all-done.11
  738.2 4.8 collective-permute-done.38
  749.1 4.8 all-to-all-start.12
  753.9 4.1 collective-permute-done.41
  763.1 3.7 gather_fusion.2
  766.8 4.0 copy.480
  776.8 36.2 %reduce-scatter.12.cloned.1.call-done = bf16[1,1024,512]{2,1,0:T(8,128)(2,1)} async-done(((bf16[8,1024,512]{2,1,0:T(8,128)(2,1)}), bf16[1,1024,512]{2,1,0:T(8,128)(2,1)}) %reduce-scatter.12.cloned.1.call-update) | async-done | bytes 1048592 | tf_op jit(solution)/shard_map/reduce_scatter | solution.py:408
  813.0 4.6 all-to-all-start.13
  827.2 60.4 %reduce-scatter.14.cloned.1.call-done = bf16[1,512,1024]{1,2,0:T(8,128)(2,1)} async-done(((bf16[8,512,1024]{1,2,0:T(8,128)(2,1)}), bf16[1,512,1024]{1,2,0:T(8,128)(2,1)}) %reduce-scatter.14.cloned.1.call-update) | async-done | bytes 1048592 | tf_op jit(solution)/shard_map/reduce_scatter | solution.py:413
  889.9 4.8 all-to-all-start.14
  909.2 11.4 %all-to-all-done.14 = bf16[512,4,256]{2,0,1:T(8,128)(2,1)} async-done(((bf16[512,4,256]{2,0,1:T(8,128)(2,1)}), bf16[512,4,256]{2,0,1:T(8,128)(2,1)}, u32[]{:S(2)}, u32[]{:S(2)}) %all-to-all-start.14) | async-done | bytes 1048608 | tf_op jit(solution)/shard_map/all_to_all | solution.py:314
  (360 shorter events, 218.6 us)
Async XLA Ops:
  7.2 181.2 %all-gather.6.cloned.1.call-start = ((), (), s32[]{:S(2)}) async-start(), calls=%async_computation.20 | async-start | bytes 7077888 | tf_op jit(solution)/shard_map/all_gather | solution.py:322
  37.4 226.9 %all-gather.8.cloned.1.call-start = ((), (), s32[]{:S(2)}) async-start(), calls=%async_computation.21 | async-start | bytes 2359296 | tf_op jit(solution)/shard_map/all_gather | solution.py:317
  50.7 303.4 %all-gather.12.cloned.1.call-start = ((), (), s32[]{:S(2)}) async-start(), calls=%async_computation.23 | async-start | bytes 9437184 | tf_op jit(solution)/shard_map/all_gather | solution.py:322
  79.8 284.8 %all-gather.10.cloned.1.call-start = ((), (), s32[]{:S(2)}) async-start(), calls=%async_computation.22 | async-start | bytes 9437184 | tf_op jit(solution)/shard_map/all_gather | solution.py:322
  112.9 28.3 %all-to-all-start.6 = ((bf16[4,512,256]{2,1,0:T(8,128)(2,1)}), bf16[4,512,256]{2,1,0:T(8,128)(2,1)S(1)}, u32[]{:S(2)}, u32[]{:S(2)}) async-start(bf16[4,512,256]{2,1,0:T(8,128)(2,1)} %bitcast.42), calls=%async_computation.6 | async-start | bytes 2097152 | tf_op jit(solution)/shard_map/all_to_all | solution.py:314
  116.5 258.6 %all-gather.14.cloned.1.call-start = ((), (), s32[]{:S(2)}) async-start(), calls=%async_computation.24 | async-start | bytes 9437184 | tf_op jit(solution)/shard_map/all_gather | solution.py:317
  125.0 18.9 %collective-permute-start = (bf16[2,128,2048]{1,2,0:T(8,128)(2,1)}, bf16[2,128,2048]{1,2,0:T(8,128)(2,1)}, u32[]{:S(2)}, u32[]{:S(2)}) collective-permute-start(bf16[2,128,2048]{1,2,0:T(8,128)(2,1)} %pad_maximum_fusion.4), channel_id=1, source_target_pairs={{0,4},{4,0},{1,5},{5,1},{2,6},{6,2},{3,7},{7,3},{8,12},{12,8},{9,1... | collective-permute-start | bytes 3145736 | tf_op jit(solution)/shard_map/ppermute | solution.py:304
  147.0 26.6 %collective-permute-start.1 = (bf16[128,2048]{1,0:T(8,128)(2,1)S(1)}, bf16[128,2048]{1,0:T(8,128)(2,1)S(1)}, u32[]{:S(2)}, u32[]{:S(2)}) collective-permute-start(bf16[128,2048]{1,0:T(8,128)(2,1)S(1)} %get-tuple-element.110), channel_id=1, source_target_pairs={{0,8},{8,24},{24,16},{16,0},{1,9},{9,25},{25,17},{17,1},{2,10},{10... | collective-permute-start | bytes 1572872 | tf_op jit(solution)/shard_map/ppermute | solution.py:214
  147.1 26.7 %collective-permute-start.2 = (bf16[128,2048]{1,0:T(8,128)(2,1)S(1)}, bf16[128,2048]{1,0:T(8,128)(2,1)S(1)}, u32[]{:S(2)}, u32[]{:S(2)}) collective-permute-start(bf16[128,2048]{1,0:T(8,128)(2,1)S(1)} %get-tuple-element.110), channel_id=1, source_target_pairs={{8,0},{24,8},{16,24},{0,16},{9,1},{25,9},{17,25},{1,17},{10,2},{26... | collective-permute-start | bytes 1572872 | tf_op jit(solution)/shard_map/ppermute | solution.py:215
  173.6 14.6 %collective-permute-start.3 = (bf16[64,2048]{1,0:T(8,128)(2,1)S(1)}, bf16[64,2048]{1,0:T(8,128)(2,1)S(1)}, u32[]{:S(2)}, u32[]{:S(2)}) collective-permute-start(bf16[64,2048]{1,0:T(8,128)(2,1)S(1)} %slice.295), channel_id=1, source_target_pairs={{0,8},{8,24},{24,16},{16,0},{1,9},{9,25},{25,17},{17,1},{2,10},{10... | collective-permute-start | bytes 786440 | tf_op jit(solution)/shard_map/ppermute | solution.py:218
  173.8 14.6 %collective-permute-start.4 = (bf16[64,2048]{1,0:T(8,128)(2,1)S(1)}, bf16[64,2048]{1,0:T(8,128)(2,1)S(1)}, u32[]{:S(2)}, u32[]{:S(2)}) collective-permute-start(bf16[64,2048]{1,0:T(8,128)(2,1)S(1)} %slice.296), channel_id=1, source_target_pairs={{8,0},{24,8},{16,24},{0,16},{9,1},{25,9},{17,25},{1,17},{10,2},{26... | collective-permute-start | bytes 786440 | tf_op jit(solution)/shard_map/ppermute | solution.py:219
  196.4 40.5 %all-to-all-start.1 = ((bf16[4,512,384]{2,1,0:T(8,128)(2,1)}), bf16[4,512,384]{2,1,0:T(8,128)(2,1)S(1)}, u32[]{:S(2)}, u32[]{:S(2)}) async-start(bf16[4,512,384]{2,1,0:T(8,128)(2,1)} %fusion.36), calls=%async_computation.1 | async-start | bytes 3145728 | tf_op jit(solution)/shard_map/all_to_all | solution.py:366
  209.4 44.2 %collective-permute-start.22 = (bf16[128,2048]{1,0:T(8,128)(2,1)}, bf16[128,2048]{1,0:T(8,128)(2,1)}, u32[]{:S(2)}, u32[]{:S(2)}) collective-permute-start(bf16[128,2048]{1,0:T(8,128)(2,1)} %squeeze.27), channel_id=1, source_target_pairs={{0,8},{8,24},{24,16},{16,0},{1,9},{9,25},{25,17},{17,1},{2,10},{10... | collective-permute-start | bytes 1572872 | tf_op jit(solution)/shard_map/ppermute | solution.py:214
  209.4 45.9 %collective-permute-start.23 = (bf16[128,2048]{1,0:T(8,128)(2,1)}, bf16[128,2048]{1,0:T(8,128)(2,1)}, u32[]{:S(2)}, u32[]{:S(2)}) collective-permute-start(bf16[128,2048]{1,0:T(8,128)(2,1)} %squeeze.27), channel_id=1, source_target_pairs={{8,0},{24,8},{16,24},{0,16},{9,1},{25,9},{17,25},{1,17},{10,2},{26... | collective-permute-start | bytes 1572872 | tf_op jit(solution)/shard_map/ppermute | solution.py:215
  247.3 16.7 %all-to-all-start.2 = ((bf16[4,512,128]{2,1,0:T(8,128)(2,1)}), bf16[4,512,128]{2,1,0:T(8,128)(2,1)S(1)}, u32[]{:S(2)}, u32[]{:S(2)}) async-start(bf16[4,512,128]{2,1,0:T(8,128)(2,1)} %get-tuple-element.15), calls=%async_computation.2 | async-start | bytes 1048576 | tf_op jit(solution)/shard_map/all_to_all | solution.py:374
  250.9 443.4 %reduce-scatter.8.cloned.1.call-start = ((), (), s32[]{:S(2)}) async-start(), calls=%async_computation.26 | async-start | bytes 2359296 | tf_op jit(solution)/shard_map/reduce_scatter | solution.py:413
  255.3 72.0 %collective-permute-start.24 = (bf16[64,2048]{1,0:T(8,128)(2,1)}, bf16[64,2048]{1,0:T(8,128)(2,1)S(1)}, u32[]{:S(2)}, u32[]{:S(2)}) collective-permute-start(bf16[64,2048]{1,0:T(8,128)(2,1)} %slice.316), channel_id=1, source_target_pairs={{0,8},{8,24},{24,16},{16,0},{1,9},{9,25},{25,17},{17,1},{2,10},{10... | collective-permute-start | bytes 786440 | tf_op jit(solution)/shard_map/ppermute | solution.py:218
  256.9 71.1 %collective-permute-start.25 = (bf16[64,2048]{1,0:T(8,128)(2,1)}, bf16[64,2048]{1,0:T(8,128)(2,1)}, u32[]{:S(2)}, u32[]{:S(2)}) collective-permute-start(bf16[64,2048]{1,0:T(8,128)(2,1)} %slice.317), channel_id=1, source_target_pairs={{8,0},{24,8},{16,24},{0,16},{9,1},{25,9},{17,25},{1,17},{10,2},{26... | collective-permute-start | bytes 786440 | tf_op jit(solution)/shard_map/ppermute | solution.py:219
  279.6 11.9 %collective-permute-start.5 = (bf16[64,2048]{1,0:T(8,128)(2,1)S(1)}, bf16[64,2048]{1,0:T(8,128)(2,1)S(1)}, u32[]{:S(2)}, u32[]{:S(2)}) collective-permute-start(bf16[64,2048]{1,0:T(8,128)(2,1)S(1)} %get-tuple-element.138), channel_id=1, source_target_pairs={{0,8},{8,24},{24,16},{16,0},{1,9},{9,25},{25,17},{17,1},{2,10},{10... | collective-permute-start | bytes 786440 | tf_op jit(solution)/shard_map/ppermute | solution.py:225
  282.2 15.6 %collective-permute-start.7 = (bf16[64,2048]{1,0:T(8,128)(2,1)S(1)}, bf16[64,2048]{1,0:T(8,128)(2,1)S(1)}, u32[]{:S(2)}, u32[]{:S(2)}) collective-permute-start(bf16[64,2048]{1,0:T(8,128)(2,1)S(1)} %get-tuple-element.139), channel_id=1, source_target_pairs={{8,0},{24,8},{16,24},{0,16},{9,1},{25,9},{17,25},{1,17},{10,2},{26... | collective-permute-start | bytes 786440 | tf_op jit(solution)/shard_map/ppermute | solution.py:226
  291.5 20.5 %collective-permute-start.6 = (bf16[128,2048]{1,0:T(8,128)(2,1)S(1)}, bf16[128,2048]{1,0:T(8,128)(2,1)S(1)}, u32[]{:S(2)}, u32[]{:S(2)}) collective-permute-start(bf16[128,2048]{1,0:T(8,128)(2,1)S(1)} %pad_maximum_fusion.8), channel_id=1, source_target_pairs={{0,8},{8,24},{24,16},{16,0},{1,9},{9,25},{25,17},{17,1},{2,10},{10... | collective-permute-start | bytes 1572872 | tf_op jit(solution)/shard_map/ppermute | solution.py:235
  297.9 23.2 %collective-permute-start.8 = (bf16[128,2048]{1,0:T(8,128)(2,1)S(1)}, bf16[128,2048]{1,0:T(8,128)(2,1)S(1)}, u32[]{:S(2)}, u32[]{:S(2)}) collective-permute-start(bf16[128,2048]{1,0:T(8,128)(2,1)S(1)} %pad_maximum_fusion.9), channel_id=1, source_target_pairs={{8,0},{24,8},{16,24},{0,16},{9,1},{25,9},{17,25},{1,17},{10,2},{26... | collective-permute-start | bytes 1572872 | tf_op jit(solution)/shard_map/ppermute | solution.py:236
  322.5 19.9 %collective-permute-start.9 = (bf16[128,2048]{1,0:T(8,128)(2,1)S(1)}, bf16[128,2048]{1,0:T(8,128)(2,1)S(1)}, u32[]{:S(2)}, u32[]{:S(2)}) collective-permute-start(bf16[128,2048]{1,0:T(8,128)(2,1)S(1)} %get-tuple-element.106), channel_id=1, source_target_pairs={{0,8},{8,24},{24,16},{16,0},{1,9},{9,25},{25,17},{17,1},{2,10},{10... | collective-permute-start | bytes 1572872 | tf_op jit(solution)/shard_map/ppermute | solution.py:214
  322.5 20.0 %collective-permute-start.10 = (bf16[128,2048]{1,0:T(8,128)(2,1)S(1)}, bf16[128,2048]{1,0:T(8,128)(2,1)S(1)}, u32[]{:S(2)}, u32[]{:S(2)}) collective-permute-start(bf16[128,2048]{1,0:T(8,128)(2,1)S(1)} %get-tuple-element.106), channel_id=1, source_target_pairs={{8,0},{24,8},{16,24},{0,16},{9,1},{25,9},{17,25},{1,17},{10,2},{26... | collective-permute-start | bytes 1572872 | tf_op jit(solution)/shard_map/ppermute | solution.py:215
  342.5 10.1 %collective-permute-start.11 = (bf16[64,2048]{1,0:T(8,128)(2,1)S(1)}, bf16[64,2048]{1,0:T(8,128)(2,1)S(1)}, u32[]{:S(2)}, u32[]{:S(2)}) collective-permute-start(bf16[64,2048]{1,0:T(8,128)(2,1)S(1)} %slice.304), channel_id=1, source_target_pairs={{0,8},{8,24},{24,16},{16,0},{1,9},{9,25},{25,17},{17,1},{2,10},{10... | collective-permute-start | bytes 786440 | tf_op jit(solution)/shard_map/ppermute | solution.py:218
  342.6 10.8 %collective-permute-start.12 = (bf16[64,2048]{1,0:T(8,128)(2,1)S(1)}, bf16[64,2048]{1,0:T(8,128)(2,1)S(1)}, u32[]{:S(2)}, u32[]{:S(2)}) collective-permute-start(bf16[64,2048]{1,0:T(8,128)(2,1)S(1)} %slice.305), channel_id=1, source_target_pairs={{8,0},{24,8},{16,24},{0,16},{9,1},{25,9},{17,25},{1,17},{10,2},{26... | collective-permute-start | bytes 786440 | tf_op jit(solution)/shard_map/ppermute | solution.py:219
  409.8 22.2 %collective-permute-start.13 = (bf16[64,2048]{1,0:T(8,128)(2,1)S(1)}, bf16[64,2048]{1,0:T(8,128)(2,1)S(1)}, u32[]{:S(2)}, u32[]{:S(2)}) collective-permute-start(bf16[64,2048]{1,0:T(8,128)(2,1)S(1)} %get-tuple-element.134), channel_id=1, source_target_pairs={{0,8},{8,24},{24,16},{16,0},{1,9},{9,25},{25,17},{17,1},{2,10},{10... | collective-permute-start | bytes 786440 | tf_op jit(solution)/shard_map/ppermute | solution.py:225
  411.2 21.0 %collective-permute-start.15 = (bf16[64,2048]{1,0:T(8,128)(2,1)S(1)}, bf16[64,2048]{1,0:T(8,128)(2,1)S(1)}, u32[]{:S(2)}, u32[]{:S(2)}) collective-permute-start(bf16[64,2048]{1,0:T(8,128)(2,1)S(1)} %get-tuple-element.135), channel_id=1, source_target_pairs={{8,0},{24,8},{16,24},{0,16},{9,1},{25,9},{17,25},{1,17},{10,2},{26... | collective-permute-start | bytes 786440 | tf_op jit(solution)/shard_map/ppermute | solution.py:226
  429.0 17.0 %collective-permute-start.26 = (bf16[64,2048]{1,0:T(8,128)(2,1)S(1)}, bf16[64,2048]{1,0:T(8,128)(2,1)S(1)}, u32[]{:S(2)}, u32[]{:S(2)}) collective-permute-start(bf16[64,2048]{1,0:T(8,128)(2,1)S(1)} %get-tuple-element.130), channel_id=1, source_target_pairs={{0,8},{8,24},{24,16},{16,0},{1,9},{9,25},{25,17},{17,1},{2,10},{10... | collective-permute-start | bytes 786440 | tf_op jit(solution)/shard_map/ppermute | solution.py:225
  429.1 17.0 %collective-permute-start.28 = (bf16[64,2048]{1,0:T(8,128)(2,1)S(1)}, bf16[64,2048]{1,0:T(8,128)(2,1)S(1)}, u32[]{:S(2)}, u32[]{:S(2)}) collective-permute-start(bf16[64,2048]{1,0:T(8,128)(2,1)S(1)} %get-tuple-element.131), channel_id=1, source_target_pairs={{8,0},{24,8},{16,24},{0,16},{9,1},{25,9},{17,25},{1,17},{10,2},{26... | collective-permute-start | bytes 786440 | tf_op jit(solution)/shard_map/ppermute | solution.py:226
  432.1 23.5 %collective-permute-start.14 = (bf16[128,2048]{1,0:T(8,128)(2,1)S(1)}, bf16[128,2048]{1,0:T(8,128)(2,1)S(1)}, u32[]{:S(2)}, u32[]{:S(2)}) collective-permute-start(bf16[128,2048]{1,0:T(8,128)(2,1)S(1)} %pad_maximum_fusion.10), channel_id=1, source_target_pairs={{0,8},{8,24},{24,16},{16,0},{1,9},{9,25},{25,17},{17,1},{2,10},{10... | collective-permute-start | bytes 1572872 | tf_op jit(solution)/shard_map/ppermute | solution.py:235
  432.3 31.3 %collective-permute-start.16 = (bf16[128,2048]{1,0:T(8,128)(2,1)S(1)}, bf16[128,2048]{1,0:T(8,128)(2,1)S(1)}, u32[]{:S(2)}, u32[]{:S(2)}) collective-permute-start(bf16[128,2048]{1,0:T(8,128)(2,1)S(1)} %pad_maximum_fusion.11), channel_id=1, source_target_pairs={{8,0},{24,8},{16,24},{0,16},{9,1},{25,9},{17,25},{1,17},{10,2},{26... | collective-permute-start | bytes 1572872 | tf_op jit(solution)/shard_map/ppermute | solution.py:236
  446.2 24.8 %collective-permute-start.27 = (bf16[128,2048]{1,0:T(8,128)(2,1)S(1)}, bf16[128,2048]{1,0:T(8,128)(2,1)S(1)}, u32[]{:S(2)}, u32[]{:S(2)}) collective-permute-start(bf16[128,2048]{1,0:T(8,128)(2,1)S(1)} %pad_maximum_fusion.12), channel_id=1, source_target_pairs={{0,8},{8,24},{24,16},{16,0},{1,9},{9,25},{25,17},{17,1},{2,10},{10... | collective-permute-start | bytes 1572872 | tf_op jit(solution)/shard_map/ppermute | solution.py:235
  446.3 29.8 %collective-permute-start.29 = (bf16[128,2048]{1,0:T(8,128)(2,1)S(1)}, bf16[128,2048]{1,0:T(8,128)(2,1)S(1)}, u32[]{:S(2)}, u32[]{:S(2)}) collective-permute-start(bf16[128,2048]{1,0:T(8,128)(2,1)S(1)} %pad_maximum_fusion.13), channel_id=1, source_target_pairs={{8,0},{24,8},{16,24},{0,16},{9,1},{25,9},{17,25},{1,17},{10,2},{26... | collective-permute-start | bytes 1572872 | tf_op jit(solution)/shard_map/ppermute | solution.py:236
  480.1 24.6 %collective-permute-start.30 = (bf16[128,2048]{1,0:T(8,128)(2,1)S(1)}, bf16[128,2048]{1,0:T(8,128)(2,1)S(1)}, u32[]{:S(2)}, u32[]{:S(2)}) collective-permute-start(bf16[128,2048]{1,0:T(8,128)(2,1)S(1)} %get-tuple-element.103), channel_id=1, source_target_pairs={{0,8},{8,24},{24,16},{16,0},{1,9},{9,25},{25,17},{17,1},{2,10},{10... | collective-permute-start | bytes 1572872 | tf_op jit(solution)/shard_map/ppermute | solution.py:214
  481.3 23.5 %collective-permute-start.31 = (bf16[128,2048]{1,0:T(8,128)(2,1)S(1)}, bf16[128,2048]{1,0:T(8,128)(2,1)S(1)}, u32[]{:S(2)}, u32[]{:S(2)}) collective-permute-start(bf16[128,2048]{1,0:T(8,128)(2,1)S(1)} %get-tuple-element.103), channel_id=1, source_target_pairs={{8,0},{24,8},{16,24},{0,16},{9,1},{25,9},{17,25},{1,17},{10,2},{26... | collective-permute-start | bytes 1572872 | tf_op jit(solution)/shard_map/ppermute | solution.py:215
  504.7 11.1 %collective-permute-start.32 = (bf16[64,2048]{1,0:T(8,128)(2,1)S(1)}, bf16[64,2048]{1,0:T(8,128)(2,1)S(1)}, u32[]{:S(2)}, u32[]{:S(2)}) collective-permute-start(bf16[64,2048]{1,0:T(8,128)(2,1)S(1)} %slice.325), channel_id=1, source_target_pairs={{0,8},{8,24},{24,16},{16,0},{1,9},{9,25},{25,17},{17,1},{2,10},{10... | collective-permute-start | bytes 786440 | tf_op jit(solution)/shard_map/ppermute | solution.py:218
  504.8 11.0 %collective-permute-start.33 = (bf16[64,2048]{1,0:T(8,128)(2,1)S(1)}, bf16[64,2048]{1,0:T(8,128)(2,1)S(1)}, u32[]{:S(2)}, u32[]{:S(2)}) collective-permute-start(bf16[64,2048]{1,0:T(8,128)(2,1)S(1)} %slice.326), channel_id=1, source_target_pairs={{8,0},{24,8},{16,24},{0,16},{9,1},{25,9},{17,25},{1,17},{10,2},{26... | collective-permute-start | bytes 786440 | tf_op jit(solution)/shard_map/ppermute | solution.py:219
  518.5 189.0 %reduce-scatter.6.cloned.1.call-start = ((), (), s32[]{:S(2)}) async-start(), calls=%async_computation.25 | async-start | bytes 7077888 | tf_op jit(solution)/shard_map/reduce_scatter | solution.py:408
  592.0 156.2 %reduce-scatter.10.cloned.1.call-start = ((), (), s32[]{:S(2)}) async-start(), calls=%async_computation.27 | async-start | bytes 9437184 | tf_op jit(solution)/shard_map/reduce_scatter | solution.py:408
  614.5 198.5 %reduce-scatter.12.cloned.1.call-start = ((), (), s32[]{:S(2)}) async-start(), calls=%async_computation.28 | async-start | bytes 9437184 | tf_op jit(solution)/shard_map/reduce_scatter | solution.py:408
  636.6 250.9 %reduce-scatter.14.cloned.1.call-start = ((), (), s32[]{:S(2)}) async-start(), calls=%async_computation.29 | async-start | bytes 9437184 | tf_op jit(solution)/shard_map/reduce_scatter | solution.py:413
  652.5 10.8 %collective-permute-start.34 = (bf16[64,2048]{1,0:T(8,128)(2,1)S(1)}, bf16[64,2048]{1,0:T(8,128)(2,1)S(1)}, u32[]{:S(2)}, u32[]{:S(2)}) collective-permute-start(bf16[64,2048]{1,0:T(8,128)(2,1)S(1)} %get-tuple-element.126), channel_id=1, source_target_pairs={{0,8},{8,24},{24,16},{16,0},{1,9},{9,25},{25,17},{17,1},{2,10},{10... | collective-permute-start | bytes 786440 | tf_op jit(solution)/shard_map/ppermute | solution.py:225
  652.6 12.0 %collective-permute-start.36 = (bf16[64,2048]{1,0:T(8,128)(2,1)S(1)}, bf16[64,2048]{1,0:T(8,128)(2,1)S(1)}, u32[]{:S(2)}, u32[]{:S(2)}) collective-permute-start(bf16[64,2048]{1,0:T(8,128)(2,1)S(1)} %get-tuple-element.127), channel_id=1, source_target_pairs={{8,0},{24,8},{16,24},{0,16},{9,1},{25,9},{17,25},{1,17},{10,2},{26... | collective-permute-start | bytes 786440 | tf_op jit(solution)/shard_map/ppermute | solution.py:226
  665.5 15.3 %collective-permute-start.35 = (bf16[128,2048]{1,0:T(8,128)(2,1)}, bf16[128,2048]{1,0:T(8,128)(2,1)}, u32[]{:S(2)}, u32[]{:S(2)}) collective-permute-start(bf16[128,2048]{1,0:T(8,128)(2,1)} %pad_maximum_fusion.14), channel_id=1, source_target_pairs={{0,8},{8,24},{24,16},{16,0},{1,9},{9,25},{25,17},{17,1},{2,10},{10... | collective-permute-start | bytes 1572872 | tf_op jit(solution)/shard_map/ppermute | solution.py:235
  666.4 22.2 %collective-permute-start.37 = (bf16[128,2048]{1,0:T(8,128)(2,1)}, bf16[128,2048]{1,0:T(8,128)(2,1)}, u32[]{:S(2)}, u32[]{:S(2)}) collective-permute-start(bf16[128,2048]{1,0:T(8,128)(2,1)} %pad_maximum_fusion.15), channel_id=1, source_target_pairs={{8,0},{24,8},{16,24},{0,16},{9,1},{25,9},{17,25},{1,17},{10,2},{26... | collective-permute-start | bytes 1572872 | tf_op jit(solution)/shard_map/ppermute | solution.py:236
  670.3 34.9 %collective-permute-start.17 = (bf16[128,2048]{0,1:T(8,128)(2,1)S(1)}, bf16[128,2048]{0,1:T(8,128)(2,1)S(1)}, u32[]{:S(2)}, u32[]{:S(2)}) collective-permute-start(bf16[128,2048]{0,1:T(8,128)(2,1)S(1)} %bitcast.378), channel_id=1, source_target_pairs={{0,1},{1,0},{2,3},{3,2},{4,5},{5,4},{6,7},{7,6},{8,9},{9,8},{10,11... | collective-permute-start | bytes 1572872 | tf_op jit(solution)/shard_map/ppermute | solution.py:246
  671.0 35.7 %collective-permute-start.18 = (bf16[128,2048]{0,1:T(8,128)(2,1)S(1)}, bf16[128,2048]{0,1:T(8,128)(2,1)}, u32[]{:S(2)}, u32[]{:S(2)}) collective-permute-start(bf16[128,2048]{0,1:T(8,128)(2,1)S(1)} %bitcast.379), channel_id=1, source_target_pairs={{0,2},{2,0},{1,3},{3,1},{4,6},{6,4},{5,7},{7,5},{8,10},{10,8},{9,1... | collective-permute-start | bytes 1572872 | tf_op jit(solution)/shard_map/ppermute | solution.py:247
  691.3 10.4 %all-to-all-start.9 = ((f32[2,32,256]{2,0,1:T(2,128)}), f32[2,32,256]{2,0,1:T(2,128)S(1)}, u32[]{:S(2)}, u32[]{:S(2)}) async-start(f32[2,32,256]{2,0,1:T(2,128)} %bitcast.95), calls=%async_computation.9 | async-start | bytes 131072 | tf_op jit(solution)/shard_map/all_to_all | solution.py:494
  701.8 12.3 %all-to-all-start.11 = ((bf16[128,4,256]{2,0,1:T(8,128)(2,1)}), bf16[128,4,256]{2,0,1:T(8,128)(2,1)S(1)}, u32[]{:S(2)}, u32[]{:S(2)}) async-start(bf16[128,4,256]{2,0,1:T(8,128)(2,1)} %copy.486), calls=%async_computation.13 | async-start | bytes 524288 | tf_op jit(solution)/shard_map/all_to_all | solution.py:314
  706.2 22.4 %collective-permute-start.20 = (bf16[64,2048]{0,1:T(8,128)(2,1)}, bf16[64,2048]{0,1:T(8,128)(2,1)}, u32[]{:S(2)}, u32[]{:S(2)}) collective-permute-start(bf16[64,2048]{0,1:T(8,128)(2,1)} %slice.314), channel_id=1, source_target_pairs={{0,2},{2,0},{1,3},{3,1},{4,6},{6,4},{5,7},{7,5},{8,10},{10,8},{9,1... | collective-permute-start | bytes 786440 | tf_op jit(solution)/shard_map/ppermute | solution.py:249
  706.7 23.4 %collective-permute-start.19 = (bf16[64,2048]{0,1:T(8,128)(2,1)}, bf16[64,2048]{0,1:T(8,128)(2,1)}, u32[]{:S(2)}, u32[]{:S(2)}) collective-permute-start(bf16[64,2048]{0,1:T(8,128)(2,1)} %bitcast.334), channel_id=1, source_target_pairs={{0,1},{1,0},{2,3},{3,2},{4,5},{5,4},{6,7},{7,6},{8,9},{9,8},{10,11... | collective-permute-start | bytes 786440 | tf_op jit(solution)/shard_map/ppermute | solution.py:249
  714.8 33.4 %all-to-all-start.10 = ((bf16[4,256,384]{1,2,0:T(8,128)(2,1)}), bf16[4,256,384]{1,2,0:T(8,128)(2,1)S(1)}, u32[]{:S(2)}, u32[]{:S(2)}) async-start(bf16[4,256,384]{1,2,0:T(8,128)(2,1)} %copy.484), calls=%async_computation.11 | async-start | bytes 1572864 | tf_op jit(solution)/shard_map/all_to_all | solution.py:314
  723.7 19.2 %collective-permute-start.38 = (bf16[128,2048]{0,1:T(8,128)(2,1)}, bf16[128,2048]{0,1:T(8,128)(2,1)}, u32[]{:S(2)}, u32[]{:S(2)}) collective-permute-start(bf16[128,2048]{0,1:T(8,128)(2,1)} %bitcast.83), channel_id=1, source_target_pairs={{0,1},{1,0},{2,3},{3,2},{4,5},{5,4},{6,7},{7,6},{8,9},{9,8},{10,11... | collective-permute-start | bytes 1572872 | tf_op jit(solution)/shard_map/ppermute | solution.py:246
  724.6 21.6 %collective-permute-start.39 = (bf16[128,2048]{0,1:T(8,128)(2,1)}, bf16[128,2048]{0,1:T(8,128)(2,1)}, u32[]{:S(2)}, u32[]{:S(2)}) collective-permute-start(bf16[128,2048]{0,1:T(8,128)(2,1)} %bitcast.83), channel_id=1, source_target_pairs={{0,2},{2,0},{1,3},{3,1},{4,6},{6,4},{5,7},{7,5},{8,10},{10,8},{9,1... | collective-permute-start | bytes 1572872 | tf_op jit(solution)/shard_map/ppermute | solution.py:247
  745.0 12.9 %collective-permute-start.41 = (bf16[64,2048]{0,1:T(8,128)(2,1)}, bf16[64,2048]{0,1:T(8,128)(2,1)}, u32[]{:S(2)}, u32[]{:S(2)}) collective-permute-start(bf16[64,2048]{0,1:T(8,128)(2,1)} %slice.335), channel_id=1, source_target_pairs={{0,2},{2,0},{1,3},{3,1},{4,6},{6,4},{5,7},{7,5},{8,10},{10,8},{9,1... | collective-permute-start | bytes 786440 | tf_op jit(solution)/shard_map/ppermute | solution.py:249
  746.2 12.4 %collective-permute-start.40 = (bf16[64,2048]{0,1:T(8,128)(2,1)}, bf16[64,2048]{0,1:T(8,128)(2,1)}, u32[]{:S(2)}, u32[]{:S(2)}) collective-permute-start(bf16[64,2048]{0,1:T(8,128)(2,1)} %bitcast.335), channel_id=1, source_target_pairs={{0,1},{1,0},{2,3},{3,2},{4,5},{5,4},{6,7},{7,6},{8,9},{9,8},{10,11... | collective-permute-start | bytes 786440 | tf_op jit(solution)/shard_map/ppermute | solution.py:249
  748.2 24.9 %collective-permute-start.21 = (bf16[256,2048]{1,0:T(8,128)(2,1)}, bf16[256,2048]{1,0:T(8,128)(2,1)}, u32[]{:S(2)}, u32[]{:S(2)}) collective-permute-start(bf16[256,2048]{1,0:T(8,128)(2,1)} %dynamic-slice_bitcast_fusion.1), channel_id=1, source_target_pairs={{0,4},{4,0},{1,5},{5,1},{2,6},{6,2},{3,7},{7,3},{8,12},{12,8},{9,1... | collective-permute-start | bytes 3145736 | tf_op jit(solution)/shard_map/ppermute | solution.py:503
  749.1 63.8 %all-to-all-start.12 = ((bf16[4,256,512]{2,1,0:T(8,128)(2,1)}), bf16[4,256,512]{2,1,0:T(8,128)(2,1)S(1)}, u32[]{:S(2)}, u32[]{:S(2)}) async-start(bf16[4,256,512]{2,1,0:T(8,128)(2,1)} %bitcast.385), calls=%async_computation.15 | async-start | bytes 2097152 | tf_op jit(solution)/shard_map/all_to_all | solution.py:314
  773.1 45.8 %collective-permute-start.42 = (bf16[256,2048]{1,0:T(8,128)(2,1)}, bf16[256,2048]{1,0:T(8,128)(2,1)}, u32[]{:S(2)}, u32[]{:S(2)}) collective-permute-start(bf16[256,2048]{1,0:T(8,128)(2,1)} %dynamic-slice_bitcast_fusion), channel_id=1, source_target_pairs={{0,4},{4,0},{1,5},{5,1},{2,6},{6,2},{3,7},{7,3},{8,12},{12,8},{9,1... | collective-permute-start | bytes 3145736 | tf_op jit(solution)/shard_map/ppermute | solution.py:503
  774.7 43.4 %copy-start.20 = (bf16[128,4,256]{2,0,1:T(8,128)(2,1)S(1)}, bf16[128,4,256]{2,0,1:T(8,128)(2,1)}, u32[]{:S(2)}) copy-start(bf16[128,4,256]{2,0,1:T(8,128)(2,1)} %copy-done.19) | copy-start | bytes 786436
  776.7 42.2 %copy-start.10 = (bf16[4,128,2048]{2,1,0:T(8,128)(2,1)S(1)}, bf16[4,128,2048]{2,1,0:T(8,128)(2,1)}, u32[]{:S(2)}) copy-start(bf16[4,128,2048]{2,1,0:T(8,128)(2,1)} %copy.480) | copy-start | bytes 6291460
  813.0 76.9 %all-to-all-start.13 = ((bf16[4,256,512]{2,1,0:T(8,128)(2,1)}), bf16[4,256,512]{2,1,0:T(8,128)(2,1)}, u32[]{:S(2)}, u32[]{:S(2)}) async-start(bf16[4,256,512]{2,1,0:T(8,128)(2,1)} %bitcast.383), calls=%async_computation.17 | async-start | bytes 2097152 | tf_op jit(solution)/shard_map/all_to_all | solution.py:314
  889.9 30.6 %all-to-all-start.14 = ((bf16[512,4,256]{2,0,1:T(8,128)(2,1)}), bf16[512,4,256]{2,0,1:T(8,128)(2,1)}, u32[]{:S(2)}, u32[]{:S(2)}) async-start(bf16[512,4,256]{2,0,1:T(8,128)(2,1)} %copy.494), calls=%async_computation.19 | async-start | bytes 2097152 | tf_op jit(solution)/shard_map/all_to_all | solution.py:314
  (37 other events, 357.1 us)
Sparse Core Ops, SparseCore 0:
  37.5 44.6 all-gather.5
  84.7 27.8 all-gather.7
  114.5 54.3 all-gather.11
  170.6 71.3 all-gather.9
  243.7 54.1 all-gather.13
  518.6 52.4 reduce-scatter.7
  592.1 58.4 reduce-scatter.5
  654.1 83.1 reduce-scatter.9
  741.2 71.6 reduce-scatter.11
  816.3 71.2 reduce-scatter.13

commit v2 on v1

v2 whole, which is shorter than its diff:
```python
import functools
import math

import jax
import jax.numpy as jnp
from jax import lax
from jax.experimental import pallas as pl
from jax.experimental.pallas import tpu as pltpu
from jax.sharding import Mesh
from jax.sharding import PartitionSpec as P

HD = 128
EPSILON = 1e-06
LOG2E = 1.4426950408889634
BF = jnp.bfloat16
F32 = jnp.float32
SHARE = 1
VM = pl.BlockSpec(memory_space=pltpu.VMEM)
SM = pl.BlockSpec(memory_space=pltpu.SMEM)


def dot_nt(left, right):
    return lax.dot_general(left, right, (((1,), (1,)), ((), ())), preferred_element_type=F32)


def dot_nn(left, right):
    return lax.dot_general(left, right, (((1,), (0,)), ((), ())), preferred_element_type=F32)


def dot_tn(left, right):
    return lax.dot_general(left, right, (((0,), (0,)), ((), ())), preferred_element_type=F32)


def call(body, grid, in_specs, out_specs, out_shape, scratch, flops, bytes_accessed, name, deps):
    known = len(in_specs)
    skip = len(deps)

    def run(*refs):
        body(*refs[:known], *refs[known + skip :])

    made = pl.pallas_call(
        run,
        grid=grid,
        in_specs=list(in_specs) + [pl.BlockSpec(memory_space=pl.ANY)] * skip,
        out_specs=out_specs,
        out_shape=out_shape,
        scratch_shapes=scratch,
        compiler_params=pltpu.CompilerParams(
            vmem_limit_bytes=48 << 20,
            dimension_semantics=("arbitrary",) * len(grid),
        ),
        cost_estimate=pl.CostEstimate(
            flops=flops // SHARE, transcendentals=0, bytes_accessed=bytes_accessed // SHARE
        ),
        name=name,
    )
    return lambda *args: made(*args, *deps)


def shape(dims, dtype):
    return jax.ShapeDtypeStruct(dims, dtype)


def attend_kernel(tab_ref, *refs, groups, chunk, tile, bias2):
    qkv_refs, (cos_ref, sin_ref) = refs[:groups], refs[groups : groups + 2]
    out_refs = refs[groups + 2 : 2 * groups + 2]
    q_ref, k_ref, v_ref, acc_ref = refs[2 * groups + 2 :]
    rows = qkv_refs[0].shape[0]
    per_group = rows // chunk
    length = groups * rows
    for j in range(length // chunk):
        g, s = divmod(j, per_group)
        here = pl.ds(s * chunk, chunk)
        there = pl.ds(pl.multiple_of(tab_ref[j] * chunk, chunk), chunk)
        cos = cos_ref[there, :]
        sin = sin_ref[there, :]
        q = qkv_refs[g][here, 0:HD].astype(F32)
        k = qkv_refs[g][here, HD : 2 * HD].astype(F32)
        q_ref[there, :] = (q * cos - pltpu.roll(q, HD // 2, 1) * sin).astype(BF)
        k_ref[there, :] = (k * cos - pltpu.roll(k, HD // 2, 1) * sin).astype(BF)
        v_ref[there, :] = qkv_refs[g][here, 2 * HD : 3 * HD]
    slope = -LOG2E / math.sqrt(HD)

    def part(i, j, masked):
        qs = q_ref[pl.ds(i * tile, tile), :]
        ks = k_ref[pl.ds(j * tile, tile), :]
        vs = v_ref[pl.ds(j * tile, tile), :]
        sig = 1.0 / (1.0 + jnp.exp2(dot_nt(qs, ks) * slope + bias2))
        if masked:
            row = lax.broadcasted_iota(jnp.int32, (tile, tile), 0)
            col = lax.broadcasted_iota(jnp.int32, (tile, tile), 1)
            sig = jnp.where(col <= row, sig, 0.0)
        return dot_nn(sig.astype(BF), vs)

    def query(i, carry):
        own = pl.ds(pl.multiple_of(i * tile, tile), tile)
        acc_ref[own, :] = part(i, i, True)

        def key(j, carry):
            acc_ref[own, :] += part(i, j, False)
            return carry

        lax.fori_loop(0, i, key, 0)
        return carry

    lax.fori_loop(0, length // tile, query, 0)
    for j in range(length // chunk):
        g, s = divmod(j, per_group)
        there = pl.ds(pl.multiple_of(tab_ref[j] * chunk, chunk), chunk)
        out_refs[g][pl.ds(s * chunk, chunk), :] = acc_ref[there, :].astype(BF)


def attend_back_kernel(tab_ref, *refs, groups, chunk, tile, bias2):
    grad_refs = refs[:groups]
    q_ref, k_ref, v_ref, cos_ref, sin_ref = refs[groups : groups + 5]
    out_refs = refs[groups + 5 : 2 * groups + 5]
    do_ref, dq_ref, dk_ref, dv_ref = refs[2 * groups + 5 :]
    rows = grad_refs[0].shape[0]
    per_group = rows // chunk
    length = groups * rows
    for j in range(length // chunk):
        g, s = divmod(j, per_group)
        there = pl.ds(pl.multiple_of(tab_ref[j] * chunk, chunk), chunk)
        do_ref[there, :] = grad_refs[g][pl.ds(s * chunk, chunk), :]
    slope = -LOG2E / math.sqrt(HD)
    scale = 1.0 / math.sqrt(HD)

    def part(i, j, masked):
        qi = pl.ds(pl.multiple_of(i * tile, tile), tile)
        kj = pl.ds(pl.multiple_of(j * tile, tile), tile)
        qs, ks, vs, dos = q_ref[qi, :], k_ref[kj, :], v_ref[kj, :], do_ref[qi, :]
        sig = 1.0 / (1.0 + jnp.exp2(dot_nt(ks, qs) * slope + bias2))
        dsc = dot_nt(vs, dos) * sig * (1.0 - sig)
        if masked:
            row = lax.broadcasted_iota(jnp.int32, (tile, tile), 0)
            col = lax.broadcasted_iota(jnp.int32, (tile, tile), 1)
            sig = jnp.where(row <= col, sig, 0.0)
            dsc = jnp.where(row <= col, dsc, 0.0)
        dsc = dsc.astype(BF)
        dv = dot_nn(sig.astype(BF), dos)
        dk = dot_nn(dsc, qs)
        dq = dot_tn(dsc, ks)
        if masked:
            dq_ref[qi, :] = dq
            dk_ref[kj, :] = dk
            dv_ref[kj, :] = dv
        else:
            dq_ref[qi, :] += dq
            dk_ref[kj, :] += dk
            dv_ref[kj, :] += dv

    def query(i, carry):
        part(i, i, True)

        def key(j, carry):
            part(i, j, False)
            return carry

        lax.fori_loop(0, i, key, 0)
        return carry

    lax.fori_loop(0, length // tile, query, 0)
    for j in range(length // chunk):
        g, s = divmod(j, per_group)
        here = pl.ds(s * chunk, chunk)
        there = pl.ds(pl.multiple_of(tab_ref[j] * chunk, chunk), chunk)
        cos = cos_ref[there, :] * scale
        sin = sin_ref[there, :] * scale
        dq = dq_ref[there, :]
        dk = dk_ref[there, :]
        out_refs[g][here, 0:HD] = (dq * cos + pltpu.roll(dq, HD // 2, 1) * sin).astype(BF)
        out_refs[g][here, HD : 2 * HD] = (dk * cos + pltpu.roll(dk, HD // 2, 1) * sin).astype(BF)
        out_refs[g][here, 2 * HD : 3 * HD] = dv_ref[there, :].astype(BF)


def attend(table, qkv, cos, sin, chunk, length):
    groups = len(qkv)
    rows = qkv[0].shape[0]
    tile = min(512, length)
    full = shape((length, HD), BF)
    out = pl.pallas_call(
        functools.partial(
            attend_kernel, groups=groups, chunk=chunk, tile=tile, bias2=math.log2(length)
        ),
        out_shape=(shape((rows, HD), BF),) * groups + (full,) * 3,
        in_specs=[SM] + [VM] * (groups + 2),
        out_specs=(VM,) * (groups + 3),
        scratch_shapes=[pltpu.VMEM((length, HD), F32)],
        compiler_params=pltpu.CompilerParams(vmem_limit_bytes=40 << 20),
        cost_estimate=pl.CostEstimate(
            flops=2 * length * length * HD * 2,
            transcendentals=length * length * 2,
            bytes_accessed=length * HD * 24 * 2,
        ),
        name="attend",
    )(table, *qkv, cos, sin)
    return out[:groups], out[groups:]


def attend_back(table, grad, saved, cos, sin, chunk, length, deps):
    groups = len(grad)
    rows = grad[0].shape[0]
    tile = min(512, length)
    known = groups + 6
    kernel = functools.partial(
        attend_back_kernel, groups=groups, chunk=chunk, tile=tile, bias2=math.log2(length)
    )

    def body(*refs):
        kernel(*refs[:known], *refs[known + len(deps) :])

    return pl.pallas_call(
        body,
        out_shape=(shape((rows, 3 * HD), BF),) * groups,
        in_specs=[SM] + [VM] * (groups + 5) + [pl.BlockSpec(memory_space=pl.ANY)] * len(deps),
        out_specs=(VM,) * groups,
        scratch_shapes=[pltpu.VMEM((length, HD), BF)] + [pltpu.VMEM((length, HD), F32)] * 3,
        compiler_params=pltpu.CompilerParams(vmem_limit_bytes=40 << 20),
        cost_estimate=pl.CostEstimate(
            flops=5 * length * length * HD * 2,
            transcendentals=length * length * 2,
            bytes_accessed=length * HD * 24 * 2,
        ),
        name="attend_back",
    )(table, *grad, *saved, cos, sin, *deps)


def ring_shapes(own, slots, half):
    return (
        (shape((2, own, half), F32),)
        + (shape((2, own, half), BF),) * (slots - 2)
        + (shape((2, own // 2, half), BF),) * 2
    )


def ring_store(refs, h, rows, own):
    refs[0][h] = rows[:own]
    at = own
    for ref in refs[1:]:
        n = ref.shape[1]
        ref[h] = rows[at : at + n].astype(BF)
        at += n


def project(x, w0, w1, at, n, name, deps=()):
    _, g, half = x.shape
    t = w0.shape[0]

    def body(x_ref, a_ref, b_ref, *outs):
        k = pl.program_id(0)
        rows = (dot_nn(x_ref[0], a_ref[0]) + dot_nn(x_ref[1], b_ref[0])).astype(BF)
        for i, out_ref in enumerate(outs):

            @pl.when(k == i)
            def _():
                out_ref[...] = rows

    w_spec = pl.BlockSpec((1, half, n), lambda k: (k, 0, at // n))
    return call(
        body,
        (t,),
        [pl.BlockSpec((2, g, half), lambda k: (0, 0, 0)), w_spec, w_spec],
        (pl.BlockSpec((g, n), lambda k: (0, 0)),) * t,
        (shape((g, n), BF),) * t,
        [],
        4 * g * half * t * n,
        4 * half * t * n + 4 * g * half + 2 * g * t * n,
        name,
        deps,
    )(x, w0, w1)


def mm_back(parts, w0, w1, at, own, name, deps=()):
    t, g, n = parts.shape
    half = w0.shape[1]
    th = min(half, 256)

    def body(p_ref, a_ref, b_ref, *outs):
        for h, w_ref in enumerate((a_ref, b_ref)):
            acc = dot_nt(p_ref[0], w_ref[0])
            for k in range(1, t):
                acc += dot_nt(p_ref[k], w_ref[k])
            ring_store(outs, h, acc, own)

    w_spec = pl.BlockSpec((t, th, n), lambda j: (0, j, at // n))
    shapes = ring_shapes(own, g // own, half)
    return call(
        body,
        (half // th,),
        [pl.BlockSpec((t, g, n), lambda j: (0, 0, 0)), w_spec, w_spec],
        tuple(pl.BlockSpec(o.shape[:2] + (th,), lambda j: (0, 0, j)) for o in shapes),
        shapes,
        [],
        4 * g * half * t * n,
        4 * half * t * n + 2 * g * t * n + 4 * g * half,
        name,
        deps,
    )(parts, w0, w1)


def gate_up(x, w0, w1, deps=()):
    _, g, half = x.shape
    t, _, n = w0.shape
    n //= 2
    tn = min(n, 256)
    steps = n // tn

    def body(x_ref, g0_ref, g1_ref, u0_ref, u1_ref, hid_ref, to_gate_ref, to_up_ref):
        gate = dot_nn(x_ref[0], g0_ref[0]) + dot_nn(x_ref[1], g1_ref[0])
        up = dot_nn(x_ref[0], u0_ref[0]) + dot_nn(x_ref[1], u1_ref[0])
        sig = 1.0 / (1.0 + jnp.exp(-gate))
        act = gate * sig
        hid_ref[0] = (act * up).astype(BF)
        to_gate_ref[0] = (up * (sig * (1.0 + gate * (1.0 - sig)))).astype(BF)
        to_up_ref[0] = act.astype(BF)

    g_spec = pl.BlockSpec((1, half, tn), lambda k, j: (k, 0, j))
    u_spec = pl.BlockSpec((1, half, tn), lambda k, j: (k, 0, j + steps))
    f_spec = pl.BlockSpec((1, g, tn), lambda k, j: (k, 0, j))
    return call(
        body,
        (t, steps),
        [pl.BlockSpec((2, g, half), lambda k, j: (0, 0, 0)), g_spec, g_spec, u_spec, u_spec],
        (f_spec,) * 3,
        (shape((t, g, n), BF),) * 3,
        [],
        1000,
        1000,
        "gate_up",
        deps,
    )(x, w0, w1, w0, w1)


def feed_back(gy, to_gate, to_up, w0, w1, d0, d1, own, deps=()):
    _, g, half = gy.shape
    t, _, n = d0.shape
    tn = min(n, 256)
    steps = n // tn

    def body(y_ref, a_ref, b_ref, g0_ref, g1_ref, u0_ref, u1_ref, d0_ref, d1_ref, *rest):
        out_ref, outs, acc_ref = rest[0], rest[1:-1], rest[-1]
        k, j = pl.program_id(0), pl.program_id(1)
        dh = dot_nn(y_ref[0], d0_ref[0]) + dot_nn(y_ref[1], d1_ref[0])
        dgate = (dh * a_ref[0].astype(F32)).astype(BF)
        dup = (dh * b_ref[0].astype(F32)).astype(BF)
        out_ref[0, 0] = dgate
        out_ref[0, 1] = dup
        first = jnp.logical_and(k == 0, j == 0)
        for h, (p_ref, q_ref) in enumerate(((g0_ref, u0_ref), (g1_ref, u1_ref))):
            part = dot_nt(dgate, p_ref[0]) + dot_nt(dup, q_ref[0])

            @pl.when(first)
            def _():
                acc_ref[h] = part

            @pl.when(jnp.logical_not(first))
            def _():
                acc_ref[h] += part

        @pl.when(jnp.logical_and(k == t - 1, j == steps - 1))
        def _():
            for h in range(2):
                ring_store(outs, h, acc_ref[h], own)

    g_spec = pl.BlockSpec((1, half, tn), lambda k, j: (k, 0, j))
    u_spec = pl.BlockSpec((1, half, tn), lambda k, j: (k, 0, j + steps))
    f_spec = pl.BlockSpec((1, g, tn), lambda k, j: (k, 0, j))
    shapes = ring_shapes(own, g // own, half)
    return call(
        body,
        (t, steps),
        [pl.BlockSpec((2, g, half), lambda k, j: (0, 0, 0)), f_spec, f_spec]
        + [g_spec, g_spec, u_spec, u_spec, g_spec, g_spec],
        (pl.BlockSpec((1, 2, g, tn), lambda k, j: (k, 0, 0, j)),)
        + tuple(pl.BlockSpec(o.shape, lambda k, j: (0, 0, 0)) for o in shapes),
        (shape((t, 2, g, n), BF),) + shapes,
        [pltpu.VMEM((2, g, half), F32)],
        12 * g * half * t * n,
        12 * half * t * n + 8 * g * t * n + 8 * g * half,
        "feed_back",
        deps,
    )(gy, to_gate, to_up, w0, w1, w0, w1, d0, d1)


def weight_grad(place, left, left_peer, right, right_peer, name, deps=()):
    g, half = left.shape
    t, m, _, n = right.shape
    tn = n if n % 256 else 256

    def body(s_ref, a_ref, b_ref, c_ref, d_ref, out_ref):
        del s_ref
        out_ref[0] = (
            dot_tn(a_ref[...], c_ref[0, 0]) + dot_tn(b_ref[...], d_ref[0, 0])
        ).astype(BF)

    l_spec = pl.BlockSpec((g, half), lambda k, i, j, s: (0, 0))
    r_spec = pl.BlockSpec((1, 1, g, tn), lambda k, i, j, s: (k, i, 0, j))
    return placed_call(
        body,
        (t, m, n // tn),
        [l_spec, l_spec, r_spec, r_spec],
        pl.BlockSpec((1, half, tn), lambda k, i, j, s: (k ^ s[0], 0, i * (n // tn) + j)),
        shape((t, half, m * n), BF),
        4 * g * half * t * m * n,
        4 * g * t * m * n + 4 * g * half + 2 * half * t * m * n,
        name,
        deps,
    )(place, left, left_peer, right, right_peer)


def weight_grad_heads(xn, xn_peer, dqkv, dqkv_peer, dres, dres_peer, mixed, mixed_peer, deps=()):
    g, half = xn.shape
    t, _, n = dqkv.shape
    m = mixed.shape[2]

    def body(a_ref, b_ref, c_ref, d_ref, e_ref, f_ref, g_ref, h_ref, out_ref):
        out_ref[0, :, :n] = (
            dot_tn(a_ref[...], c_ref[0]) + dot_tn(b_ref[...], d_ref[0])
        ).astype(BF)
        out_ref[0, :, n:] = (
            dot_tn(e_ref[...], g_ref[0]) + dot_tn(f_ref[...], h_ref[0])
        ).astype(BF)

    l_spec = pl.BlockSpec((g, half), lambda k: (0, 0))
    n_spec = pl.BlockSpec((1, g, n), lambda k: (k, 0, 0))
    m_spec = pl.BlockSpec((1, g, m), lambda k: (k, 0, 0))
    return call(
        body,
        (t,),
        [l_spec, l_spec, n_spec, n_spec, l_spec, l_spec, m_spec, m_spec],
        pl.BlockSpec((1, half, n + m), lambda k: (k, 0, 0)),
        shape((t, half, n + m), BF),
        [],
        4 * g * half * t * (n + m),
        4 * g * t * (n + m) + 8 * g * half + 2 * half * t * (n + m),
        "g_heads",
        deps,
    )(xn, xn_peer, dqkv, dqkv_peer, dres, dres_peer, mixed, mixed_peer)


def placed_call(body, grid, in_specs, out_specs, out_shape, flops, bytes_accessed, name, deps):
    known = len(in_specs) + 1
    skip = len(deps)

    def run(*refs):
        body(*refs[:known], *refs[known + skip :])

    made = pl.pallas_call(
        run,
        grid_spec=pltpu.PrefetchScalarGridSpec(
            num_scalar_prefetch=1,
            grid=grid,
            in_specs=list(in_specs) + [pl.BlockSpec(memory_space=pl.ANY)] * skip,
            out_specs=out_specs,
        ),
        out_shape=out_shape,
        compiler_params=pltpu.CompilerParams(
            vmem_limit_bytes=48 << 20,
            dimension_semantics=("arbitrary",) * len(grid),
        ),
        cost_estimate=pl.CostEstimate(
            flops=flops // SHARE, transcendentals=0, bytes_accessed=bytes_accessed // SHARE
        ),
        name=name,
    )
    return lambda *args: made(*args, *deps)


def pack_weights(columns, rows, parts, apart, name, deps=()):
    k, n = columns[0].shape
    n //= parts
    count = len(columns)

    def body(*refs):
        out_ref = refs[count + 1]
        for i, ref in enumerate(refs[:count]):
            out_ref[0, :, i * n : (i + 1) * n] = ref[...].astype(BF)
        turned = jnp.transpose(refs[count][...]).astype(BF)
        if apart:
            refs[-1][0] = turned
        else:
            out_ref[0, :, count * n :] = turned

    widths = (count * n, n) if apart else ((count + 1) * n,)
    return call(
        body,
        (parts,),
        [pl.BlockSpec((k, n), lambda p: (0, p))] * count + [pl.BlockSpec((n, k), lambda p: (p, 0))],
        tuple(pl.BlockSpec((1, k, w), lambda p: (p, 0, 0)) for w in widths),
        tuple(shape((parts, k, w), BF) for w in widths),
        [],
        1000,
        1000,
        name,
        deps,
    )(*columns, rows)


def unpack_columns(parts, count, transposed, name):
    z, k, n = parts.shape
    n //= count

    def body(in_ref, *outs):
        for i, ref in enumerate(outs):
            part = in_ref[0, :, i * n : (i + 1) * n].astype(F32)
            ref[...] = jnp.transpose(part) if transposed and i == count - 1 else part

    straight = (pl.BlockSpec((k, n), lambda p: (0, p)), shape((k, z * n), F32))
    turned = (pl.BlockSpec((n, k), lambda p: (p, 0)), shape((z * n, k), F32))
    outs = [straight] * (count - 1) + [turned if transposed else straight]
    return call(
        body,
        (z,),
        [pl.BlockSpec((1, k, count * n), lambda p: (p, 0, 0))],
        tuple(o[0] for o in outs),
        tuple(o[1] for o in outs),
        [],
        1000,
        1000,
        name,
        (),
    )(parts)


def place_blocks(index, sources, dtype):
    counts = [x.shape[0] for x in sources]
    rows, width = sources[0].shape[1:]
    blocks = index.shape[0]

    def body(s_ref, *refs):
        out_ref = refs[-1]
        wanted = s_ref[pl.program_id(0)]
        at = 0
        for n, ref in zip(counts, refs):
            for i in range(n):

                @pl.when(wanted == at)
                def _():
                    out_ref[0] = ref[i].astype(dtype)

                at += 1

    return placed_call(
        body,
        (blocks,),
        [pl.BlockSpec(x.shape, lambda b, s: (0, 0, 0)) for x in sources],
        pl.BlockSpec((1, rows, width), lambda b, s: (b, 0, 0)),
        shape((blocks, rows, width), dtype),
        0,
        12 * blocks * rows * width,
        "place",
        (),
    )(index, *sources)


def after(x, *deps):
    for d in deps:
        corner = lax.slice(d, [n - 1 for n in d.shape], d.shape).reshape(())
        x = x + (corner.astype(F32) * 0.0).astype(x.dtype)
    return x


def tie(x, *deps):
    anywhere = pl.BlockSpec(memory_space=pl.ANY)
    return pl.pallas_call(
        lambda *refs: None,
        in_specs=[anywhere] * (1 + len(deps)),
        out_specs=anywhere,
        out_shape=shape(x.shape, x.dtype),
        input_output_aliases={0: 0},
        name="tie",
    )(x, *deps)


def build(z_size, tp_size):
    shards = 2 * z_size
    ring = [0] + list(range(1, z_size, 2)) + list(range(z_size - 2, 0, -2))
    place = [ring.index(z) for z in range(z_size)]
    forward = [(ring[i], ring[(i + 1) % z_size]) for i in range(z_size)]
    backward = [(b, a) for a, b in forward]
    half_ring = z_size // 2
    offsets = [0]
    for k in range(1, half_ring):
        offsets += [-k, k]
    offsets += [half_ring]
    holder = [[ring[(place[z] + off) % z_size] for off in offsets] for z in range(z_size)]
    swap_core = [(0, 1), (1, 0)]

    def hop(x, bit):
        return lax.ppermute(x, "tp", [(t, t ^ bit) for t in range(tp_size)])

    def swap(x):
        return lax.ppermute(x, "core", swap_core)

    def ring_first(x):
        chunks = [x]
        ahead = back = x
        for _ in range(1, half_ring):
            ahead = lax.ppermute(ahead, "z", forward)
            back = lax.ppermute(back, "z", backward)
            chunks += [ahead, back]
        return chunks

    def ring_last(chunks, *deps):
        ahead, back = chunks[-2:]
        mid = ahead.shape[1] // 2
        one = lax.ppermute(after(ahead[:, :mid], back, *deps), "z", forward)
        two = lax.ppermute(after(back[:, mid:], ahead, *deps), "z", backward)
        return chunks + [one, two]

    def gather_ring(x, *deps):
        return ring_last(ring_first(x), *deps)

    def join_rows(chunks):
        return jnp.concatenate(chunks, axis=1)

    def scatter_first(parts):
        return (
            lax.ppermute(parts[-2], "z", forward),
            lax.ppermute(parts[-1], "z", backward),
        )

    def scatter_last(parts, came, *deps):
        one, two = came
        mid = parts[0].shape[1] // 2
        for k in range(half_ring - 1, 0, -1):
            fwd, bwd = parts[offsets.index(k)], parts[offsets.index(-k)]
            if k == half_ring - 1:
                fwd = jnp.concatenate([fwd[:, :mid] + one, fwd[:, mid:]], axis=1)
                bwd = jnp.concatenate([bwd[:, :mid], bwd[:, mid:] + two], axis=1)
            else:
                fwd = fwd + one
                bwd = bwd + two
            one = lax.ppermute(fwd, "z", forward)
            two = lax.ppermute(bwd, "z", backward)
        return after(parts[0] + one.astype(F32) + two.astype(F32), *deps)

    def scatter_ring(parts, *deps):
        return scatter_last(parts, scatter_first(parts), *deps)

    def tick(x):
        corner = lax.slice(x.reshape((-1,) + x.shape[-1:]), (0, 0), (16, 128))
        return swap(corner.astype(BF))

    def near_tp(x):
        return (hop(x, 1), hop(x, 2)) if tp_size == 4 else ()

    def far_tp(x, near, *deps):
        if tp_size != 4:
            return ()
        mid = x.shape[0] // 2
        return (
            hop(after(near[1][:mid], *deps), 1),
            hop(after(near[0][mid:], *deps), 2),
        )

    def stack_tp(x, near, far, *deps):
        if tp_size == 4:
            return after(jnp.stack([x, *near, jnp.concatenate(far, axis=0)]), *deps)
        held = x[None]
        bit = 1
        while bit < tp_size:
            held = jnp.concatenate([held, hop(held, bit)], axis=0)
            bit *= 2
        return held

    def gather_tp(x):
        near = near_tp(x)
        return stack_tp(x, near, far_tp(x, near))

    def scatter_tp_first(part):
        if tp_size == 4:
            mid = part.shape[1] // 2
            top, low = part[:, :mid], part[:, mid:]
            return hop(jnp.stack([top[1], top[3]]), 1), hop(jnp.stack([low[2], low[3]]), 2)
        return ()

    def scatter_tp_last(part, came):
        if tp_size == 4:
            over_x, over_y = came
            mid = part.shape[1] // 2
            top, low = part[:, :mid], part[:, mid:]
            top2 = hop(top[2] + over_x[1], 2)
            low1 = hop(low[1] + over_y[1], 1)
            return jnp.concatenate([top[0] + over_x[0] + top2, low[0] + over_y[0] + low1], axis=0)
        bit = tp_size // 2
        while bit:
            part = part[:bit] + hop(part[bit:], bit)
            bit //= 2
        return part[0]

    def to_z(x):
        return lax.all_to_all(x, "z", split_axis=0, concat_axis=0, tiled=True)

    def on_device(
        layer_in,
        positions,
        seq_ids,
        norm1_gain,
        norm2_gain,
        w_query,
        w_key,
        w_value,
        w_out,
        w_gate,
        w_up,
        w_down,
        out_grad,
    ):
        z, core, tp = lax.axis_index("z"), lax.axis_index("core"), lax.axis_index("tp")
        rows, width = layer_in.shape
        half = width // 2
        block = rows // 4
        own = rows // tp_size
        group = own * z_size
        length = rows * shards // 2
        k_rows = width // shards
        heads = w_query.shape[1] * tp_size // HD
        heads_here = heads // z_size
        plain = w_query.shape[1] == z_size * HD and heads_here == tp_size
        flipped = core == 1

        def split(x):
            lead = x.shape[:-1]
            x = x.reshape(lead + (z_size, 2, k_rows))
            even, odd = x[..., 0, :].reshape(lead + (half,)), x[..., 1, :].reshape(lead + (half,))
            return jnp.stack([jnp.where(flipped, odd, even), jnp.where(flipped, even, odd)])

        def join(x):
            lead = x.shape[1:-1]
            even, odd = jnp.where(flipped, x[1], x[0]), jnp.where(flipped, x[0], x[1])
            even = even.reshape(lead + (z_size, 1, k_rows))
            odd = odd.reshape(lead + (z_size, 1, k_rows))
            return jnp.concatenate([even, odd], axis=-2).reshape(lead + (width,))

        sound = positions[0] >= 0

        def stage(run):
            outs = jax.eval_shape(run)
            blank = lambda: jax.tree.map(lambda o: jnp.zeros(o.shape, o.dtype), outs)
            return lax.cond(sound, run, blank)

        key = seq_ids.reshape(4, block)[:, 0] * (4 * length) + positions.reshape(4, block)[:, 0]
        rank = jnp.sum((key[None, :] < key[:, None]).astype(jnp.int32), axis=1)
        source_core = tp // (tp_size // 2)
        offset = (tp % (tp_size // 2)) * own

        def piece(x, seq):
            wanted = 2 * seq + offset // block
            start = jnp.sum(jnp.where(rank == wanted, jnp.arange(4, dtype=jnp.int32), 0)) * block
            return lax.dynamic_slice(x, (start + offset % block, 0), (own, width))

        def take_own(x):
            return split(jnp.where(core == source_core, piece(x, core), swap(piece(x, 1 - core))))

        x_own = take_own(layer_in).astype(F32)
        gy_own = take_own(out_grad)
        gain1 = split(norm1_gain)[:, None]
        gain2 = split(norm2_gain)[:, None]
        scale1 = lax.rsqrt(jnp.mean(x_own * x_own, axis=(0, 2), keepdims=True) + EPSILON)
        xn1_own = x_own * scale1 * gain1

        quarter = HD // 2
        frequency = jnp.power(F32(10000.0), -jnp.arange(quarter, dtype=F32) / quarter)
        phase = jnp.arange(length, dtype=jnp.int32).astype(F32)[:, None] * frequency[None, :]

        def rotations(*deps):
            turned = after(phase, *deps)
            rot_cos, rot_sin = jnp.cos(turned), jnp.sin(turned)
            cos = jnp.concatenate([rot_cos, rot_cos], axis=1)
            return cos, jnp.concatenate([rot_sin, -rot_sin], axis=1)

        def exchange(w):
            return to_z(w).reshape(half, w.shape[2])

        if plain:
            (low,) = pack_weights(
                (w_query, w_key, w_value), w_out, z_size, False, "pack_heads"
            )
            low = exchange(low)
            xn1_low = after(xn1_own, low).astype(BF)

            def begin():
                chunks = ring_first(xn1_low)
                near = near_tp(low)
                started = tick(low)
                turns = rotations(started)
                far = far_tp(low, near, *chunks[1:3], turns[0])
                ffn_low = pack_weights(
                    (w_gate, w_up), w_down, z_size, True, "pack_ffn", (tick(chunks[-1]),)
                )
                chunks = ring_last(chunks)
                full = stack_tp(low, near, far, *chunks[-2:])
                return join_rows(chunks), (full, swap(full)), turns, ffn_low

            xn1, head_w, (cos, sin), ffn_low = stage(begin)
        else:
            at_head = z * heads_here * HD

            def columns(w):
                w = lax.all_gather(w.astype(BF), "tp", axis=1, tiled=True)
                w = lax.all_gather(w, ("z", "core"), axis=0, tiled=True)
                w = lax.dynamic_slice(w, (0, at_head), (width, heads_here * HD))
                return jnp.swapaxes(split(w.T).reshape(2, heads_here, HD, half), 2, 3)

            low = [columns(w) for w in (w_query, w_key, w_value, w_out.T)]
            low = jnp.concatenate(low, axis=3)
            head_w = (low[0], low[1])
            xn1 = join_rows(gather_ring(xn1_own.astype(BF)))
            cos, sin = rotations()
            ffn_low = pack_weights((w_gate, w_up), w_down, z_size, True, "pack_ffn")
        gate_up_one = exchange(ffn_low[0])

        t_all = jnp.arange(tp_size, dtype=jnp.int32)[:, None]
        if plain:
            t_all = jnp.bitwise_xor(t_all, tp)
        z_all = jnp.asarray(holder, jnp.int32)[z][None, :]
        off_all = (t_all % (tp_size // 2)) * own
        shard_all = 2 * z_all + t_all // (tp_size // 2)
        block_all = jnp.where(off_all < block, shard_all, 2 * shards - 1 - shard_all)
        table = ((block_all * block + off_all % block) // own).reshape(-1)

        def to_heads(x):
            if plain:
                return [x[0]] + [hop(x[k], k) for k in range(1, tp_size)]
            every = lax.all_gather(jnp.stack(x), "tp", axis=0)
            every = lax.dynamic_index_in_dim(
                every, tp * heads_here // tp_size, axis=1, keepdims=False
            )
            return [every[k] for k in range(tp_size)]

        def to_tokens(x):
            if plain:
                return jnp.stack([x[0]] + [hop(x[k], k) for k in range(1, tp_size)])
            every = lax.all_gather(jnp.stack(x), "tp", axis=0)[:: tp_size // heads_here]
            return lax.dynamic_index_in_dim(every, tp, axis=1, keepdims=False)

        qkv = project(xn1, *head_w, 0, 3 * HD, "qkv")
        heads_out, saved = attend(table, to_heads(qkv), cos, sin, own, length)
        mixed = to_tokens(heads_out)
        attn = mm_back(mixed, *head_w, 3 * HD, own, "attn_out")

        def first():
            return x_own + scatter_ring(attn), near_tp(gate_up_one)

        hres, gate_up_near = stage(first)
        down_one = exchange(tie(ffn_low[1], hres))

        scale2 = lax.rsqrt(jnp.mean(hres * hres, axis=(0, 2), keepdims=True) + EPSILON)
        xn2_own = (hres * scale2 * gain2).astype(BF)

        def second():
            chunks = ring_first(xn2_own)
            far = far_tp(gate_up_one, gate_up_near, tick(xn2_own))
            low = stack_tp(gate_up_one, gate_up_near, far, *(tick(x) for x in chunks[1:3]))
            peer = swap(low)
            return join_rows(ring_last(chunks)), (low, peer)

        xn2, gate_up_w = stage(second)

        def third():
            chunks = ring_first(gy_own)
            near = near_tp(down_one)
            xn2_peer = swap(xn2[1])
            out = gate_up(xn2, *gate_up_w)
            far = far_tp(down_one, near, *chunks[1:3], out[0])
            chunks = ring_last(chunks, out[0])
            low = stack_tp(down_one, near, far)
            return join_rows(chunks), (low, swap(low)), out, xn2_peer

        gy, down_w, (hid, to_gate, to_up), xn2_peer = stage(third)
        dgu, *dx = feed_back(gy, to_gate, to_up, *gate_up_w, *down_w, own)
        here = jnp.broadcast_to(tp, (1,)).astype(jnp.int32)

        def fourth():
            came = scatter_first(dx)
            gy_peer, hid_peer, dgu_peer = swap(gy[1]), swap(hid), swap(dgu)
            g_down = weight_grad(here, gy[0], gy_peer, hid[:, None], hid_peer[:, None], "g_down")
            g_gu = weight_grad(here, xn2[0], xn2_peer, dgu, dgu_peer, "g_gate_up", (g_down, *came))
            return scatter_last(dx, came, g_gu), g_down, g_gu

        dxn2, g_down, g_gu = stage(fourth)

        def sum_tp(part):
            return lax.psum_scatter(part, "tp", scatter_dimension=0, tiled=False)

        def place_columns(part, *deps):
            return to_z(after(part.reshape(z_size, k_rows, part.shape[1]), *deps))

        gain2_part = jnp.sum(dxn2 * hres * scale2, axis=1)
        e2 = dxn2 * gain2
        dres = (
            gy_own.astype(F32)
            + scale2 * e2
            - hres
            * (scale2 * scale2 * scale2)
            * jnp.mean(e2 * hres, axis=(0, 2), keepdims=True)
        )
        dres_low = dres.astype(BF)
        g_down, g_gu = tie(sum_tp(g_down)), tie(sum_tp(g_gu))

        def fifth():
            chunks = ring_first(dres_low)
            ffn = mm_back(hid, *down_w, 0, own, "ffn_out", (tick(dres_low),))
            return join_rows(ring_last(chunks)), ffn

        dres_all, ffn = stage(fifth)
        dmix = project(dres_all, *head_w, 3 * HD, HD, "dmix")
        dmix, came = stage(lambda: (to_heads(dmix), scatter_first(ffn)))
        dheads = attend_back(table, dmix, saved, cos, sin, own, length, ())

        def sixth():
            return to_tokens(dheads), hres + scatter_last(ffn, came), place_columns(g_down)

        dqkv, layer_own, g_down = stage(sixth)
        dx = mm_back(dqkv, *head_w, 0, own, "dxn1")

        def seventh():
            came = scatter_first(dx)
            peers = swap(xn1[1]), swap(dqkv), swap(dres_all[1]), swap(mixed)
            g_heads = weight_grad_heads(
                xn1[0], peers[0], dqkv, peers[1], dres_all[0], peers[2], mixed, peers[3]
            )
            heads_came = scatter_tp_first(g_heads) if plain else ()
            return scatter_last(dx, came), g_heads, heads_came

        dxn1, g_heads, heads_came = stage(seventh)
        gain1_part = jnp.sum(dxn1 * x_own * scale1, axis=1)
        e1 = dxn1 * gain1
        in_own = (
            dres
            + scale1 * e1
            - x_own
            * (scale1 * scale1 * scale1)
            * jnp.mean(e1 * x_own, axis=(0, 2), keepdims=True)
        )

        in_own = join(in_own).astype(BF)
        layer_own = join(layer_own).astype(BF)

        gains = join(jnp.stack([gain1_part, gain2_part], axis=1)).reshape(2, shards, 1, k_rows)
        gains = jnp.broadcast_to(gains, (2, shards, tp_size, k_rows))
        gains = jnp.swapaxes(gains.reshape(2, shards * tp_size, k_rows), 0, 1)

        def eighth():
            near = near_tp(in_own)
            heads = scatter_tp_last(g_heads, heads_came) if plain else g_heads
            in_all = spread_over(in_own, near, heads)
            layer_low = after(layer_own, heads)
            layer_all = spread_over(layer_low, near_tp(layer_low))
            placed = place_columns(g_gu)
            if plain:
                heads = place_columns(heads, placed)
            return in_all, layer_all, placed, heads

        def spread_over(x, near, *deps):
            far = far_tp(x, near, *deps)
            if not (tp_size == 4 and own == block):
                return stack_tp(x, near, far)
            far = jnp.concatenate(far, axis=0)
            matched = core == tp // 2
            sent = jnp.where(matched, jnp.stack([near[1], far]), jnp.stack([x, near[0]]))
            return x[None], near[0][None], near[1][None], far[None], swap(sent)

        in_all, layer_all, g_gu, g_heads = stage(eighth)
        gains = lax.all_to_all(
            gains, ("z", "core", "tp"), split_axis=0, concat_axis=0, tiled=True
        )
        gains = jnp.sum(gains, axis=0)
        g_gate, g_up = unpack_columns(g_gu, 2, False, "unpack_gate_up")
        (g_down,) = unpack_columns(g_down, 1, True, "unpack_down")
        if plain:
            g_query, g_key, g_value, g_out = unpack_columns(g_heads, 4, True, "unpack_heads")
        else:

            def back_columns(i):
                part = jnp.swapaxes(g_heads[:, :, i * HD : (i + 1) * HD], 1, 2)
                part = join(jnp.stack([part, swap(part)])).reshape(heads_here * HD, width).T
                out = jnp.zeros((width, heads * HD), BF)
                out = lax.dynamic_update_slice(out, part, (0, at_head))
                out = jnp.where(flipped, jnp.zeros_like(out), out)
                out = lax.psum_scatter(out, ("z", "core"), scatter_dimension=0, tiled=True)
                return lax.psum_scatter(out, "tp", scatter_dimension=1, tiled=True).astype(F32)

            g_query, g_key, g_value, g_out = (back_columns(i) for i in range(4))
            g_out = g_out.T
        def spread_rows(every, dtype):
            if tp_size == 4 and own == block:
                slot = jnp.bitwise_xor(rank % 2, tp % 2)
                kept = slot + jnp.where(core == tp // 2, 0, 2)
                index = jnp.where(rank // 2 == core, kept, slot + 4)
                return place_blocks(index, every, dtype).reshape(rows, width)
            order = jnp.bitwise_xor(jnp.arange(tp_size, dtype=jnp.int32), tp)
            every = jnp.take(every, order, axis=0, mode="clip").reshape(2, rows // 2, width)
            kept = lax.dynamic_index_in_dim(every, core, axis=0, keepdims=False)
            sent = lax.dynamic_index_in_dim(every, 1 - core, axis=0, keepdims=False)
            blocks = jnp.concatenate([kept, swap(sent)]).reshape(4, block, width)
            index = jnp.where(flipped, jnp.bitwise_xor(rank, 2), rank)
            return jnp.take(blocks, index, axis=0, mode="clip").reshape(rows, width).astype(dtype)

        in_grad = spread_rows(in_all, F32)
        layer_out = spread_rows(layer_all, BF)
        return (
            layer_out,
            in_grad,
            gains[0],
            gains[1],
            g_query,
            g_key,
            g_value,
            g_out,
            g_gate,
            g_up,
            g_down,
        )

    return on_device


def solution(mesh):
    tp_size = mesh.shape["tp"]
    z_size = mesh.shape["seq"] // 2
    split = Mesh(mesh.devices.reshape(z_size, 2, tp_size), ("z", "core", "tp"))
    seq = ("z", "core")
    in_specs = (
        P(seq, None),
        P(seq),
        P(seq),
        P(),
        P(),
        P(seq, "tp"),
        P(seq, "tp"),
        P(seq, "tp"),
        P("tp", seq),
        P(seq, "tp"),
        P(seq, "tp"),
        P("tp", seq),
        P(seq, None),
    )
    out_specs = (
        P(seq, None),
        P(seq, None),
        P(seq),
        P(seq),
        P(seq, "tp"),
        P(seq, "tp"),
        P(seq, "tp"),
        P("tp", seq),
        P(seq, "tp"),
        P(seq, "tp"),
        P("tp", seq),
    )
    return jax.shard_map(
        build(z_size, tp_size), mesh=split, in_specs=in_specs, out_specs=out_specs, check_vma=False
    )
```

time: 941 us -> 791 us (0.84)
  Pallas kernels: 18.5 us -> 163 us
  blocking collectives: 134 us -> 0 us
  matrix products: 122 us -> 0 us
  local copies, waits for them, and re-layouts: 147 us -> 83.4 us
  waiting for transfers between devices: 352 us -> 310 us
  starting transfers between devices: 89 us -> 118 us
  other arithmetic: 50.3 us -> 73.1 us
  loops' own time: 0 us -> 13.6 us
    pallas_call x2 -> x22, Pallas kernels: 18.5 us -> 163 us  [the longest x13 106 us: call(): return lambda *args: made(*args, *deps)]
    all_to_all x6 -> x0, blocking collectives: 134 us -> none  [the longest x4 93.1 us: exchange(): lax.all_to_all(w, 'z', split_axis=split, concat_axis=concat, tiled=True)]
    dot_general x15 -> x0, matrix products: 122 us -> none  [the longest x1 14.4 us: on_device(): jnp.einsum('mcd,ctfd->tmf', gy.reshape(group, 2, width // 2), down_w, pre...]
    reduce_scatter x5 -> x0, waiting for transfers between devices: 96.6 us -> none  [the longest x2 60.4 us: reduce_rows(): lax.psum_scatter(part, ('core', 'tp'), scatter_dimension=0, tiled=False)]
    ppermute x43 -> x89, waiting for transfers between devices: 189 us -> 282 us  [the longest x36 101 us: hop(): return lax.ppermute(x, 'tp', [(t, t ^ bit) for t in range(tp_size)])]
    all_to_all x9 -> x7, waiting for transfers between devices: 66.1 us -> 27.1 us  [the longest x6 27.1 us: to_z(): return lax.all_to_all(x, 'z', split_axis=0, concat_axis=0, tiled=True)]
    convert_element_type x11 -> x2, local copies, waits for them, and re-layouts: 38.6 us -> 3.42 us  [on_device(): in_own = join(in_own).astype(BF)]
    add x0 -> x29, other arithmetic: none -> 32.2 us  [the longest x21 21.9 us: after(): x = x + (corner.astype(F32) * 0.0).astype(x.dtype)]
  transfers between devices with their start and end apart: 62 -> 98, of which waited for: 32 -> 43; matrix products, arithmetic and copies ran while one was open for 28% -> 18% of each run, Pallas kernels for 2% -> 15%
where the time goes in v2:
time: 791 us; the launch traced here: 779 us
  waiting for transfers between devices  310 us (39%)
  Pallas kernels  163 us (21%)
  starting transfers between devices  118 us (15%)
  local copies, waits for them, and re-layouts  83.4 us (11%)
  other arithmetic  73.1 us (9%)
  between operations  17.8 us (2%)
  loops' own time  13.6 us (2%)
    pallas_call x13, Pallas kernels, call(): return lambda *args: made(*args, *deps)  106 us
    ppermute x36, waiting for transfers between devices, hop(): return lax.ppermute(x, 'tp', [(t, t ^ bit) for t in range(tp_size)])  101 us
    ppermute x4, waiting for transfers between devices, ring_last(): one = lax.ppermute(after(ahead[:, :mid], back, *deps), 'z', forward)  40.2 us
    ppermute x36, starting transfers between devices, hop(): return lax.ppermute(x, 'tp', [(t, t ^ bit) for t in range(tp_size)])  39.5 us
    ppermute x4, waiting for transfers between devices, ring_first(): back = lax.ppermute(back, 'z', backward)  38.3 us
    ppermute x4, waiting for transfers between devices, scatter_last(): one = lax.ppermute(fwd, 'z', forward)  37.9 us
    pallas_call x4, Pallas kernels, placed_call(): return lambda *args: made(*args, *deps)  35.9 us
    all_to_all x6, starting transfers between devices, to_z(): return lax.all_to_all(x, 'z', split_axis=0, concat_axis=0, tiled=True)  29.8 us
  transfers between devices with their start and end apart: 98, of which 43 were waited for; matrix products, arithmetic and copies ran while one was open for 18% of the time, Pallas kernels for 15%

profile of v2, /device:TPU:0, one launch (start us, length us, event | category | flops | bytes accessed | tf_op | source)
XLA Modules:
  0.0 779.2 jit_solution(7831262307435771819)
XLA Ops:
  13.3 6.3 all-to-all-start.3
  31.6 13.7 %all-to-all-done.3 = bf16[4,256,512]{2,1,0:T(8,128)(2,1)S(1)} async-done(((bf16[4,256,512]{2,1,0:T(8,128)(2,1)}), bf16[4,256,512]{2,1,0:T(8,128)(2,1)S(1)}, u32[]{:S(2)}, u32[]{:S(2)}) %all-to-all-start.3) | async-done | bytes 1048608 | tf_op jit(solution)/shard_map/all_to_all | solution.py:693
  47.0 64.1 %conditional.10 = (bf16[2,512,1024]{2,1,0:T(8,128)(2,1)}, bf16[4,1024,512]{2,1,0:T(8,128)(2,1)}, bf16[4,1024,512]{2,1,0:T(8,128)(2,1)}, f32[2048,128]{1,0:T(8,12...) conditional(s32[]{:T(128)} %bitcast.73, () %tuple.99, ...), branch_computations={%region_4.5_spmd, %region_5.6_spmd} | conditional | flops 15336558 | bytes 84994448 | solution.py:741
  55.5 3.8 fusion.1
  60.5 14.3 %collective-permute-done.6 = bf16[2,128,1024]{2,1,0:T(8,128)(2,1)S(1)} collective-permute-done((bf16[2,128,1024]{2,1,0:T(8,128)(2,1)}, bf16[2,128,1024]{2,1,0:T(8,128)(2,1)S(1)}, u32[]{:S(2)}, u32[]{:S(2)}) %collective-permute-start.6) | collective-permute-done | bytes 524320 | tf_op jit(solution)/shard_map/cond/branch_1_fun/ppermute | solution.py:600
  80.9 3.0 collective-permute-start.8
  83.8 9.9 %collective-permute-done.7 = bf16[2,64,1024]{2,1,0:T(8,128)(2,1)S(1)} collective-permute-done((bf16[2,64,1024]{2,1,0:T(8,128)(2,1)S(1)}, bf16[2,64,1024]{2,1,0:T(8,128)(2,1)S(1)}, u32[]{:S(2)}, u32[]{:S(2)}) %collective-permute-start.7) | collective-permute-done | bytes 262176 | tf_op jit(solution)/shard_map/cond/branch_1_fun/ppermute | solution.py:607
  96.4 3.5 fusion
  111.0 4.8 all-to-all-start.4
  116.9 7.4 qkv.1
  128.0 8.3 %collective-permute-done.83.refs_1_ = bf16[512,384]{1,0:T(8,128)(2,1)S(1)} collective-permute-done((bf16[512,384]{1,0:T(8,128)(2,1)S(1)}, bf16[512,384]{1,0:T(8,128)(2,1)S(1)}, u32[]{:S(2)}, u32[]{:S(2)}) %collective-permute-start.83) | collective-permute-done | bytes 393248 | tf_op jit(solution)/shard_map/ppermute | solution.py:590
  136.3 8.8 %collective-permute-done.84.refs_2_ = bf16[512,384]{1,0:T(8,128)(2,1)S(1)} collective-permute-done((bf16[512,384]{1,0:T(8,128)(2,1)S(1)}, bf16[512,384]{1,0:T(8,128)(2,1)S(1)}, u32[]{:S(2)}, u32[]{:S(2)}) %collective-permute-start.84) | collective-permute-done | bytes 393248 | tf_op jit(solution)/shard_map/ppermute | solution.py:590
  145.2 7.9 %attend.1 = (bf16[512,128]{1,0:T(8,128)(2,1)S(1)}, bf16[512,128]{1,0:T(8,128)(2,1)S(1)}, bf16[512,128]{1,0:T(8,128)(2,1)S(1)}, bf16[512,128]{1,0:T(8,128)(2,1)S(...) custom-call(s32[16]{0:T(128)S(1)} %and_select_fusion.tab_ref.refs_0_, ...), custom_call_target="tpu_custom_call" | custom-call | flops 2147483648 | bytes 12582912 | tf_op jit(solution)/shard_map/attend/pallas_call | solution.py:181
  161.9 5.5 attn_out.1
  167.4 47.2 %conditional.11 = (f32[2,128,1024]{2,1,0:T(8,128)}, bf16[1024,1024]{1,0:T(8,128)(2,1)}, bf16[1024,1024]{1,0:T(8,128)(2,1)}, f32[1,128,1]{1,2,0:T(1,128)S(1)}, f32[2,128,1024]{1,2,0:T(8,128)S(1)}) conditional(s32[]{:T(128)} %bitcast.73, () %tuple.98, (bf16[2,128,1024]{2,1,0:T(8,128)(2,1)}, bf16[2,64,1024]{2,1,0:T(8,128)(2,1)}, ...), branch_computations={%region_6.7_spmd, %region_7.9_spmd} | conditional | flops 4194176 | bytes 38273844 | solution.py:741
  172.6 10.4 %collective-permute-done.75 = bf16[2,64,1024]{2,1,0:T(8,128)(2,1)S(1)} collective-permute-done((bf16[2,64,1024]{2,1,0:T(8,128)(2,1)}, bf16[2,64,1024]{2,1,0:T(8,128)(2,1)S(1)}, u32[]{:S(2)}, u32[]{:S(2)}) %collective-permute-start.75) | collective-permute-done | bytes 262176 | tf_op jit(solution)/shard_map/cond/branch_1_fun/ppermute | solution.py:619
  189.1 16.8 %collective-permute-done.76 = bf16[2,128,1024]{2,1,0:T(8,128)(2,1)S(1)} collective-permute-done((bf16[2,128,1024]{2,1,0:T(8,128)(2,1)}, bf16[2,128,1024]{2,1,0:T(8,128)(2,1)S(1)}, u32[]{:S(2)}, u32[]{:S(2)}) %collective-permute-start.76) | collective-permute-done | bytes 524320 | tf_op jit(solution)/shard_map/cond/branch_1_fun/ppermute | solution.py:634
  210.1 3.2 collective-permute-done.80
  214.6 4.9 all-to-all-start.5
  220.9 74.0 %conditional.12 = (bf16[2,512,1024]{2,1,0:T(8,128)(2,1)}, bf16[4,1024,1024]{2,1,0:T(8,128)(2,1)}, bf16[4,1024,1024]{2,1,0:T(8,128)(2,1)}) conditional(s32[]{:T(128)} %bitcast.73, () %tuple.104, (bf16[2,128,1024]{1,2,0:T(8,128)(2,1)S(1)}, bf16[4,256,1024]{2,1,0:T(8,128)(2,1)}, bf16[1024,1024]{1,0:T(8,128)(2,1)}, bf16[1024,1024]{1,0:T(8,128)(2,1)}) %tuple.105), branch_computations={%region_9.10_spmd, %region_10.11_spmd} | conditional | flops 26476548 | bytes 83960360 | solution.py:741
  230.7 18.0 %collective-permute-done.17 = bf16[2,128,1024]{2,1,0:T(8,128)(2,1)S(1)} collective-permute-done((bf16[2,128,1024]{2,1,0:T(8,128)(2,1)S(1)}, bf16[2,128,1024]{2,1,0:T(8,128)(2,1)S(1)}, u32[]{:S(2)}, u32[]{:S(2)}) %collective-permute-start.17) | collective-permute-done | bytes 524320 | tf_op jit(solution)/shard_map/cond/branch_1_fun/ppermute | solution.py:600
  248.8 16.4 %collective-permute-done.16 = bf16[2,128,1024]{2,1,0:T(8,128)(2,1)S(1)} collective-permute-done((bf16[2,128,1024]{2,1,0:T(8,128)(2,1)S(1)}, bf16[2,128,1024]{2,1,0:T(8,128)(2,1)S(1)}, u32[]{:S(2)}, u32[]{:S(2)}) %collective-permute-start.16) | collective-permute-done | bytes 524320 | tf_op jit(solution)/shard_map/cond/branch_1_fun/ppermute | solution.py:599
  267.9 6.9 fusion.8
  283.4 10.1 %collective-permute-done.18 = bf16[2,64,1024]{2,1,0:T(8,128)(2,1)S(1)} collective-permute-done((bf16[2,64,1024]{2,1,0:T(8,128)(2,1)S(1)}, bf16[2,64,1024]{2,1,0:T(8,128)(2,1)S(1)}, u32[]{:S(2)}, u32[]{:S(2)}) %collective-permute-start.18) | collective-permute-done | bytes 262176 | tf_op jit(solution)/shard_map/cond/branch_1_fun/ppermute | solution.py:607
  295.0 69.3 %conditional.13 = (bf16[2,512,1024]{2,1,0:T(8,128)(2,1)}, bf16[4,1024,512]{2,1,0:T(8,128)(2,1)}, bf16[4,1024,512]{2,1,0:T(8,128)(2,1)}, bf16[4,512,512]{2,1,0:T(...) conditional(s32[]{:T(128)} %bitcast.73, () %tuple.103, ...), branch_computations={%region_11.12_spmd, %region_12.13_spmd} | conditional | flops 10486763 | bytes 60818920 | solution.py:741
  300.6 15.6 %gate_up.1 = (bf16[4,512,512]{2,1,0:T(8,128)(2,1)}, bf16[4,512,512]{2,1,0:T(8,128)(2,1)}, bf16[4,512,512]{2,1,0:T(8,128)(2,1)S(1)}) custom-call(bf16[2,512,1024]{2,1,0:T(8,128)(2,1)} %get-tuple-element.193.refs_0_, bf16[4,1024,1024]{2,1,0:T(8,128)(2,1)} %get-tuple-element.194.refs_1_.refs_3_, bf16[4,1024,1024]{2,1,0:T(8,128)(2,1)} %get-tuple-element.195.refs_2_.refs_4_, ...), custom_call_target="tpu_custom_call" | custom-call | flops 1000 | bytes 1000 | tf_op jit(solution)/shard_map/cond/branch_1_fun/gate_up/pallas_call | solution.py:57
  318.1 4.3 collective-permute-done.27
  329.8 8.5 %collective-permute-done.32 = bf16[512,512]{1,0:T(8,128)(2,1)S(1)} collective-permute-done((bf16[512,512]{1,0:T(8,128)(2,1)S(1)}, bf16[512,512]{1,0:T(8,128)(2,1)S(1)}, u32[]{:S(2)}, u32[]{:S(2)}) %collective-permute-start.32) | collective-permute-done | bytes 524320 | tf_op jit(solution)/shard_map/cond/branch_1_fun/ppermute | solution.py:590
  340.4 3.7 pad_maximum_fusion.4
  352.6 10.1 %collective-permute-done.28 = bf16[2,64,1024]{2,1,0:T(8,128)(2,1)S(1)} collective-permute-done((bf16[2,64,1024]{2,1,0:T(8,128)(2,1)S(1)}, bf16[2,64,1024]{2,1,0:T(8,128)(2,1)S(1)}, u32[]{:S(2)}, u32[]{:S(2)}) %collective-permute-start.28) | collective-permute-done | bytes 262176 | tf_op jit(solution)/shard_map/cond/branch_1_fun/ppermute | solution.py:607
  364.3 32.1 %feed_back.1 = (bf16[4,2,512,512]{3,2,1,0:T(8,128)(2,1)}, f32[2,128,1024]{2,1,0:T(8,128)S(1)}, bf16[2,128,1024]{2,1,0:T(8,128)(2,1)S(1)}, bf16[2,128,1024]{2,1,0...) custom-call(bf16[2,512,1024]{2,1,0:T(8,128)(2,1)} %get-tuple-element.389.refs_0_, ...), custom_call_target="tpu_custom_call" | custom-call | flops 12884901888 | bytes 37748736 | tf_op jit(solution)/shard_map/feed_back/pallas_call | solution.py:57
  396.3 49.2 %conditional.14 = (bf16[4,1024,512]{2,1,0:T(8,128)(2,1)}, bf16[4,1024,1024]{2,1,0:T(8,128)(2,1)}, f32[2,128,1024]{1,2,0:T(8,128)S(1)}) conditional(s32[]{:T(128)} %bitcast.73, () %tuple.102, (bf16[2,128,1024]{2,1,0:T(8,128)(2,1)S(1)}, bf16[2,64,1024]{2,1,0:T(8,128)(2,1)S(1)}, f32[2,128,1024]{2,1,0:T(8,128)S(1)}, ...), branch_computations={%region_13.14_spmd, %region_14.15_spmd} | conditional | flops 12888571904 | bytes 81264968 | solution.py:741
  402.9 10.8 %collective-permute-done.55.refs_7_ = bf16[2,64,1024]{2,1,0:T(8,128)(2,1)S(1)} collective-permute-done((bf16[2,64,1024]{2,1,0:T(8,128)(2,1)S(1)}, bf16[2,64,1024]{2,1,0:T(8,128)(2,1)S(1)}, u32[]{:S(2)}, u32[]{:S(2)}) %collective-permute-start.55) | collective-permute-done | bytes 262176 | tf_op jit(solution)/shard_map/cond/branch_1_fun/ppermute | solution.py:620
  416.1 9.4 %g_down.1.refs_5_ = bf16[4,1024,512]{2,1,0:T(8,128)(2,1)} custom-call(s32[1]{0:T(128)} %bitcast.36.refs_0_, bf16[512,1024]{1,0:T(8,128)(2,1)S(1)} %get-tuple-element.628.refs_1_, bf16[512,1024]{1,0:T(8,128)(2,1)S(1)} %collective-permute-done.58.refs_2_, bf16[4,1,512,512]{3,2,1,0:T(8,128)(2,1)} %bitcast.39.refs_3_, bf16[4,1,512,512]{3,2,1,0:T(8,128)(2,1)S(1)} %bitcast.130), custom_call_target="tpu_custom_call" | custom-call | flops 4294967296 | bytes 10485760 | tf_op jit(solution)/shard_map/cond/branch_1_fun/g_down/pallas_call | solution.py:466
  425.5 17.6 %g_gate_up.1 = bf16[4,1024,1024]{2,1,0:T(8,128)(2,1)} custom-call(s32[1]{0:T(128)} %bitcast.36.refs_0_, bf16[512,1024]{1,0:T(8,128)(2,1)S(1)} %slice_bitcast_fusion.3.refs_1_, bf16[512,1024]{1,0:T(8,128)(2,1)} %get-tuple-element.207.refs_2_, bf16[4,2,512,512]{3,2,1,0:T(8,128)(2,1)} %get-tuple-element.208.refs_3_, ...), custom_call_target="tpu_custom_call" | custom-call | flops 8589934592 | bytes 18874368 | tf_op jit(solution)/shard_map/cond/branch_1_fun/g_gate_up/pallas_call | solution.py:466
  449.6 44.9 %conditional.15 = (bf16[2,512,1024]{2,1,0:T(8,128)(2,1)}, f32[2,128,1024]{2,1,0:T(8,128)}, bf16[2,128,1024]{2,1,0:T(8,128)(2,1)}, bf16[2,128,1024]{2,1,0:T(8,128...) conditional(s32[]{:T(128)} %bitcast.73, () %tuple.111, (bf16[2,128,1024]{1,2,0:T(8,128)(2,1)}, ...), branch_computations={%region_16.17_spmd, %region_17.18_spmd} | conditional | flops 4295229440 | bytes 25190676 | solution.py:741
  454.3 8.9 %ffn_out.1 = (f32[2,128,1024]{2,1,0:T(8,128)}, bf16[2,128,1024]{2,1,0:T(8,128)(2,1)}, bf16[2,128,1024]{2,1,0:T(8,128)(2,1)}, bf16[2,64,1024]{2,1,0:T(8,128)(2,1)}, bf16[2,64,1024]{2,1,0:T(8,128)(2,1)}) custom-call(bf16[4,512,512]{2,1,0:T(8,128)(2,1)} %get-tuple-element.212.refs_0_, bf16[4,1024,512]{2,1,0:T(8,128)(2,1)} %get-tuple-element.213.refs_1_, ...), custom_call_target="tpu_custom_call" | custom-call | flops 4294967296 | bytes 12582912 | tf_op jit(solution)/shard_map/cond/branch_1_fun/ffn_out/pallas_call | solution.py:57
  466.0 11.1 %collective-permute-done.36 = bf16[2,128,1024]{2,1,0:T(8,128)(2,1)S(1)} collective-permute-done((bf16[2,128,1024]{2,1,0:T(8,128)(2,1)S(1)}, bf16[2,128,1024]{2,1,0:T(8,128)(2,1)S(1)}, u32[]{:S(2)}, u32[]{:S(2)}) %collective-permute-start.36) | collective-permute-done | bytes 524320 | tf_op jit(solution)/shard_map/cond/branch_1_fun/ppermute | solution.py:599
  483.0 10.1 %collective-permute-done.38 = bf16[2,64,1024]{2,1,0:T(8,128)(2,1)S(1)} collective-permute-done((bf16[2,64,1024]{2,1,0:T(8,128)(2,1)S(1)}, bf16[2,64,1024]{2,1,0:T(8,128)(2,1)S(1)}, u32[]{:S(2)}, u32[]{:S(2)}) %collective-permute-start.38) | collective-permute-done | bytes 262176 | tf_op jit(solution)/shard_map/cond/branch_1_fun/ppermute | solution.py:607
  494.6 5.2 dmix.1
  499.8 14.5 %conditional.16 = (bf16[512,128]{1,0:T(8,128)(2,1)S(1)}, bf16[512,128]{1,0:T(8,128)(2,1)}, bf16[512,128]{1,0:T(8,128)(2,1)}, bf16[512,128]{1,0:T(8,128)(2,1)}, b...) conditional(s32[]{:T(128)} %bitcast.73, () %tuple.110, (bf16[512,128]{1,0:T(8,128)(2,1)S(1)}, ...), branch_computations={%region_18.19_spmd, %region_19.20_spmd} | conditional | bytes 3670264 | solution.py:741
  514.3 13.1 %attend_back.1 = (bf16[512,384]{1,0:T(8,128)(2,1)}, bf16[512,384]{1,0:T(8,128)(2,1)}, bf16[512,384]{1,0:T(8,128)(2,1)}, bf16[512,384]{1,0:T(8,128)(2,1)}) custom-call(s32[16]{0:T(128)S(1)} %and_select_fusion.tab_ref.refs_0_, bf16[512,128]{1,0:T(8,128)(2,1)S(1)} %get-tuple-element.410.refs_1_, bf16[512,128]{1,0:T(8,128)(2,1)} %get-tuple-element.411.refs_2_, ...), custom_call_target="tpu_custom_call" | custom-call | flops 5368709120 | bytes 12582912 | tf_op jit(solution)/shard_map/attend_back/pallas_call | solution.py:212
  528.9 57.4 %conditional.17 = (bf16[4,512,384]{2,1,0:T(8,128)(2,1)}, bf16[2,128,1024]{2,1,0:T(8,128)(2,1)}, bf16[4,256,512]{2,1,0:T(8,128)(2,1)}, bf16[1,128,1024]{2,1,0:T(8...) conditional(s32[]{:T(128)} %bitcast.73, () %tuple.109, ...), branch_computations={%region_21.22_spmd, %region_22.23_spmd} | conditional | flops 6291456 | bytes 27263292 | solution.py:741
  528.9 4.3 all-to-all-start.2
  541.0 12.9 %collective-permute-done.60 = bf16[512,384]{1,0:T(8,128)(2,1)S(1)} collective-permute-done((bf16[512,384]{1,0:T(8,128)(2,1)}, bf16[512,384]{1,0:T(8,128)(2,1)S(1)}, u32[]{:S(2)}, u32[]{:S(2)}) %collective-permute-start.60) | collective-permute-done | bytes 393248 | tf_op jit(solution)/shard_map/cond/branch_1_fun/ppermute | solution.py:590
  554.6 16.0 %collective-permute-done.62 = bf16[512,384]{1,0:T(8,128)(2,1)S(1)} collective-permute-done((bf16[512,384]{1,0:T(8,128)(2,1)}, bf16[512,384]{1,0:T(8,128)(2,1)S(1)}, u32[]{:S(2)}, u32[]{:S(2)}) %collective-permute-start.62) | collective-permute-done | bytes 393248 | tf_op jit(solution)/shard_map/cond/branch_1_fun/ppermute | solution.py:590
  572.0 7.8 %collective-permute-done.63 = bf16[2,128,1024]{2,1,0:T(8,128)(2,1)S(1)} collective-permute-done((bf16[2,128,1024]{2,1,0:T(8,128)(2,1)S(1)}, bf16[2,128,1024]{2,1,0:T(8,128)(2,1)S(1)}, u32[]{:S(2)}, u32[]{:S(2)}) %collective-permute-start.63) | collective-permute-done | bytes 524320 | tf_op jit(solution)/shard_map/cond/branch_1_fun/ppermute | solution.py:634
  586.4 7.8 dxn1.1
  594.3 56.6 %conditional.18 = (bf16[4,1024,512]{2,1,0:T(8,128)(2,1)}, bf16[2,512,512]{2,1,0:T(8,128)(2,1)}, bf16[2,512,512]{2,1,0:T(8,128)(2,1)}, f32[2,128,1024]{1,2,0:T(8,128)S(1)}) conditional(s32[]{:T(128)} %bitcast.73, () %tuple.108, (bf16[2,128,1024]{2,1,0:T(8,128)(2,1)S(1)}, bf16[2,64,1024]{2,1,0:T(8,128)(2,1)S(1)}, f32[2,128,1024]{2,1,0:T(8,128)S(1)}, ...), branch_computations={%region_23.24_spmd, %region_24.25_spmd} | conditional | flops 4298899456 | bytes 74973640 | solution.py:741
  599.0 8.2 %collective-permute-done.67 = bf16[2,64,1024]{2,1,0:T(8,128)(2,1)S(1)} collective-permute-done((bf16[2,64,1024]{2,1,0:T(8,128)(2,1)S(1)}, bf16[2,64,1024]{2,1,0:T(8,128)(2,1)S(1)}, u32[]{:S(2)}, u32[]{:S(2)}) %collective-permute-start.67) | collective-permute-done | bytes 262176 | tf_op jit(solution)/shard_map/cond/branch_1_fun/ppermute | solution.py:620
  611.5 9.7 %g_heads.1 = bf16[4,1024,512]{2,1,0:T(8,128)(2,1)} custom-call(bf16[512,1024]{1,0:T(8,128)(2,1)S(1)} %get-tuple-element.646.refs_0_, bf16[512,1024]{1,0:T(8,128)(2,1)S(1)} %collective-permute-done.69.refs_1_, bf16[4,512,384]{2,1,0:T(8,128)(2,1)} %get-tuple-element.243.refs_2_, bf16[4,512,384]{2,1,0:T(8,128)(2,1)} %copy-done.62, ...), custom_call_target="tpu_custom_call" | custom-call | flops 4294967296 | bytes 12582912 | tf_op jit(solution)/shard_map/cond/branch_1_fun/g_heads/pallas_call | solution.py:57
  627.8 13.2 %collective-permute-done.66 = bf16[2,128,1024]{2,1,0:T(8,128)(2,1)S(1)} collective-permute-done((bf16[2,128,1024]{2,1,0:T(8,128)(2,1)S(1)}, bf16[2,128,1024]{2,1,0:T(8,128)(2,1)S(1)}, u32[]{:S(2)}, u32[]{:S(2)}) %collective-permute-start.66) | collective-permute-done | bytes 524320 | tf_op jit(solution)/shard_map/cond/branch_1_fun/ppermute | solution.py:634
  641.6 8.6 %collective-permute-done.73 = bf16[2,512,512]{2,1,0:T(8,128)(2,1)} collective-permute-done((bf16[2,512,512]{2,1,0:T(8,128)(2,1)}, bf16[2,512,512]{2,1,0:T(8,128)(2,1)}, u32[]{:S(2)}, u32[]{:S(2)}) %collective-permute-start.73) | collective-permute-done | bytes 1048608 | tf_op jit(solution)/shard_map/cond/branch_1_fun/ppermute | solution.py:590
  653.8 3.6 all-to-all-start.6
  661.0 3.8 unpack_down.1
  668.4 88.8 %conditional.19 = (bf16[1,128,2048]{2,1,0:T(8,128)(2,1)}, bf16[1,128,2048]{2,1,0:T(8,128)(2,1)S(1)}, bf16[1,128,2048]{2,1,0:T(8,128)(2,1)S(1)}, bf16[1,128,2048]...) conditional(s32[]{:T(128)} %bitcast.73, () %tuple.97, ...), branch_computations={%region_27.28_spmd, %region_28.29_spmd} | conditional | flops 10485778 | bytes 92275768 | solution.py:741
  668.4 5.0 all-to-all-start
  681.2 9.9 %collective-permute-done.52 = bf16[512,512]{1,0:T(8,128)(2,1)} collective-permute-done((bf16[512,512]{1,0:T(8,128)(2,1)}, bf16[512,512]{1,0:T(8,128)(2,1)}, u32[]{:S(2)}, u32[]{:S(2)}) %collective-permute-start.52) | collective-permute-done | bytes 524320 | tf_op jit(solution)/shard_map/cond/branch_1_fun/ppermute | solution.py:590
  712.0 7.9 %collective-permute-done.44 = bf16[64,2048]{1,0:T(8,128)(2,1)} collective-permute-done((bf16[64,2048]{1,0:T(8,128)(2,1)S(1)}, bf16[64,2048]{1,0:T(8,128)(2,1)}, u32[]{:S(2)}, u32[]{:S(2)}) %collective-permute-start.44) | collective-permute-done | bytes 262176 | tf_op jit(solution)/shard_map/cond/branch_1_fun/ppermute | solution.py:590
  731.2 4.5 all-to-all-start.1
  743.8 13.3 %all-to-all-done.1 = bf16[4,256,512]{2,1,0:T(8,128)(2,1)} async-done(((bf16[4,256,512]{2,1,0:T(8,128)(2,1)}), bf16[4,256,512]{2,1,0:T(8,128)(2,1)}, u32[]{:S(2)}, u32[]{:S(2)}) %all-to-all-start.1) | async-done | bytes 1048608 | tf_op jit(solution)/shard_map/cond/branch_1_fun/all_to_all | solution.py:693
  757.2 3.6 unpack_heads.1
  763.1 4.3 place.2
  767.4 4.6 place.3
  (474 shorter events, 254.2 us)
Async XLA Ops:
  13.3 32.0 %all-to-all-start.3 = ((bf16[4,256,512]{2,1,0:T(8,128)(2,1)}), bf16[4,256,512]{2,1,0:T(8,128)(2,1)S(1)}, u32[]{:S(2)}, u32[]{:S(2)}) async-start(bf16[4,256,512]{2,1,0:T(8,128)(2,1)} %pack_heads.1), calls=%async_computation.3 | async-start | bytes 2097152 | tf_op jit(solution)/shard_map/all_to_all | solution.py:693
  47.0 30.4 %collective-permute-start.10 = (bf16[1024,512]{1,0:T(8,128)(2,1)S(1)}, bf16[1024,512]{1,0:T(8,128)(2,1)}, u32[]{:S(2)}, u32[]{:S(2)}) collective-permute-start(bf16[1024,512]{1,0:T(8,128)(2,1)S(1)} %get-tuple-element.173), channel_id=1, source_target_pairs={{0,2},{1,3},{2,0},{3,1},{4,6},{5,7},{6,4},{7,5},{8,10},{9,11},{10,... | collective-permute-start | bytes 3145736 | tf_op jit(solution)/shard_map/cond/branch_1_fun/ppermute | solution.py:590
  48.6 30.5 %collective-permute-start.9 = (bf16[1024,512]{1,0:T(8,128)(2,1)S(1)}, bf16[1024,512]{1,0:T(8,128)(2,1)}, u32[]{:S(2)}, u32[]{:S(2)}) collective-permute-start(bf16[1024,512]{1,0:T(8,128)(2,1)S(1)} %get-tuple-element.173), channel_id=1, source_target_pairs={{0,1},{1,0},{2,3},{3,2},{4,5},{5,4},{6,7},{7,6},{8,9},{9,8},{10,11... | collective-permute-start | bytes 3145736 | tf_op jit(solution)/shard_map/cond/branch_1_fun/ppermute | solution.py:590
  51.1 23.8 %collective-permute-start.6 = (bf16[2,128,1024]{2,1,0:T(8,128)(2,1)}, bf16[2,128,1024]{2,1,0:T(8,128)(2,1)S(1)}, u32[]{:S(2)}, u32[]{:S(2)}) collective-permute-start(bf16[2,128,1024]{2,1,0:T(8,128)(2,1)} %copy.109), channel_id=1, source_target_pairs={{8,0},{24,8},{16,24},{0,16},{9,1},{25,9},{17,25},{1,17},{10,2},{26... | collective-permute-start | bytes 1572872 | tf_op jit(solution)/shard_map/cond/branch_1_fun/ppermute | solution.py:600
  51.1 25.0 %collective-permute-start.5 = (bf16[2,128,1024]{2,1,0:T(8,128)(2,1)}, bf16[2,128,1024]{2,1,0:T(8,128)(2,1)S(1)}, u32[]{:S(2)}, u32[]{:S(2)}) collective-permute-start(bf16[2,128,1024]{2,1,0:T(8,128)(2,1)} %copy.109), channel_id=1, source_target_pairs={{0,8},{8,24},{24,16},{16,0},{1,9},{9,25},{25,17},{17,1},{2,10},{10... | collective-permute-start | bytes 1572872 | tf_op jit(solution)/shard_map/cond/branch_1_fun/ppermute | solution.py:599
  78.5 17.8 %collective-permute-start.12 = (bf16[512,512]{1,0:T(8,128)(2,1)S(1)}, bf16[512,512]{1,0:T(8,128)(2,1)S(1)}, u32[]{:S(2)}, u32[]{:S(2)}) collective-permute-start(bf16[512,512]{1,0:T(8,128)(2,1)S(1)} %fusion.6), channel_id=1, source_target_pairs={{0,1},{1,0},{2,3},{3,2},{4,5},{5,4},{6,7},{7,6},{8,9},{9,8},{10,11... | collective-permute-start | bytes 1572872 | tf_op jit(solution)/shard_map/cond/branch_1_fun/ppermute | solution.py:590
  80.2 16.1 %collective-permute-start.13 = (bf16[512,512]{1,0:T(8,128)(2,1)S(1)}, bf16[512,512]{1,0:T(8,128)(2,1)S(1)}, u32[]{:S(2)}, u32[]{:S(2)}) collective-permute-start(bf16[512,512]{1,0:T(8,128)(2,1)S(1)} %fusion.4), channel_id=1, source_target_pairs={{0,2},{1,3},{2,0},{3,1},{4,6},{5,7},{6,4},{7,5},{8,10},{9,11},{10,... | collective-permute-start | bytes 1572872 | tf_op jit(solution)/shard_map/cond/branch_1_fun/ppermute | solution.py:590
  111.0 56.3 %all-to-all-start.4 = ((bf16[4,256,1024]{2,1,0:T(8,128)(2,1)}), bf16[4,256,1024]{2,1,0:T(8,128)(2,1)}, u32[]{:S(2)}, u32[]{:S(2)}) async-start(bf16[4,256,1024]{2,1,0:T(8,128)(2,1)} %get-tuple-element.380), calls=%async_computation.4 | async-start | bytes 4194304 | tf_op jit(solution)/shard_map/all_to_all | solution.py:693
  125.9 19.3 %collective-permute-start.84 = (bf16[512,384]{1,0:T(8,128)(2,1)S(1)}, bf16[512,384]{1,0:T(8,128)(2,1)S(1)}, u32[]{:S(2)}, u32[]{:S(2)}) collective-permute-start(bf16[512,384]{1,0:T(8,128)(2,1)S(1)} %get-tuple-element.367), channel_id=1, source_target_pairs={{0,2},{1,3},{2,0},{3,1},{4,6},{5,7},{6,4},{7,5},{8,10},{9,11},{10,... | collective-permute-start | bytes 1179656 | tf_op jit(solution)/shard_map/ppermute | solution.py:590
  127.4 17.8 %collective-permute-start.85 = (bf16[512,384]{1,0:T(8,128)(2,1)S(1)}, bf16[512,384]{1,0:T(8,128)(2,1)S(1)}, u32[]{:S(2)}, u32[]{:S(2)}) collective-permute-start(bf16[512,384]{1,0:T(8,128)(2,1)S(1)} %get-tuple-element.368), channel_id=1, source_target_pairs={{0,3},{1,2},{2,1},{3,0},{4,7},{5,6},{6,5},{7,4},{8,11},{9,10},{10,... | collective-permute-start | bytes 1179656 | tf_op jit(solution)/shard_map/ppermute | solution.py:590
  167.4 45.9 %collective-permute-start.80 = (bf16[1024,1024]{1,0:T(8,128)(2,1)}, bf16[1024,1024]{1,0:T(8,128)(2,1)}, u32[]{:S(2)}, u32[]{:S(2)}) collective-permute-start(bf16[1024,1024]{1,0:T(8,128)(2,1)} %bitcast.13), channel_id=1, source_target_pairs={{0,2},{1,3},{2,0},{3,1},{4,6},{5,7},{6,4},{7,5},{8,10},{9,11},{10,... | collective-permute-start | bytes 6291464 | tf_op jit(solution)/shard_map/cond/branch_1_fun/ppermute | solution.py:590
  168.7 45.9 %collective-permute-start.79 = (bf16[1024,1024]{1,0:T(8,128)(2,1)}, bf16[1024,1024]{1,0:T(8,128)(2,1)}, u32[]{:S(2)}, u32[]{:S(2)}) collective-permute-start(bf16[1024,1024]{1,0:T(8,128)(2,1)} %bitcast.13), channel_id=1, source_target_pairs={{0,1},{1,0},{2,3},{3,2},{4,5},{5,4},{6,7},{7,6},{8,9},{9,8},{10,11... | collective-permute-start | bytes 6291464 | tf_op jit(solution)/shard_map/cond/branch_1_fun/ppermute | solution.py:590
  185.0 21.0 %collective-permute-start.76 = (bf16[2,128,1024]{2,1,0:T(8,128)(2,1)}, bf16[2,128,1024]{2,1,0:T(8,128)(2,1)S(1)}, u32[]{:S(2)}, u32[]{:S(2)}) collective-permute-start(bf16[2,128,1024]{2,1,0:T(8,128)(2,1)} %pad_maximum_fusion.2), channel_id=1, source_target_pairs={{0,8},{8,24},{24,16},{16,0},{1,9},{9,25},{25,17},{17,1},{2,10},{10... | collective-permute-start | bytes 1572872 | tf_op jit(solution)/shard_map/cond/branch_1_fun/ppermute | solution.py:634
  185.9 20.1 %collective-permute-start.78 = (bf16[2,128,1024]{2,1,0:T(8,128)(2,1)}, bf16[2,128,1024]{2,1,0:T(8,128)(2,1)}, u32[]{:S(2)}, u32[]{:S(2)}) collective-permute-start(bf16[2,128,1024]{2,1,0:T(8,128)(2,1)} %pad_maximum_fusion.3), channel_id=1, source_target_pairs={{8,0},{24,8},{16,24},{0,16},{9,1},{25,9},{17,25},{1,17},{10,2},{26... | collective-permute-start | bytes 1572872 | tf_op jit(solution)/shard_map/cond/branch_1_fun/ppermute | solution.py:635
  214.6 80.4 %all-to-all-start.5 = ((bf16[4,256,512]{2,1,0:T(8,128)(2,1)}), bf16[4,256,512]{2,1,0:T(8,128)(2,1)}, u32[]{:S(2)}, u32[]{:S(2)}) async-start(bf16[4,256,512]{2,1,0:T(8,128)(2,1)} %tie.3), calls=%async_computation.5 | async-start | bytes 2097152 | tf_op jit(solution)/shard_map/all_to_all | solution.py:693
  219.5 307.9 %reduce-scatter.7.cloned.1.call-start = ((), (), s32[]{:S(2)}) async-start(), calls=%async_computation.9 | async-start | bytes 5242880
  226.3 41.4 %collective-permute-start.21 = (bf16[512,1024]{1,0:T(8,128)(2,1)S(1)}, bf16[512,1024]{1,0:T(8,128)(2,1)S(1)}, u32[]{:S(2)}, u32[]{:S(2)}) collective-permute-start(bf16[512,1024]{1,0:T(8,128)(2,1)S(1)} %slice_add_fusion.7), channel_id=1, source_target_pairs={{0,1},{1,0},{2,3},{3,2},{4,5},{5,4},{6,7},{7,6},{8,9},{9,8},{10,11... | collective-permute-start | bytes 3145736 | tf_op jit(solution)/shard_map/cond/branch_1_fun/ppermute | solution.py:590
  226.9 40.8 %collective-permute-start.22 = (bf16[512,1024]{1,0:T(8,128)(2,1)S(1)}, bf16[512,1024]{1,0:T(8,128)(2,1)S(1)}, u32[]{:S(2)}, u32[]{:S(2)}) collective-permute-start(bf16[512,1024]{1,0:T(8,128)(2,1)S(1)} %slice_add_fusion.6), channel_id=1, source_target_pairs={{0,2},{1,3},{2,0},{3,1},{4,6},{5,7},{6,4},{7,5},{8,10},{9,11},{10,... | collective-permute-start | bytes 3145736 | tf_op jit(solution)/shard_map/cond/branch_1_fun/ppermute | solution.py:590
  227.9 20.9 %collective-permute-start.17 = (bf16[2,128,1024]{2,1,0:T(8,128)(2,1)S(1)}, bf16[2,128,1024]{2,1,0:T(8,128)(2,1)S(1)}, u32[]{:S(2)}, u32[]{:S(2)}) collective-permute-start(bf16[2,128,1024]{2,1,0:T(8,128)(2,1)S(1)} %copy.112), channel_id=1, source_target_pairs={{8,0},{24,8},{16,24},{0,16},{9,1},{25,9},{17,25},{1,17},{10,2},{26... | collective-permute-start | bytes 1572872 | tf_op jit(solution)/shard_map/cond/branch_1_fun/ppermute | solution.py:600
  230.7 34.5 %collective-permute-start.16 = (bf16[2,128,1024]{2,1,0:T(8,128)(2,1)S(1)}, bf16[2,128,1024]{2,1,0:T(8,128)(2,1)S(1)}, u32[]{:S(2)}, u32[]{:S(2)}) collective-permute-start(bf16[2,128,1024]{2,1,0:T(8,128)(2,1)S(1)} %copy.112), channel_id=1, source_target_pairs={{0,8},{8,24},{24,16},{16,0},{1,9},{9,25},{25,17},{17,1},{2,10},{10... | collective-permute-start | bytes 1572872 | tf_op jit(solution)/shard_map/cond/branch_1_fun/ppermute | solution.py:599
  248.7 16.4 %collective-permute-start.24 = (bf16[16,128]{1,0:T(8,128)(2,1)S(1)}, bf16[16,128]{1,0:T(8,128)(2,1)S(1)}, u32[]{:S(2)}, u32[]{:S(2)}) collective-permute-start(bf16[16,128]{1,0:T(8,128)(2,1)S(1)} %slice.370), channel_id=1, source_target_pairs={{0,4},{4,0},{1,5},{5,1},{2,6},{6,2},{3,7},{7,3},{8,12},{12,8},{9,1... | collective-permute-start | bytes 12296 | tf_op jit(solution)/shard_map/cond/branch_1_fun/ppermute | solution.py:593
  274.8 20.1 %collective-permute-start.25 = (bf16[4,1024,1024]{2,1,0:T(8,128)(2,1)}, bf16[4,1024,1024]{2,1,0:T(8,128)(2,1)}, u32[]{:S(2)}, u32[]{:S(2)}) collective-permute-start(bf16[4,1024,1024]{2,1,0:T(8,128)(2,1)} %fusion.8), channel_id=1, source_target_pairs={{0,4},{4,0},{1,5},{5,1},{2,6},{6,2},{3,7},{7,3},{8,12},{12,8},{9,1... | collective-permute-start | bytes 25165832 | tf_op jit(solution)/shard_map/cond/branch_1_fun/ppermute | solution.py:593
  278.7 14.8 %collective-permute-start.18 = (bf16[2,64,1024]{2,1,0:T(8,128)(2,1)S(1)}, bf16[2,64,1024]{2,1,0:T(8,128)(2,1)S(1)}, u32[]{:S(2)}, u32[]{:S(2)}) collective-permute-start(bf16[2,64,1024]{2,1,0:T(8,128)(2,1)S(1)} %slice_add_fusion.9), channel_id=1, source_target_pairs={{0,8},{8,24},{24,16},{16,0},{1,9},{9,25},{25,17},{17,1},{2,10},{10... | collective-permute-start | bytes 786440 | tf_op jit(solution)/shard_map/cond/branch_1_fun/ppermute | solution.py:607
  278.8 15.5 %collective-permute-start.19 = (bf16[2,64,1024]{2,1,0:T(8,128)(2,1)S(1)}, bf16[2,64,1024]{2,1,0:T(8,128)(2,1)S(1)}, u32[]{:S(2)}, u32[]{:S(2)}) collective-permute-start(bf16[2,64,1024]{2,1,0:T(8,128)(2,1)S(1)} %slice_add_fusion.8), channel_id=1, source_target_pairs={{8,0},{24,8},{16,24},{0,16},{9,1},{25,9},{17,25},{1,17},{10,2},{26... | collective-permute-start | bytes 786440 | tf_op jit(solution)/shard_map/cond/branch_1_fun/ppermute | solution.py:608
  295.0 30.0 %collective-permute-start.31 = (bf16[1024,512]{1,0:T(8,128)(2,1)}, bf16[1024,512]{1,0:T(8,128)(2,1)}, u32[]{:S(2)}, u32[]{:S(2)}) collective-permute-start(bf16[1024,512]{1,0:T(8,128)(2,1)} %bitcast.31), channel_id=1, source_target_pairs={{0,2},{1,3},{2,0},{3,1},{4,6},{5,7},{6,4},{7,5},{8,10},{9,11},{10,... | collective-permute-start | bytes 3145736 | tf_op jit(solution)/shard_map/cond/branch_1_fun/ppermute | solution.py:590
  295.5 31.6 %collective-permute-start.30 = (bf16[1024,512]{1,0:T(8,128)(2,1)}, bf16[1024,512]{1,0:T(8,128)(2,1)}, u32[]{:S(2)}, u32[]{:S(2)}) collective-permute-start(bf16[1024,512]{1,0:T(8,128)(2,1)} %bitcast.31), channel_id=1, source_target_pairs={{0,1},{1,0},{2,3},{3,2},{4,5},{5,4},{6,7},{7,6},{8,9},{9,8},{10,11... | collective-permute-start | bytes 3145736 | tf_op jit(solution)/shard_map/cond/branch_1_fun/ppermute | solution.py:590
  298.5 23.9 %collective-permute-start.27 = (bf16[2,128,1024]{2,1,0:T(8,128)(2,1)}, bf16[2,128,1024]{2,1,0:T(8,128)(2,1)S(1)}, u32[]{:S(2)}, u32[]{:S(2)}) collective-permute-start(bf16[2,128,1024]{2,1,0:T(8,128)(2,1)} %copy.113), channel_id=1, source_target_pairs={{8,0},{24,8},{16,24},{0,16},{9,1},{25,9},{17,25},{1,17},{10,2},{26... | collective-permute-start | bytes 1572872 | tf_op jit(solution)/shard_map/cond/branch_1_fun/ppermute | solution.py:600
  298.5 25.1 %collective-permute-start.26 = (bf16[2,128,1024]{2,1,0:T(8,128)(2,1)}, bf16[2,128,1024]{2,1,0:T(8,128)(2,1)S(1)}, u32[]{:S(2)}, u32[]{:S(2)}) collective-permute-start(bf16[2,128,1024]{2,1,0:T(8,128)(2,1)} %copy.113), channel_id=1, source_target_pairs={{0,8},{8,24},{24,16},{16,0},{1,9},{9,25},{25,17},{17,1},{2,10},{10... | collective-permute-start | bytes 1572872 | tf_op jit(solution)/shard_map/cond/branch_1_fun/ppermute | solution.py:599
  344.0 20.1 %collective-permute-start.34 = (bf16[4,1024,512]{2,1,0:T(8,128)(2,1)}, bf16[4,1024,512]{2,1,0:T(8,128)(2,1)}, u32[]{:S(2)}, u32[]{:S(2)}) collective-permute-start(bf16[4,1024,512]{2,1,0:T(8,128)(2,1)} %pad_maximum_fusion.4), channel_id=1, source_target_pairs={{0,4},{4,0},{1,5},{5,1},{2,6},{6,2},{3,7},{7,3},{8,12},{12,8},{9,1... | collective-permute-start | bytes 12582920 | tf_op jit(solution)/shard_map/cond/branch_1_fun/ppermute | solution.py:593
  345.3 18.8 %collective-permute-start.35 = (bf16[512,1024]{1,0:T(8,128)(2,1)S(1)}, bf16[512,1024]{1,0:T(8,128)(2,1)}, u32[]{:S(2)}, u32[]{:S(2)}) collective-permute-start(bf16[512,1024]{1,0:T(8,128)(2,1)S(1)} %slice_bitcast_fusion), channel_id=1, source_target_pairs={{0,4},{4,0},{1,5},{5,1},{2,6},{6,2},{3,7},{7,3},{8,12},{12,8},{9,1... | collective-permute-start | bytes 3145736 | tf_op jit(solution)/shard_map/cond/branch_1_fun/ppermute | solution.py:593
  347.8 14.8 %collective-permute-start.28 = (bf16[2,64,1024]{2,1,0:T(8,128)(2,1)S(1)}, bf16[2,64,1024]{2,1,0:T(8,128)(2,1)S(1)}, u32[]{:S(2)}, u32[]{:S(2)}) collective-permute-start(bf16[2,64,1024]{2,1,0:T(8,128)(2,1)S(1)} %fusion.14), channel_id=1, source_target_pairs={{0,8},{8,24},{24,16},{16,0},{1,9},{9,25},{25,17},{17,1},{2,10},{10... | collective-permute-start | bytes 786440 | tf_op jit(solution)/shard_map/cond/branch_1_fun/ppermute | solution.py:607
  347.9 15.5 %collective-permute-start.29 = (bf16[2,64,1024]{2,1,0:T(8,128)(2,1)S(1)}, bf16[2,64,1024]{2,1,0:T(8,128)(2,1)S(1)}, u32[]{:S(2)}, u32[]{:S(2)}) collective-permute-start(bf16[2,64,1024]{2,1,0:T(8,128)(2,1)S(1)} %fusion.13), channel_id=1, source_target_pairs={{8,0},{24,8},{16,24},{0,16},{9,1},{25,9},{17,25},{1,17},{10,2},{26... | collective-permute-start | bytes 786440 | tf_op jit(solution)/shard_map/cond/branch_1_fun/ppermute | solution.py:608
  396.3 29.2 %collective-permute-start.57 = (bf16[4,2,512,512]{3,2,1,0:T(8,128)(2,1)}, bf16[4,2,512,512]{3,2,1,0:T(8,128)(2,1)S(1)}, u32[]{:S(2)}, u32[]{:S(2)}) collective-permute-start(bf16[4,2,512,512]{3,2,1,0:T(8,128)(2,1)} %get-tuple-element.208.refs_3_), channel_id=1, source_target_pairs={{0,4},{4,0},{1,5},{5,1},{2,6},{6,2},{3,7},{7,3},{8,12},{12,8},{9,1... | collective-permute-start | bytes 12582920 | tf_op jit(solution)/shard_map/cond/branch_1_fun/ppermute | solution.py:593
  396.4 19.7 %collective-permute-start.59 = (bf16[4,512,512]{2,1,0:T(8,128)(2,1)}, bf16[4,512,512]{2,1,0:T(8,128)(2,1)S(1)}, u32[]{:S(2)}, u32[]{:S(2)}) collective-permute-start(bf16[4,512,512]{2,1,0:T(8,128)(2,1)} %get-tuple-element.210), channel_id=1, source_target_pairs={{0,4},{4,0},{1,5},{5,1},{2,6},{6,2},{3,7},{7,3},{8,12},{12,8},{9,1... | collective-permute-start | bytes 6291464 | tf_op jit(solution)/shard_map/cond/branch_1_fun/ppermute | solution.py:593
  398.6 17.5 %collective-permute-start.58 = (bf16[512,1024]{1,0:T(8,128)(2,1)S(1)}, bf16[512,1024]{1,0:T(8,128)(2,1)S(1)}, u32[]{:S(2)}, u32[]{:S(2)}) collective-permute-start(bf16[512,1024]{1,0:T(8,128)(2,1)S(1)} %get-tuple-element.627), channel_id=1, source_target_pairs={{0,4},{4,0},{1,5},{5,1},{2,6},{6,2},{3,7},{7,3},{8,12},{12,8},{9,1... | collective-permute-start | bytes 3145736 | tf_op jit(solution)/shard_map/cond/branch_1_fun/ppermute | solution.py:593
  398.7 15.7 %collective-permute-start.53 = (bf16[2,64,1024]{2,1,0:T(8,128)(2,1)S(1)}, bf16[2,64,1024]{2,1,0:T(8,128)(2,1)S(1)}, u32[]{:S(2)}, u32[]{:S(2)}) collective-permute-start(bf16[2,64,1024]{2,1,0:T(8,128)(2,1)S(1)} %get-tuple-element.202), channel_id=1, source_target_pairs={{0,8},{8,24},{24,16},{16,0},{1,9},{9,25},{25,17},{17,1},{2,10},{10... | collective-permute-start | bytes 786440 | tf_op jit(solution)/shard_map/cond/branch_1_fun/ppermute | solution.py:619
  398.7 15.0 %collective-permute-start.55 = (bf16[2,64,1024]{2,1,0:T(8,128)(2,1)S(1)}, bf16[2,64,1024]{2,1,0:T(8,128)(2,1)S(1)}, u32[]{:S(2)}, u32[]{:S(2)}) collective-permute-start(bf16[2,64,1024]{2,1,0:T(8,128)(2,1)S(1)} %get-tuple-element.204), channel_id=1, source_target_pairs={{8,0},{24,8},{16,24},{0,16},{9,1},{25,9},{17,25},{1,17},{10,2},{26... | collective-permute-start | bytes 786440 | tf_op jit(solution)/shard_map/cond/branch_1_fun/ppermute | solution.py:620
  413.8 31.2 %collective-permute-start.56 = (bf16[2,128,1024]{2,1,0:T(8,128)(2,1)S(1)}, bf16[2,128,1024]{2,1,0:T(8,128)(2,1)S(1)}, u32[]{:S(2)}, u32[]{:S(2)}) collective-permute-start(bf16[2,128,1024]{2,1,0:T(8,128)(2,1)S(1)} %pad_maximum_fusion.6), channel_id=1, source_target_pairs={{8,0},{24,8},{16,24},{0,16},{9,1},{25,9},{17,25},{1,17},{10,2},{26... | collective-permute-start | bytes 1572872 | tf_op jit(solution)/shard_map/cond/branch_1_fun/ppermute | solution.py:635
  414.5 30.5 %collective-permute-start.54 = (bf16[2,128,1024]{2,1,0:T(8,128)(2,1)S(1)}, bf16[2,128,1024]{2,1,0:T(8,128)(2,1)S(1)}, u32[]{:S(2)}, u32[]{:S(2)}) collective-permute-start(bf16[2,128,1024]{2,1,0:T(8,128)(2,1)S(1)} %pad_maximum_fusion.5), channel_id=1, source_target_pairs={{0,8},{8,24},{24,16},{16,0},{1,9},{9,25},{25,17},{17,1},{2,10},{10... | collective-permute-start | bytes 1572872 | tf_op jit(solution)/shard_map/cond/branch_1_fun/ppermute | solution.py:634
  445.6 222.7 %reduce-scatter.9.cloned.1.call-start = ((), (), s32[]{:S(2)}) async-start(), calls=%async_computation.10 | async-start | bytes 10485760
  452.4 24.7 %collective-permute-start.36 = (bf16[2,128,1024]{2,1,0:T(8,128)(2,1)S(1)}, bf16[2,128,1024]{2,1,0:T(8,128)(2,1)S(1)}, u32[]{:S(2)}, u32[]{:S(2)}) collective-permute-start(bf16[2,128,1024]{2,1,0:T(8,128)(2,1)S(1)} %copy.117), channel_id=1, source_target_pairs={{0,8},{8,24},{24,16},{16,0},{1,9},{9,25},{25,17},{17,1},{2,10},{10... | collective-permute-start | bytes 1572872 | tf_op jit(solution)/shard_map/cond/branch_1_fun/ppermute | solution.py:599
  478.3 14.8 %collective-permute-start.38 = (bf16[2,64,1024]{2,1,0:T(8,128)(2,1)S(1)}, bf16[2,64,1024]{2,1,0:T(8,128)(2,1)S(1)}, u32[]{:S(2)}, u32[]{:S(2)}) collective-permute-start(bf16[2,64,1024]{2,1,0:T(8,128)(2,1)S(1)} %slice_add_fusion.17), channel_id=1, source_target_pairs={{0,8},{8,24},{24,16},{16,0},{1,9},{9,25},{25,17},{17,1},{2,10},{10... | collective-permute-start | bytes 786440 | tf_op jit(solution)/shard_map/cond/branch_1_fun/ppermute | solution.py:607
  478.4 15.5 %collective-permute-start.39 = (bf16[2,64,1024]{2,1,0:T(8,128)(2,1)S(1)}, bf16[2,64,1024]{2,1,0:T(8,128)(2,1)S(1)}, u32[]{:S(2)}, u32[]{:S(2)}) collective-permute-start(bf16[2,64,1024]{2,1,0:T(8,128)(2,1)S(1)} %slice_add_fusion.16), channel_id=1, source_target_pairs={{8,0},{24,8},{16,24},{0,16},{9,1},{25,9},{17,25},{1,17},{10,2},{26... | collective-permute-start | bytes 786440 | tf_op jit(solution)/shard_map/cond/branch_1_fun/ppermute | solution.py:608
  528.9 57.4 %all-to-all-start.2 = ((bf16[4,256,512]{2,1,0:T(8,128)(2,1)}), bf16[4,256,512]{2,1,0:T(8,128)(2,1)}, u32[]{:S(2)}, u32[]{:S(2)}) async-start(bf16[4,256,512]{2,1,0:T(8,128)(2,1)} %bitcast.153), calls=%async_computation.2 | async-start | bytes 2097152 | tf_op jit(solution)/shard_map/cond/branch_1_fun/all_to_all | solution.py:693
  533.2 20.6 %collective-permute-start.60 = (bf16[512,384]{1,0:T(8,128)(2,1)}, bf16[512,384]{1,0:T(8,128)(2,1)S(1)}, u32[]{:S(2)}, u32[]{:S(2)}) collective-permute-start(bf16[512,384]{1,0:T(8,128)(2,1)} %get-tuple-element.227), channel_id=1, source_target_pairs={{0,1},{1,0},{2,3},{3,2},{4,5},{5,4},{6,7},{7,6},{8,9},{9,8},{10,11... | collective-permute-start | bytes 1179656 | tf_op jit(solution)/shard_map/cond/branch_1_fun/ppermute | solution.py:590
  534.2 20.4 %collective-permute-start.61 = (bf16[512,384]{1,0:T(8,128)(2,1)}, bf16[512,384]{1,0:T(8,128)(2,1)S(1)}, u32[]{:S(2)}, u32[]{:S(2)}) collective-permute-start(bf16[512,384]{1,0:T(8,128)(2,1)} %get-tuple-element.228), channel_id=1, source_target_pairs={{0,2},{1,3},{2,0},{3,1},{4,6},{5,7},{6,4},{7,5},{8,10},{9,11},{10,... | collective-permute-start | bytes 1179656 | tf_op jit(solution)/shard_map/cond/branch_1_fun/ppermute | solution.py:590
  535.7 34.9 %collective-permute-start.62 = (bf16[512,384]{1,0:T(8,128)(2,1)}, bf16[512,384]{1,0:T(8,128)(2,1)S(1)}, u32[]{:S(2)}, u32[]{:S(2)}) collective-permute-start(bf16[512,384]{1,0:T(8,128)(2,1)} %get-tuple-element.229), channel_id=1, source_target_pairs={{0,3},{1,2},{2,1},{3,0},{4,7},{5,6},{6,5},{7,4},{8,11},{9,10},{10,... | collective-permute-start | bytes 1179656 | tf_op jit(solution)/shard_map/cond/branch_1_fun/ppermute | solution.py:590
  538.0 34.0 %collective-permute-start.64 = (bf16[2,128,1024]{2,1,0:T(8,128)(2,1)S(1)}, bf16[2,128,1024]{2,1,0:T(8,128)(2,1)S(1)}, u32[]{:S(2)}, u32[]{:S(2)}) collective-permute-start(bf16[2,128,1024]{2,1,0:T(8,128)(2,1)S(1)} %pad_maximum_fusion.9), channel_id=1, source_target_pairs={{8,0},{24,8},{16,24},{0,16},{9,1},{25,9},{17,25},{1,17},{10,2},{26... | collective-permute-start | bytes 1572872 | tf_op jit(solution)/shard_map/cond/branch_1_fun/ppermute | solution.py:635
  540.9 38.9 %collective-permute-start.63 = (bf16[2,128,1024]{2,1,0:T(8,128)(2,1)S(1)}, bf16[2,128,1024]{2,1,0:T(8,128)(2,1)S(1)}, u32[]{:S(2)}, u32[]{:S(2)}) collective-permute-start(bf16[2,128,1024]{2,1,0:T(8,128)(2,1)S(1)} %pad_maximum_fusion.8), channel_id=1, source_target_pairs={{0,8},{8,24},{24,16},{16,0},{1,9},{9,25},{25,17},{17,1},{2,10},{10... | collective-permute-start | bytes 1572872 | tf_op jit(solution)/shard_map/cond/branch_1_fun/ppermute | solution.py:634
  594.3 16.0 %collective-permute-start.70 = (bf16[4,512,384]{2,1,0:T(8,128)(2,1)}, bf16[4,512,384]{2,1,0:T(8,128)(2,1)S(1)}, u32[]{:S(2)}, u32[]{:S(2)}) collective-permute-start(bf16[4,512,384]{2,1,0:T(8,128)(2,1)} %get-tuple-element.243.refs_2_), channel_id=1, source_target_pairs={{0,4},{4,0},{1,5},{5,1},{2,6},{6,2},{3,7},{7,3},{8,12},{12,8},{9,1... | collective-permute-start | bytes 4718600 | tf_op jit(solution)/shard_map/cond/branch_1_fun/ppermute | solution.py:593
  607.2 20.4 %collective-permute-start.65 = (bf16[2,64,1024]{2,1,0:T(8,128)(2,1)S(1)}, bf16[2,64,1024]{2,1,0:T(8,128)(2,1)S(1)}, u32[]{:S(2)}, u32[]{:S(2)}) collective-permute-start(bf16[2,64,1024]{2,1,0:T(8,128)(2,1)S(1)} %get-tuple-element.239), channel_id=1, source_target_pairs={{0,8},{8,24},{24,16},{16,0},{1,9},{9,25},{25,17},{17,1},{2,10},{10... | collective-permute-start | bytes 786440 | tf_op jit(solution)/shard_map/cond/branch_1_fun/ppermute | solution.py:619
  607.8 20.0 %collective-permute-start.68 = (bf16[2,128,1024]{2,1,0:T(8,128)(2,1)S(1)}, bf16[2,128,1024]{2,1,0:T(8,128)(2,1)S(1)}, u32[]{:S(2)}, u32[]{:S(2)}) collective-permute-start(bf16[2,128,1024]{2,1,0:T(8,128)(2,1)S(1)} %pad_maximum_fusion.12), channel_id=1, source_target_pairs={{8,0},{24,8},{16,24},{0,16},{9,1},{25,9},{17,25},{1,17},{10,2},{26... | collective-permute-start | bytes 1572872 | tf_op jit(solution)/shard_map/cond/branch_1_fun/ppermute | solution.py:635
  625.8 24.5 %collective-permute-start.73 = (bf16[2,512,512]{2,1,0:T(8,128)(2,1)}, bf16[2,512,512]{2,1,0:T(8,128)(2,1)}, u32[]{:S(2)}, u32[]{:S(2)}) collective-permute-start(bf16[2,512,512]{2,1,0:T(8,128)(2,1)} %pad_maximum_fusion.10), channel_id=1, source_target_pairs={{0,1},{1,0},{2,3},{3,2},{4,5},{5,4},{6,7},{7,6},{8,9},{9,8},{10,11... | collective-permute-start | bytes 3145736 | tf_op jit(solution)/shard_map/cond/branch_1_fun/ppermute | solution.py:590
  626.7 24.2 %collective-permute-start.74 = (bf16[2,512,512]{2,1,0:T(8,128)(2,1)}, bf16[2,512,512]{2,1,0:T(8,128)(2,1)}, u32[]{:S(2)}, u32[]{:S(2)}) collective-permute-start(bf16[2,512,512]{2,1,0:T(8,128)(2,1)} %stack.133), channel_id=1, source_target_pairs={{0,2},{1,3},{2,0},{3,1},{4,6},{5,7},{6,4},{7,5},{8,10},{9,11},{10,... | collective-permute-start | bytes 3145736 | tf_op jit(solution)/shard_map/cond/branch_1_fun/ppermute | solution.py:590
  668.4 59.1 %all-to-all-start = ((bf16[4,256,1024]{2,1,0:T(8,128)(2,1)}), bf16[4,256,1024]{2,1,0:T(8,128)(2,1)S(1)}, u32[]{:S(2)}, u32[]{:S(2)}) async-start(bf16[4,256,1024]{2,1,0:T(8,128)(2,1)} %bitcast.142), calls=%async_computation | async-start | bytes 4194304 | tf_op jit(solution)/shard_map/cond/branch_1_fun/all_to_all | solution.py:693
  676.0 15.1 %collective-permute-start.52 = (bf16[512,512]{1,0:T(8,128)(2,1)}, bf16[512,512]{1,0:T(8,128)(2,1)}, u32[]{:S(2)}, u32[]{:S(2)}) collective-permute-start(bf16[512,512]{1,0:T(8,128)(2,1)} %get-tuple-element.653), channel_id=1, source_target_pairs={{0,2},{1,3},{2,0},{3,1},{4,6},{5,7},{6,4},{7,5},{8,10},{9,11},{10,... | collective-permute-start | bytes 1572872 | tf_op jit(solution)/shard_map/cond/branch_1_fun/ppermute | solution.py:590
  677.5 15.2 %collective-permute-start.43 = (bf16[512,512]{1,0:T(8,128)(2,1)}, bf16[512,512]{1,0:T(8,128)(2,1)}, u32[]{:S(2)}, u32[]{:S(2)}) collective-permute-start(bf16[512,512]{1,0:T(8,128)(2,1)} %get-tuple-element.654), channel_id=1, source_target_pairs={{0,1},{1,0},{2,3},{3,2},{4,5},{5,4},{6,7},{7,6},{8,9},{9,8},{10,11... | collective-permute-start | bytes 1572872 | tf_op jit(solution)/shard_map/cond/branch_1_fun/ppermute | solution.py:590
  680.2 24.4 %collective-permute-start.42 = (bf16[128,2048]{1,0:T(8,128)(2,1)}, bf16[128,2048]{1,0:T(8,128)(2,1)S(1)}, u32[]{:S(2)}, u32[]{:S(2)}) collective-permute-start(bf16[128,2048]{1,0:T(8,128)(2,1)} %convert_element_type.282), channel_id=1, source_target_pairs={{0,2},{1,3},{2,0},{3,1},{4,6},{5,7},{6,4},{7,5},{8,10},{9,11},{10,... | collective-permute-start | bytes 1572872 | tf_op jit(solution)/shard_map/cond/branch_1_fun/ppermute | solution.py:590
  680.7 24.5 %collective-permute-start.41 = (bf16[128,2048]{1,0:T(8,128)(2,1)}, bf16[128,2048]{1,0:T(8,128)(2,1)S(1)}, u32[]{:S(2)}, u32[]{:S(2)}) collective-permute-start(bf16[128,2048]{1,0:T(8,128)(2,1)} %convert_element_type.282), channel_id=1, source_target_pairs={{0,1},{1,0},{2,3},{3,2},{4,5},{5,4},{6,7},{7,6},{8,9},{9,8},{10,11... | collective-permute-start | bytes 1572872 | tf_op jit(solution)/shard_map/cond/branch_1_fun/ppermute | solution.py:590
  702.6 19.2 %collective-permute-start.48 = (bf16[128,2048]{1,0:T(8,128)(2,1)}, bf16[128,2048]{1,0:T(8,128)(2,1)}, u32[]{:S(2)}, u32[]{:S(2)}) collective-permute-start(bf16[128,2048]{1,0:T(8,128)(2,1)} %add.413), channel_id=1, source_target_pairs={{0,2},{1,3},{2,0},{3,1},{4,6},{5,7},{6,4},{7,5},{8,10},{9,11},{10,... | collective-permute-start | bytes 1572872 | tf_op jit(solution)/shard_map/cond/branch_1_fun/ppermute | solution.py:590
  703.1 21.2 %collective-permute-start.47 = (bf16[128,2048]{1,0:T(8,128)(2,1)}, bf16[128,2048]{1,0:T(8,128)(2,1)}, u32[]{:S(2)}, u32[]{:S(2)}) collective-permute-start(bf16[128,2048]{1,0:T(8,128)(2,1)} %add.413), channel_id=1, source_target_pairs={{0,1},{1,0},{2,3},{3,2},{4,5},{5,4},{6,7},{7,6},{8,9},{9,8},{10,11... | collective-permute-start | bytes 1572872 | tf_op jit(solution)/shard_map/cond/branch_1_fun/ppermute | solution.py:590
  704.6 15.3 %collective-permute-start.44 = (bf16[64,2048]{1,0:T(8,128)(2,1)S(1)}, bf16[64,2048]{1,0:T(8,128)(2,1)}, u32[]{:S(2)}, u32[]{:S(2)}) collective-permute-start(bf16[64,2048]{1,0:T(8,128)(2,1)S(1)} %slice_add_fusion.23), channel_id=1, source_target_pairs={{0,1},{1,0},{2,3},{3,2},{4,5},{5,4},{6,7},{7,6},{8,9},{9,8},{10,11... | collective-permute-start | bytes 786440 | tf_op jit(solution)/shard_map/cond/branch_1_fun/ppermute | solution.py:590
  722.8 14.4 %collective-permute-start.49 = (bf16[64,2048]{1,0:T(8,128)(2,1)S(1)}, bf16[64,2048]{1,0:T(8,128)(2,1)}, u32[]{:S(2)}, u32[]{:S(2)}) collective-permute-start(bf16[64,2048]{1,0:T(8,128)(2,1)S(1)} %slice.391), channel_id=1, source_target_pairs={{0,1},{1,0},{2,3},{3,2},{4,5},{5,4},{6,7},{7,6},{8,9},{9,8},{10,11... | collective-permute-start | bytes 786440 | tf_op jit(solution)/shard_map/cond/branch_1_fun/ppermute | solution.py:590
  731.2 26.0 %all-to-all-start.1 = ((bf16[4,256,512]{2,1,0:T(8,128)(2,1)}), bf16[4,256,512]{2,1,0:T(8,128)(2,1)}, u32[]{:S(2)}, u32[]{:S(2)}) async-start(bf16[4,256,512]{2,1,0:T(8,128)(2,1)} %bitcast.150), calls=%async_computation.1 | async-start | bytes 2097152 | tf_op jit(solution)/shard_map/cond/branch_1_fun/all_to_all | solution.py:693
  (97 other events, 2125.0 us)
Sparse Core Ops, SparseCore 0:
  445.7 50.8 reduce-scatter.6
  500.0 103.8 reduce-scatter.8

commit v3 on v2

--- a/solution.py
+++ b/solution.py
@@ -611,8 +611,8 @@
     def gather_ring(x, *deps):
         return ring_last(ring_first(x), *deps)
 
-    def join_rows(chunks):
-        return jnp.concatenate(chunks, axis=1)
+    def join_rows(chunks, *deps):
+        return after(jnp.concatenate(chunks, axis=1), *deps)
 
     def scatter_first(parts):
         return (
@@ -675,14 +675,19 @@
             return hop(jnp.stack([top[1], top[3]]), 1), hop(jnp.stack([low[2], low[3]]), 2)
         return ()
 
-    def scatter_tp_last(part, came):
+    def scatter_tp_sums(part, came):
+        if tp_size != 4:
+            return (part,)
+        over_x, over_y = came
+        mid = part.shape[1] // 2
+        top, low = part[:, :mid], part[:, mid:]
+        return top[0] + over_x[0], low[0] + over_y[0], top[2] + over_x[1], low[1] + over_y[1]
+
+    def scatter_tp_last(sums):
         if tp_size == 4:
-            over_x, over_y = came
-            mid = part.shape[1] // 2
-            top, low = part[:, :mid], part[:, mid:]
-            top2 = hop(top[2] + over_x[1], 2)
-            low1 = hop(low[1] + over_y[1], 1)
-            return jnp.concatenate([top[0] + over_x[0] + top2, low[0] + over_y[0] + low1], axis=0)
+            top, low, top_on, low_on = sums
+            return jnp.concatenate([top + hop(top_on, 2), low + hop(low_on, 1)], axis=0)
+        (part,) = sums
         bit = tp_size // 2
         while bit:
             part = part[:bit] + hop(part[bit:], bit)
@@ -876,10 +881,9 @@
             came = scatter_first(dx)
             gy_peer, hid_peer, dgu_peer = swap(gy[1]), swap(hid), swap(dgu)
             g_down = weight_grad(here, gy[0], gy_peer, hid[:, None], hid_peer[:, None], "g_down")
-            g_gu = weight_grad(here, xn2[0], xn2_peer, dgu, dgu_peer, "g_gate_up", (g_down, *came))
-            return scatter_last(dx, came, g_gu), g_down, g_gu
-
-        dxn2, g_down, g_gu = stage(fourth)
+            return scatter_last(dx, came, g_down), g_down, dgu_peer
+
+        dxn2, g_down, dgu_peer = stage(fourth)
 
         def sum_tp(part):
             return lax.psum_scatter(part, "tp", scatter_dimension=0, tiled=False)
@@ -897,14 +901,17 @@
             * jnp.mean(e2 * hres, axis=(0, 2), keepdims=True)
         )
         dres_low = dres.astype(BF)
-        g_down, g_gu = tie(sum_tp(g_down)), tie(sum_tp(g_gu))
+        g_down = tie(sum_tp(g_down))
 
         def fifth():
             chunks = ring_first(dres_low)
-            ffn = mm_back(hid, *down_w, 0, own, "ffn_out", (tick(dres_low),))
-            return join_rows(ring_last(chunks)), ffn
-
-        dres_all, ffn = stage(fifth)
+            started = (tick(dres_low),)
+            ffn = mm_back(hid, *down_w, 0, own, "ffn_out", started)
+            g_gu = weight_grad(here, xn2[0], xn2_peer, dgu, dgu_peer, "g_gate_up", started)
+            return join_rows(ring_last(chunks), g_gu), ffn, g_gu
+
+        dres_all, ffn, g_gu = stage(fifth)
+        g_gu = tie(sum_tp(g_gu))
         dmix = project(dres_all, *head_w, 3 * HD, HD, "dmix")
         dmix, came = stage(lambda: (to_heads(dmix), scatter_first(ffn)))
         dheads = attend_back(table, dmix, saved, cos, sin, own, length, ())
@@ -921,10 +928,11 @@
             g_heads = weight_grad_heads(
                 xn1[0], peers[0], dqkv, peers[1], dres_all[0], peers[2], mixed, peers[3]
             )
-            heads_came = scatter_tp_first(g_heads) if plain else ()
-            return scatter_last(dx, came), g_heads, heads_came
-
-        dxn1, g_heads, heads_came = stage(seventh)
+            if plain:
+                g_heads = scatter_tp_sums(g_heads, scatter_tp_first(g_heads))
+            return scatter_last(dx, came), g_heads
+
+        dxn1, g_heads = stage(seventh)
         gain1_part = jnp.sum(dxn1 * x_own * scale1, axis=1)
         e1 = dxn1 * gain1
         in_own = (
@@ -942,48 +950,6 @@
         gains = jnp.broadcast_to(gains, (2, shards, tp_size, k_rows))
         gains = jnp.swapaxes(gains.reshape(2, shards * tp_size, k_rows), 0, 1)
 
-        def eighth():
-            near = near_tp(in_own)
-            heads = scatter_tp_last(g_heads, heads_came) if plain else g_heads
-            in_all = spread_over(in_own, near, heads)
-            layer_low = after(layer_own, heads)
-            layer_all = spread_over(layer_low, near_tp(layer_low))
-            placed = place_columns(g_gu)
-            if plain:
-                heads = place_columns(heads, placed)
-            return in_all, layer_all, placed, heads
-
-        def spread_over(x, near, *deps):
-            far = far_tp(x, near, *deps)
-            if not (tp_size == 4 and own == block):
-                return stack_tp(x, near, far)
-            far = jnp.concatenate(far, axis=0)
-            matched = core == tp // 2
-            sent = jnp.where(matched, jnp.stack([near[1], far]), jnp.stack([x, near[0]]))
-            return x[None], near[0][None], near[1][None], far[None], swap(sent)
-
-        in_all, layer_all, g_gu, g_heads = stage(eighth)
-        gains = lax.all_to_all(
-            gains, ("z", "core", "tp"), split_axis=0, concat_axis=0, tiled=True
-        )
-        gains = jnp.sum(gains, axis=0)
-        g_gate, g_up = unpack_columns(g_gu, 2, False, "unpack_gate_up")
-        (g_down,) = unpack_columns(g_down, 1, True, "unpack_down")
-        if plain:
-            g_query, g_key, g_value, g_out = unpack_columns(g_heads, 4, True, "unpack_heads")
-        else:
-
-            def back_columns(i):
-                part = jnp.swapaxes(g_heads[:, :, i * HD : (i + 1) * HD], 1, 2)
-                part = join(jnp.stack([part, swap(part)])).reshape(heads_here * HD, width).T
-                out = jnp.zeros((width, heads * HD), BF)
-                out = lax.dynamic_update_slice(out, part, (0, at_head))
-                out = jnp.where(flipped, jnp.zeros_like(out), out)
-                out = lax.psum_scatter(out, ("z", "core"), scatter_dimension=0, tiled=True)
-                return lax.psum_scatter(out, "tp", scatter_dimension=1, tiled=True).astype(F32)
-
-            g_query, g_key, g_value, g_out = (back_columns(i) for i in range(4))
-            g_out = g_out.T
         def spread_rows(every, dtype):
             if tp_size == 4 and own == block:
                 slot = jnp.bitwise_xor(rank % 2, tp % 2)
@@ -998,8 +964,48 @@
             index = jnp.where(flipped, jnp.bitwise_xor(rank, 2), rank)
             return jnp.take(blocks, index, axis=0, mode="clip").reshape(rows, width).astype(dtype)
 
-        in_grad = spread_rows(in_all, F32)
-        layer_out = spread_rows(layer_all, BF)
+        def eighth():
+            near = near_tp(in_own)
+            heads = scatter_tp_last(g_heads) if plain else g_heads
+            in_all = spread_over(in_own, near)
+            layer_all = spread_over(layer_own, near_tp(layer_own))
+            placed = place_columns(g_gu)
+            if plain:
+                heads = place_columns(heads)
+            in_grad, layer_out = spread_rows(in_all, F32), spread_rows(layer_all, BF)
+            gate_up = unpack_columns(placed, 2, False, "unpack_gate_up")
+            down = unpack_columns(g_down, 1, True, "unpack_down")
+            return in_grad, layer_out, (*gate_up, *down), heads
+
+        def spread_over(x, near, *deps):
+            far = far_tp(x, near, *deps)
+            if not (tp_size == 4 and own == block):
+                return stack_tp(x, near, far)
+            far = jnp.concatenate(far, axis=0)
+            matched = core == tp // 2
+            sent = jnp.where(matched, jnp.stack([near[1], far]), jnp.stack([x, near[0]]))
+            return x[None], near[0][None], near[1][None], far[None], swap(sent)
+
+        in_grad, layer_out, (g_gate, g_up, g_down), g_heads = stage(eighth)
+        gains = lax.all_to_all(
+            gains, ("z", "core", "tp"), split_axis=0, concat_axis=0, tiled=True
+        )
+        gains = jnp.sum(gains, axis=0)
+        if plain:
+            g_query, g_key, g_value, g_out = unpack_columns(g_heads, 4, True, "unpack_heads")
+        else:
+
+            def back_columns(i):
+                part = jnp.swapaxes(g_heads[:, :, i * HD : (i + 1) * HD], 1, 2)
+                part = join(jnp.stack([part, swap(part)])).reshape(heads_here * HD, width).T
+                out = jnp.zeros((width, heads * HD), BF)
+                out = lax.dynamic_update_slice(out, part, (0, at_head))
+                out = jnp.where(flipped, jnp.zeros_like(out), out)
+                out = lax.psum_scatter(out, ("z", "core"), scatter_dimension=0, tiled=True)
+                return lax.psum_scatter(out, "tp", scatter_dimension=1, tiled=True).astype(F32)
+
+            g_query, g_key, g_value, g_out = (back_columns(i) for i in range(4))
+            g_out = g_out.T
         return (
             layer_out,
             in_grad,

time: 791 us -> 780 us (0.986)
  waiting for transfers between devices: 310 us -> 290 us
    all_to_all x6, waiting for transfers between devices: 27.1 us -> 16.8 us  [to_z(): return lax.all_to_all(x, 'z', split_axis=0, concat_axis=0, tiled=True)]
    ppermute x4, waiting for transfers between devices: 37.9 us -> 46.9 us  [scatter_last(): one = lax.ppermute(fwd, 'z', forward)]
    ppermute x4, waiting for transfers between devices: 27.5 us -> 19 us  [ring_first(): ahead = lax.ppermute(ahead, 'z', forward)]
    ppermute x4, waiting for transfers between devices: 38.3 us -> 30.4 us  [ring_first(): back = lax.ppermute(back, 'z', backward)]
    cond x51 -> x49, local copies, waits for them, and re-layouts: 19 us -> 16.9 us
    add x21 -> x18, other arithmetic: 21.9 us -> 20.2 us  [after(): x = x + (corner.astype(F32) * 0.0).astype(x.dtype)]
  transfers between devices with their start and end apart: 98 -> 98, of which waited for: 43 -> 44; matrix products, arithmetic and copies ran while one was open for 18% -> 18% of each run, Pallas kernels for 15% -> 16%
where the time goes in v3:
time: 780 us; the launch traced here: 768 us
  waiting for transfers between devices  290 us (37%)
  Pallas kernels  164 us (21%)
  starting transfers between devices  118 us (15%)
  local copies, waits for them, and re-layouts  84.4 us (11%)
  other arithmetic  73.7 us (9%)
  loops' own time  21.2 us (3%)
  between operations  17.7 us (2%)
    pallas_call x13, Pallas kernels, call(): return lambda *args: made(*args, *deps)  107 us
    ppermute x36, waiting for transfers between devices, hop(): return lax.ppermute(x, 'tp', [(t, t ^ bit) for t in range(tp_size)])  99.7 us
    ppermute x4, waiting for transfers between devices, scatter_last(): one = lax.ppermute(fwd, 'z', forward)  46.9 us
    ppermute x4, waiting for transfers between devices, ring_last(): one = lax.ppermute(after(ahead[:, :mid], back, *deps), 'z', forward)  42.4 us
    ppermute x36, starting transfers between devices, hop(): return lax.ppermute(x, 'tp', [(t, t ^ bit) for t in range(tp_size)])  38.2 us
    pallas_call x4, Pallas kernels, placed_call(): return lambda *args: made(*args, *deps)  36 us
    ppermute x4, waiting for transfers between devices, ring_first(): back = lax.ppermute(back, 'z', backward)  30.4 us
    all_to_all x6, starting transfers between devices, to_z(): return lax.all_to_all(x, 'z', split_axis=0, concat_axis=0, tiled=True)  28 us
  transfers between devices with their start and end apart: 98, of which 44 were waited for; matrix products, arithmetic and copies ran while one was open for 18% of the time, Pallas kernels for 16%

profile of v3, /device:TPU:0, one launch (start us, length us, event | category | flops | bytes accessed | tf_op | source)
XLA Modules:
  0.0 767.8 jit_solution(16904603379939935834)
XLA Ops:
  13.3 6.3 all-to-all-start.3
  30.4 14.9 %all-to-all-done.3 = bf16[4,256,512]{2,1,0:T(8,128)(2,1)S(1)} async-done(((bf16[4,256,512]{2,1,0:T(8,128)(2,1)}), bf16[4,256,512]{2,1,0:T(8,128)(2,1)S(1)}, u32[]{:S(2)}, u32[]{:S(2)}) %all-to-all-start.3) | async-done | bytes 1048608 | tf_op jit(solution)/shard_map/all_to_all | solution.py:698
  47.0 63.1 %conditional.10 = (bf16[2,512,1024]{2,1,0:T(8,128)(2,1)}, bf16[4,1024,512]{2,1,0:T(8,128)(2,1)}, bf16[4,1024,512]{2,1,0:T(8,128)(2,1)}, f32[2048,128]{1,0:T(8,12...) conditional(s32[]{:T(128)} %bitcast.71, () %tuple.99, ...), branch_computations={%region_4.5_spmd, %region_5.6_spmd} | conditional | flops 15336558 | bytes 84994448 | solution.py:746
  54.8 3.8 fusion.1
  59.8 14.1 %collective-permute-done.6 = bf16[2,128,1024]{2,1,0:T(8,128)(2,1)S(1)} collective-permute-done((bf16[2,128,1024]{2,1,0:T(8,128)(2,1)S(1)}, bf16[2,128,1024]{2,1,0:T(8,128)(2,1)S(1)}, u32[]{:S(2)}, u32[]{:S(2)}) %collective-permute-start.6) | collective-permute-done | bytes 524320 | tf_op jit(solution)/shard_map/cond/branch_1_fun/ppermute | solution.py:600
  82.9 9.9 %collective-permute-done.7 = bf16[2,64,1024]{2,1,0:T(8,128)(2,1)S(1)} collective-permute-done((bf16[2,64,1024]{2,1,0:T(8,128)(2,1)S(1)}, bf16[2,64,1024]{2,1,0:T(8,128)(2,1)S(1)}, u32[]{:S(2)}, u32[]{:S(2)}) %collective-permute-start.7) | collective-permute-done | bytes 262176 | tf_op jit(solution)/shard_map/cond/branch_1_fun/ppermute | solution.py:607
  95.4 3.5 fusion
  110.1 4.7 all-to-all-start.4
  115.9 7.4 qkv.1
  127.0 8.3 %collective-permute-done.83.refs_1_ = bf16[512,384]{1,0:T(8,128)(2,1)S(1)} collective-permute-done((bf16[512,384]{1,0:T(8,128)(2,1)S(1)}, bf16[512,384]{1,0:T(8,128)(2,1)S(1)}, u32[]{:S(2)}, u32[]{:S(2)}) %collective-permute-start.83) | collective-permute-done | bytes 393248 | tf_op jit(solution)/shard_map/ppermute | solution.py:590
  135.3 8.8 %collective-permute-done.84.refs_2_ = bf16[512,384]{1,0:T(8,128)(2,1)S(1)} collective-permute-done((bf16[512,384]{1,0:T(8,128)(2,1)S(1)}, bf16[512,384]{1,0:T(8,128)(2,1)S(1)}, u32[]{:S(2)}, u32[]{:S(2)}) %collective-permute-start.84) | collective-permute-done | bytes 393248 | tf_op jit(solution)/shard_map/ppermute | solution.py:590
  144.1 7.9 %attend.1 = (bf16[512,128]{1,0:T(8,128)(2,1)S(1)}, bf16[512,128]{1,0:T(8,128)(2,1)S(1)}, bf16[512,128]{1,0:T(8,128)(2,1)S(1)}, bf16[512,128]{1,0:T(8,128)(2,1)S(...) custom-call(s32[16]{0:T(128)S(1)} %and_select_fusion.2.tab_ref.refs_0_, ...), custom_call_target="tpu_custom_call" | custom-call | flops 2147483648 | bytes 12582912 | tf_op jit(solution)/shard_map/attend/pallas_call | solution.py:181
  160.8 5.2 attn_out.1
  166.0 47.2 %conditional.11 = (f32[2,128,1024]{2,1,0:T(8,128)}, bf16[1024,1024]{1,0:T(8,128)(2,1)}, bf16[1024,1024]{1,0:T(8,128)(2,1)}, f32[1,128,1]{1,2,0:T(1,128)S(1)}, f32[2,128,1024]{1,2,0:T(8,128)S(1)}) conditional(s32[]{:T(128)} %bitcast.71, () %tuple.98, (bf16[2,128,1024]{2,1,0:T(8,128)(2,1)S(1)}, bf16[2,64,1024]{2,1,0:T(8,128)(2,1)S(1)}, ...), branch_computations={%region_6.7_spmd, %region_7.9_spmd} | conditional | flops 4194176 | bytes 38273844 | solution.py:746
  171.3 11.0 %collective-permute-done.75 = bf16[2,64,1024]{2,1,0:T(8,128)(2,1)S(1)} collective-permute-done((bf16[2,64,1024]{2,1,0:T(8,128)(2,1)S(1)}, bf16[2,64,1024]{2,1,0:T(8,128)(2,1)S(1)}, u32[]{:S(2)}, u32[]{:S(2)}) %collective-permute-start.75) | collective-permute-done | bytes 262176 | tf_op jit(solution)/shard_map/cond/branch_1_fun/ppermute | solution.py:619
  188.6 16.1 %collective-permute-done.76 = bf16[2,128,1024]{2,1,0:T(8,128)(2,1)S(1)} collective-permute-done((bf16[2,128,1024]{2,1,0:T(8,128)(2,1)}, bf16[2,128,1024]{2,1,0:T(8,128)(2,1)S(1)}, u32[]{:S(2)}, u32[]{:S(2)}) %collective-permute-start.76) | collective-permute-done | bytes 524320 | tf_op jit(solution)/shard_map/cond/branch_1_fun/ppermute | solution.py:634
  213.3 4.9 all-to-all-start.5
  220.2 73.2 %conditional.12 = (bf16[2,512,1024]{2,1,0:T(8,128)(2,1)}, bf16[4,1024,1024]{2,1,0:T(8,128)(2,1)}, bf16[4,1024,1024]{2,1,0:T(8,128)(2,1)}) conditional(s32[]{:T(128)} %bitcast.71, () %tuple.104, (bf16[2,128,1024]{1,2,0:T(8,128)(2,1)}, bf16[4,256,1024]{2,1,0:T(8,128)(2,1)}, bf16[1024,1024]{1,0:T(8,128)(2,1)}, bf16[1024,1024]{1,0:T(8,128)(2,1)}) %tuple.105), branch_computations={%region_9.10_spmd, %region_10.11_spmd} | conditional | flops 26476548 | bytes 81863176 | solution.py:746
  232.5 12.4 %collective-permute-done.17 = bf16[2,128,1024]{2,1,0:T(8,128)(2,1)S(1)} collective-permute-done((bf16[2,128,1024]{2,1,0:T(8,128)(2,1)S(1)}, bf16[2,128,1024]{2,1,0:T(8,128)(2,1)S(1)}, u32[]{:S(2)}, u32[]{:S(2)}) %collective-permute-start.17) | collective-permute-done | bytes 524320 | tf_op jit(solution)/shard_map/cond/branch_1_fun/ppermute | solution.py:600
  244.8 19.0 %collective-permute-done.16 = bf16[2,128,1024]{2,1,0:T(8,128)(2,1)S(1)} collective-permute-done((bf16[2,128,1024]{2,1,0:T(8,128)(2,1)S(1)}, bf16[2,128,1024]{2,1,0:T(8,128)(2,1)S(1)}, u32[]{:S(2)}, u32[]{:S(2)}) %collective-permute-start.16) | collective-permute-done | bytes 524320 | tf_op jit(solution)/shard_map/cond/branch_1_fun/ppermute | solution.py:599
  266.5 6.8 fusion.8
  281.9 10.1 %collective-permute-done.18 = bf16[2,64,1024]{2,1,0:T(8,128)(2,1)S(1)} collective-permute-done((bf16[2,64,1024]{2,1,0:T(8,128)(2,1)S(1)}, bf16[2,64,1024]{2,1,0:T(8,128)(2,1)S(1)}, u32[]{:S(2)}, u32[]{:S(2)}) %collective-permute-start.18) | collective-permute-done | bytes 262176 | tf_op jit(solution)/shard_map/cond/branch_1_fun/ppermute | solution.py:607
  293.4 76.5 %conditional.13 = (bf16[2,512,1024]{2,1,0:T(8,128)(2,1)}, bf16[4,1024,512]{2,1,0:T(8,128)(2,1)}, bf16[4,1024,512]{2,1,0:T(8,128)(2,1)}, bf16[4,512,512]{2,1,0:T(...) conditional(s32[]{:T(128)} %bitcast.71, () %tuple.103, ...), branch_computations={%region_11.12_spmd, %region_12.13_spmd} | conditional | flops 10486763 | bytes 62916100 | solution.py:746
  299.1 16.0 %gate_up.1 = (bf16[4,512,512]{2,1,0:T(8,128)(2,1)}, bf16[4,512,512]{2,1,0:T(8,128)(2,1)}, bf16[4,512,512]{2,1,0:T(8,128)(2,1)}) custom-call(bf16[2,512,1024]{2,1,0:T(8,128)(2,1)} %get-tuple-element.204.refs_0_, bf16[4,1024,1024]{2,1,0:T(8,128)(2,1)} %get-tuple-element.205.refs_1_.refs_3_, bf16[4,1024,1024]{2,1,0:T(8,128)(2,1)} %get-tuple-element.206.refs_2_.refs_4_, ...), custom_call_target="tpu_custom_call" | custom-call | flops 1000 | bytes 1000 | tf_op jit(solution)/shard_map/cond/branch_1_fun/gate_up/pallas_call | solution.py:57
  317.0 3.9 collective-permute-done.27
  328.3 8.6 %collective-permute-done.32 = bf16[512,512]{1,0:T(8,128)(2,1)S(1)} collective-permute-done((bf16[512,512]{1,0:T(8,128)(2,1)S(1)}, bf16[512,512]{1,0:T(8,128)(2,1)S(1)}, u32[]{:S(2)}, u32[]{:S(2)}) %collective-permute-start.32) | collective-permute-done | bytes 524320 | tf_op jit(solution)/shard_map/cond/branch_1_fun/ppermute | solution.py:590
  338.8 3.7 pad_maximum_fusion.4
  350.0 10.1 %collective-permute-done.28 = bf16[2,64,1024]{2,1,0:T(8,128)(2,1)S(1)} collective-permute-done((bf16[2,64,1024]{2,1,0:T(8,128)(2,1)S(1)}, bf16[2,64,1024]{2,1,0:T(8,128)(2,1)S(1)}, u32[]{:S(2)}, u32[]{:S(2)}) %collective-permute-start.28) | collective-permute-done | bytes 262176 | tf_op jit(solution)/shard_map/cond/branch_1_fun/ppermute | solution.py:607
  369.9 32.6 %feed_back.1 = (bf16[4,2,512,512]{3,2,1,0:T(8,128)(2,1)}, f32[2,128,1024]{2,1,0:T(8,128)S(1)}, bf16[2,128,1024]{2,1,0:T(8,128)(2,1)S(1)}, bf16[2,128,1024]{2,1,0...) custom-call(bf16[2,512,1024]{2,1,0:T(8,128)(2,1)} %get-tuple-element.402.refs_0_, ...), custom_call_target="tpu_custom_call" | custom-call | flops 12884901888 | bytes 37748736 | tf_op jit(solution)/shard_map/feed_back/pallas_call | solution.py:57
  402.5 41.4 %conditional.14 = (bf16[4,1024,512]{2,1,0:T(8,128)(2,1)}, bf16[4,2,512,512]{3,2,1,0:T(8,128)(2,1)}, f32[2,128,1024]{1,2,0:T(8,128)}) conditional(s32[]{:T(128)} %bitcast.71, () %tuple.102, (bf16[2,128,1024]{2,1,0:T(8,128)(2,1)S(1)}, bf16[2,64,1024]{2,1,0:T(8,128)(2,1)S(1)}, f32[2,128,1024]{2,1,0:T(8,128)S(1)}, ...), branch_computations={%region_13.14_spmd, %region_14.15_spmd} | conditional | flops 4298637312 | bytes 60293444 | solution.py:746
  406.9 4.5 collective-permute-done.55
  411.5 5.8 collective-permute-start.56
  418.4 9.5 %g_down.1 = bf16[4,1024,512]{2,1,0:T(8,128)(2,1)} custom-call(s32[1]{0:T(128)} %get-tuple-element.216.refs_0_, bf16[512,1024]{1,0:T(8,128)(2,1)S(1)} %get-tuple-element.667.refs_1_, bf16[512,1024]{1,0:T(8,128)(2,1)S(1)} %collective-permute-done.57.refs_2_, bf16[4,1,512,512]{3,2,1,0:T(8,128)(2,1)} %bitcast.38.refs_3_, bf16[4,1,512,512]{3,2,1,0:T(8,128)(2,1)S(1)} %bitcast.133), custom_call_target="tpu_custom_call" | custom-call | flops 4294967296 | bytes 10485760 | tf_op jit(solution)/shard_map/cond/branch_1_fun/g_down/pallas_call | solution.py:466
  432.5 7.7 collective-permute-done.54
  448.2 53.3 %conditional.15 = (bf16[2,512,1024]{2,1,0:T(8,128)(2,1)}, f32[2,128,1024]{2,1,0:T(8,128)}, bf16[2,128,1024]{2,1,0:T(8,128)(2,1)}, bf16[2,128,1024]{2,1,0:T(8,128...) conditional(s32[]{:T(128)} %bitcast.71, () %tuple.111, ...), branch_computations={%region_16.17_spmd, %region_17.18_spmd} | conditional | flops 12886212608 | bytes 50356520 | solution.py:746
  453.1 18.4 %g_gate_up.1 = bf16[4,1024,1024]{2,1,0:T(8,128)(2,1)} custom-call(s32[1]{0:T(128)} %get-tuple-element.221.refs_0_, bf16[512,1024]{1,0:T(8,128)(2,1)S(1)} %slice_bitcast_fusion.3.refs_1_, bf16[512,1024]{1,0:T(8,128)(2,1)} %get-tuple-element.223.refs_2_, bf16[4,2,512,512]{3,2,1,0:T(8,128)(2,1)} %get-tuple-element.224.refs_3_, ...), custom_call_target="tpu_custom_call" | custom-call | flops 8589934592 | bytes 18874368 | tf_op jit(solution)/shard_map/cond/branch_1_fun/g_gate_up/pallas_call | solution.py:466
  473.3 8.8 %ffn_out.1 = (f32[2,128,1024]{2,1,0:T(8,128)}, bf16[2,128,1024]{2,1,0:T(8,128)(2,1)}, bf16[2,128,1024]{2,1,0:T(8,128)(2,1)}, bf16[2,64,1024]{2,1,0:T(8,128)(2,1)}, bf16[2,64,1024]{2,1,0:T(8,128)(2,1)}) custom-call(bf16[4,512,512]{2,1,0:T(8,128)(2,1)} %get-tuple-element.226.refs_0_, bf16[4,1024,512]{2,1,0:T(8,128)(2,1)} %get-tuple-element.227.refs_1_, ...), custom_call_target="tpu_custom_call" | custom-call | flops 4294967296 | bytes 12582912 | tf_op jit(solution)/shard_map/cond/branch_1_fun/ffn_out/pallas_call | solution.py:57
  487.8 12.2 %collective-permute-done.38 = bf16[2,64,1024]{2,1,0:T(8,128)(2,1)S(1)} collective-permute-done((bf16[2,64,1024]{2,1,0:T(8,128)(2,1)S(1)}, bf16[2,64,1024]{2,1,0:T(8,128)(2,1)S(1)}, u32[]{:S(2)}, u32[]{:S(2)}) %collective-permute-start.38) | collective-permute-done | bytes 262176 | tf_op jit(solution)/shard_map/cond/branch_1_fun/ppermute | solution.py:607
  501.5 5.1 dmix.1
  506.7 17.4 %conditional.16 = (bf16[512,128]{1,0:T(8,128)(2,1)S(1)}, bf16[512,128]{1,0:T(8,128)(2,1)}, bf16[512,128]{1,0:T(8,128)(2,1)}, bf16[512,128]{1,0:T(8,128)(2,1)}, b...) conditional(s32[]{:T(128)} %bitcast.71, () %tuple.110, (bf16[512,128]{1,0:T(8,128)(2,1)S(1)}, ...), branch_computations={%region_18.19_spmd, %region_19.20_spmd} | conditional | bytes 3670264 | solution.py:746
  513.2 5.8 collective-permute-done
  519.2 4.6 collective-permute-done.2
  524.1 12.9 %attend_back.1 = (bf16[512,384]{1,0:T(8,128)(2,1)}, bf16[512,384]{1,0:T(8,128)(2,1)}, bf16[512,384]{1,0:T(8,128)(2,1)}, bf16[512,384]{1,0:T(8,128)(2,1)}) custom-call(s32[16]{0:T(128)S(1)} %and_select_fusion.2.tab_ref.refs_0_, bf16[512,128]{1,0:T(8,128)(2,1)S(1)} %get-tuple-element.424.refs_1_, bf16[512,128]{1,0:T(8,128)(2,1)} %get-tuple-element.425.refs_2_, ...), custom_call_target="tpu_custom_call" | custom-call | flops 5368709120 | bytes 12582912 | tf_op jit(solution)/shard_map/attend_back/pallas_call | solution.py:212
  537.0 58.0 %conditional.17 = (bf16[4,512,384]{2,1,0:T(8,128)(2,1)}, bf16[2,128,1024]{2,1,0:T(8,128)(2,1)}, bf16[4,256,512]{2,1,0:T(8,128)(2,1)}, bf16[1,128,1024]{2,1,0:T(8...) conditional(s32[]{:T(128)} %bitcast.71, () %tuple.109, ...), branch_computations={%region_21.22_spmd, %region_22.23_spmd} | conditional | flops 6291456 | bytes 27263292 | solution.py:746
  537.0 4.2 all-to-all-start.2
  549.3 12.6 %collective-permute-done.60 = bf16[512,384]{1,0:T(8,128)(2,1)S(1)} collective-permute-done((bf16[512,384]{1,0:T(8,128)(2,1)}, bf16[512,384]{1,0:T(8,128)(2,1)S(1)}, u32[]{:S(2)}, u32[]{:S(2)}) %collective-permute-start.60) | collective-permute-done | bytes 393248 | tf_op jit(solution)/shard_map/cond/branch_1_fun/ppermute | solution.py:590
  563.4 13.4 %collective-permute-done.62 = bf16[512,384]{1,0:T(8,128)(2,1)S(1)} collective-permute-done((bf16[512,384]{1,0:T(8,128)(2,1)}, bf16[512,384]{1,0:T(8,128)(2,1)S(1)}, u32[]{:S(2)}, u32[]{:S(2)}) %collective-permute-start.62) | collective-permute-done | bytes 393248 | tf_op jit(solution)/shard_map/cond/branch_1_fun/ppermute | solution.py:590
  578.1 9.9 %collective-permute-done.63 = bf16[2,128,1024]{2,1,0:T(8,128)(2,1)S(1)} collective-permute-done((bf16[2,128,1024]{2,1,0:T(8,128)(2,1)S(1)}, bf16[2,128,1024]{2,1,0:T(8,128)(2,1)S(1)}, u32[]{:S(2)}, u32[]{:S(2)}) %collective-permute-start.63) | collective-permute-done | bytes 524320 | tf_op jit(solution)/shard_map/cond/branch_1_fun/ppermute | solution.py:634
  595.0 7.7 %dxn1.1 = (f32[2,128,1024]{2,1,0:T(8,128)S(1)}, bf16[2,128,1024]{2,1,0:T(8,128)(2,1)S(1)}, bf16[2,128,1024]{2,1,0:T(8,128)(2,1)S(1)}, bf16[2,64,1024]{2,1,0:T(8,128)(2,1)S(1)}, bf16[2,64,1024]{2,1,0:T(8,128)(2,1)S(1)}) custom-call(bf16[4,512,384]{2,1,0:T(8,128)(2,1)} %get-tuple-element.441.refs_0_, bf16[4,1024,512]{2,1,0:T(8,128)(2,1)} %get-tuple-element.376.refs_1_, ...), custom_call_target="tpu_custom_call" | custom-call | flops 3221225472 | bytes 9961472 | tf_op jit(solution)/shard_map/dxn1/pallas_call | solution.py:57
  602.8 59.5 %conditional.18 = (bf16[512,512]{1,0:T(8,128)(2,1)}, bf16[512,512]{1,0:T(8,128)(2,1)S(1)}, bf16[512,512]{1,0:T(8,128)(2,1)}, bf16[512,512]{1,0:T(8,128)(2,1)}, f32[2,128,1024]{1,2,0:T(8,128)S(1)}) conditional(s32[]{:T(128)} %bitcast.71, () %tuple.108, (bf16[2,128,1024]{2,1,0:T(8,128)(2,1)S(1)}, bf16[2,64,1024]{2,1,0:T(8,128)(2,1)S(1)}, ...), branch_computations={%region_23.24_spmd, %region_24.25_spmd} | conditional | flops 4299948032 | bytes 81265104 | solution.py:746
  607.5 8.2 %collective-permute-done.67 = bf16[2,64,1024]{2,1,0:T(8,128)(2,1)S(1)} collective-permute-done((bf16[2,64,1024]{2,1,0:T(8,128)(2,1)S(1)}, bf16[2,64,1024]{2,1,0:T(8,128)(2,1)S(1)}, u32[]{:S(2)}, u32[]{:S(2)}) %collective-permute-start.67) | collective-permute-done | bytes 262176 | tf_op jit(solution)/shard_map/cond/branch_1_fun/ppermute | solution.py:620
  620.0 9.8 %g_heads.1 = bf16[4,1024,512]{2,1,0:T(8,128)(2,1)} custom-call(bf16[512,1024]{1,0:T(8,128)(2,1)S(1)} %get-tuple-element.691.refs_0_, bf16[512,1024]{1,0:T(8,128)(2,1)S(1)} %collective-permute-done.69.refs_1_, bf16[4,512,384]{2,1,0:T(8,128)(2,1)} %get-tuple-element.257.refs_2_, bf16[4,512,384]{2,1,0:T(8,128)(2,1)} %copy-done.45, ...), custom_call_target="tpu_custom_call" | custom-call | flops 4294967296 | bytes 12582912 | tf_op jit(solution)/shard_map/cond/branch_1_fun/g_heads/pallas_call | solution.py:57
  636.2 13.2 %collective-permute-done.66 = bf16[2,128,1024]{2,1,0:T(8,128)(2,1)S(1)} collective-permute-done((bf16[2,128,1024]{2,1,0:T(8,128)(2,1)S(1)}, bf16[2,128,1024]{2,1,0:T(8,128)(2,1)S(1)}, u32[]{:S(2)}, u32[]{:S(2)}) %collective-permute-start.66) | collective-permute-done | bytes 524320 | tf_op jit(solution)/shard_map/cond/branch_1_fun/ppermute | solution.py:634
  652.3 6.6 collective-permute-done.73
  675.6 81.4 %conditional.19 = (f32[512,2048]{1,0:T(8,128)}, bf16[512,2048]{1,0:T(8,128)(2,1)}, f32[256,2048]{1,0:T(8,128)}, f32[256,2048]{1,0:T(8,128)}, f32[2048,256]{1,0:T(8,128)}, /*index=5*/bf16[4,256,512]{2,1,0:T(8,128)(2,1)}) conditional(s32[]{:T(128)} %bitcast.71, () %tuple.97, (s32[4]{0:T(128)S(1)}, s32[]{:T(128)}, s32[]{:T(128)}, ...), branch_computations={%region_27.28_spmd, %region_28.29_spmd} | conditional | flops 7866437 | bytes 97520640 | solution.py:746
  675.6 3.6 all-to-all-start
  689.2 6.3 collective-permute-done.42
  698.2 8.6 %collective-permute-done.47 = bf16[128,2048]{1,0:T(8,128)(2,1)} collective-permute-done((bf16[128,2048]{1,0:T(8,128)(2,1)}, bf16[128,2048]{1,0:T(8,128)(2,1)}, u32[]{:S(2)}, u32[]{:S(2)}) %collective-permute-start.47) | collective-permute-done | bytes 524320 | tf_op jit(solution)/shard_map/cond/branch_1_fun/ppermute | solution.py:590
  715.0 3.6 collective-permute-done.52
  727.4 4.3 all-to-all-start.1
  738.9 3.8 unpack_down.1
  745.9 4.2 place.2
  750.1 4.0 place.3
  757.0 3.5 unpack_heads.1
  (441 shorter events, 256.2 us)
Async XLA Ops:
  13.3 32.0 %all-to-all-start.3 = ((bf16[4,256,512]{2,1,0:T(8,128)(2,1)}), bf16[4,256,512]{2,1,0:T(8,128)(2,1)S(1)}, u32[]{:S(2)}, u32[]{:S(2)}) async-start(bf16[4,256,512]{2,1,0:T(8,128)(2,1)} %pack_heads.1), calls=%async_computation.3 | async-start | bytes 2097152 | tf_op jit(solution)/shard_map/all_to_all | solution.py:698
  47.0 29.4 %collective-permute-start.10 = (bf16[1024,512]{1,0:T(8,128)(2,1)S(1)}, bf16[1024,512]{1,0:T(8,128)(2,1)}, u32[]{:S(2)}, u32[]{:S(2)}) collective-permute-start(bf16[1024,512]{1,0:T(8,128)(2,1)S(1)} %get-tuple-element.184), channel_id=1, source_target_pairs={{0,2},{1,3},{2,0},{3,1},{4,6},{5,7},{6,4},{7,5},{8,10},{9,11},{10,... | collective-permute-start | bytes 3145736 | tf_op jit(solution)/shard_map/cond/branch_1_fun/ppermute | solution.py:590
  48.6 29.6 %collective-permute-start.9 = (bf16[1024,512]{1,0:T(8,128)(2,1)S(1)}, bf16[1024,512]{1,0:T(8,128)(2,1)}, u32[]{:S(2)}, u32[]{:S(2)}) collective-permute-start(bf16[1024,512]{1,0:T(8,128)(2,1)S(1)} %get-tuple-element.184), channel_id=1, source_target_pairs={{0,1},{1,0},{2,3},{3,2},{4,5},{5,4},{6,7},{7,6},{8,9},{9,8},{10,11... | collective-permute-start | bytes 3145736 | tf_op jit(solution)/shard_map/cond/branch_1_fun/ppermute | solution.py:590
  50.3 23.6 %collective-permute-start.6 = (bf16[2,128,1024]{2,1,0:T(8,128)(2,1)S(1)}, bf16[2,128,1024]{2,1,0:T(8,128)(2,1)S(1)}, u32[]{:S(2)}, u32[]{:S(2)}) collective-permute-start(bf16[2,128,1024]{2,1,0:T(8,128)(2,1)S(1)} %copy.109), channel_id=1, source_target_pairs={{8,0},{24,8},{16,24},{0,16},{9,1},{25,9},{17,25},{1,17},{10,2},{26... | collective-permute-start | bytes 1572872 | tf_op jit(solution)/shard_map/cond/branch_1_fun/ppermute | solution.py:600
  50.4 24.8 %collective-permute-start.5 = (bf16[2,128,1024]{2,1,0:T(8,128)(2,1)S(1)}, bf16[2,128,1024]{2,1,0:T(8,128)(2,1)S(1)}, u32[]{:S(2)}, u32[]{:S(2)}) collective-permute-start(bf16[2,128,1024]{2,1,0:T(8,128)(2,1)S(1)} %copy.109), channel_id=1, source_target_pairs={{0,8},{8,24},{24,16},{16,0},{1,9},{9,25},{25,17},{17,1},{2,10},{10... | collective-permute-start | bytes 1572872 | tf_op jit(solution)/shard_map/cond/branch_1_fun/ppermute | solution.py:599
  77.5 17.8 %collective-permute-start.12 = (bf16[512,512]{1,0:T(8,128)(2,1)S(1)}, bf16[512,512]{1,0:T(8,128)(2,1)S(1)}, u32[]{:S(2)}, u32[]{:S(2)}) collective-permute-start(bf16[512,512]{1,0:T(8,128)(2,1)S(1)} %fusion.6), channel_id=1, source_target_pairs={{0,1},{1,0},{2,3},{3,2},{4,5},{5,4},{6,7},{7,6},{8,9},{9,8},{10,11... | collective-permute-start | bytes 1572872 | tf_op jit(solution)/shard_map/cond/branch_1_fun/ppermute | solution.py:590
  79.2 16.1 %collective-permute-start.13 = (bf16[512,512]{1,0:T(8,128)(2,1)S(1)}, bf16[512,512]{1,0:T(8,128)(2,1)S(1)}, u32[]{:S(2)}, u32[]{:S(2)}) collective-permute-start(bf16[512,512]{1,0:T(8,128)(2,1)S(1)} %fusion.4), channel_id=1, source_target_pairs={{0,2},{1,3},{2,0},{3,1},{4,6},{5,7},{6,4},{7,5},{8,10},{9,11},{10,... | collective-permute-start | bytes 1572872 | tf_op jit(solution)/shard_map/cond/branch_1_fun/ppermute | solution.py:590
  110.1 56.0 %all-to-all-start.4 = ((bf16[4,256,1024]{2,1,0:T(8,128)(2,1)}), bf16[4,256,1024]{2,1,0:T(8,128)(2,1)}, u32[]{:S(2)}, u32[]{:S(2)}) async-start(bf16[4,256,1024]{2,1,0:T(8,128)(2,1)} %get-tuple-element.393), calls=%async_computation.4 | async-start | bytes 4194304 | tf_op jit(solution)/shard_map/all_to_all | solution.py:698
  124.8 19.3 %collective-permute-start.84 = (bf16[512,384]{1,0:T(8,128)(2,1)S(1)}, bf16[512,384]{1,0:T(8,128)(2,1)S(1)}, u32[]{:S(2)}, u32[]{:S(2)}) collective-permute-start(bf16[512,384]{1,0:T(8,128)(2,1)S(1)} %get-tuple-element.380), channel_id=1, source_target_pairs={{0,2},{1,3},{2,0},{3,1},{4,6},{5,7},{6,4},{7,5},{8,10},{9,11},{10,... | collective-permute-start | bytes 1179656 | tf_op jit(solution)/shard_map/ppermute | solution.py:590
  126.4 17.8 %collective-permute-start.85 = (bf16[512,384]{1,0:T(8,128)(2,1)S(1)}, bf16[512,384]{1,0:T(8,128)(2,1)S(1)}, u32[]{:S(2)}, u32[]{:S(2)}) collective-permute-start(bf16[512,384]{1,0:T(8,128)(2,1)S(1)} %get-tuple-element.381), channel_id=1, source_target_pairs={{0,3},{1,2},{2,1},{3,0},{4,7},{5,6},{6,5},{7,4},{8,11},{9,10},{10,... | collective-permute-start | bytes 1179656 | tf_op jit(solution)/shard_map/ppermute | solution.py:590
  166.1 45.9 %collective-permute-start.80 = (bf16[1024,1024]{1,0:T(8,128)(2,1)}, bf16[1024,1024]{1,0:T(8,128)(2,1)}, u32[]{:S(2)}, u32[]{:S(2)}) collective-permute-start(bf16[1024,1024]{1,0:T(8,128)(2,1)} %bitcast.13), channel_id=1, source_target_pairs={{0,2},{1,3},{2,0},{3,1},{4,6},{5,7},{6,4},{7,5},{8,10},{9,11},{10,... | collective-permute-start | bytes 6291464 | tf_op jit(solution)/shard_map/cond/branch_1_fun/ppermute | solution.py:590
  167.4 45.9 %collective-permute-start.79 = (bf16[1024,1024]{1,0:T(8,128)(2,1)}, bf16[1024,1024]{1,0:T(8,128)(2,1)}, u32[]{:S(2)}, u32[]{:S(2)}) collective-permute-start(bf16[1024,1024]{1,0:T(8,128)(2,1)} %bitcast.13), channel_id=1, source_target_pairs={{0,1},{1,0},{2,3},{3,2},{4,5},{5,4},{6,7},{7,6},{8,9},{9,8},{10,11... | collective-permute-start | bytes 6291464 | tf_op jit(solution)/shard_map/cond/branch_1_fun/ppermute | solution.py:590
  183.2 21.5 %collective-permute-start.76 = (bf16[2,128,1024]{2,1,0:T(8,128)(2,1)}, bf16[2,128,1024]{2,1,0:T(8,128)(2,1)S(1)}, u32[]{:S(2)}, u32[]{:S(2)}) collective-permute-start(bf16[2,128,1024]{2,1,0:T(8,128)(2,1)} %pad_maximum_fusion.2), channel_id=1, source_target_pairs={{0,8},{8,24},{24,16},{16,0},{1,9},{9,25},{25,17},{17,1},{2,10},{10... | collective-permute-start | bytes 1572872 | tf_op jit(solution)/shard_map/cond/branch_1_fun/ppermute | solution.py:634
  184.1 20.6 %collective-permute-start.78 = (bf16[2,128,1024]{2,1,0:T(8,128)(2,1)}, bf16[2,128,1024]{2,1,0:T(8,128)(2,1)}, u32[]{:S(2)}, u32[]{:S(2)}) collective-permute-start(bf16[2,128,1024]{2,1,0:T(8,128)(2,1)} %pad_maximum_fusion.3), channel_id=1, source_target_pairs={{8,0},{24,8},{16,24},{0,16},{9,1},{25,9},{17,25},{1,17},{10,2},{26... | collective-permute-start | bytes 1572872 | tf_op jit(solution)/shard_map/cond/branch_1_fun/ppermute | solution.py:635
  213.3 80.2 %all-to-all-start.5 = ((bf16[4,256,512]{2,1,0:T(8,128)(2,1)}), bf16[4,256,512]{2,1,0:T(8,128)(2,1)}, u32[]{:S(2)}, u32[]{:S(2)}) async-start(bf16[4,256,512]{2,1,0:T(8,128)(2,1)} %tie.3), calls=%async_computation.5 | async-start | bytes 2097152 | tf_op jit(solution)/shard_map/all_to_all | solution.py:698
  218.2 318.8 %reduce-scatter.7.cloned.1.call-start = ((), (), s32[]{:S(2)}) async-start(), calls=%async_computation.9 | async-start | bytes 5242880
  228.0 38.3 %collective-permute-start.21 = (bf16[512,1024]{1,0:T(8,128)(2,1)S(1)}, bf16[512,1024]{1,0:T(8,128)(2,1)S(1)}, u32[]{:S(2)}, u32[]{:S(2)}) collective-permute-start(bf16[512,1024]{1,0:T(8,128)(2,1)S(1)} %slice_add_fusion.7), channel_id=1, source_target_pairs={{0,1},{1,0},{2,3},{3,2},{4,5},{5,4},{6,7},{7,6},{8,9},{9,8},{10,11... | collective-permute-start | bytes 3145736 | tf_op jit(solution)/shard_map/cond/branch_1_fun/ppermute | solution.py:590
  228.6 37.7 %collective-permute-start.22 = (bf16[512,1024]{1,0:T(8,128)(2,1)S(1)}, bf16[512,1024]{1,0:T(8,128)(2,1)S(1)}, u32[]{:S(2)}, u32[]{:S(2)}) collective-permute-start(bf16[512,1024]{1,0:T(8,128)(2,1)S(1)} %slice_add_fusion.6), channel_id=1, source_target_pairs={{0,2},{1,3},{2,0},{3,1},{4,6},{5,7},{6,4},{7,5},{8,10},{9,11},{10,... | collective-permute-start | bytes 3145736 | tf_op jit(solution)/shard_map/cond/branch_1_fun/ppermute | solution.py:590
  229.6 15.2 %collective-permute-start.17 = (bf16[2,128,1024]{2,1,0:T(8,128)(2,1)S(1)}, bf16[2,128,1024]{2,1,0:T(8,128)(2,1)S(1)}, u32[]{:S(2)}, u32[]{:S(2)}) collective-permute-start(bf16[2,128,1024]{2,1,0:T(8,128)(2,1)S(1)} %copy-done.20), channel_id=1, source_target_pairs={{8,0},{24,8},{16,24},{0,16},{9,1},{25,9},{17,25},{1,17},{10,2},{26... | collective-permute-start | bytes 1572872 | tf_op jit(solution)/shard_map/cond/branch_1_fun/ppermute | solution.py:600
  232.5 31.4 %collective-permute-start.16 = (bf16[2,128,1024]{2,1,0:T(8,128)(2,1)S(1)}, bf16[2,128,1024]{2,1,0:T(8,128)(2,1)S(1)}, u32[]{:S(2)}, u32[]{:S(2)}) collective-permute-start(bf16[2,128,1024]{2,1,0:T(8,128)(2,1)S(1)} %copy-done.20), channel_id=1, source_target_pairs={{0,8},{8,24},{24,16},{16,0},{1,9},{9,25},{25,17},{17,1},{2,10},{10... | collective-permute-start | bytes 1572872 | tf_op jit(solution)/shard_map/cond/branch_1_fun/ppermute | solution.py:599
  244.8 19.0 %collective-permute-start.24 = (bf16[16,128]{1,0:T(8,128)(2,1)S(1)}, bf16[16,128]{1,0:T(8,128)(2,1)S(1)}, u32[]{:S(2)}, u32[]{:S(2)}) collective-permute-start(bf16[16,128]{1,0:T(8,128)(2,1)S(1)} %slice.365), channel_id=1, source_target_pairs={{0,4},{4,0},{1,5},{5,1},{2,6},{6,2},{3,7},{7,3},{8,12},{12,8},{9,1... | collective-permute-start | bytes 12296 | tf_op jit(solution)/shard_map/cond/branch_1_fun/ppermute | solution.py:593
  273.3 20.1 %collective-permute-start.25 = (bf16[4,1024,1024]{2,1,0:T(8,128)(2,1)}, bf16[4,1024,1024]{2,1,0:T(8,128)(2,1)}, u32[]{:S(2)}, u32[]{:S(2)}) collective-permute-start(bf16[4,1024,1024]{2,1,0:T(8,128)(2,1)} %fusion.8), channel_id=1, source_target_pairs={{0,4},{4,0},{1,5},{5,1},{2,6},{6,2},{3,7},{7,3},{8,12},{12,8},{9,1... | collective-permute-start | bytes 25165832 | tf_op jit(solution)/shard_map/cond/branch_1_fun/ppermute | solution.py:593
  277.2 15.5 %collective-permute-start.19 = (bf16[2,64,1024]{2,1,0:T(8,128)(2,1)S(1)}, bf16[2,64,1024]{2,1,0:T(8,128)(2,1)S(1)}, u32[]{:S(2)}, u32[]{:S(2)}) collective-permute-start(bf16[2,64,1024]{2,1,0:T(8,128)(2,1)S(1)} %slice_add_fusion.8), channel_id=1, source_target_pairs={{8,0},{24,8},{16,24},{0,16},{9,1},{25,9},{17,25},{1,17},{10,2},{26... | collective-permute-start | bytes 786440 | tf_op jit(solution)/shard_map/cond/branch_1_fun/ppermute | solution.py:608
  293.4 30.0 %collective-permute-start.31 = (bf16[1024,512]{1,0:T(8,128)(2,1)}, bf16[1024,512]{1,0:T(8,128)(2,1)}, u32[]{:S(2)}, u32[]{:S(2)}) collective-permute-start(bf16[1024,512]{1,0:T(8,128)(2,1)} %bitcast.31), channel_id=1, source_target_pairs={{0,2},{1,3},{2,0},{3,1},{4,6},{5,7},{6,4},{7,5},{8,10},{9,11},{10,... | collective-permute-start | bytes 3145736 | tf_op jit(solution)/shard_map/cond/branch_1_fun/ppermute | solution.py:590
  294.0 31.6 %collective-permute-start.30 = (bf16[1024,512]{1,0:T(8,128)(2,1)}, bf16[1024,512]{1,0:T(8,128)(2,1)}, u32[]{:S(2)}, u32[]{:S(2)}) collective-permute-start(bf16[1024,512]{1,0:T(8,128)(2,1)} %bitcast.31), channel_id=1, source_target_pairs={{0,1},{1,0},{2,3},{3,2},{4,5},{5,4},{6,7},{7,6},{8,9},{9,8},{10,11... | collective-permute-start | bytes 3145736 | tf_op jit(solution)/shard_map/cond/branch_1_fun/ppermute | solution.py:590
  297.0 23.9 %collective-permute-start.27 = (bf16[2,128,1024]{2,1,0:T(8,128)(2,1)}, bf16[2,128,1024]{2,1,0:T(8,128)(2,1)S(1)}, u32[]{:S(2)}, u32[]{:S(2)}) collective-permute-start(bf16[2,128,1024]{2,1,0:T(8,128)(2,1)} %copy.113), channel_id=1, source_target_pairs={{8,0},{24,8},{16,24},{0,16},{9,1},{25,9},{17,25},{1,17},{10,2},{26... | collective-permute-start | bytes 1572872 | tf_op jit(solution)/shard_map/cond/branch_1_fun/ppermute | solution.py:600
  297.1 25.1 %collective-permute-start.26 = (bf16[2,128,1024]{2,1,0:T(8,128)(2,1)}, bf16[2,128,1024]{2,1,0:T(8,128)(2,1)S(1)}, u32[]{:S(2)}, u32[]{:S(2)}) collective-permute-start(bf16[2,128,1024]{2,1,0:T(8,128)(2,1)} %copy.113), channel_id=1, source_target_pairs={{0,8},{8,24},{24,16},{16,0},{1,9},{9,25},{25,17},{17,1},{2,10},{10... | collective-permute-start | bytes 1572872 | tf_op jit(solution)/shard_map/cond/branch_1_fun/ppermute | solution.py:599
  342.5 19.1 %collective-permute-start.34 = (bf16[4,1024,512]{2,1,0:T(8,128)(2,1)}, bf16[4,1024,512]{2,1,0:T(8,128)(2,1)}, u32[]{:S(2)}, u32[]{:S(2)}) collective-permute-start(bf16[4,1024,512]{2,1,0:T(8,128)(2,1)} %pad_maximum_fusion.4), channel_id=1, source_target_pairs={{0,4},{4,0},{1,5},{5,1},{2,6},{6,2},{3,7},{7,3},{8,12},{12,8},{9,1... | collective-permute-start | bytes 12582920 | tf_op jit(solution)/shard_map/cond/branch_1_fun/ppermute | solution.py:593
  343.9 17.7 %collective-permute-start.35 = (bf16[512,1024]{1,0:T(8,128)(2,1)S(1)}, bf16[512,1024]{1,0:T(8,128)(2,1)}, u32[]{:S(2)}, u32[]{:S(2)}) collective-permute-start(bf16[512,1024]{1,0:T(8,128)(2,1)S(1)} %slice_bitcast_fusion), channel_id=1, source_target_pairs={{0,4},{4,0},{1,5},{5,1},{2,6},{6,2},{3,7},{7,3},{8,12},{12,8},{9,1... | collective-permute-start | bytes 3145736 | tf_op jit(solution)/shard_map/cond/branch_1_fun/ppermute | solution.py:593
  345.4 15.5 %collective-permute-start.29 = (bf16[2,64,1024]{2,1,0:T(8,128)(2,1)S(1)}, bf16[2,64,1024]{2,1,0:T(8,128)(2,1)S(1)}, u32[]{:S(2)}, u32[]{:S(2)}) collective-permute-start(bf16[2,64,1024]{2,1,0:T(8,128)(2,1)S(1)} %fusion.13), channel_id=1, source_target_pairs={{8,0},{24,8},{16,24},{0,16},{9,1},{25,9},{17,25},{1,17},{10,2},{26... | collective-permute-start | bytes 786440 | tf_op jit(solution)/shard_map/cond/branch_1_fun/ppermute | solution.py:608
  402.5 41.4 %collective-permute-start.59 = (bf16[4,2,512,512]{3,2,1,0:T(8,128)(2,1)}, bf16[4,2,512,512]{3,2,1,0:T(8,128)(2,1)}, u32[]{:S(2)}, u32[]{:S(2)}) collective-permute-start(bf16[4,2,512,512]{3,2,1,0:T(8,128)(2,1)} %get-tuple-element.219), channel_id=1, source_target_pairs={{0,4},{4,0},{1,5},{5,1},{2,6},{6,2},{3,7},{7,3},{8,12},{12,8},{9,1... | collective-permute-start | bytes 12582920 | tf_op jit(solution)/shard_map/cond/branch_1_fun/ppermute | solution.py:593
  402.5 15.9 %collective-permute-start.58 = (bf16[4,512,512]{2,1,0:T(8,128)(2,1)}, bf16[4,512,512]{2,1,0:T(8,128)(2,1)S(1)}, u32[]{:S(2)}, u32[]{:S(2)}) collective-permute-start(bf16[4,512,512]{2,1,0:T(8,128)(2,1)} %get-tuple-element.218), channel_id=1, source_target_pairs={{0,4},{4,0},{1,5},{5,1},{2,6},{6,2},{3,7},{7,3},{8,12},{12,8},{9,1... | collective-permute-start | bytes 6291464 | tf_op jit(solution)/shard_map/cond/branch_1_fun/ppermute | solution.py:593
  411.5 21.0 %collective-permute-start.56 = (bf16[2,128,1024]{2,1,0:T(8,128)(2,1)S(1)}, bf16[2,128,1024]{2,1,0:T(8,128)(2,1)S(1)}, u32[]{:S(2)}, u32[]{:S(2)}) collective-permute-start(bf16[2,128,1024]{2,1,0:T(8,128)(2,1)S(1)} %pad_maximum_fusion.6), channel_id=1, source_target_pairs={{8,0},{24,8},{16,24},{0,16},{9,1},{25,9},{17,25},{1,17},{10,2},{26... | collective-permute-start | bytes 1572872 | tf_op jit(solution)/shard_map/cond/branch_1_fun/ppermute | solution.py:635
  418.3 21.8 %collective-permute-start.54 = (bf16[2,128,1024]{2,1,0:T(8,128)(2,1)S(1)}, bf16[2,128,1024]{2,1,0:T(8,128)(2,1)S(1)}, u32[]{:S(2)}, u32[]{:S(2)}) collective-permute-start(bf16[2,128,1024]{2,1,0:T(8,128)(2,1)S(1)} %pad_maximum_fusion.5), channel_id=1, source_target_pairs={{0,8},{8,24},{24,16},{16,0},{1,9},{9,25},{25,17},{17,1},{2,10},{10... | collective-permute-start | bytes 1572872 | tf_op jit(solution)/shard_map/cond/branch_1_fun/ppermute | solution.py:634
  443.9 231.1 %reduce-scatter.9.cloned.1.call-start = ((), (), s32[]{:S(2)}) async-start(), calls=%async_computation.10 | async-start | bytes 10485760
  449.6 32.5 %collective-permute-start.37 = (bf16[2,128,1024]{2,1,0:T(8,128)(2,1)S(1)}, bf16[2,128,1024]{2,1,0:T(8,128)(2,1)S(1)}, u32[]{:S(2)}, u32[]{:S(2)}) collective-permute-start(bf16[2,128,1024]{2,1,0:T(8,128)(2,1)S(1)} %copy.117), channel_id=1, source_target_pairs={{8,0},{24,8},{16,24},{0,16},{9,1},{25,9},{17,25},{1,17},{10,2},{26... | collective-permute-start | bytes 1572872 | tf_op jit(solution)/shard_map/cond/branch_1_fun/ppermute | solution.py:600
  450.1 33.3 %collective-permute-start.36 = (bf16[2,128,1024]{2,1,0:T(8,128)(2,1)S(1)}, bf16[2,128,1024]{2,1,0:T(8,128)(2,1)S(1)}, u32[]{:S(2)}, u32[]{:S(2)}) collective-permute-start(bf16[2,128,1024]{2,1,0:T(8,128)(2,1)S(1)} %copy.117), channel_id=1, source_target_pairs={{0,8},{8,24},{24,16},{16,0},{1,9},{9,25},{25,17},{17,1},{2,10},{10... | collective-permute-start | bytes 1572872 | tf_op jit(solution)/shard_map/cond/branch_1_fun/ppermute | solution.py:599
  484.7 15.3 %collective-permute-start.38 = (bf16[2,64,1024]{2,1,0:T(8,128)(2,1)S(1)}, bf16[2,64,1024]{2,1,0:T(8,128)(2,1)S(1)}, u32[]{:S(2)}, u32[]{:S(2)}) collective-permute-start(bf16[2,64,1024]{2,1,0:T(8,128)(2,1)S(1)} %slice_add_fusion.17), channel_id=1, source_target_pairs={{0,8},{8,24},{24,16},{16,0},{1,9},{9,25},{25,17},{17,1},{2,10},{10... | collective-permute-start | bytes 786440 | tf_op jit(solution)/shard_map/cond/branch_1_fun/ppermute | solution.py:607
  485.0 15.0 %collective-permute-start.39 = (bf16[2,64,1024]{2,1,0:T(8,128)(2,1)S(1)}, bf16[2,64,1024]{2,1,0:T(8,128)(2,1)S(1)}, u32[]{:S(2)}, u32[]{:S(2)}) collective-permute-start(bf16[2,64,1024]{2,1,0:T(8,128)(2,1)S(1)} %slice_add_fusion.16), channel_id=1, source_target_pairs={{8,0},{24,8},{16,24},{0,16},{9,1},{25,9},{17,25},{1,17},{10,2},{26... | collective-permute-start | bytes 786440 | tf_op jit(solution)/shard_map/cond/branch_1_fun/ppermute | solution.py:608
  506.7 17.2 %collective-permute-start.3 = (bf16[2,64,1024]{2,1,0:T(8,128)(2,1)}, bf16[2,64,1024]{2,1,0:T(8,128)(2,1)}, u32[]{:S(2)}, u32[]{:S(2)}) collective-permute-start(bf16[2,64,1024]{2,1,0:T(8,128)(2,1)} %get-tuple-element.238), channel_id=1, source_target_pairs={{0,8},{8,24},{24,16},{16,0},{1,9},{9,25},{25,17},{17,1},{2,10},{10... | collective-permute-start | bytes 786440 | tf_op jit(solution)/shard_map/cond/branch_1_fun/ppermute | solution.py:619
  507.2 16.7 %collective-permute-start.4 = (bf16[2,64,1024]{2,1,0:T(8,128)(2,1)}, bf16[2,64,1024]{2,1,0:T(8,128)(2,1)}, u32[]{:S(2)}, u32[]{:S(2)}) collective-permute-start(bf16[2,64,1024]{2,1,0:T(8,128)(2,1)} %get-tuple-element.239), channel_id=1, source_target_pairs={{8,0},{24,8},{16,24},{0,16},{9,1},{25,9},{17,25},{1,17},{10,2},{26... | collective-permute-start | bytes 786440 | tf_op jit(solution)/shard_map/cond/branch_1_fun/ppermute | solution.py:620
  537.0 58.0 %all-to-all-start.2 = ((bf16[4,256,512]{2,1,0:T(8,128)(2,1)}), bf16[4,256,512]{2,1,0:T(8,128)(2,1)}, u32[]{:S(2)}, u32[]{:S(2)}) async-start(bf16[4,256,512]{2,1,0:T(8,128)(2,1)} %bitcast.156), calls=%async_computation.2 | async-start | bytes 2097152 | tf_op jit(solution)/shard_map/cond/branch_1_fun/all_to_all | solution.py:698
  541.2 20.6 %collective-permute-start.60 = (bf16[512,384]{1,0:T(8,128)(2,1)}, bf16[512,384]{1,0:T(8,128)(2,1)S(1)}, u32[]{:S(2)}, u32[]{:S(2)}) collective-permute-start(bf16[512,384]{1,0:T(8,128)(2,1)} %get-tuple-element.241), channel_id=1, source_target_pairs={{0,1},{1,0},{2,3},{3,2},{4,5},{5,4},{6,7},{7,6},{8,9},{9,8},{10,11... | collective-permute-start | bytes 1179656 | tf_op jit(solution)/shard_map/cond/branch_1_fun/ppermute | solution.py:590
  542.2 21.2 %collective-permute-start.61 = (bf16[512,384]{1,0:T(8,128)(2,1)}, bf16[512,384]{1,0:T(8,128)(2,1)S(1)}, u32[]{:S(2)}, u32[]{:S(2)}) collective-permute-start(bf16[512,384]{1,0:T(8,128)(2,1)} %get-tuple-element.242), channel_id=1, source_target_pairs={{0,2},{1,3},{2,0},{3,1},{4,6},{5,7},{6,4},{7,5},{8,10},{9,11},{10,... | collective-permute-start | bytes 1179656 | tf_op jit(solution)/shard_map/cond/branch_1_fun/ppermute | solution.py:590
  543.1 33.7 %collective-permute-start.62 = (bf16[512,384]{1,0:T(8,128)(2,1)}, bf16[512,384]{1,0:T(8,128)(2,1)S(1)}, u32[]{:S(2)}, u32[]{:S(2)}) collective-permute-start(bf16[512,384]{1,0:T(8,128)(2,1)} %get-tuple-element.243), channel_id=1, source_target_pairs={{0,3},{1,2},{2,1},{3,0},{4,7},{5,6},{6,5},{7,4},{8,11},{9,10},{10,... | collective-permute-start | bytes 1179656 | tf_op jit(solution)/shard_map/cond/branch_1_fun/ppermute | solution.py:590
  546.3 31.8 %collective-permute-start.64 = (bf16[2,128,1024]{2,1,0:T(8,128)(2,1)S(1)}, bf16[2,128,1024]{2,1,0:T(8,128)(2,1)S(1)}, u32[]{:S(2)}, u32[]{:S(2)}) collective-permute-start(bf16[2,128,1024]{2,1,0:T(8,128)(2,1)S(1)} %pad_maximum_fusion.9), channel_id=1, source_target_pairs={{8,0},{24,8},{16,24},{0,16},{9,1},{25,9},{17,25},{1,17},{10,2},{26... | collective-permute-start | bytes 1572872 | tf_op jit(solution)/shard_map/cond/branch_1_fun/ppermute | solution.py:635
  549.2 38.8 %collective-permute-start.63 = (bf16[2,128,1024]{2,1,0:T(8,128)(2,1)S(1)}, bf16[2,128,1024]{2,1,0:T(8,128)(2,1)S(1)}, u32[]{:S(2)}, u32[]{:S(2)}) collective-permute-start(bf16[2,128,1024]{2,1,0:T(8,128)(2,1)S(1)} %pad_maximum_fusion.8), channel_id=1, source_target_pairs={{0,8},{8,24},{24,16},{16,0},{1,9},{9,25},{25,17},{17,1},{2,10},{10... | collective-permute-start | bytes 1572872 | tf_op jit(solution)/shard_map/cond/branch_1_fun/ppermute | solution.py:634
  602.8 16.0 %collective-permute-start.70 = (bf16[4,512,384]{2,1,0:T(8,128)(2,1)}, bf16[4,512,384]{2,1,0:T(8,128)(2,1)S(1)}, u32[]{:S(2)}, u32[]{:S(2)}) collective-permute-start(bf16[4,512,384]{2,1,0:T(8,128)(2,1)} %get-tuple-element.257.refs_2_), channel_id=1, source_target_pairs={{0,4},{4,0},{1,5},{5,1},{2,6},{6,2},{3,7},{7,3},{8,12},{12,8},{9,1... | collective-permute-start | bytes 4718600 | tf_op jit(solution)/shard_map/cond/branch_1_fun/ppermute | solution.py:593
  615.7 20.3 %collective-permute-start.65 = (bf16[2,64,1024]{2,1,0:T(8,128)(2,1)S(1)}, bf16[2,64,1024]{2,1,0:T(8,128)(2,1)S(1)}, u32[]{:S(2)}, u32[]{:S(2)}) collective-permute-start(bf16[2,64,1024]{2,1,0:T(8,128)(2,1)S(1)} %get-tuple-element.253), channel_id=1, source_target_pairs={{0,8},{8,24},{24,16},{16,0},{1,9},{9,25},{25,17},{17,1},{2,10},{10... | collective-permute-start | bytes 786440 | tf_op jit(solution)/shard_map/cond/branch_1_fun/ppermute | solution.py:619
  616.1 20.1 %collective-permute-start.68 = (bf16[2,128,1024]{2,1,0:T(8,128)(2,1)S(1)}, bf16[2,128,1024]{2,1,0:T(8,128)(2,1)S(1)}, u32[]{:S(2)}, u32[]{:S(2)}) collective-permute-start(bf16[2,128,1024]{2,1,0:T(8,128)(2,1)S(1)} %pad_maximum_fusion.12), channel_id=1, source_target_pairs={{8,0},{24,8},{16,24},{0,16},{9,1},{25,9},{17,25},{1,17},{10,2},{26... | collective-permute-start | bytes 1572872 | tf_op jit(solution)/shard_map/cond/branch_1_fun/ppermute | solution.py:635
  634.4 24.5 %collective-permute-start.73 = (bf16[2,512,512]{2,1,0:T(8,128)(2,1)}, bf16[2,512,512]{2,1,0:T(8,128)(2,1)}, u32[]{:S(2)}, u32[]{:S(2)}) collective-permute-start(bf16[2,512,512]{2,1,0:T(8,128)(2,1)} %pad_maximum_fusion.10), channel_id=1, source_target_pairs={{0,1},{1,0},{2,3},{3,2},{4,5},{5,4},{6,7},{7,6},{8,9},{9,8},{10,11... | collective-permute-start | bytes 3145736 | tf_op jit(solution)/shard_map/cond/branch_1_fun/ppermute | solution.py:590
  634.8 24.2 %collective-permute-start.74 = (bf16[2,512,512]{2,1,0:T(8,128)(2,1)}, bf16[2,512,512]{2,1,0:T(8,128)(2,1)}, u32[]{:S(2)}, u32[]{:S(2)}) collective-permute-start(bf16[2,512,512]{2,1,0:T(8,128)(2,1)} %stack.133), channel_id=1, source_target_pairs={{0,2},{1,3},{2,0},{3,1},{4,6},{5,7},{6,4},{7,5},{8,10},{9,11},{10,... | collective-permute-start | bytes 3145736 | tf_op jit(solution)/shard_map/cond/branch_1_fun/ppermute | solution.py:590
  675.6 51.8 %all-to-all-start = ((bf16[4,256,1024]{2,1,0:T(8,128)(2,1)}), bf16[4,256,1024]{2,1,0:T(8,128)(2,1)S(1)}, u32[]{:S(2)}, u32[]{:S(2)}) async-start(bf16[4,256,1024]{2,1,0:T(8,128)(2,1)} %bitcast.145), calls=%async_computation | async-start | bytes 4194304 | tf_op jit(solution)/shard_map/cond/branch_1_fun/all_to_all | solution.py:698
  680.4 15.1 %collective-permute-start.42 = (bf16[128,2048]{1,0:T(8,128)(2,1)}, bf16[128,2048]{1,0:T(8,128)(2,1)S(1)}, u32[]{:S(2)}, u32[]{:S(2)}) collective-permute-start(bf16[128,2048]{1,0:T(8,128)(2,1)} %convert_element_type.276), channel_id=1, source_target_pairs={{0,2},{1,3},{2,0},{3,1},{4,6},{5,7},{6,4},{7,5},{8,10},{9,11},{10,... | collective-permute-start | bytes 1572872 | tf_op jit(solution)/shard_map/cond/branch_1_fun/ppermute | solution.py:590
  680.9 15.1 %collective-permute-start.41 = (bf16[128,2048]{1,0:T(8,128)(2,1)}, bf16[128,2048]{1,0:T(8,128)(2,1)S(1)}, u32[]{:S(2)}, u32[]{:S(2)}) collective-permute-start(bf16[128,2048]{1,0:T(8,128)(2,1)} %convert_element_type.276), channel_id=1, source_target_pairs={{0,1},{1,0},{2,3},{3,2},{4,5},{5,4},{6,7},{7,6},{8,9},{9,8},{10,11... | collective-permute-start | bytes 1572872 | tf_op jit(solution)/shard_map/cond/branch_1_fun/ppermute | solution.py:590
  686.6 20.2 %collective-permute-start.47 = (bf16[128,2048]{1,0:T(8,128)(2,1)}, bf16[128,2048]{1,0:T(8,128)(2,1)}, u32[]{:S(2)}, u32[]{:S(2)}) collective-permute-start(bf16[128,2048]{1,0:T(8,128)(2,1)} %convert_element_type.279), channel_id=1, source_target_pairs={{0,2},{1,3},{2,0},{3,1},{4,6},{5,7},{6,4},{7,5},{8,10},{9,11},{10,... | collective-permute-start | bytes 1572872 | tf_op jit(solution)/shard_map/cond/branch_1_fun/ppermute | solution.py:590
  687.2 24.6 %collective-permute-start.46 = (bf16[128,2048]{1,0:T(8,128)(2,1)}, bf16[128,2048]{1,0:T(8,128)(2,1)}, u32[]{:S(2)}, u32[]{:S(2)}) collective-permute-start(bf16[128,2048]{1,0:T(8,128)(2,1)} %convert_element_type.279), channel_id=1, source_target_pairs={{0,1},{1,0},{2,3},{3,2},{4,5},{5,4},{6,7},{7,6},{8,9},{9,8},{10,11... | collective-permute-start | bytes 1572872 | tf_op jit(solution)/shard_map/cond/branch_1_fun/ppermute | solution.py:590
  688.7 29.8 %collective-permute-start.52 = (bf16[512,512]{1,0:T(8,128)(2,1)}, bf16[512,512]{1,0:T(8,128)(2,1)}, u32[]{:S(2)}, u32[]{:S(2)}) collective-permute-start(bf16[512,512]{1,0:T(8,128)(2,1)} %get-tuple-element.272), channel_id=1, source_target_pairs={{0,1},{1,0},{2,3},{3,2},{4,5},{5,4},{6,7},{7,6},{8,9},{9,8},{10,11... | collective-permute-start | bytes 1572872 | tf_op jit(solution)/shard_map/cond/branch_1_fun/ppermute | solution.py:590
  695.5 25.9 %collective-permute-start.51 = (bf16[512,512]{1,0:T(8,128)(2,1)}, bf16[512,512]{1,0:T(8,128)(2,1)}, u32[]{:S(2)}, u32[]{:S(2)}) collective-permute-start(bf16[512,512]{1,0:T(8,128)(2,1)} %get-tuple-element.270), channel_id=1, source_target_pairs={{0,2},{1,3},{2,0},{3,1},{4,6},{5,7},{6,4},{7,5},{8,10},{9,11},{10,... | collective-permute-start | bytes 1572872 | tf_op jit(solution)/shard_map/cond/branch_1_fun/ppermute | solution.py:590
  696.0 28.2 %collective-permute-start.43 = (bf16[64,2048]{1,0:T(8,128)(2,1)S(1)}, bf16[64,2048]{1,0:T(8,128)(2,1)}, u32[]{:S(2)}, u32[]{:S(2)}) collective-permute-start(bf16[64,2048]{1,0:T(8,128)(2,1)S(1)} %slice.392), channel_id=1, source_target_pairs={{0,1},{1,0},{2,3},{3,2},{4,5},{5,4},{6,7},{7,6},{8,9},{9,8},{10,11... | collective-permute-start | bytes 786440 | tf_op jit(solution)/shard_map/cond/branch_1_fun/ppermute | solution.py:590
  706.8 17.3 %collective-permute-start.44 = (bf16[64,2048]{1,0:T(8,128)(2,1)}, bf16[64,2048]{1,0:T(8,128)(2,1)}, u32[]{:S(2)}, u32[]{:S(2)}) collective-permute-start(bf16[64,2048]{1,0:T(8,128)(2,1)} %slice.393), channel_id=1, source_target_pairs={{0,2},{1,3},{2,0},{3,1},{4,6},{5,7},{6,4},{7,5},{8,10},{9,11},{10,... | collective-permute-start | bytes 786440 | tf_op jit(solution)/shard_map/cond/branch_1_fun/ppermute | solution.py:590
  711.8 22.4 %collective-permute-start.48 = (bf16[64,2048]{1,0:T(8,128)(2,1)}, bf16[64,2048]{1,0:T(8,128)(2,1)}, u32[]{:S(2)}, u32[]{:S(2)}) collective-permute-start(bf16[64,2048]{1,0:T(8,128)(2,1)} %slice.394), channel_id=1, source_target_pairs={{0,1},{1,0},{2,3},{3,2},{4,5},{5,4},{6,7},{7,6},{8,9},{9,8},{10,11... | collective-permute-start | bytes 786440 | tf_op jit(solution)/shard_map/cond/branch_1_fun/ppermute | solution.py:590
  718.5 15.7 %collective-permute-start.49 = (bf16[64,2048]{1,0:T(8,128)(2,1)}, bf16[64,2048]{1,0:T(8,128)(2,1)}, u32[]{:S(2)}, u32[]{:S(2)}) collective-permute-start(bf16[64,2048]{1,0:T(8,128)(2,1)} %slice.395), channel_id=1, source_target_pairs={{0,2},{1,3},{2,0},{3,1},{4,6},{5,7},{6,4},{7,5},{8,10},{9,11},{10,... | collective-permute-start | bytes 786440 | tf_op jit(solution)/shard_map/cond/branch_1_fun/ppermute | solution.py:590
  727.4 29.6 %all-to-all-start.1 = ((bf16[4,256,512]{2,1,0:T(8,128)(2,1)}), bf16[4,256,512]{2,1,0:T(8,128)(2,1)}, u32[]{:S(2)}, u32[]{:S(2)}) async-start(bf16[4,256,512]{2,1,0:T(8,128)(2,1)} %bitcast.157), calls=%async_computation.1 | async-start | bytes 2097152 | tf_op jit(solution)/shard_map/cond/branch_1_fun/all_to_all | solution.py:698
  (80 other events, 906.4 us)
Sparse Core Ops, SparseCore 0:
  444.0 50.9 reduce-scatter.6
  501.6 106.2 reduce-scatter.8

commit v4 on v3

--- a/solution.py
+++ b/solution.py
@@ -870,7 +870,7 @@
             out = gate_up(xn2, *gate_up_w)
             far = far_tp(down_one, near, *chunks[1:3], out[0])
             chunks = ring_last(chunks, out[0])
-            low = stack_tp(down_one, near, far)
+            low = stack_tp(down_one, near, far, *chunks[-2:])
             return join_rows(chunks), (low, swap(low)), out, xn2_peer
 
         gy, down_w, (hid, to_gate, to_up), xn2_peer = stage(third)
@@ -906,8 +906,9 @@
         def fifth():
             chunks = ring_first(dres_low)
             started = (tick(dres_low),)
+            g_gu = weight_grad(here, xn2[0], xn2_peer, dgu, dgu_peer, "g_gate_up", started)
+            started = tuple(tick(x) for x in chunks[1:3])
             ffn = mm_back(hid, *down_w, 0, own, "ffn_out", started)
-            g_gu = weight_grad(here, xn2[0], xn2_peer, dgu, dgu_peer, "g_gate_up", started)
             return join_rows(ring_last(chunks), g_gu), ffn, g_gu
 
         dres_all, ffn, g_gu = stage(fifth)
@@ -944,8 +945,6 @@
         )
 
         in_own = join(in_own).astype(BF)
-        layer_own = join(layer_own).astype(BF)
-
         gains = join(jnp.stack([gain1_part, gain2_part], axis=1)).reshape(2, shards, 1, k_rows)
         gains = jnp.broadcast_to(gains, (2, shards, tp_size, k_rows))
         gains = jnp.swapaxes(gains.reshape(2, shards * tp_size, k_rows), 0, 1)
@@ -968,7 +967,8 @@
             near = near_tp(in_own)
             heads = scatter_tp_last(g_heads) if plain else g_heads
             in_all = spread_over(in_own, near)
-            layer_all = spread_over(layer_own, near_tp(layer_own))
+            layer_low = join(layer_own).astype(BF)
+            layer_all = spread_over(layer_low, near_tp(layer_low))
             placed = place_columns(g_gu)
             if plain:
                 heads = place_columns(heads)

time: 780 us -> 744 us (0.954)
  local copies, waits for them, and re-layouts: 84.4 us -> 68.6 us
  other arithmetic: 73.7 us -> 63.2 us
    cond x54, local copies, waits for them, and re-layouts: 24.8 us -> 15.6 us
    ppermute x4, waiting for transfers between devices: 2.71 us -> 11.3 us  [scatter_last(): two = lax.ppermute(bwd, 'z', backward)]
    ppermute x4, waiting for transfers between devices: 42.4 us -> 34.2 us  [ring_last(): one = lax.ppermute(after(ahead[:, :mid], back, *deps), 'z', forward)]
    ppermute x4, waiting for transfers between devices: 12.7 us -> 20.7 us  [scatter_first(): lax.ppermute(parts[-1], 'z', backward)]
    add x18 -> x19, other arithmetic: 20.2 us -> 18.3 us  [after(): x = x + (corner.astype(F32) * 0.0).astype(x.dtype)]
  transfers between devices with their start and end apart: 98 -> 100, of which waited for: 44 -> 47; matrix products, arithmetic and copies ran while one was open for 18% -> 16% of each run, Pallas kernels for 16% -> 17%
where the time goes in v4:
time: 744 us; the launch traced here: 731 us
  waiting for transfers between devices  296 us (40%)
  Pallas kernels  159 us (21%)
  starting transfers between devices  112 us (15%)
  local copies, waits for them, and re-layouts  68.6 us (9%)
  other arithmetic  63.2 us (8%)
  between operations  17.7 us (2%)
  loops' own time  15 us (2%)
    pallas_call x13, Pallas kernels, call(): return lambda *args: made(*args, *deps)  105 us
    ppermute x36, waiting for transfers between devices, hop(): return lax.ppermute(x, 'tp', [(t, t ^ bit) for t in range(tp_size)])  96.8 us
    ppermute x4, waiting for transfers between devices, scatter_last(): one = lax.ppermute(fwd, 'z', forward)  41.4 us
    ppermute x36, starting transfers between devices, hop(): return lax.ppermute(x, 'tp', [(t, t ^ bit) for t in range(tp_size)])  35.1 us
    ppermute x4, waiting for transfers between devices, ring_last(): one = lax.ppermute(after(ahead[:, :mid], back, *deps), 'z', forward)  34.2 us
    pallas_call x4, Pallas kernels, placed_call(): return lambda *args: made(*args, *deps)  33.6 us
    ppermute x4, waiting for transfers between devices, ring_first(): back = lax.ppermute(back, 'z', backward)  32.9 us
    all_to_all x6, starting transfers between devices, to_z(): return lax.all_to_all(x, 'z', split_axis=0, concat_axis=0, tiled=True)  28.6 us
  transfers between devices with their start and end apart: 100, of which 47 were waited for; matrix products, arithmetic and copies ran while one was open for 16% of the time, Pallas kernels for 17%

profile of v4, /device:TPU:0, one launch (start us, length us, event | category | flops | bytes accessed | tf_op | source)
XLA Modules:
  0.0 731.1 jit_solution(8682358106825564827)
XLA Ops:
  15.2 6.3 all-to-all-start.3
  32.0 15.5 %all-to-all-done.3 = bf16[4,256,512]{2,1,0:T(8,128)(2,1)S(1)} async-done(((bf16[4,256,512]{2,1,0:T(8,128)(2,1)}), bf16[4,256,512]{2,1,0:T(8,128)(2,1)S(1)}, u32[]{:S(2)}, u32[]{:S(2)}) %all-to-all-start.3) | async-done | bytes 1048608 | tf_op jit(solution)/shard_map/all_to_all | solution.py:698
  49.0 59.8 %conditional.10 = (bf16[2,512,1024]{2,1,0:T(8,128)(2,1)}, bf16[4,1024,512]{2,1,0:T(8,128)(2,1)}, bf16[4,1024,512]{2,1,0:T(8,128)(2,1)}, f32[2048,128]{1,0:T(8,12...) conditional(s32[]{:T(128)} %bitcast.73, () %tuple.97, ...), branch_computations={%region_4.5_spmd, %region_5.6_spmd} | conditional | flops 15336558 | bytes 83945872 | solution.py:746
  56.5 3.8 fusion.1
  61.5 14.2 %collective-permute-done.6 = bf16[2,128,1024]{2,1,0:T(8,128)(2,1)S(1)} collective-permute-done((bf16[2,128,1024]{2,1,0:T(8,128)(2,1)S(1)}, bf16[2,128,1024]{2,1,0:T(8,128)(2,1)S(1)}, u32[]{:S(2)}, u32[]{:S(2)}) %collective-permute-start.6) | collective-permute-done | bytes 524320 | tf_op jit(solution)/shard_map/cond/branch_1_fun/ppermute | solution.py:600
  82.6 9.9 %collective-permute-done.7 = bf16[2,64,1024]{2,1,0:T(8,128)(2,1)S(1)} collective-permute-done((bf16[2,64,1024]{2,1,0:T(8,128)(2,1)S(1)}, bf16[2,64,1024]{2,1,0:T(8,128)(2,1)S(1)}, u32[]{:S(2)}, u32[]{:S(2)}) %collective-permute-start.7) | collective-permute-done | bytes 262176 | tf_op jit(solution)/shard_map/cond/branch_1_fun/ppermute | solution.py:607
  108.7 4.5 all-to-all-start.4
  114.3 7.4 %qkv.1 = (bf16[512,384]{1,0:T(8,128)(2,1)S(1)}, bf16[512,384]{1,0:T(8,128)(2,1)S(1)}, bf16[512,384]{1,0:T(8,128)(2,1)S(1)}, bf16[512,384]{1,0:T(8,128)(2,1)S(1)}) custom-call(bf16[2,512,1024]{2,1,0:T(8,128)(2,1)} %get-tuple-element.371.refs_0_, bf16[4,1024,512]{2,1,0:T(8,128)(2,1)} %get-tuple-element.372.refs_1_, ...), custom_call_target="tpu_custom_call" | custom-call | flops 3221225472 | bytes 9961472 | tf_op jit(solution)/shard_map/qkv/pallas_call | solution.py:57
  125.4 8.3 %collective-permute-done.85.refs_1_ = bf16[512,384]{1,0:T(8,128)(2,1)S(1)} collective-permute-done((bf16[512,384]{1,0:T(8,128)(2,1)S(1)}, bf16[512,384]{1,0:T(8,128)(2,1)S(1)}, u32[]{:S(2)}, u32[]{:S(2)}) %collective-permute-start.85) | collective-permute-done | bytes 393248 | tf_op jit(solution)/shard_map/ppermute | solution.py:590
  133.7 8.8 %collective-permute-done.86.refs_2_ = bf16[512,384]{1,0:T(8,128)(2,1)S(1)} collective-permute-done((bf16[512,384]{1,0:T(8,128)(2,1)S(1)}, bf16[512,384]{1,0:T(8,128)(2,1)S(1)}, u32[]{:S(2)}, u32[]{:S(2)}) %collective-permute-start.86) | collective-permute-done | bytes 393248 | tf_op jit(solution)/shard_map/ppermute | solution.py:590
  142.5 7.9 %attend.1 = (bf16[512,128]{1,0:T(8,128)(2,1)S(1)}, bf16[512,128]{1,0:T(8,128)(2,1)S(1)}, bf16[512,128]{1,0:T(8,128)(2,1)S(1)}, bf16[512,128]{1,0:T(8,128)(2,1)S(...) custom-call(s32[16]{0:T(128)S(1)} %and_select_fusion.2.tab_ref.refs_0_, ...), custom_call_target="tpu_custom_call" | custom-call | flops 2147483648 | bytes 12582912 | tf_op jit(solution)/shard_map/attend/pallas_call | solution.py:181
  159.2 5.5 attn_out.1
  164.7 47.2 %conditional.11 = (f32[2,128,1024]{2,1,0:T(8,128)S(1)}, bf16[1024,1024]{1,0:T(8,128)(2,1)}, bf16[1024,1024]{1,0:T(8,128)(2,1)}, f32[1,128,1]{1,2,0:T(1,128)S(1)}) conditional(s32[]{:T(128)} %bitcast.73, () %tuple.96, (bf16[2,128,1024]{2,1,0:T(8,128)(2,1)}, bf16[2,64,1024]{2,1,0:T(8,128)(2,1)}, f32[2,128,1024]{2,1,0:T(8,128)}, ...), branch_computations={%region_6.7_spmd, %region_7.9_spmd} | conditional | flops 4194176 | bytes 42468196 | solution.py:746
  169.3 8.0 %collective-permute-done.79 = bf16[2,64,1024]{2,1,0:T(8,128)(2,1)S(1)} collective-permute-done((bf16[2,64,1024]{2,1,0:T(8,128)(2,1)}, bf16[2,64,1024]{2,1,0:T(8,128)(2,1)S(1)}, u32[]{:S(2)}, u32[]{:S(2)}) %collective-permute-start.79) | collective-permute-done | bytes 262176 | tf_op jit(solution)/shard_map/cond/branch_1_fun/ppermute | solution.py:620
  184.4 9.1 %collective-permute-done.80 = bf16[2,128,1024]{2,1,0:T(8,128)(2,1)S(1)} collective-permute-done((bf16[2,128,1024]{2,1,0:T(8,128)(2,1)S(1)}, bf16[2,128,1024]{2,1,0:T(8,128)(2,1)S(1)}, u32[]{:S(2)}, u32[]{:S(2)}) %collective-permute-start.80) | collective-permute-done | bytes 524320 | tf_op jit(solution)/shard_map/cond/branch_1_fun/ppermute | solution.py:635
  193.5 9.0 %collective-permute-done.78 = bf16[2,128,1024]{2,1,0:T(8,128)(2,1)S(1)} collective-permute-done((bf16[2,128,1024]{2,1,0:T(8,128)(2,1)S(1)}, bf16[2,128,1024]{2,1,0:T(8,128)(2,1)S(1)}, u32[]{:S(2)}, u32[]{:S(2)}) %collective-permute-start.78) | collective-permute-done | bytes 524320 | tf_op jit(solution)/shard_map/cond/branch_1_fun/ppermute | solution.py:634
  202.9 7.6 %collective-permute-done.82 = bf16[1024,1024]{1,0:T(8,128)(2,1)} collective-permute-done((bf16[1024,1024]{1,0:T(8,128)(2,1)}, bf16[1024,1024]{1,0:T(8,128)(2,1)}, u32[]{:S(2)}, u32[]{:S(2)}) %collective-permute-start.82) | collective-permute-done | bytes 2097184 | tf_op jit(solution)/shard_map/cond/branch_1_fun/ppermute | solution.py:590
  211.9 4.9 all-to-all-start.5
  220.7 71.4 %conditional.12 = (bf16[2,512,1024]{2,1,0:T(8,128)(2,1)}, bf16[4,1024,1024]{2,1,0:T(8,128)(2,1)}, bf16[4,1024,1024]{2,1,0:T(8,128)(2,1)}) conditional(s32[]{:T(128)} %bitcast.73, () %tuple.102, (bf16[2,128,1024]{2,1,0:T(8,128)(2,1)S(1)}, bf16[4,256,1024]{2,1,0:T(8,128)(2,1)}, bf16[1024,1024]{1,0:T(8,128)(2,1)}, bf16[1024,1024]{1,0:T(8,128)(2,1)}) %tuple.103), branch_computations={%region_9.10_spmd, %region_10.11_spmd} | conditional | flops 26476548 | bytes 78717424 | solution.py:746
  230.2 13.5 %collective-permute-done.17 = bf16[2,128,1024]{2,1,0:T(8,128)(2,1)S(1)} collective-permute-done((bf16[2,128,1024]{2,1,0:T(8,128)(2,1)S(1)}, bf16[2,128,1024]{2,1,0:T(8,128)(2,1)S(1)}, u32[]{:S(2)}, u32[]{:S(2)}) %collective-permute-start.17) | collective-permute-done | bytes 524320 | tf_op jit(solution)/shard_map/cond/branch_1_fun/ppermute | solution.py:600
  243.7 18.7 %collective-permute-done.16 = bf16[2,128,1024]{2,1,0:T(8,128)(2,1)S(1)} collective-permute-done((bf16[2,128,1024]{2,1,0:T(8,128)(2,1)S(1)}, bf16[2,128,1024]{2,1,0:T(8,128)(2,1)S(1)}, u32[]{:S(2)}, u32[]{:S(2)}) %collective-permute-start.16) | collective-permute-done | bytes 524320 | tf_op jit(solution)/shard_map/cond/branch_1_fun/ppermute | solution.py:599
  265.1 6.8 fusion.8
  280.5 10.1 %collective-permute-done.18 = bf16[2,64,1024]{2,1,0:T(8,128)(2,1)S(1)} collective-permute-done((bf16[2,64,1024]{2,1,0:T(8,128)(2,1)S(1)}, bf16[2,64,1024]{2,1,0:T(8,128)(2,1)S(1)}, u32[]{:S(2)}, u32[]{:S(2)}) %collective-permute-start.18) | collective-permute-done | bytes 262176 | tf_op jit(solution)/shard_map/cond/branch_1_fun/ppermute | solution.py:607
  292.1 58.5 %conditional.13 = (bf16[2,512,1024]{2,1,0:T(8,128)(2,1)}, bf16[4,1024,512]{2,1,0:T(8,128)(2,1)}, bf16[4,1024,512]{2,1,0:T(8,128)(2,1)}, bf16[4,512,512]{2,1,0:T(...) conditional(s32[]{:T(128)} %bitcast.73, () %tuple.101, ...), branch_computations={%region_11.12_spmd, %region_12.13_spmd} | conditional | flops 14681069 | bytes 76547640 | solution.py:746
  296.0 14.6 %gate_up.1 = (bf16[4,512,512]{2,1,0:T(8,128)(2,1)S(1)}, bf16[4,512,512]{2,1,0:T(8,128)(2,1)S(1)}, bf16[4,512,512]{2,1,0:T(8,128)(2,1)S(1)}) custom-call(bf16[2,512,1024]{2,1,0:T(8,128)(2,1)} %get-tuple-element.200.refs_0_, bf16[4,1024,1024]{2,1,0:T(8,128)(2,1)} %get-tuple-element.201.refs_1_.refs_3_, ...), custom_call_target="tpu_custom_call" | custom-call | flops 1000 | bytes 1000 | tf_op jit(solution)/shard_map/cond/branch_1_fun/gate_up/pallas_call | solution.py:57
  312.0 5.3 collective-permute-done.27
  325.6 9.9 %collective-permute-done.28 = bf16[2,64,1024]{2,1,0:T(8,128)(2,1)S(1)} collective-permute-done((bf16[2,64,1024]{2,1,0:T(8,128)(2,1)S(1)}, bf16[2,64,1024]{2,1,0:T(8,128)(2,1)S(1)}, u32[]{:S(2)}, u32[]{:S(2)}) %collective-permute-start.28) | collective-permute-done | bytes 262176 | tf_op jit(solution)/shard_map/cond/branch_1_fun/ppermute | solution.py:607
  338.1 3.4 fusion.9
  350.5 32.8 %feed_back.1 = (bf16[4,2,512,512]{3,2,1,0:T(8,128)(2,1)}, f32[2,128,1024]{2,1,0:T(8,128)S(1)}, bf16[2,128,1024]{2,1,0:T(8,128)(2,1)S(1)}, bf16[2,128,1024]{2,1,0...) custom-call(bf16[2,512,1024]{2,1,0:T(8,128)(2,1)} %get-tuple-element.398.refs_0_, ...), custom_call_target="tpu_custom_call" | custom-call | flops 12884901888 | bytes 37748736 | tf_op jit(solution)/shard_map/feed_back/pallas_call | solution.py:57
  383.4 38.7 %conditional.14 = (f32[2,128,1024]{2,1,0:T(8,128)}, bf16[4,1024,512]{2,1,0:T(8,128)(2,1)}, bf16[4,2,512,512]{3,2,1,0:T(8,128)(2,1)}) conditional(s32[]{:T(128)} %bitcast.73, () %tuple.100, (bf16[2,128,1024]{2,1,0:T(8,128)(2,1)S(1)}, bf16[2,64,1024]{2,1,0:T(8,128)(2,1)S(1)}, f32[2,128,1024]{2,1,0:T(8,128)S(1)}, ...), branch_computations={%region_13.14_spmd, %region_14.15_spmd} | conditional | flops 4298637312 | bytes 58196292 | solution.py:746
  387.8 4.6 collective-permute-done.57
  394.2 4.7 collective-permute-done.55
  399.0 7.7 %g_down.1 = bf16[4,1024,512]{2,1,0:T(8,128)(2,1)} custom-call(s32[1]{0:T(128)} %get-tuple-element.212.refs_0_, bf16[512,1024]{1,0:T(8,128)(2,1)S(1)} %get-tuple-element.483.refs_1_, bf16[512,1024]{1,0:T(8,128)(2,1)S(1)} %collective-permute-done.59.refs_2_, bf16[4,1,512,512]{3,2,1,0:T(8,128)(2,1)S(1)} %bitcast.150, bf16[4,1,512,512]{3,2,1,0:T(8,128)(2,1)S(1)} %bitcast.135), custom_call_target="tpu_custom_call" | custom-call | flops 4294967296 | bytes 10485760 | tf_op jit(solution)/shard_map/cond/branch_1_fun/g_down/pallas_call | solution.py:466
  410.1 10.8 %collective-permute-done.56 = bf16[2,128,1024]{2,1,0:T(8,128)(2,1)S(1)} collective-permute-done((bf16[2,128,1024]{2,1,0:T(8,128)(2,1)S(1)}, bf16[2,128,1024]{2,1,0:T(8,128)(2,1)S(1)}, u32[]{:S(2)}, u32[]{:S(2)}) %collective-permute-start.56) | collective-permute-done | bytes 524320 | tf_op jit(solution)/shard_map/cond/branch_1_fun/ppermute | solution.py:634
  426.6 43.3 %conditional.15 = (bf16[2,512,1024]{2,1,0:T(8,128)(2,1)}, f32[2,128,1024]{2,1,0:T(8,128)}, bf16[2,128,1024]{2,1,0:T(8,128)(2,1)}, bf16[2,128,1024]{2,1,0:T(8,128...) conditional(s32[]{:T(128)} %bitcast.73, () %tuple.109, ...), branch_computations={%region_16.17_spmd, %region_17.18_spmd} | conditional | flops 12886212608 | bytes 49357176 | solution.py:746
  430.0 17.7 %g_gate_up.1 = bf16[4,1024,1024]{2,1,0:T(8,128)(2,1)} custom-call(s32[1]{0:T(128)} %get-tuple-element.217.refs_0_, bf16[512,1024]{1,0:T(8,128)(2,1)S(1)} %slice_bitcast_fusion.3.refs_1_, bf16[512,1024]{1,0:T(8,128)(2,1)} %get-tuple-element.219.refs_2_, bf16[4,2,512,512]{3,2,1,0:T(8,128)(2,1)S(1)} %get-tuple-element.220.refs_3_, ...), custom_call_target="tpu_custom_call" | custom-call | flops 8589934592 | bytes 18874368 | tf_op jit(solution)/shard_map/cond/branch_1_fun/g_gate_up/pallas_call | solution.py:466
  456.3 7.8 %ffn_out.1 = (f32[2,128,1024]{2,1,0:T(8,128)}, bf16[2,128,1024]{2,1,0:T(8,128)(2,1)}, bf16[2,128,1024]{2,1,0:T(8,128)(2,1)S(1)}, bf16[2,64,1024]{2,1,0:T(8,128)(2,1)}, bf16[2,64,1024]{2,1,0:T(8,128)(2,1)}) custom-call(bf16[4,512,512]{2,1,0:T(8,128)(2,1)S(1)} %get-tuple-element.222.refs_0_, bf16[4,1024,512]{2,1,0:T(8,128)(2,1)} %get-tuple-element.223.refs_1_, ...), custom_call_target="tpu_custom_call" | custom-call | flops 4294967296 | bytes 12582912 | tf_op jit(solution)/shard_map/cond/branch_1_fun/ffn_out/pallas_call | solution.py:57
  464.1 4.3 collective-permute-done.38
  470.6 5.1 dmix.1
  475.7 14.9 %conditional.16 = (bf16[512,128]{1,0:T(8,128)(2,1)S(1)}, bf16[512,128]{1,0:T(8,128)(2,1)}, bf16[512,128]{1,0:T(8,128)(2,1)}, bf16[512,128]{1,0:T(8,128)(2,1)}, b...) conditional(s32[]{:T(128)} %bitcast.73, () %tuple.108, (bf16[512,128]{1,0:T(8,128)(2,1)S(1)}, ...), branch_computations={%region_18.19_spmd, %region_19.20_spmd} | conditional | bytes 3670264 | solution.py:746
  490.6 13.0 %attend_back.1 = (bf16[512,384]{1,0:T(8,128)(2,1)}, bf16[512,384]{1,0:T(8,128)(2,1)}, bf16[512,384]{1,0:T(8,128)(2,1)}, bf16[512,384]{1,0:T(8,128)(2,1)}) custom-call(s32[16]{0:T(128)S(1)} %and_select_fusion.2.tab_ref.refs_0_, bf16[512,128]{1,0:T(8,128)(2,1)S(1)} %get-tuple-element.420.refs_1_, bf16[512,128]{1,0:T(8,128)(2,1)} %get-tuple-element.421.refs_2_, ...), custom_call_target="tpu_custom_call" | custom-call | flops 5368709120 | bytes 12582912 | tf_op jit(solution)/shard_map/attend_back/pallas_call | solution.py:212
  503.6 54.2 %conditional.17 = (bf16[4,512,384]{2,1,0:T(8,128)(2,1)}, bf16[2,128,1024]{2,1,0:T(8,128)(2,1)S(1)}, bf16[4,256,512]{2,1,0:T(8,128)(2,1)}) conditional(s32[]{:T(128)} %bitcast.73, () %tuple.107, (bf16[512,384]{1,0:T(8,128)(2,1)}, bf16[512,384]{1,0:T(8,128)(2,1)}, bf16[512,384]{1,0:T(8,128)(2,1)}, bf16[512,384]{1,0:T(8,128)(2,1)}, ...), branch_computations={%region_21.22_spmd, %region_22.23_spmd} | conditional | flops 6291456 | bytes 25166108 | solution.py:746
  503.6 4.2 all-to-all-start.2
  515.8 12.7 %collective-permute-done.62 = bf16[512,384]{1,0:T(8,128)(2,1)S(1)} collective-permute-done((bf16[512,384]{1,0:T(8,128)(2,1)}, bf16[512,384]{1,0:T(8,128)(2,1)S(1)}, u32[]{:S(2)}, u32[]{:S(2)}) %collective-permute-start.62) | collective-permute-done | bytes 393248 | tf_op jit(solution)/shard_map/cond/branch_1_fun/ppermute | solution.py:590
  529.8 15.1 %collective-permute-done.64 = bf16[512,384]{1,0:T(8,128)(2,1)S(1)} collective-permute-done((bf16[512,384]{1,0:T(8,128)(2,1)}, bf16[512,384]{1,0:T(8,128)(2,1)S(1)}, u32[]{:S(2)}, u32[]{:S(2)}) %collective-permute-start.64) | collective-permute-done | bytes 393248 | tf_op jit(solution)/shard_map/cond/branch_1_fun/ppermute | solution.py:590
  546.3 9.9 %collective-permute-done.65 = bf16[2,128,1024]{2,1,0:T(8,128)(2,1)S(1)} collective-permute-done((bf16[2,128,1024]{2,1,0:T(8,128)(2,1)S(1)}, bf16[2,128,1024]{2,1,0:T(8,128)(2,1)S(1)}, u32[]{:S(2)}, u32[]{:S(2)}) %collective-permute-start.65) | collective-permute-done | bytes 524320 | tf_op jit(solution)/shard_map/cond/branch_1_fun/ppermute | solution.py:634
  557.8 7.7 %dxn1.1 = (f32[2,128,1024]{2,1,0:T(8,128)S(1)}, bf16[2,128,1024]{2,1,0:T(8,128)(2,1)S(1)}, bf16[2,128,1024]{2,1,0:T(8,128)(2,1)S(1)}, bf16[2,64,1024]{2,1,0:T(8,128)(2,1)S(1)}, bf16[2,64,1024]{2,1,0:T(8,128)(2,1)S(1)}) custom-call(bf16[4,512,384]{2,1,0:T(8,128)(2,1)} %get-tuple-element.437.refs_0_, bf16[4,1024,512]{2,1,0:T(8,128)(2,1)} %get-tuple-element.372.refs_1_, ...), custom_call_target="tpu_custom_call" | custom-call | flops 3221225472 | bytes 9961472 | tf_op jit(solution)/shard_map/dxn1/pallas_call | solution.py:57
  565.6 54.8 %conditional.18 = (f32[2,128,1024]{2,1,0:T(8,128)S(1)}, bf16[512,512]{1,0:T(8,128)(2,1)}, bf16[512,512]{1,0:T(8,128)(2,1)}, bf16[512,512]{1,0:T(8,128)(2,1)}, bf16[512,512]{1,0:T(8,128)(2,1)S(1)}) conditional(s32[]{:T(128)} %bitcast.73, () %tuple.106, (bf16[2,128,1024]{2,1,0:T(8,128)(2,1)S(1)}, bf16[2,64,1024]{2,1,0:T(8,128)(2,1)S(1)}, ...), branch_computations={%region_23.24_spmd, %region_24.25_spmd} | conditional | flops 4299948032 | bytes 95945200 | solution.py:746
  570.4 8.1 %collective-permute-done.69 = bf16[2,64,1024]{2,1,0:T(8,128)(2,1)S(1)} collective-permute-done((bf16[2,64,1024]{2,1,0:T(8,128)(2,1)S(1)}, bf16[2,64,1024]{2,1,0:T(8,128)(2,1)S(1)}, u32[]{:S(2)}, u32[]{:S(2)}) %collective-permute-start.69) | collective-permute-done | bytes 262176 | tf_op jit(solution)/shard_map/cond/branch_1_fun/ppermute | solution.py:620
  582.8 9.7 %g_heads.1 = bf16[4,1024,512]{2,1,0:T(8,128)(2,1)} custom-call(bf16[512,1024]{1,0:T(8,128)(2,1)S(1)} %get-tuple-element.505.refs_0_, bf16[512,1024]{1,0:T(8,128)(2,1)S(1)} %collective-permute-done.71.refs_1_, bf16[4,512,384]{2,1,0:T(8,128)(2,1)} %get-tuple-element.253.refs_2_, bf16[4,512,384]{2,1,0:T(8,128)(2,1)} %copy-done.45, ...), custom_call_target="tpu_custom_call" | custom-call | flops 4294967296 | bytes 12582912 | tf_op jit(solution)/shard_map/cond/branch_1_fun/g_heads/pallas_call | solution.py:57
  598.2 11.6 %collective-permute-done.68 = bf16[2,128,1024]{2,1,0:T(8,128)(2,1)S(1)} collective-permute-done((bf16[2,128,1024]{2,1,0:T(8,128)(2,1)S(1)}, bf16[2,128,1024]{2,1,0:T(8,128)(2,1)S(1)}, u32[]{:S(2)}, u32[]{:S(2)}) %collective-permute-start.68) | collective-permute-done | bytes 524320 | tf_op jit(solution)/shard_map/cond/branch_1_fun/ppermute | solution.py:634
  610.1 8.9 %collective-permute-done.75 = bf16[2,512,512]{2,1,0:T(8,128)(2,1)S(1)} collective-permute-done((bf16[2,512,512]{2,1,0:T(8,128)(2,1)S(1)}, bf16[2,512,512]{2,1,0:T(8,128)(2,1)S(1)}, u32[]{:S(2)}, u32[]{:S(2)}) %collective-permute-start.75) | collective-permute-done | bytes 1048608 | tf_op jit(solution)/shard_map/cond/branch_1_fun/ppermute | solution.py:590
  621.4 3.5 all-to-all-start.6
  627.9 4.6 all-to-all-done.6
  634.1 86.2 %conditional.19 = (f32[512,2048]{1,0:T(8,128)}, bf16[512,2048]{1,0:T(8,128)(2,1)}, f32[256,2048]{1,0:T(8,128)}, f32[256,2048]{1,0:T(8,128)}, f32[2048,256]{1,0:T(8,128)}, /*index=5*/bf16[4,256,512]{2,1,0:T(8,128)(2,1)}) conditional(s32[]{:T(128)} %bitcast.73, () %tuple.95, (s32[4]{0:T(128)S(1)}, s32[]{:T(128)}, s32[]{:T(128)}, ...), branch_computations={%region_27.28_spmd, %region_28.29_spmd} | conditional | flops 9177157 | bytes 99617792 | solution.py:746
  634.3 3.6 all-to-all-start
  651.6 8.4 %collective-permute-done.49 = bf16[128,2048]{1,0:T(8,128)(2,1)S(1)} collective-permute-done((bf16[128,2048]{1,0:T(8,128)(2,1)}, bf16[128,2048]{1,0:T(8,128)(2,1)S(1)}, u32[]{:S(2)}, u32[]{:S(2)}) %collective-permute-start.49) | collective-permute-done | bytes 524320 | tf_op jit(solution)/shard_map/cond/branch_1_fun/ppermute | solution.py:590
  662.8 8.5 %collective-permute-done.44 = bf16[128,2048]{1,0:T(8,128)(2,1)} collective-permute-done((bf16[128,2048]{1,0:T(8,128)(2,1)}, bf16[128,2048]{1,0:T(8,128)(2,1)}, u32[]{:S(2)}, u32[]{:S(2)}) %collective-permute-start.44) | collective-permute-done | bytes 524320 | tf_op jit(solution)/shard_map/cond/branch_1_fun/ppermute | solution.py:590
  678.7 3.8 collective-permute-done.53
  690.4 5.1 all-to-all-start.1
  702.8 3.8 unpack_down.1
  709.7 3.6 place.3
  713.3 4.5 place.2
  720.3 3.5 unpack_heads.1
  (444 shorter events, 235.8 us)
Async XLA Ops:
  15.2 32.2 %all-to-all-start.3 = ((bf16[4,256,512]{2,1,0:T(8,128)(2,1)}), bf16[4,256,512]{2,1,0:T(8,128)(2,1)S(1)}, u32[]{:S(2)}, u32[]{:S(2)}) async-start(bf16[4,256,512]{2,1,0:T(8,128)(2,1)} %pack_heads.1), calls=%async_computation.3 | async-start | bytes 2097152 | tf_op jit(solution)/shard_map/all_to_all | solution.py:698
  49.0 29.2 %collective-permute-start.10 = (bf16[1024,512]{1,0:T(8,128)(2,1)S(1)}, bf16[1024,512]{1,0:T(8,128)(2,1)S(1)}, u32[]{:S(2)}, u32[]{:S(2)}) collective-permute-start(bf16[1024,512]{1,0:T(8,128)(2,1)S(1)} %get-tuple-element.180), channel_id=1, source_target_pairs={{0,2},{1,3},{2,0},{3,1},{4,6},{5,7},{6,4},{7,5},{8,10},{9,11},{10,... | collective-permute-start | bytes 3145736 | tf_op jit(solution)/shard_map/cond/branch_1_fun/ppermute | solution.py:590
  50.6 28.3 %collective-permute-start.9 = (bf16[1024,512]{1,0:T(8,128)(2,1)S(1)}, bf16[1024,512]{1,0:T(8,128)(2,1)S(1)}, u32[]{:S(2)}, u32[]{:S(2)}) collective-permute-start(bf16[1024,512]{1,0:T(8,128)(2,1)S(1)} %get-tuple-element.180), channel_id=1, source_target_pairs={{0,1},{1,0},{2,3},{3,2},{4,5},{5,4},{6,7},{7,6},{8,9},{9,8},{10,11... | collective-permute-start | bytes 3145736 | tf_op jit(solution)/shard_map/cond/branch_1_fun/ppermute | solution.py:590
  52.1 23.6 %collective-permute-start.6 = (bf16[2,128,1024]{2,1,0:T(8,128)(2,1)S(1)}, bf16[2,128,1024]{2,1,0:T(8,128)(2,1)S(1)}, u32[]{:S(2)}, u32[]{:S(2)}) collective-permute-start(bf16[2,128,1024]{2,1,0:T(8,128)(2,1)S(1)} %get-tuple-element.178), channel_id=1, source_target_pairs={{8,0},{24,8},{16,24},{0,16},{9,1},{25,9},{17,25},{1,17},{10,2},{26... | collective-permute-start | bytes 1572872 | tf_op jit(solution)/shard_map/cond/branch_1_fun/ppermute | solution.py:600
  52.1 24.8 %collective-permute-start.5 = (bf16[2,128,1024]{2,1,0:T(8,128)(2,1)S(1)}, bf16[2,128,1024]{2,1,0:T(8,128)(2,1)S(1)}, u32[]{:S(2)}, u32[]{:S(2)}) collective-permute-start(bf16[2,128,1024]{2,1,0:T(8,128)(2,1)S(1)} %get-tuple-element.178), channel_id=1, source_target_pairs={{0,8},{8,24},{24,16},{16,0},{1,9},{9,25},{25,17},{17,1},{2,10},{10... | collective-permute-start | bytes 1572872 | tf_op jit(solution)/shard_map/cond/branch_1_fun/ppermute | solution.py:599
  78.3 16.7 %collective-permute-start.12 = (bf16[512,512]{1,0:T(8,128)(2,1)S(1)}, bf16[512,512]{1,0:T(8,128)(2,1)S(1)}, u32[]{:S(2)}, u32[]{:S(2)}) collective-permute-start(bf16[512,512]{1,0:T(8,128)(2,1)S(1)} %fusion.6), channel_id=1, source_target_pairs={{0,1},{1,0},{2,3},{3,2},{4,5},{5,4},{6,7},{7,6},{8,9},{9,8},{10,11... | collective-permute-start | bytes 1572872 | tf_op jit(solution)/shard_map/cond/branch_1_fun/ppermute | solution.py:590
  78.9 16.1 %collective-permute-start.13 = (bf16[512,512]{1,0:T(8,128)(2,1)S(1)}, bf16[512,512]{1,0:T(8,128)(2,1)S(1)}, u32[]{:S(2)}, u32[]{:S(2)}) collective-permute-start(bf16[512,512]{1,0:T(8,128)(2,1)S(1)} %fusion.4), channel_id=1, source_target_pairs={{0,2},{1,3},{2,0},{3,1},{4,6},{5,7},{6,4},{7,5},{8,10},{9,11},{10,... | collective-permute-start | bytes 1572872 | tf_op jit(solution)/shard_map/cond/branch_1_fun/ppermute | solution.py:590
  108.7 55.9 %all-to-all-start.4 = ((bf16[4,256,1024]{2,1,0:T(8,128)(2,1)}), bf16[4,256,1024]{2,1,0:T(8,128)(2,1)}, u32[]{:S(2)}, u32[]{:S(2)}) async-start(bf16[4,256,1024]{2,1,0:T(8,128)(2,1)} %get-tuple-element.389), calls=%async_computation.4 | async-start | bytes 4194304 | tf_op jit(solution)/shard_map/all_to_all | solution.py:698
  123.2 19.3 %collective-permute-start.86 = (bf16[512,384]{1,0:T(8,128)(2,1)S(1)}, bf16[512,384]{1,0:T(8,128)(2,1)S(1)}, u32[]{:S(2)}, u32[]{:S(2)}) collective-permute-start(bf16[512,384]{1,0:T(8,128)(2,1)S(1)} %get-tuple-element.376), channel_id=1, source_target_pairs={{0,2},{1,3},{2,0},{3,1},{4,6},{5,7},{6,4},{7,5},{8,10},{9,11},{10,... | collective-permute-start | bytes 1179656 | tf_op jit(solution)/shard_map/ppermute | solution.py:590
  124.8 17.8 %collective-permute-start.87 = (bf16[512,384]{1,0:T(8,128)(2,1)S(1)}, bf16[512,384]{1,0:T(8,128)(2,1)S(1)}, u32[]{:S(2)}, u32[]{:S(2)}) collective-permute-start(bf16[512,384]{1,0:T(8,128)(2,1)S(1)} %get-tuple-element.377), channel_id=1, source_target_pairs={{0,3},{1,2},{2,1},{3,0},{4,7},{5,6},{6,5},{7,4},{8,11},{9,10},{10,... | collective-permute-start | bytes 1179656 | tf_op jit(solution)/shard_map/ppermute | solution.py:590
  164.7 45.9 %collective-permute-start.82 = (bf16[1024,1024]{1,0:T(8,128)(2,1)}, bf16[1024,1024]{1,0:T(8,128)(2,1)}, u32[]{:S(2)}, u32[]{:S(2)}) collective-permute-start(bf16[1024,1024]{1,0:T(8,128)(2,1)} %bitcast.13), channel_id=1, source_target_pairs={{0,2},{1,3},{2,0},{3,1},{4,6},{5,7},{6,4},{7,5},{8,10},{9,11},{10,... | collective-permute-start | bytes 6291464 | tf_op jit(solution)/shard_map/cond/branch_1_fun/ppermute | solution.py:590
  166.0 45.9 %collective-permute-start.81 = (bf16[1024,1024]{1,0:T(8,128)(2,1)}, bf16[1024,1024]{1,0:T(8,128)(2,1)}, u32[]{:S(2)}, u32[]{:S(2)}) collective-permute-start(bf16[1024,1024]{1,0:T(8,128)(2,1)} %bitcast.13), channel_id=1, source_target_pairs={{0,1},{1,0},{2,3},{3,2},{4,5},{5,4},{6,7},{7,6},{8,9},{9,8},{10,11... | collective-permute-start | bytes 6291464 | tf_op jit(solution)/shard_map/cond/branch_1_fun/ppermute | solution.py:590
  169.3 14.2 %collective-permute-start.77 = (bf16[2,64,1024]{2,1,0:T(8,128)(2,1)}, bf16[2,64,1024]{2,1,0:T(8,128)(2,1)S(1)}, u32[]{:S(2)}, u32[]{:S(2)}) collective-permute-start(bf16[2,64,1024]{2,1,0:T(8,128)(2,1)} %get-tuple-element.191), channel_id=1, source_target_pairs={{0,8},{8,24},{24,16},{16,0},{1,9},{9,25},{25,17},{17,1},{2,10},{10... | collective-permute-start | bytes 786440 | tf_op jit(solution)/shard_map/cond/branch_1_fun/ppermute | solution.py:619
  178.6 14.9 %collective-permute-start.80 = (bf16[2,128,1024]{2,1,0:T(8,128)(2,1)S(1)}, bf16[2,128,1024]{2,1,0:T(8,128)(2,1)S(1)}, u32[]{:S(2)}, u32[]{:S(2)}) collective-permute-start(bf16[2,128,1024]{2,1,0:T(8,128)(2,1)S(1)} %pad_maximum_fusion.3), channel_id=1, source_target_pairs={{8,0},{24,8},{16,24},{0,16},{9,1},{25,9},{17,25},{1,17},{10,2},{26... | collective-permute-start | bytes 1572872 | tf_op jit(solution)/shard_map/cond/branch_1_fun/ppermute | solution.py:635
  183.7 18.9 %collective-permute-start.78 = (bf16[2,128,1024]{2,1,0:T(8,128)(2,1)S(1)}, bf16[2,128,1024]{2,1,0:T(8,128)(2,1)S(1)}, u32[]{:S(2)}, u32[]{:S(2)}) collective-permute-start(bf16[2,128,1024]{2,1,0:T(8,128)(2,1)S(1)} %pad_maximum_fusion.2), channel_id=1, source_target_pairs={{0,8},{8,24},{24,16},{16,0},{1,9},{9,25},{25,17},{17,1},{2,10},{10... | collective-permute-start | bytes 1572872 | tf_op jit(solution)/shard_map/cond/branch_1_fun/ppermute | solution.py:634
  211.9 80.2 %all-to-all-start.5 = ((bf16[4,256,512]{2,1,0:T(8,128)(2,1)}), bf16[4,256,512]{2,1,0:T(8,128)(2,1)}, u32[]{:S(2)}, u32[]{:S(2)}) async-start(bf16[4,256,512]{2,1,0:T(8,128)(2,1)} %tie.3), calls=%async_computation.5 | async-start | bytes 2097152 | tf_op jit(solution)/shard_map/all_to_all | solution.py:698
  216.8 286.8 %reduce-scatter.7.cloned.1.call-start = ((), (), s32[]{:S(2)}) async-start(), calls=%async_computation.9 | async-start | bytes 5242880
  225.8 39.1 %collective-permute-start.21 = (bf16[512,1024]{1,0:T(8,128)(2,1)S(1)}, bf16[512,1024]{1,0:T(8,128)(2,1)S(1)}, u32[]{:S(2)}, u32[]{:S(2)}) collective-permute-start(bf16[512,1024]{1,0:T(8,128)(2,1)S(1)} %slice_add_fusion.7), channel_id=1, source_target_pairs={{0,1},{1,0},{2,3},{3,2},{4,5},{5,4},{6,7},{7,6},{8,9},{9,8},{10,11... | collective-permute-start | bytes 3145736 | tf_op jit(solution)/shard_map/cond/branch_1_fun/ppermute | solution.py:590
  226.4 38.5 %collective-permute-start.22 = (bf16[512,1024]{1,0:T(8,128)(2,1)S(1)}, bf16[512,1024]{1,0:T(8,128)(2,1)S(1)}, u32[]{:S(2)}, u32[]{:S(2)}) collective-permute-start(bf16[512,1024]{1,0:T(8,128)(2,1)S(1)} %slice_add_fusion.6), channel_id=1, source_target_pairs={{0,2},{1,3},{2,0},{3,1},{4,6},{5,7},{6,4},{7,5},{8,10},{9,11},{10,... | collective-permute-start | bytes 3145736 | tf_op jit(solution)/shard_map/cond/branch_1_fun/ppermute | solution.py:590
  227.4 16.3 %collective-permute-start.17 = (bf16[2,128,1024]{2,1,0:T(8,128)(2,1)S(1)}, bf16[2,128,1024]{2,1,0:T(8,128)(2,1)S(1)}, u32[]{:S(2)}, u32[]{:S(2)}) collective-permute-start(bf16[2,128,1024]{2,1,0:T(8,128)(2,1)S(1)} %get-tuple-element.195), channel_id=1, source_target_pairs={{8,0},{24,8},{16,24},{0,16},{9,1},{25,9},{17,25},{1,17},{10,2},{26... | collective-permute-start | bytes 1572872 | tf_op jit(solution)/shard_map/cond/branch_1_fun/ppermute | solution.py:600
  230.2 32.2 %collective-permute-start.16 = (bf16[2,128,1024]{2,1,0:T(8,128)(2,1)S(1)}, bf16[2,128,1024]{2,1,0:T(8,128)(2,1)S(1)}, u32[]{:S(2)}, u32[]{:S(2)}) collective-permute-start(bf16[2,128,1024]{2,1,0:T(8,128)(2,1)S(1)} %get-tuple-element.195), channel_id=1, source_target_pairs={{0,8},{8,24},{24,16},{16,0},{1,9},{9,25},{25,17},{17,1},{2,10},{10... | collective-permute-start | bytes 1572872 | tf_op jit(solution)/shard_map/cond/branch_1_fun/ppermute | solution.py:599
  243.7 18.7 %collective-permute-start.24 = (bf16[16,128]{1,0:T(8,128)(2,1)S(1)}, bf16[16,128]{1,0:T(8,128)(2,1)S(1)}, u32[]{:S(2)}, u32[]{:S(2)}) collective-permute-start(bf16[16,128]{1,0:T(8,128)(2,1)S(1)} %slice.371), channel_id=1, source_target_pairs={{0,4},{4,0},{1,5},{5,1},{2,6},{6,2},{3,7},{7,3},{8,12},{12,8},{9,1... | collective-permute-start | bytes 12296 | tf_op jit(solution)/shard_map/cond/branch_1_fun/ppermute | solution.py:593
  271.9 20.1 %collective-permute-start.25 = (bf16[4,1024,1024]{2,1,0:T(8,128)(2,1)}, bf16[4,1024,1024]{2,1,0:T(8,128)(2,1)}, u32[]{:S(2)}, u32[]{:S(2)}) collective-permute-start(bf16[4,1024,1024]{2,1,0:T(8,128)(2,1)} %fusion.8), channel_id=1, source_target_pairs={{0,4},{4,0},{1,5},{5,1},{2,6},{6,2},{3,7},{7,3},{8,12},{12,8},{9,1... | collective-permute-start | bytes 25165832 | tf_op jit(solution)/shard_map/cond/branch_1_fun/ppermute | solution.py:593
  275.8 14.8 %collective-permute-start.18 = (bf16[2,64,1024]{2,1,0:T(8,128)(2,1)S(1)}, bf16[2,64,1024]{2,1,0:T(8,128)(2,1)S(1)}, u32[]{:S(2)}, u32[]{:S(2)}) collective-permute-start(bf16[2,64,1024]{2,1,0:T(8,128)(2,1)S(1)} %slice_add_fusion.9), channel_id=1, source_target_pairs={{0,8},{8,24},{24,16},{16,0},{1,9},{9,25},{25,17},{17,1},{2,10},{10... | collective-permute-start | bytes 786440 | tf_op jit(solution)/shard_map/cond/branch_1_fun/ppermute | solution.py:607
  275.9 15.5 %collective-permute-start.19 = (bf16[2,64,1024]{2,1,0:T(8,128)(2,1)S(1)}, bf16[2,64,1024]{2,1,0:T(8,128)(2,1)S(1)}, u32[]{:S(2)}, u32[]{:S(2)}) collective-permute-start(bf16[2,64,1024]{2,1,0:T(8,128)(2,1)S(1)} %slice_add_fusion.8), channel_id=1, source_target_pairs={{8,0},{24,8},{16,24},{0,16},{9,1},{25,9},{17,25},{1,17},{10,2},{26... | collective-permute-start | bytes 786440 | tf_op jit(solution)/shard_map/cond/branch_1_fun/ppermute | solution.py:608
  292.1 27.7 %collective-permute-start.31 = (bf16[1024,512]{1,0:T(8,128)(2,1)}, bf16[1024,512]{1,0:T(8,128)(2,1)S(1)}, u32[]{:S(2)}, u32[]{:S(2)}) collective-permute-start(bf16[1024,512]{1,0:T(8,128)(2,1)} %bitcast.31), channel_id=1, source_target_pairs={{0,2},{1,3},{2,0},{3,1},{4,6},{5,7},{6,4},{7,5},{8,10},{9,11},{10,... | collective-permute-start | bytes 3145736 | tf_op jit(solution)/shard_map/cond/branch_1_fun/ppermute | solution.py:590
  292.6 28.3 %collective-permute-start.30 = (bf16[1024,512]{1,0:T(8,128)(2,1)}, bf16[1024,512]{1,0:T(8,128)(2,1)S(1)}, u32[]{:S(2)}, u32[]{:S(2)}) collective-permute-start(bf16[1024,512]{1,0:T(8,128)(2,1)} %bitcast.31), channel_id=1, source_target_pairs={{0,1},{1,0},{2,3},{3,2},{4,5},{5,4},{6,7},{7,6},{8,9},{9,8},{10,11... | collective-permute-start | bytes 3145736 | tf_op jit(solution)/shard_map/cond/branch_1_fun/ppermute | solution.py:590
  293.6 23.7 %collective-permute-start.27 = (bf16[2,128,1024]{2,1,0:T(8,128)(2,1)S(1)}, bf16[2,128,1024]{2,1,0:T(8,128)(2,1)S(1)}, u32[]{:S(2)}, u32[]{:S(2)}) collective-permute-start(bf16[2,128,1024]{2,1,0:T(8,128)(2,1)S(1)} %get-tuple-element.199), channel_id=1, source_target_pairs={{8,0},{24,8},{16,24},{0,16},{9,1},{25,9},{17,25},{1,17},{10,2},{26... | collective-permute-start | bytes 1572872 | tf_op jit(solution)/shard_map/cond/branch_1_fun/ppermute | solution.py:600
  293.6 24.9 %collective-permute-start.26 = (bf16[2,128,1024]{2,1,0:T(8,128)(2,1)S(1)}, bf16[2,128,1024]{2,1,0:T(8,128)(2,1)S(1)}, u32[]{:S(2)}, u32[]{:S(2)}) collective-permute-start(bf16[2,128,1024]{2,1,0:T(8,128)(2,1)S(1)} %get-tuple-element.199), channel_id=1, source_target_pairs={{0,8},{8,24},{24,16},{16,0},{1,9},{9,25},{25,17},{17,1},{2,10},{10... | collective-permute-start | bytes 1572872 | tf_op jit(solution)/shard_map/cond/branch_1_fun/ppermute | solution.py:599
  319.9 18.2 %collective-permute-start.32 = (bf16[512,512]{1,0:T(8,128)(2,1)S(1)}, bf16[512,512]{1,0:T(8,128)(2,1)S(1)}, u32[]{:S(2)}, u32[]{:S(2)}) collective-permute-start(bf16[512,512]{1,0:T(8,128)(2,1)S(1)} %fusion.13), channel_id=1, source_target_pairs={{0,1},{1,0},{2,3},{3,2},{4,5},{5,4},{6,7},{7,6},{8,9},{9,8},{10,11... | collective-permute-start | bytes 1572872 | tf_op jit(solution)/shard_map/cond/branch_1_fun/ppermute | solution.py:590
  321.0 17.0 %collective-permute-start.33 = (bf16[512,512]{1,0:T(8,128)(2,1)S(1)}, bf16[512,512]{1,0:T(8,128)(2,1)S(1)}, u32[]{:S(2)}, u32[]{:S(2)}) collective-permute-start(bf16[512,512]{1,0:T(8,128)(2,1)S(1)} %fusion.11), channel_id=1, source_target_pairs={{0,2},{1,3},{2,0},{3,1},{4,6},{5,7},{6,4},{7,5},{8,10},{9,11},{10,... | collective-permute-start | bytes 1572872 | tf_op jit(solution)/shard_map/cond/branch_1_fun/ppermute | solution.py:590
  383.4 38.7 %collective-permute-start.61 = (bf16[4,2,512,512]{3,2,1,0:T(8,128)(2,1)}, bf16[4,2,512,512]{3,2,1,0:T(8,128)(2,1)}, u32[]{:S(2)}, u32[]{:S(2)}) collective-permute-start(bf16[4,2,512,512]{3,2,1,0:T(8,128)(2,1)} %get-tuple-element.215), channel_id=1, source_target_pairs={{0,4},{4,0},{1,5},{5,1},{2,6},{6,2},{3,7},{7,3},{8,12},{12,8},{9,1... | collective-permute-start | bytes 12582920 | tf_op jit(solution)/shard_map/cond/branch_1_fun/ppermute | solution.py:593
  383.6 15.5 %collective-permute-start.60 = (bf16[4,512,512]{2,1,0:T(8,128)(2,1)S(1)}, bf16[4,512,512]{2,1,0:T(8,128)(2,1)S(1)}, u32[]{:S(2)}, u32[]{:S(2)}) collective-permute-start(bf16[4,512,512]{2,1,0:T(8,128)(2,1)S(1)} %get-tuple-element.214), channel_id=1, source_target_pairs={{0,4},{4,0},{1,5},{5,1},{2,6},{6,2},{3,7},{7,3},{8,12},{12,8},{9,1... | collective-permute-start | bytes 6291464 | tf_op jit(solution)/shard_map/cond/branch_1_fun/ppermute | solution.py:593
  392.5 17.6 %collective-permute-start.58 = (bf16[2,128,1024]{2,1,0:T(8,128)(2,1)S(1)}, bf16[2,128,1024]{2,1,0:T(8,128)(2,1)S(1)}, u32[]{:S(2)}, u32[]{:S(2)}) collective-permute-start(bf16[2,128,1024]{2,1,0:T(8,128)(2,1)S(1)} %pad_maximum_fusion.5), channel_id=1, source_target_pairs={{8,0},{24,8},{16,24},{0,16},{9,1},{25,9},{17,25},{1,17},{10,2},{26... | collective-permute-start | bytes 1572872 | tf_op jit(solution)/shard_map/cond/branch_1_fun/ppermute | solution.py:635
  399.0 21.9 %collective-permute-start.56 = (bf16[2,128,1024]{2,1,0:T(8,128)(2,1)S(1)}, bf16[2,128,1024]{2,1,0:T(8,128)(2,1)S(1)}, u32[]{:S(2)}, u32[]{:S(2)}) collective-permute-start(bf16[2,128,1024]{2,1,0:T(8,128)(2,1)S(1)} %pad_maximum_fusion.4), channel_id=1, source_target_pairs={{0,8},{8,24},{24,16},{16,0},{1,9},{9,25},{25,17},{17,1},{2,10},{10... | collective-permute-start | bytes 1572872 | tf_op jit(solution)/shard_map/cond/branch_1_fun/ppermute | solution.py:634
  422.1 211.0 %reduce-scatter.9.cloned.1.call-start = ((), (), s32[]{:S(2)}) async-start(), calls=%async_computation.10 | async-start | bytes 10485760
  426.6 23.0 %collective-permute-start.37 = (bf16[2,128,1024]{2,1,0:T(8,128)(2,1)S(1)}, bf16[2,128,1024]{2,1,0:T(8,128)(2,1)S(1)}, u32[]{:S(2)}, u32[]{:S(2)}) collective-permute-start(bf16[2,128,1024]{2,1,0:T(8,128)(2,1)S(1)} %get-tuple-element.216), channel_id=1, source_target_pairs={{8,0},{24,8},{16,24},{0,16},{9,1},{25,9},{17,25},{1,17},{10,2},{26... | collective-permute-start | bytes 1572872 | tf_op jit(solution)/shard_map/cond/branch_1_fun/ppermute | solution.py:600
  427.2 24.5 %collective-permute-start.36 = (bf16[2,128,1024]{2,1,0:T(8,128)(2,1)S(1)}, bf16[2,128,1024]{2,1,0:T(8,128)(2,1)S(1)}, u32[]{:S(2)}, u32[]{:S(2)}) collective-permute-start(bf16[2,128,1024]{2,1,0:T(8,128)(2,1)S(1)} %get-tuple-element.216), channel_id=1, source_target_pairs={{0,8},{8,24},{24,16},{16,0},{1,9},{9,25},{25,17},{17,1},{2,10},{10... | collective-permute-start | bytes 1572872 | tf_op jit(solution)/shard_map/cond/branch_1_fun/ppermute | solution.py:599
  453.1 15.3 %collective-permute-start.38 = (bf16[2,64,1024]{2,1,0:T(8,128)(2,1)S(1)}, bf16[2,64,1024]{2,1,0:T(8,128)(2,1)S(1)}, u32[]{:S(2)}, u32[]{:S(2)}) collective-permute-start(bf16[2,64,1024]{2,1,0:T(8,128)(2,1)S(1)} %slice_add_fusion.17), channel_id=1, source_target_pairs={{0,8},{8,24},{24,16},{16,0},{1,9},{9,25},{25,17},{17,1},{2,10},{10... | collective-permute-start | bytes 786440 | tf_op jit(solution)/shard_map/cond/branch_1_fun/ppermute | solution.py:607
  453.8 14.6 %collective-permute-start.39 = (bf16[2,64,1024]{2,1,0:T(8,128)(2,1)S(1)}, bf16[2,64,1024]{2,1,0:T(8,128)(2,1)S(1)}, u32[]{:S(2)}, u32[]{:S(2)}) collective-permute-start(bf16[2,64,1024]{2,1,0:T(8,128)(2,1)S(1)} %slice_add_fusion.16), channel_id=1, source_target_pairs={{8,0},{24,8},{16,24},{0,16},{9,1},{25,9},{17,25},{1,17},{10,2},{26... | collective-permute-start | bytes 786440 | tf_op jit(solution)/shard_map/cond/branch_1_fun/ppermute | solution.py:608
  475.7 14.7 %collective-permute-start.3 = (bf16[2,64,1024]{2,1,0:T(8,128)(2,1)}, bf16[2,64,1024]{2,1,0:T(8,128)(2,1)}, u32[]{:S(2)}, u32[]{:S(2)}) collective-permute-start(bf16[2,64,1024]{2,1,0:T(8,128)(2,1)} %get-tuple-element.234), channel_id=1, source_target_pairs={{0,8},{8,24},{24,16},{16,0},{1,9},{9,25},{25,17},{17,1},{2,10},{10... | collective-permute-start | bytes 786440 | tf_op jit(solution)/shard_map/cond/branch_1_fun/ppermute | solution.py:619
  503.6 54.2 %all-to-all-start.2 = ((bf16[4,256,512]{2,1,0:T(8,128)(2,1)}), bf16[4,256,512]{2,1,0:T(8,128)(2,1)}, u32[]{:S(2)}, u32[]{:S(2)}) async-start(bf16[4,256,512]{2,1,0:T(8,128)(2,1)} %bitcast.142), calls=%async_computation.2 | async-start | bytes 2097152 | tf_op jit(solution)/shard_map/cond/branch_1_fun/all_to_all | solution.py:698
  507.9 20.6 %collective-permute-start.62 = (bf16[512,384]{1,0:T(8,128)(2,1)}, bf16[512,384]{1,0:T(8,128)(2,1)S(1)}, u32[]{:S(2)}, u32[]{:S(2)}) collective-permute-start(bf16[512,384]{1,0:T(8,128)(2,1)} %get-tuple-element.237), channel_id=1, source_target_pairs={{0,1},{1,0},{2,3},{3,2},{4,5},{5,4},{6,7},{7,6},{8,9},{9,8},{10,11... | collective-permute-start | bytes 1179656 | tf_op jit(solution)/shard_map/cond/branch_1_fun/ppermute | solution.py:590
  508.7 21.1 %collective-permute-start.63 = (bf16[512,384]{1,0:T(8,128)(2,1)}, bf16[512,384]{1,0:T(8,128)(2,1)S(1)}, u32[]{:S(2)}, u32[]{:S(2)}) collective-permute-start(bf16[512,384]{1,0:T(8,128)(2,1)} %get-tuple-element.238), channel_id=1, source_target_pairs={{0,2},{1,3},{2,0},{3,1},{4,6},{5,7},{6,4},{7,5},{8,10},{9,11},{10,... | collective-permute-start | bytes 1179656 | tf_op jit(solution)/shard_map/cond/branch_1_fun/ppermute | solution.py:590
  509.7 35.2 %collective-permute-start.64 = (bf16[512,384]{1,0:T(8,128)(2,1)}, bf16[512,384]{1,0:T(8,128)(2,1)S(1)}, u32[]{:S(2)}, u32[]{:S(2)}) collective-permute-start(bf16[512,384]{1,0:T(8,128)(2,1)} %get-tuple-element.239), channel_id=1, source_target_pairs={{0,3},{1,2},{2,1},{3,0},{4,7},{5,6},{6,5},{7,4},{8,11},{9,10},{10,... | collective-permute-start | bytes 1179656 | tf_op jit(solution)/shard_map/cond/branch_1_fun/ppermute | solution.py:590
  512.8 33.5 %collective-permute-start.66 = (bf16[2,128,1024]{2,1,0:T(8,128)(2,1)S(1)}, bf16[2,128,1024]{2,1,0:T(8,128)(2,1)S(1)}, u32[]{:S(2)}, u32[]{:S(2)}) collective-permute-start(bf16[2,128,1024]{2,1,0:T(8,128)(2,1)S(1)} %pad_maximum_fusion.8), channel_id=1, source_target_pairs={{8,0},{24,8},{16,24},{0,16},{9,1},{25,9},{17,25},{1,17},{10,2},{26... | collective-permute-start | bytes 1572872 | tf_op jit(solution)/shard_map/cond/branch_1_fun/ppermute | solution.py:635
  515.7 40.5 %collective-permute-start.65 = (bf16[2,128,1024]{2,1,0:T(8,128)(2,1)S(1)}, bf16[2,128,1024]{2,1,0:T(8,128)(2,1)S(1)}, u32[]{:S(2)}, u32[]{:S(2)}) collective-permute-start(bf16[2,128,1024]{2,1,0:T(8,128)(2,1)S(1)} %pad_maximum_fusion.7), channel_id=1, source_target_pairs={{0,8},{8,24},{24,16},{16,0},{1,9},{9,25},{25,17},{17,1},{2,10},{10... | collective-permute-start | bytes 1572872 | tf_op jit(solution)/shard_map/cond/branch_1_fun/ppermute | solution.py:634
  565.6 16.0 %collective-permute-start.72 = (bf16[4,512,384]{2,1,0:T(8,128)(2,1)}, bf16[4,512,384]{2,1,0:T(8,128)(2,1)S(1)}, u32[]{:S(2)}, u32[]{:S(2)}) collective-permute-start(bf16[4,512,384]{2,1,0:T(8,128)(2,1)} %get-tuple-element.253.refs_2_), channel_id=1, source_target_pairs={{0,4},{4,0},{1,5},{5,1},{2,6},{6,2},{3,7},{7,3},{8,12},{12,8},{9,1... | collective-permute-start | bytes 4718600 | tf_op jit(solution)/shard_map/cond/branch_1_fun/ppermute | solution.py:593
  578.5 18.9 %collective-permute-start.67 = (bf16[2,64,1024]{2,1,0:T(8,128)(2,1)S(1)}, bf16[2,64,1024]{2,1,0:T(8,128)(2,1)S(1)}, u32[]{:S(2)}, u32[]{:S(2)}) collective-permute-start(bf16[2,64,1024]{2,1,0:T(8,128)(2,1)S(1)} %get-tuple-element.249), channel_id=1, source_target_pairs={{0,8},{8,24},{24,16},{16,0},{1,9},{9,25},{25,17},{17,1},{2,10},{10... | collective-permute-start | bytes 786440 | tf_op jit(solution)/shard_map/cond/branch_1_fun/ppermute | solution.py:619
  579.1 19.1 %collective-permute-start.70 = (bf16[2,128,1024]{2,1,0:T(8,128)(2,1)S(1)}, bf16[2,128,1024]{2,1,0:T(8,128)(2,1)S(1)}, u32[]{:S(2)}, u32[]{:S(2)}) collective-permute-start(bf16[2,128,1024]{2,1,0:T(8,128)(2,1)S(1)} %pad_maximum_fusion.11), channel_id=1, source_target_pairs={{8,0},{24,8},{16,24},{0,16},{9,1},{25,9},{17,25},{1,17},{10,2},{26... | collective-permute-start | bytes 1572872 | tf_op jit(solution)/shard_map/cond/branch_1_fun/ppermute | solution.py:635
  595.1 23.9 %collective-permute-start.75 = (bf16[2,512,512]{2,1,0:T(8,128)(2,1)S(1)}, bf16[2,512,512]{2,1,0:T(8,128)(2,1)S(1)}, u32[]{:S(2)}, u32[]{:S(2)}) collective-permute-start(bf16[2,512,512]{2,1,0:T(8,128)(2,1)S(1)} %pad_maximum_fusion.9), channel_id=1, source_target_pairs={{0,1},{1,0},{2,3},{3,2},{4,5},{5,4},{6,7},{7,6},{8,9},{9,8},{10,11... | collective-permute-start | bytes 3145736 | tf_op jit(solution)/shard_map/cond/branch_1_fun/ppermute | solution.py:590
  595.2 24.0 %collective-permute-start.76 = (bf16[2,512,512]{2,1,0:T(8,128)(2,1)S(1)}, bf16[2,512,512]{2,1,0:T(8,128)(2,1)S(1)}, u32[]{:S(2)}, u32[]{:S(2)}) collective-permute-start(bf16[2,512,512]{2,1,0:T(8,128)(2,1)S(1)} %stack.133), channel_id=1, source_target_pairs={{0,2},{1,3},{2,0},{3,1},{4,6},{5,7},{6,4},{7,5},{8,10},{9,11},{10,... | collective-permute-start | bytes 3145736 | tf_op jit(solution)/shard_map/cond/branch_1_fun/ppermute | solution.py:590
  634.3 56.1 %all-to-all-start = ((bf16[4,256,1024]{2,1,0:T(8,128)(2,1)}), bf16[4,256,1024]{2,1,0:T(8,128)(2,1)S(1)}, u32[]{:S(2)}, u32[]{:S(2)}) async-start(bf16[4,256,1024]{2,1,0:T(8,128)(2,1)} %bitcast.137), calls=%async_computation | async-start | bytes 4194304 | tf_op jit(solution)/shard_map/cond/branch_1_fun/all_to_all | solution.py:698
  644.9 15.1 %collective-permute-start.49 = (bf16[128,2048]{1,0:T(8,128)(2,1)}, bf16[128,2048]{1,0:T(8,128)(2,1)S(1)}, u32[]{:S(2)}, u32[]{:S(2)}) collective-permute-start(bf16[128,2048]{1,0:T(8,128)(2,1)} %convert_element_type.300), channel_id=1, source_target_pairs={{0,2},{1,3},{2,0},{3,1},{4,6},{5,7},{6,4},{7,5},{8,10},{9,11},{10,... | collective-permute-start | bytes 1572872 | tf_op jit(solution)/shard_map/cond/branch_1_fun/ppermute | solution.py:590
  645.3 15.0 %collective-permute-start.48 = (bf16[128,2048]{1,0:T(8,128)(2,1)}, bf16[128,2048]{1,0:T(8,128)(2,1)S(1)}, u32[]{:S(2)}, u32[]{:S(2)}) collective-permute-start(bf16[128,2048]{1,0:T(8,128)(2,1)} %convert_element_type.300), channel_id=1, source_target_pairs={{0,1},{1,0},{2,3},{3,2},{4,5},{5,4},{6,7},{7,6},{8,9},{9,8},{10,11... | collective-permute-start | bytes 1572872 | tf_op jit(solution)/shard_map/cond/branch_1_fun/ppermute | solution.py:590
  648.3 23.0 %collective-permute-start.44 = (bf16[128,2048]{1,0:T(8,128)(2,1)}, bf16[128,2048]{1,0:T(8,128)(2,1)}, u32[]{:S(2)}, u32[]{:S(2)}) collective-permute-start(bf16[128,2048]{1,0:T(8,128)(2,1)} %convert_element_type.297), channel_id=1, source_target_pairs={{0,2},{1,3},{2,0},{3,1},{4,6},{5,7},{6,4},{7,5},{8,10},{9,11},{10,... | collective-permute-start | bytes 1572872 | tf_op jit(solution)/shard_map/cond/branch_1_fun/ppermute | solution.py:590
  649.6 26.7 %collective-permute-start.43 = (bf16[128,2048]{1,0:T(8,128)(2,1)}, bf16[128,2048]{1,0:T(8,128)(2,1)}, u32[]{:S(2)}, u32[]{:S(2)}) collective-permute-start(bf16[128,2048]{1,0:T(8,128)(2,1)} %convert_element_type.297), channel_id=1, source_target_pairs={{0,1},{1,0},{2,3},{3,2},{4,5},{5,4},{6,7},{7,6},{8,9},{9,8},{10,11... | collective-permute-start | bytes 1572872 | tf_op jit(solution)/shard_map/cond/branch_1_fun/ppermute | solution.py:590
  651.1 31.4 %collective-permute-start.53 = (bf16[512,512]{1,0:T(8,128)(2,1)}, bf16[512,512]{1,0:T(8,128)(2,1)}, u32[]{:S(2)}, u32[]{:S(2)}) collective-permute-start(bf16[512,512]{1,0:T(8,128)(2,1)} %get-tuple-element.267), channel_id=1, source_target_pairs={{0,2},{1,3},{2,0},{3,1},{4,6},{5,7},{6,4},{7,5},{8,10},{9,11},{10,... | collective-permute-start | bytes 1572872 | tf_op jit(solution)/shard_map/cond/branch_1_fun/ppermute | solution.py:590
  659.9 24.3 %collective-permute-start.54 = (bf16[512,512]{1,0:T(8,128)(2,1)}, bf16[512,512]{1,0:T(8,128)(2,1)}, u32[]{:S(2)}, u32[]{:S(2)}) collective-permute-start(bf16[512,512]{1,0:T(8,128)(2,1)} %get-tuple-element.269), channel_id=1, source_target_pairs={{0,1},{1,0},{2,3},{3,2},{4,5},{5,4},{6,7},{7,6},{8,9},{9,8},{10,11... | collective-permute-start | bytes 1572872 | tf_op jit(solution)/shard_map/cond/branch_1_fun/ppermute | solution.py:590
  660.4 28.2 %collective-permute-start.50 = (bf16[64,2048]{1,0:T(8,128)(2,1)S(1)}, bf16[64,2048]{1,0:T(8,128)(2,1)}, u32[]{:S(2)}, u32[]{:S(2)}) collective-permute-start(bf16[64,2048]{1,0:T(8,128)(2,1)S(1)} %slice.402), channel_id=1, source_target_pairs={{0,1},{1,0},{2,3},{3,2},{4,5},{5,4},{6,7},{7,6},{8,9},{9,8},{10,11... | collective-permute-start | bytes 786440 | tf_op jit(solution)/shard_map/cond/branch_1_fun/ppermute | solution.py:590
  671.3 17.3 %collective-permute-start.51 = (bf16[64,2048]{1,0:T(8,128)(2,1)}, bf16[64,2048]{1,0:T(8,128)(2,1)}, u32[]{:S(2)}, u32[]{:S(2)}) collective-permute-start(bf16[64,2048]{1,0:T(8,128)(2,1)} %slice.403), channel_id=1, source_target_pairs={{0,2},{1,3},{2,0},{3,1},{4,6},{5,7},{6,4},{7,5},{8,10},{9,11},{10,... | collective-permute-start | bytes 786440 | tf_op jit(solution)/shard_map/cond/branch_1_fun/ppermute | solution.py:590
  676.2 21.8 %collective-permute-start.45 = (bf16[64,2048]{1,0:T(8,128)(2,1)}, bf16[64,2048]{1,0:T(8,128)(2,1)}, u32[]{:S(2)}, u32[]{:S(2)}) collective-permute-start(bf16[64,2048]{1,0:T(8,128)(2,1)} %slice.400), channel_id=1, source_target_pairs={{0,1},{1,0},{2,3},{3,2},{4,5},{5,4},{6,7},{7,6},{8,9},{9,8},{10,11... | collective-permute-start | bytes 786440 | tf_op jit(solution)/shard_map/cond/branch_1_fun/ppermute | solution.py:590
  682.5 15.5 %collective-permute-start.46 = (bf16[64,2048]{1,0:T(8,128)(2,1)}, bf16[64,2048]{1,0:T(8,128)(2,1)}, u32[]{:S(2)}, u32[]{:S(2)}) collective-permute-start(bf16[64,2048]{1,0:T(8,128)(2,1)} %slice.401), channel_id=1, source_target_pairs={{0,2},{1,3},{2,0},{3,1},{4,6},{5,7},{6,4},{7,5},{8,10},{9,11},{10,... | collective-permute-start | bytes 786440 | tf_op jit(solution)/shard_map/cond/branch_1_fun/ppermute | solution.py:590
  690.4 29.8 %all-to-all-start.1 = ((bf16[4,256,512]{2,1,0:T(8,128)(2,1)}), bf16[4,256,512]{2,1,0:T(8,128)(2,1)}, u32[]{:S(2)}, u32[]{:S(2)}) async-start(bf16[4,256,512]{2,1,0:T(8,128)(2,1)} %bitcast.143), calls=%async_computation.1 | async-start | bytes 2097152 | tf_op jit(solution)/shard_map/cond/branch_1_fun/all_to_all | solution.py:698
  (82 other events, 934.0 us)
Sparse Core Ops, SparseCore 0:
  422.2 50.5 reduce-scatter.6
  476.2 104.1 reduce-scatter.8

commit v5 on v4

--- a/solution.py
+++ b/solution.py
@@ -273,7 +273,7 @@
 def mm_back(parts, w0, w1, at, own, name, deps=()):
     t, g, n = parts.shape
     half = w0.shape[1]
-    th = min(half, 256)
+    th = min(half, 512)
 
     def body(p_ref, a_ref, b_ref, *outs):
         for h, w_ref in enumerate((a_ref, b_ref)):
@@ -302,7 +302,7 @@
     _, g, half = x.shape
     t, _, n = w0.shape
     n //= 2
-    tn = min(n, 256)
+    tn = min(n, 512)
     steps = n // tn
 
     def body(x_ref, g0_ref, g1_ref, u0_ref, u1_ref, hid_ref, to_gate_ref, to_up_ref):
@@ -334,7 +334,7 @@
 def feed_back(gy, to_gate, to_up, w0, w1, d0, d1, own, deps=()):
     _, g, half = gy.shape
     t, _, n = d0.shape
-    tn = min(n, 256)
+    tn = min(n, 512)
     steps = n // tn
 
     def body(y_ref, a_ref, b_ref, g0_ref, g1_ref, u0_ref, u1_ref, d0_ref, d1_ref, *rest):
@@ -385,7 +385,7 @@
 def weight_grad(place, left, left_peer, right, right_peer, name, deps=()):
     g, half = left.shape
     t, m, _, n = right.shape
-    tn = n if n % 256 else 256
+    tn = n if n % 256 else min(n, 512)
 
     def body(s_ref, a_ref, b_ref, c_ref, d_ref, out_ref):
         del s_ref

time: 744 us -> 732 us (0.984)
  Pallas kernels: 159 us -> 142 us
    pallas_call x13, Pallas kernels: 105 us -> 93.5 us  [call(): return lambda *args: made(*args, *deps)]
  transfers between devices with their start and end apart: 100 -> 100, of which waited for: 47 -> 46; matrix products, arithmetic and copies ran while one was open for 16% -> 16% of each run, Pallas kernels for 17% -> 16%
where the time goes in v5:
time: 732 us; the launch traced here: 720 us
  waiting for transfers between devices  301 us (41%)
  Pallas kernels  142 us (19%)
  starting transfers between devices  113 us (15%)
  local copies, waits for them, and re-layouts  68.4 us (9%)
  other arithmetic  63.2 us (9%)
  between operations  17.7 us (2%)
  loops' own time  14.7 us (2%)
    ppermute x36, waiting for transfers between devices, hop(): return lax.ppermute(x, 'tp', [(t, t ^ bit) for t in range(tp_size)])  96.6 us
    pallas_call x13, Pallas kernels, call(): return lambda *args: made(*args, *deps)  93.5 us
    ppermute x4, waiting for transfers between devices, scatter_last(): one = lax.ppermute(fwd, 'z', forward)  40.9 us
    ppermute x36, starting transfers between devices, hop(): return lax.ppermute(x, 'tp', [(t, t ^ bit) for t in range(tp_size)])  36.4 us
    ppermute x4, waiting for transfers between devices, ring_first(): back = lax.ppermute(back, 'z', backward)  33.9 us
    ppermute x4, waiting for transfers between devices, ring_last(): one = lax.ppermute(after(ahead[:, :mid], back, *deps), 'z', forward)  33.8 us
    all_to_all x6, starting transfers between devices, to_z(): return lax.all_to_all(x, 'z', split_axis=0, concat_axis=0, tiled=True)  28.6 us
    pallas_call x4, Pallas kernels, placed_call(): return lambda *args: made(*args, *deps)  27.7 us
  transfers between devices with their start and end apart: 100, of which 46 were waited for; matrix products, arithmetic and copies ran while one was open for 16% of the time, Pallas kernels for 16%

profile of v5, /device:TPU:0, one launch (start us, length us, event | category | flops | bytes accessed | tf_op | source)
XLA Modules:
  0.0 720.3 jit_solution(12979997504689364085)
XLA Ops:
  15.2 6.3 all-to-all-start.3
  32.0 15.5 %all-to-all-done.3 = bf16[4,256,512]{2,1,0:T(8,128)(2,1)S(1)} async-done(((bf16[4,256,512]{2,1,0:T(8,128)(2,1)}), bf16[4,256,512]{2,1,0:T(8,128)(2,1)S(1)}, u32[]{:S(2)}, u32[]{:S(2)}) %all-to-all-start.3) | async-done | bytes 1048608 | tf_op jit(solution)/shard_map/all_to_all | solution.py:698
  49.0 59.8 %conditional.10 = (bf16[2,512,1024]{2,1,0:T(8,128)(2,1)}, bf16[4,1024,512]{2,1,0:T(8,128)(2,1)}, bf16[4,1024,512]{2,1,0:T(8,128)(2,1)}, f32[2048,128]{1,0:T(8,12...) conditional(s32[]{:T(128)} %bitcast.73, () %tuple.97, ...), branch_computations={%region_4.5_spmd, %region_5.6_spmd} | conditional | flops 15336558 | bytes 83945872 | solution.py:746
  56.5 3.8 fusion.1
  61.5 14.2 %collective-permute-done.6 = bf16[2,128,1024]{2,1,0:T(8,128)(2,1)S(1)} collective-permute-done((bf16[2,128,1024]{2,1,0:T(8,128)(2,1)S(1)}, bf16[2,128,1024]{2,1,0:T(8,128)(2,1)S(1)}, u32[]{:S(2)}, u32[]{:S(2)}) %collective-permute-start.6) | collective-permute-done | bytes 524320 | tf_op jit(solution)/shard_map/cond/branch_1_fun/ppermute | solution.py:600
  82.6 9.9 %collective-permute-done.7 = bf16[2,64,1024]{2,1,0:T(8,128)(2,1)S(1)} collective-permute-done((bf16[2,64,1024]{2,1,0:T(8,128)(2,1)S(1)}, bf16[2,64,1024]{2,1,0:T(8,128)(2,1)S(1)}, u32[]{:S(2)}, u32[]{:S(2)}) %collective-permute-start.7) | collective-permute-done | bytes 262176 | tf_op jit(solution)/shard_map/cond/branch_1_fun/ppermute | solution.py:607
  108.7 4.5 all-to-all-start.4
  114.3 7.4 %qkv.1 = (bf16[512,384]{1,0:T(8,128)(2,1)S(1)}, bf16[512,384]{1,0:T(8,128)(2,1)S(1)}, bf16[512,384]{1,0:T(8,128)(2,1)S(1)}, bf16[512,384]{1,0:T(8,128)(2,1)S(1)}) custom-call(bf16[2,512,1024]{2,1,0:T(8,128)(2,1)} %get-tuple-element.371.refs_0_, bf16[4,1024,512]{2,1,0:T(8,128)(2,1)} %get-tuple-element.372.refs_1_, ...), custom_call_target="tpu_custom_call" | custom-call | flops 3221225472 | bytes 9961472 | tf_op jit(solution)/shard_map/qkv/pallas_call | solution.py:57
  125.4 8.3 %collective-permute-done.85.refs_1_ = bf16[512,384]{1,0:T(8,128)(2,1)S(1)} collective-permute-done((bf16[512,384]{1,0:T(8,128)(2,1)S(1)}, bf16[512,384]{1,0:T(8,128)(2,1)S(1)}, u32[]{:S(2)}, u32[]{:S(2)}) %collective-permute-start.85) | collective-permute-done | bytes 393248 | tf_op jit(solution)/shard_map/ppermute | solution.py:590
  133.7 8.8 %collective-permute-done.86.refs_2_ = bf16[512,384]{1,0:T(8,128)(2,1)S(1)} collective-permute-done((bf16[512,384]{1,0:T(8,128)(2,1)S(1)}, bf16[512,384]{1,0:T(8,128)(2,1)S(1)}, u32[]{:S(2)}, u32[]{:S(2)}) %collective-permute-start.86) | collective-permute-done | bytes 393248 | tf_op jit(solution)/shard_map/ppermute | solution.py:590
  142.5 7.9 %attend.1 = (bf16[512,128]{1,0:T(8,128)(2,1)S(1)}, bf16[512,128]{1,0:T(8,128)(2,1)S(1)}, bf16[512,128]{1,0:T(8,128)(2,1)S(1)}, bf16[512,128]{1,0:T(8,128)(2,1)S(...) custom-call(s32[16]{0:T(128)S(1)} %and_select_fusion.2.tab_ref.refs_0_, ...), custom_call_target="tpu_custom_call" | custom-call | flops 2147483648 | bytes 12582912 | tf_op jit(solution)/shard_map/attend/pallas_call | solution.py:181
  159.2 5.0 attn_out.1
  164.2 47.2 %conditional.11 = (f32[2,128,1024]{2,1,0:T(8,128)S(1)}, bf16[1024,1024]{1,0:T(8,128)(2,1)}, bf16[1024,1024]{1,0:T(8,128)(2,1)}, f32[1,128,1]{1,2,0:T(1,128)S(1)}) conditional(s32[]{:T(128)} %bitcast.73, () %tuple.96, (bf16[2,128,1024]{2,1,0:T(8,128)(2,1)}, bf16[2,64,1024]{2,1,0:T(8,128)(2,1)}, f32[2,128,1024]{2,1,0:T(8,128)}, ...), branch_computations={%region_6.7_spmd, %region_7.9_spmd} | conditional | flops 4194176 | bytes 42468196 | solution.py:746
  168.8 7.9 %collective-permute-done.79 = bf16[2,64,1024]{2,1,0:T(8,128)(2,1)S(1)} collective-permute-done((bf16[2,64,1024]{2,1,0:T(8,128)(2,1)}, bf16[2,64,1024]{2,1,0:T(8,128)(2,1)S(1)}, u32[]{:S(2)}, u32[]{:S(2)}) %collective-permute-start.79) | collective-permute-done | bytes 262176 | tf_op jit(solution)/shard_map/cond/branch_1_fun/ppermute | solution.py:620
  180.4 6.2 collective-permute-done.77
  186.7 6.5 collective-permute-done.80
  193.2 8.8 %collective-permute-done.78 = bf16[2,128,1024]{2,1,0:T(8,128)(2,1)S(1)} collective-permute-done((bf16[2,128,1024]{2,1,0:T(8,128)(2,1)S(1)}, bf16[2,128,1024]{2,1,0:T(8,128)(2,1)S(1)}, u32[]{:S(2)}, u32[]{:S(2)}) %collective-permute-start.78) | collective-permute-done | bytes 524320 | tf_op jit(solution)/shard_map/cond/branch_1_fun/ppermute | solution.py:634
  202.4 7.7 %collective-permute-done.82 = bf16[1024,1024]{1,0:T(8,128)(2,1)} collective-permute-done((bf16[1024,1024]{1,0:T(8,128)(2,1)}, bf16[1024,1024]{1,0:T(8,128)(2,1)}, u32[]{:S(2)}, u32[]{:S(2)}) %collective-permute-start.82) | collective-permute-done | bytes 2097184 | tf_op jit(solution)/shard_map/cond/branch_1_fun/ppermute | solution.py:590
  211.4 4.9 all-to-all-start.5
  220.2 71.4 %conditional.12 = (bf16[2,512,1024]{2,1,0:T(8,128)(2,1)}, bf16[4,1024,1024]{2,1,0:T(8,128)(2,1)}, bf16[4,1024,1024]{2,1,0:T(8,128)(2,1)}) conditional(s32[]{:T(128)} %bitcast.73, () %tuple.102, (bf16[2,128,1024]{2,1,0:T(8,128)(2,1)S(1)}, bf16[4,256,1024]{2,1,0:T(8,128)(2,1)}, bf16[1024,1024]{1,0:T(8,128)(2,1)}, bf16[1024,1024]{1,0:T(8,128)(2,1)}) %tuple.103), branch_computations={%region_9.10_spmd, %region_10.11_spmd} | conditional | flops 26476548 | bytes 78717424 | solution.py:746
  229.8 13.5 %collective-permute-done.17 = bf16[2,128,1024]{2,1,0:T(8,128)(2,1)S(1)} collective-permute-done((bf16[2,128,1024]{2,1,0:T(8,128)(2,1)S(1)}, bf16[2,128,1024]{2,1,0:T(8,128)(2,1)S(1)}, u32[]{:S(2)}, u32[]{:S(2)}) %collective-permute-start.17) | collective-permute-done | bytes 524320 | tf_op jit(solution)/shard_map/cond/branch_1_fun/ppermute | solution.py:600
  243.2 18.7 %collective-permute-done.16 = bf16[2,128,1024]{2,1,0:T(8,128)(2,1)S(1)} collective-permute-done((bf16[2,128,1024]{2,1,0:T(8,128)(2,1)S(1)}, bf16[2,128,1024]{2,1,0:T(8,128)(2,1)S(1)}, u32[]{:S(2)}, u32[]{:S(2)}) %collective-permute-start.16) | collective-permute-done | bytes 524320 | tf_op jit(solution)/shard_map/cond/branch_1_fun/ppermute | solution.py:599
  264.6 6.8 fusion.8
  280.0 10.1 %collective-permute-done.18 = bf16[2,64,1024]{2,1,0:T(8,128)(2,1)S(1)} collective-permute-done((bf16[2,64,1024]{2,1,0:T(8,128)(2,1)S(1)}, bf16[2,64,1024]{2,1,0:T(8,128)(2,1)S(1)}, u32[]{:S(2)}, u32[]{:S(2)}) %collective-permute-start.18) | collective-permute-done | bytes 262176 | tf_op jit(solution)/shard_map/cond/branch_1_fun/ppermute | solution.py:607
  291.6 58.5 %conditional.13 = (bf16[2,512,1024]{2,1,0:T(8,128)(2,1)}, bf16[4,1024,512]{2,1,0:T(8,128)(2,1)}, bf16[4,1024,512]{2,1,0:T(8,128)(2,1)}, bf16[4,512,512]{2,1,0:T(...) conditional(s32[]{:T(128)} %bitcast.73, () %tuple.101, ...), branch_computations={%region_11.12_spmd, %region_12.13_spmd} | conditional | flops 14681069 | bytes 76547640 | solution.py:746
  295.6 13.5 %gate_up.1 = (bf16[4,512,512]{2,1,0:T(8,128)(2,1)S(1)}, bf16[4,512,512]{2,1,0:T(8,128)(2,1)S(1)}, bf16[4,512,512]{2,1,0:T(8,128)(2,1)S(1)}) custom-call(bf16[2,512,1024]{2,1,0:T(8,128)(2,1)} %get-tuple-element.200.refs_0_, bf16[4,1024,1024]{2,1,0:T(8,128)(2,1)} %get-tuple-element.201.refs_1_.refs_3_, ...), custom_call_target="tpu_custom_call" | custom-call | flops 1000 | bytes 1000 | tf_op jit(solution)/shard_map/cond/branch_1_fun/gate_up/pallas_call | solution.py:57
  310.5 6.3 collective-permute-done.27
  325.2 9.9 %collective-permute-done.28 = bf16[2,64,1024]{2,1,0:T(8,128)(2,1)S(1)} collective-permute-done((bf16[2,64,1024]{2,1,0:T(8,128)(2,1)S(1)}, bf16[2,64,1024]{2,1,0:T(8,128)(2,1)S(1)}, u32[]{:S(2)}, u32[]{:S(2)}) %collective-permute-start.28) | collective-permute-done | bytes 262176 | tf_op jit(solution)/shard_map/cond/branch_1_fun/ppermute | solution.py:607
  350.1 22.8 %feed_back.1 = (bf16[4,2,512,512]{3,2,1,0:T(8,128)(2,1)}, f32[2,128,1024]{2,1,0:T(8,128)S(1)}, bf16[2,128,1024]{2,1,0:T(8,128)(2,1)S(1)}, bf16[2,128,1024]{2,1,0...) custom-call(bf16[2,512,1024]{2,1,0:T(8,128)(2,1)} %get-tuple-element.398.refs_0_, ...), custom_call_target="tpu_custom_call" | custom-call | flops 12884901888 | bytes 37748736 | tf_op jit(solution)/shard_map/feed_back/pallas_call | solution.py:57
  372.8 38.7 %conditional.14 = (f32[2,128,1024]{2,1,0:T(8,128)}, bf16[4,1024,512]{2,1,0:T(8,128)(2,1)}, bf16[4,2,512,512]{3,2,1,0:T(8,128)(2,1)}) conditional(s32[]{:T(128)} %bitcast.73, () %tuple.100, (bf16[2,128,1024]{2,1,0:T(8,128)(2,1)S(1)}, bf16[2,64,1024]{2,1,0:T(8,128)(2,1)S(1)}, f32[2,128,1024]{2,1,0:T(8,128)S(1)}, ...), branch_computations={%region_13.14_spmd, %region_14.15_spmd} | conditional | flops 4298637312 | bytes 58196292 | solution.py:746
  377.3 4.6 collective-permute-done.57
  383.6 4.7 collective-permute-done.55
  388.5 6.2 g_down.1
  399.5 10.8 %collective-permute-done.56 = bf16[2,128,1024]{2,1,0:T(8,128)(2,1)S(1)} collective-permute-done((bf16[2,128,1024]{2,1,0:T(8,128)(2,1)S(1)}, bf16[2,128,1024]{2,1,0:T(8,128)(2,1)S(1)}, u32[]{:S(2)}, u32[]{:S(2)}) %collective-permute-start.56) | collective-permute-done | bytes 524320 | tf_op jit(solution)/shard_map/cond/branch_1_fun/ppermute | solution.py:634
  416.1 43.3 %conditional.15 = (bf16[2,512,1024]{2,1,0:T(8,128)(2,1)}, f32[2,128,1024]{2,1,0:T(8,128)}, bf16[2,128,1024]{2,1,0:T(8,128)(2,1)}, bf16[2,128,1024]{2,1,0:T(8,128...) conditional(s32[]{:T(128)} %bitcast.73, () %tuple.109, ...), branch_computations={%region_16.17_spmd, %region_17.18_spmd} | conditional | flops 12886212608 | bytes 49357176 | solution.py:746
  419.5 13.3 %g_gate_up.1 = bf16[4,1024,1024]{2,1,0:T(8,128)(2,1)} custom-call(s32[1]{0:T(128)} %get-tuple-element.217.refs_0_, bf16[512,1024]{1,0:T(8,128)(2,1)S(1)} %slice_bitcast_fusion.3.refs_1_, bf16[512,1024]{1,0:T(8,128)(2,1)} %get-tuple-element.219.refs_2_, bf16[4,2,512,512]{3,2,1,0:T(8,128)(2,1)S(1)} %get-tuple-element.220.refs_3_, ...), custom_call_target="tpu_custom_call" | custom-call | flops 8589934592 | bytes 18874368 | tf_op jit(solution)/shard_map/cond/branch_1_fun/g_gate_up/pallas_call | solution.py:466
  436.6 4.6 collective-permute-done.36
  445.7 8.3 %ffn_out.1 = (f32[2,128,1024]{2,1,0:T(8,128)}, bf16[2,128,1024]{2,1,0:T(8,128)(2,1)}, bf16[2,128,1024]{2,1,0:T(8,128)(2,1)S(1)}, bf16[2,64,1024]{2,1,0:T(8,128)(2,1)}, bf16[2,64,1024]{2,1,0:T(8,128)(2,1)}) custom-call(bf16[4,512,512]{2,1,0:T(8,128)(2,1)S(1)} %get-tuple-element.222.refs_0_, bf16[4,1024,512]{2,1,0:T(8,128)(2,1)} %get-tuple-element.223.refs_1_, ...), custom_call_target="tpu_custom_call" | custom-call | flops 4294967296 | bytes 12582912 | tf_op jit(solution)/shard_map/cond/branch_1_fun/ffn_out/pallas_call | solution.py:57
  454.0 3.9 collective-permute-done.38
  460.0 5.1 dmix.1
  465.1 15.1 %conditional.16 = (bf16[512,128]{1,0:T(8,128)(2,1)S(1)}, bf16[512,128]{1,0:T(8,128)(2,1)}, bf16[512,128]{1,0:T(8,128)(2,1)}, bf16[512,128]{1,0:T(8,128)(2,1)}, b...) conditional(s32[]{:T(128)} %bitcast.73, () %tuple.108, (bf16[512,128]{1,0:T(8,128)(2,1)S(1)}, ...), branch_computations={%region_18.19_spmd, %region_19.20_spmd} | conditional | bytes 3670264 | solution.py:746
  480.2 13.0 %attend_back.1 = (bf16[512,384]{1,0:T(8,128)(2,1)}, bf16[512,384]{1,0:T(8,128)(2,1)}, bf16[512,384]{1,0:T(8,128)(2,1)}, bf16[512,384]{1,0:T(8,128)(2,1)}) custom-call(s32[16]{0:T(128)S(1)} %and_select_fusion.2.tab_ref.refs_0_, bf16[512,128]{1,0:T(8,128)(2,1)S(1)} %get-tuple-element.420.refs_1_, bf16[512,128]{1,0:T(8,128)(2,1)} %get-tuple-element.421.refs_2_, ...), custom_call_target="tpu_custom_call" | custom-call | flops 5368709120 | bytes 12582912 | tf_op jit(solution)/shard_map/attend_back/pallas_call | solution.py:212
  493.2 53.8 %conditional.17 = (bf16[4,512,384]{2,1,0:T(8,128)(2,1)}, bf16[2,128,1024]{2,1,0:T(8,128)(2,1)S(1)}, bf16[4,256,512]{2,1,0:T(8,128)(2,1)}) conditional(s32[]{:T(128)} %bitcast.73, () %tuple.107, (bf16[512,384]{1,0:T(8,128)(2,1)}, bf16[512,384]{1,0:T(8,128)(2,1)}, bf16[512,384]{1,0:T(8,128)(2,1)}, bf16[512,384]{1,0:T(8,128)(2,1)}, ...), branch_computations={%region_21.22_spmd, %region_22.23_spmd} | conditional | flops 6291456 | bytes 25166108 | solution.py:746
  493.2 4.2 all-to-all-start.2
  505.4 12.8 %collective-permute-done.62 = bf16[512,384]{1,0:T(8,128)(2,1)S(1)} collective-permute-done((bf16[512,384]{1,0:T(8,128)(2,1)}, bf16[512,384]{1,0:T(8,128)(2,1)S(1)}, u32[]{:S(2)}, u32[]{:S(2)}) %collective-permute-start.62) | collective-permute-done | bytes 393248 | tf_op jit(solution)/shard_map/cond/branch_1_fun/ppermute | solution.py:590
  519.5 14.9 %collective-permute-done.64 = bf16[512,384]{1,0:T(8,128)(2,1)S(1)} collective-permute-done((bf16[512,384]{1,0:T(8,128)(2,1)}, bf16[512,384]{1,0:T(8,128)(2,1)S(1)}, u32[]{:S(2)}, u32[]{:S(2)}) %collective-permute-start.64) | collective-permute-done | bytes 393248 | tf_op jit(solution)/shard_map/cond/branch_1_fun/ppermute | solution.py:590
  535.8 9.7 %collective-permute-done.65 = bf16[2,128,1024]{2,1,0:T(8,128)(2,1)S(1)} collective-permute-done((bf16[2,128,1024]{2,1,0:T(8,128)(2,1)S(1)}, bf16[2,128,1024]{2,1,0:T(8,128)(2,1)S(1)}, u32[]{:S(2)}, u32[]{:S(2)}) %collective-permute-start.65) | collective-permute-done | bytes 524320 | tf_op jit(solution)/shard_map/cond/branch_1_fun/ppermute | solution.py:634
  547.0 7.5 %dxn1.1 = (f32[2,128,1024]{2,1,0:T(8,128)S(1)}, bf16[2,128,1024]{2,1,0:T(8,128)(2,1)S(1)}, bf16[2,128,1024]{2,1,0:T(8,128)(2,1)S(1)}, bf16[2,64,1024]{2,1,0:T(8,128)(2,1)S(1)}, bf16[2,64,1024]{2,1,0:T(8,128)(2,1)S(1)}) custom-call(bf16[4,512,384]{2,1,0:T(8,128)(2,1)} %get-tuple-element.437.refs_0_, bf16[4,1024,512]{2,1,0:T(8,128)(2,1)} %get-tuple-element.372.refs_1_, ...), custom_call_target="tpu_custom_call" | custom-call | flops 3221225472 | bytes 9961472 | tf_op jit(solution)/shard_map/dxn1/pallas_call | solution.py:57
  554.6 55.2 %conditional.18 = (f32[2,128,1024]{2,1,0:T(8,128)S(1)}, bf16[512,512]{1,0:T(8,128)(2,1)}, bf16[512,512]{1,0:T(8,128)(2,1)}, bf16[512,512]{1,0:T(8,128)(2,1)}, bf16[512,512]{1,0:T(8,128)(2,1)S(1)}) conditional(s32[]{:T(128)} %bitcast.73, () %tuple.106, (bf16[2,128,1024]{2,1,0:T(8,128)(2,1)S(1)}, bf16[2,64,1024]{2,1,0:T(8,128)(2,1)S(1)}, ...), branch_computations={%region_23.24_spmd, %region_24.25_spmd} | conditional | flops 4299948032 | bytes 95945200 | solution.py:746
  559.4 8.2 %collective-permute-done.69 = bf16[2,64,1024]{2,1,0:T(8,128)(2,1)S(1)} collective-permute-done((bf16[2,64,1024]{2,1,0:T(8,128)(2,1)S(1)}, bf16[2,64,1024]{2,1,0:T(8,128)(2,1)S(1)}, u32[]{:S(2)}, u32[]{:S(2)}) %collective-permute-start.69) | collective-permute-done | bytes 262176 | tf_op jit(solution)/shard_map/cond/branch_1_fun/ppermute | solution.py:620
  571.9 9.7 %g_heads.1 = bf16[4,1024,512]{2,1,0:T(8,128)(2,1)} custom-call(bf16[512,1024]{1,0:T(8,128)(2,1)S(1)} %get-tuple-element.505.refs_0_, bf16[512,1024]{1,0:T(8,128)(2,1)S(1)} %collective-permute-done.71.refs_1_, bf16[4,512,384]{2,1,0:T(8,128)(2,1)} %get-tuple-element.253.refs_2_, bf16[4,512,384]{2,1,0:T(8,128)(2,1)} %copy-done.45, ...), custom_call_target="tpu_custom_call" | custom-call | flops 4294967296 | bytes 12582912 | tf_op jit(solution)/shard_map/cond/branch_1_fun/g_heads/pallas_call | solution.py:57
  587.9 11.6 %collective-permute-done.68 = bf16[2,128,1024]{2,1,0:T(8,128)(2,1)S(1)} collective-permute-done((bf16[2,128,1024]{2,1,0:T(8,128)(2,1)S(1)}, bf16[2,128,1024]{2,1,0:T(8,128)(2,1)S(1)}, u32[]{:S(2)}, u32[]{:S(2)}) %collective-permute-start.68) | collective-permute-done | bytes 524320 | tf_op jit(solution)/shard_map/cond/branch_1_fun/ppermute | solution.py:634
  599.8 8.8 %collective-permute-done.75 = bf16[2,512,512]{2,1,0:T(8,128)(2,1)S(1)} collective-permute-done((bf16[2,512,512]{2,1,0:T(8,128)(2,1)S(1)}, bf16[2,512,512]{2,1,0:T(8,128)(2,1)S(1)}, u32[]{:S(2)}, u32[]{:S(2)}) %collective-permute-start.75) | collective-permute-done | bytes 1048608 | tf_op jit(solution)/shard_map/cond/branch_1_fun/ppermute | solution.py:590
  610.9 3.6 all-to-all-start.6
  617.4 4.6 all-to-all-done.6
  623.6 85.9 %conditional.19 = (f32[512,2048]{1,0:T(8,128)}, bf16[512,2048]{1,0:T(8,128)(2,1)}, f32[256,2048]{1,0:T(8,128)}, f32[256,2048]{1,0:T(8,128)}, f32[2048,256]{1,0:T(8,128)}, /*index=5*/bf16[4,256,512]{2,1,0:T(8,128)(2,1)}) conditional(s32[]{:T(128)} %bitcast.73, () %tuple.95, (s32[4]{0:T(128)S(1)}, s32[]{:T(128)}, s32[]{:T(128)}, ...), branch_computations={%region_27.28_spmd, %region_28.29_spmd} | conditional | flops 9177157 | bytes 99617792 | solution.py:746
  623.6 3.6 all-to-all-start
  640.8 8.4 %collective-permute-done.49 = bf16[128,2048]{1,0:T(8,128)(2,1)S(1)} collective-permute-done((bf16[128,2048]{1,0:T(8,128)(2,1)}, bf16[128,2048]{1,0:T(8,128)(2,1)S(1)}, u32[]{:S(2)}, u32[]{:S(2)}) %collective-permute-start.49) | collective-permute-done | bytes 524320 | tf_op jit(solution)/shard_map/cond/branch_1_fun/ppermute | solution.py:590
  652.1 8.5 %collective-permute-done.44 = bf16[128,2048]{1,0:T(8,128)(2,1)} collective-permute-done((bf16[128,2048]{1,0:T(8,128)(2,1)}, bf16[128,2048]{1,0:T(8,128)(2,1)}, u32[]{:S(2)}, u32[]{:S(2)}) %collective-permute-start.44) | collective-permute-done | bytes 524320 | tf_op jit(solution)/shard_map/cond/branch_1_fun/ppermute | solution.py:590
  667.9 3.8 collective-permute-done.53
  679.7 5.1 all-to-all-start.1
  692.0 3.8 unpack_down.1
  699.0 3.6 place.3
  702.6 4.6 place.2
  (444 shorter events, 241.6 us)
Async XLA Ops:
  15.2 32.3 %all-to-all-start.3 = ((bf16[4,256,512]{2,1,0:T(8,128)(2,1)}), bf16[4,256,512]{2,1,0:T(8,128)(2,1)S(1)}, u32[]{:S(2)}, u32[]{:S(2)}) async-start(bf16[4,256,512]{2,1,0:T(8,128)(2,1)} %pack_heads.1), calls=%async_computation.3 | async-start | bytes 2097152 | tf_op jit(solution)/shard_map/all_to_all | solution.py:698
  49.0 29.2 %collective-permute-start.10 = (bf16[1024,512]{1,0:T(8,128)(2,1)S(1)}, bf16[1024,512]{1,0:T(8,128)(2,1)S(1)}, u32[]{:S(2)}, u32[]{:S(2)}) collective-permute-start(bf16[1024,512]{1,0:T(8,128)(2,1)S(1)} %get-tuple-element.180), channel_id=1, source_target_pairs={{0,2},{1,3},{2,0},{3,1},{4,6},{5,7},{6,4},{7,5},{8,10},{9,11},{10,... | collective-permute-start | bytes 3145736 | tf_op jit(solution)/shard_map/cond/branch_1_fun/ppermute | solution.py:590
  50.6 28.3 %collective-permute-start.9 = (bf16[1024,512]{1,0:T(8,128)(2,1)S(1)}, bf16[1024,512]{1,0:T(8,128)(2,1)S(1)}, u32[]{:S(2)}, u32[]{:S(2)}) collective-permute-start(bf16[1024,512]{1,0:T(8,128)(2,1)S(1)} %get-tuple-element.180), channel_id=1, source_target_pairs={{0,1},{1,0},{2,3},{3,2},{4,5},{5,4},{6,7},{7,6},{8,9},{9,8},{10,11... | collective-permute-start | bytes 3145736 | tf_op jit(solution)/shard_map/cond/branch_1_fun/ppermute | solution.py:590
  52.1 23.6 %collective-permute-start.6 = (bf16[2,128,1024]{2,1,0:T(8,128)(2,1)S(1)}, bf16[2,128,1024]{2,1,0:T(8,128)(2,1)S(1)}, u32[]{:S(2)}, u32[]{:S(2)}) collective-permute-start(bf16[2,128,1024]{2,1,0:T(8,128)(2,1)S(1)} %get-tuple-element.178), channel_id=1, source_target_pairs={{8,0},{24,8},{16,24},{0,16},{9,1},{25,9},{17,25},{1,17},{10,2},{26... | collective-permute-start | bytes 1572872 | tf_op jit(solution)/shard_map/cond/branch_1_fun/ppermute | solution.py:600
  52.1 24.8 %collective-permute-start.5 = (bf16[2,128,1024]{2,1,0:T(8,128)(2,1)S(1)}, bf16[2,128,1024]{2,1,0:T(8,128)(2,1)S(1)}, u32[]{:S(2)}, u32[]{:S(2)}) collective-permute-start(bf16[2,128,1024]{2,1,0:T(8,128)(2,1)S(1)} %get-tuple-element.178), channel_id=1, source_target_pairs={{0,8},{8,24},{24,16},{16,0},{1,9},{9,25},{25,17},{17,1},{2,10},{10... | collective-permute-start | bytes 1572872 | tf_op jit(solution)/shard_map/cond/branch_1_fun/ppermute | solution.py:599
  78.2 16.7 %collective-permute-start.12 = (bf16[512,512]{1,0:T(8,128)(2,1)S(1)}, bf16[512,512]{1,0:T(8,128)(2,1)S(1)}, u32[]{:S(2)}, u32[]{:S(2)}) collective-permute-start(bf16[512,512]{1,0:T(8,128)(2,1)S(1)} %fusion.6), channel_id=1, source_target_pairs={{0,1},{1,0},{2,3},{3,2},{4,5},{5,4},{6,7},{7,6},{8,9},{9,8},{10,11... | collective-permute-start | bytes 1572872 | tf_op jit(solution)/shard_map/cond/branch_1_fun/ppermute | solution.py:590
  78.9 16.1 %collective-permute-start.13 = (bf16[512,512]{1,0:T(8,128)(2,1)S(1)}, bf16[512,512]{1,0:T(8,128)(2,1)S(1)}, u32[]{:S(2)}, u32[]{:S(2)}) collective-permute-start(bf16[512,512]{1,0:T(8,128)(2,1)S(1)} %fusion.4), channel_id=1, source_target_pairs={{0,2},{1,3},{2,0},{3,1},{4,6},{5,7},{6,4},{7,5},{8,10},{9,11},{10,... | collective-permute-start | bytes 1572872 | tf_op jit(solution)/shard_map/cond/branch_1_fun/ppermute | solution.py:590
  108.7 55.4 %all-to-all-start.4 = ((bf16[4,256,1024]{2,1,0:T(8,128)(2,1)}), bf16[4,256,1024]{2,1,0:T(8,128)(2,1)}, u32[]{:S(2)}, u32[]{:S(2)}) async-start(bf16[4,256,1024]{2,1,0:T(8,128)(2,1)} %get-tuple-element.389), calls=%async_computation.4 | async-start | bytes 4194304 | tf_op jit(solution)/shard_map/all_to_all | solution.py:698
  123.2 19.3 %collective-permute-start.86 = (bf16[512,384]{1,0:T(8,128)(2,1)S(1)}, bf16[512,384]{1,0:T(8,128)(2,1)S(1)}, u32[]{:S(2)}, u32[]{:S(2)}) collective-permute-start(bf16[512,384]{1,0:T(8,128)(2,1)S(1)} %get-tuple-element.376), channel_id=1, source_target_pairs={{0,2},{1,3},{2,0},{3,1},{4,6},{5,7},{6,4},{7,5},{8,10},{9,11},{10,... | collective-permute-start | bytes 1179656 | tf_op jit(solution)/shard_map/ppermute | solution.py:590
  124.8 17.8 %collective-permute-start.87 = (bf16[512,384]{1,0:T(8,128)(2,1)S(1)}, bf16[512,384]{1,0:T(8,128)(2,1)S(1)}, u32[]{:S(2)}, u32[]{:S(2)}) collective-permute-start(bf16[512,384]{1,0:T(8,128)(2,1)S(1)} %get-tuple-element.377), channel_id=1, source_target_pairs={{0,3},{1,2},{2,1},{3,0},{4,7},{5,6},{6,5},{7,4},{8,11},{9,10},{10,... | collective-permute-start | bytes 1179656 | tf_op jit(solution)/shard_map/ppermute | solution.py:590
  164.2 45.9 %collective-permute-start.82 = (bf16[1024,1024]{1,0:T(8,128)(2,1)}, bf16[1024,1024]{1,0:T(8,128)(2,1)}, u32[]{:S(2)}, u32[]{:S(2)}) collective-permute-start(bf16[1024,1024]{1,0:T(8,128)(2,1)} %bitcast.13), channel_id=1, source_target_pairs={{0,2},{1,3},{2,0},{3,1},{4,6},{5,7},{6,4},{7,5},{8,10},{9,11},{10,... | collective-permute-start | bytes 6291464 | tf_op jit(solution)/shard_map/cond/branch_1_fun/ppermute | solution.py:590
  165.5 45.8 %collective-permute-start.81 = (bf16[1024,1024]{1,0:T(8,128)(2,1)}, bf16[1024,1024]{1,0:T(8,128)(2,1)}, u32[]{:S(2)}, u32[]{:S(2)}) collective-permute-start(bf16[1024,1024]{1,0:T(8,128)(2,1)} %bitcast.13), channel_id=1, source_target_pairs={{0,1},{1,0},{2,3},{3,2},{4,5},{5,4},{6,7},{7,6},{8,9},{9,8},{10,11... | collective-permute-start | bytes 6291464 | tf_op jit(solution)/shard_map/cond/branch_1_fun/ppermute | solution.py:590
  168.8 17.7 %collective-permute-start.77 = (bf16[2,64,1024]{2,1,0:T(8,128)(2,1)}, bf16[2,64,1024]{2,1,0:T(8,128)(2,1)S(1)}, u32[]{:S(2)}, u32[]{:S(2)}) collective-permute-start(bf16[2,64,1024]{2,1,0:T(8,128)(2,1)} %get-tuple-element.191), channel_id=1, source_target_pairs={{0,8},{8,24},{24,16},{16,0},{1,9},{9,25},{25,17},{17,1},{2,10},{10... | collective-permute-start | bytes 786440 | tf_op jit(solution)/shard_map/cond/branch_1_fun/ppermute | solution.py:619
  178.0 15.2 %collective-permute-start.80 = (bf16[2,128,1024]{2,1,0:T(8,128)(2,1)S(1)}, bf16[2,128,1024]{2,1,0:T(8,128)(2,1)S(1)}, u32[]{:S(2)}, u32[]{:S(2)}) collective-permute-start(bf16[2,128,1024]{2,1,0:T(8,128)(2,1)S(1)} %pad_maximum_fusion.3), channel_id=1, source_target_pairs={{8,0},{24,8},{16,24},{0,16},{9,1},{25,9},{17,25},{1,17},{10,2},{26... | collective-permute-start | bytes 1572872 | tf_op jit(solution)/shard_map/cond/branch_1_fun/ppermute | solution.py:635
  186.6 15.3 %collective-permute-start.78 = (bf16[2,128,1024]{2,1,0:T(8,128)(2,1)S(1)}, bf16[2,128,1024]{2,1,0:T(8,128)(2,1)S(1)}, u32[]{:S(2)}, u32[]{:S(2)}) collective-permute-start(bf16[2,128,1024]{2,1,0:T(8,128)(2,1)S(1)} %pad_maximum_fusion.2), channel_id=1, source_target_pairs={{0,8},{8,24},{24,16},{16,0},{1,9},{9,25},{25,17},{17,1},{2,10},{10... | collective-permute-start | bytes 1572872 | tf_op jit(solution)/shard_map/cond/branch_1_fun/ppermute | solution.py:634
  211.4 80.2 %all-to-all-start.5 = ((bf16[4,256,512]{2,1,0:T(8,128)(2,1)}), bf16[4,256,512]{2,1,0:T(8,128)(2,1)}, u32[]{:S(2)}, u32[]{:S(2)}) async-start(bf16[4,256,512]{2,1,0:T(8,128)(2,1)} %tie.3), calls=%async_computation.5 | async-start | bytes 2097152 | tf_op jit(solution)/shard_map/all_to_all | solution.py:698
  216.3 276.9 %reduce-scatter.7.cloned.1.call-start = ((), (), s32[]{:S(2)}) async-start(), calls=%async_computation.9 | async-start | bytes 5242880
  225.3 39.1 %collective-permute-start.21 = (bf16[512,1024]{1,0:T(8,128)(2,1)S(1)}, bf16[512,1024]{1,0:T(8,128)(2,1)S(1)}, u32[]{:S(2)}, u32[]{:S(2)}) collective-permute-start(bf16[512,1024]{1,0:T(8,128)(2,1)S(1)} %slice_add_fusion.7), channel_id=1, source_target_pairs={{0,1},{1,0},{2,3},{3,2},{4,5},{5,4},{6,7},{7,6},{8,9},{9,8},{10,11... | collective-permute-start | bytes 3145736 | tf_op jit(solution)/shard_map/cond/branch_1_fun/ppermute | solution.py:590
  225.9 38.5 %collective-permute-start.22 = (bf16[512,1024]{1,0:T(8,128)(2,1)S(1)}, bf16[512,1024]{1,0:T(8,128)(2,1)S(1)}, u32[]{:S(2)}, u32[]{:S(2)}) collective-permute-start(bf16[512,1024]{1,0:T(8,128)(2,1)S(1)} %slice_add_fusion.6), channel_id=1, source_target_pairs={{0,2},{1,3},{2,0},{3,1},{4,6},{5,7},{6,4},{7,5},{8,10},{9,11},{10,... | collective-permute-start | bytes 3145736 | tf_op jit(solution)/shard_map/cond/branch_1_fun/ppermute | solution.py:590
  226.9 16.3 %collective-permute-start.17 = (bf16[2,128,1024]{2,1,0:T(8,128)(2,1)S(1)}, bf16[2,128,1024]{2,1,0:T(8,128)(2,1)S(1)}, u32[]{:S(2)}, u32[]{:S(2)}) collective-permute-start(bf16[2,128,1024]{2,1,0:T(8,128)(2,1)S(1)} %get-tuple-element.195), channel_id=1, source_target_pairs={{8,0},{24,8},{16,24},{0,16},{9,1},{25,9},{17,25},{1,17},{10,2},{26... | collective-permute-start | bytes 1572872 | tf_op jit(solution)/shard_map/cond/branch_1_fun/ppermute | solution.py:600
  229.7 32.2 %collective-permute-start.16 = (bf16[2,128,1024]{2,1,0:T(8,128)(2,1)S(1)}, bf16[2,128,1024]{2,1,0:T(8,128)(2,1)S(1)}, u32[]{:S(2)}, u32[]{:S(2)}) collective-permute-start(bf16[2,128,1024]{2,1,0:T(8,128)(2,1)S(1)} %get-tuple-element.195), channel_id=1, source_target_pairs={{0,8},{8,24},{24,16},{16,0},{1,9},{9,25},{25,17},{17,1},{2,10},{10... | collective-permute-start | bytes 1572872 | tf_op jit(solution)/shard_map/cond/branch_1_fun/ppermute | solution.py:599
  243.2 18.7 %collective-permute-start.24 = (bf16[16,128]{1,0:T(8,128)(2,1)S(1)}, bf16[16,128]{1,0:T(8,128)(2,1)S(1)}, u32[]{:S(2)}, u32[]{:S(2)}) collective-permute-start(bf16[16,128]{1,0:T(8,128)(2,1)S(1)} %slice.371), channel_id=1, source_target_pairs={{0,4},{4,0},{1,5},{5,1},{2,6},{6,2},{3,7},{7,3},{8,12},{12,8},{9,1... | collective-permute-start | bytes 12296 | tf_op jit(solution)/shard_map/cond/branch_1_fun/ppermute | solution.py:593
  271.4 20.1 %collective-permute-start.25 = (bf16[4,1024,1024]{2,1,0:T(8,128)(2,1)}, bf16[4,1024,1024]{2,1,0:T(8,128)(2,1)}, u32[]{:S(2)}, u32[]{:S(2)}) collective-permute-start(bf16[4,1024,1024]{2,1,0:T(8,128)(2,1)} %fusion.8), channel_id=1, source_target_pairs={{0,4},{4,0},{1,5},{5,1},{2,6},{6,2},{3,7},{7,3},{8,12},{12,8},{9,1... | collective-permute-start | bytes 25165832 | tf_op jit(solution)/shard_map/cond/branch_1_fun/ppermute | solution.py:593
  275.3 14.8 %collective-permute-start.18 = (bf16[2,64,1024]{2,1,0:T(8,128)(2,1)S(1)}, bf16[2,64,1024]{2,1,0:T(8,128)(2,1)S(1)}, u32[]{:S(2)}, u32[]{:S(2)}) collective-permute-start(bf16[2,64,1024]{2,1,0:T(8,128)(2,1)S(1)} %slice_add_fusion.9), channel_id=1, source_target_pairs={{0,8},{8,24},{24,16},{16,0},{1,9},{9,25},{25,17},{17,1},{2,10},{10... | collective-permute-start | bytes 786440 | tf_op jit(solution)/shard_map/cond/branch_1_fun/ppermute | solution.py:607
  275.4 15.5 %collective-permute-start.19 = (bf16[2,64,1024]{2,1,0:T(8,128)(2,1)S(1)}, bf16[2,64,1024]{2,1,0:T(8,128)(2,1)S(1)}, u32[]{:S(2)}, u32[]{:S(2)}) collective-permute-start(bf16[2,64,1024]{2,1,0:T(8,128)(2,1)S(1)} %slice_add_fusion.8), channel_id=1, source_target_pairs={{8,0},{24,8},{16,24},{0,16},{9,1},{25,9},{17,25},{1,17},{10,2},{26... | collective-permute-start | bytes 786440 | tf_op jit(solution)/shard_map/cond/branch_1_fun/ppermute | solution.py:608
  291.6 27.7 %collective-permute-start.31 = (bf16[1024,512]{1,0:T(8,128)(2,1)}, bf16[1024,512]{1,0:T(8,128)(2,1)S(1)}, u32[]{:S(2)}, u32[]{:S(2)}) collective-permute-start(bf16[1024,512]{1,0:T(8,128)(2,1)} %bitcast.31), channel_id=1, source_target_pairs={{0,2},{1,3},{2,0},{3,1},{4,6},{5,7},{6,4},{7,5},{8,10},{9,11},{10,... | collective-permute-start | bytes 3145736 | tf_op jit(solution)/shard_map/cond/branch_1_fun/ppermute | solution.py:590
  292.2 28.3 %collective-permute-start.30 = (bf16[1024,512]{1,0:T(8,128)(2,1)}, bf16[1024,512]{1,0:T(8,128)(2,1)S(1)}, u32[]{:S(2)}, u32[]{:S(2)}) collective-permute-start(bf16[1024,512]{1,0:T(8,128)(2,1)} %bitcast.31), channel_id=1, source_target_pairs={{0,1},{1,0},{2,3},{3,2},{4,5},{5,4},{6,7},{7,6},{8,9},{9,8},{10,11... | collective-permute-start | bytes 3145736 | tf_op jit(solution)/shard_map/cond/branch_1_fun/ppermute | solution.py:590
  293.2 23.7 %collective-permute-start.27 = (bf16[2,128,1024]{2,1,0:T(8,128)(2,1)S(1)}, bf16[2,128,1024]{2,1,0:T(8,128)(2,1)S(1)}, u32[]{:S(2)}, u32[]{:S(2)}) collective-permute-start(bf16[2,128,1024]{2,1,0:T(8,128)(2,1)S(1)} %get-tuple-element.199), channel_id=1, source_target_pairs={{8,0},{24,8},{16,24},{0,16},{9,1},{25,9},{17,25},{1,17},{10,2},{26... | collective-permute-start | bytes 1572872 | tf_op jit(solution)/shard_map/cond/branch_1_fun/ppermute | solution.py:600
  293.2 24.9 %collective-permute-start.26 = (bf16[2,128,1024]{2,1,0:T(8,128)(2,1)S(1)}, bf16[2,128,1024]{2,1,0:T(8,128)(2,1)S(1)}, u32[]{:S(2)}, u32[]{:S(2)}) collective-permute-start(bf16[2,128,1024]{2,1,0:T(8,128)(2,1)S(1)} %get-tuple-element.199), channel_id=1, source_target_pairs={{0,8},{8,24},{24,16},{16,0},{1,9},{9,25},{25,17},{17,1},{2,10},{10... | collective-permute-start | bytes 1572872 | tf_op jit(solution)/shard_map/cond/branch_1_fun/ppermute | solution.py:599
  319.4 18.2 %collective-permute-start.32 = (bf16[512,512]{1,0:T(8,128)(2,1)S(1)}, bf16[512,512]{1,0:T(8,128)(2,1)S(1)}, u32[]{:S(2)}, u32[]{:S(2)}) collective-permute-start(bf16[512,512]{1,0:T(8,128)(2,1)S(1)} %fusion.13), channel_id=1, source_target_pairs={{0,1},{1,0},{2,3},{3,2},{4,5},{5,4},{6,7},{7,6},{8,9},{9,8},{10,11... | collective-permute-start | bytes 1572872 | tf_op jit(solution)/shard_map/cond/branch_1_fun/ppermute | solution.py:590
  320.6 17.0 %collective-permute-start.33 = (bf16[512,512]{1,0:T(8,128)(2,1)S(1)}, bf16[512,512]{1,0:T(8,128)(2,1)S(1)}, u32[]{:S(2)}, u32[]{:S(2)}) collective-permute-start(bf16[512,512]{1,0:T(8,128)(2,1)S(1)} %fusion.11), channel_id=1, source_target_pairs={{0,2},{1,3},{2,0},{3,1},{4,6},{5,7},{6,4},{7,5},{8,10},{9,11},{10,... | collective-permute-start | bytes 1572872 | tf_op jit(solution)/shard_map/cond/branch_1_fun/ppermute | solution.py:590
  372.8 38.7 %collective-permute-start.61 = (bf16[4,2,512,512]{3,2,1,0:T(8,128)(2,1)}, bf16[4,2,512,512]{3,2,1,0:T(8,128)(2,1)}, u32[]{:S(2)}, u32[]{:S(2)}) collective-permute-start(bf16[4,2,512,512]{3,2,1,0:T(8,128)(2,1)} %get-tuple-element.215), channel_id=1, source_target_pairs={{0,4},{4,0},{1,5},{5,1},{2,6},{6,2},{3,7},{7,3},{8,12},{12,8},{9,1... | collective-permute-start | bytes 12582920 | tf_op jit(solution)/shard_map/cond/branch_1_fun/ppermute | solution.py:593
  373.0 15.5 %collective-permute-start.60 = (bf16[4,512,512]{2,1,0:T(8,128)(2,1)S(1)}, bf16[4,512,512]{2,1,0:T(8,128)(2,1)S(1)}, u32[]{:S(2)}, u32[]{:S(2)}) collective-permute-start(bf16[4,512,512]{2,1,0:T(8,128)(2,1)S(1)} %get-tuple-element.214), channel_id=1, source_target_pairs={{0,4},{4,0},{1,5},{5,1},{2,6},{6,2},{3,7},{7,3},{8,12},{12,8},{9,1... | collective-permute-start | bytes 6291464 | tf_op jit(solution)/shard_map/cond/branch_1_fun/ppermute | solution.py:593
  382.0 17.6 %collective-permute-start.58 = (bf16[2,128,1024]{2,1,0:T(8,128)(2,1)S(1)}, bf16[2,128,1024]{2,1,0:T(8,128)(2,1)S(1)}, u32[]{:S(2)}, u32[]{:S(2)}) collective-permute-start(bf16[2,128,1024]{2,1,0:T(8,128)(2,1)S(1)} %pad_maximum_fusion.5), channel_id=1, source_target_pairs={{8,0},{24,8},{16,24},{0,16},{9,1},{25,9},{17,25},{1,17},{10,2},{26... | collective-permute-start | bytes 1572872 | tf_op jit(solution)/shard_map/cond/branch_1_fun/ppermute | solution.py:635
  388.4 21.9 %collective-permute-start.56 = (bf16[2,128,1024]{2,1,0:T(8,128)(2,1)S(1)}, bf16[2,128,1024]{2,1,0:T(8,128)(2,1)S(1)}, u32[]{:S(2)}, u32[]{:S(2)}) collective-permute-start(bf16[2,128,1024]{2,1,0:T(8,128)(2,1)S(1)} %pad_maximum_fusion.4), channel_id=1, source_target_pairs={{0,8},{8,24},{24,16},{16,0},{1,9},{9,25},{25,17},{17,1},{2,10},{10... | collective-permute-start | bytes 1572872 | tf_op jit(solution)/shard_map/cond/branch_1_fun/ppermute | solution.py:634
  411.6 211.0 %reduce-scatter.9.cloned.1.call-start = ((), (), s32[]{:S(2)}) async-start(), calls=%async_computation.10 | async-start | bytes 10485760
  416.1 18.6 %collective-permute-start.37 = (bf16[2,128,1024]{2,1,0:T(8,128)(2,1)S(1)}, bf16[2,128,1024]{2,1,0:T(8,128)(2,1)S(1)}, u32[]{:S(2)}, u32[]{:S(2)}) collective-permute-start(bf16[2,128,1024]{2,1,0:T(8,128)(2,1)S(1)} %get-tuple-element.216), channel_id=1, source_target_pairs={{8,0},{24,8},{16,24},{0,16},{9,1},{25,9},{17,25},{1,17},{10,2},{26... | collective-permute-start | bytes 1572872 | tf_op jit(solution)/shard_map/cond/branch_1_fun/ppermute | solution.py:600
  416.7 24.5 %collective-permute-start.36 = (bf16[2,128,1024]{2,1,0:T(8,128)(2,1)S(1)}, bf16[2,128,1024]{2,1,0:T(8,128)(2,1)S(1)}, u32[]{:S(2)}, u32[]{:S(2)}) collective-permute-start(bf16[2,128,1024]{2,1,0:T(8,128)(2,1)S(1)} %get-tuple-element.216), channel_id=1, source_target_pairs={{0,8},{8,24},{24,16},{16,0},{1,9},{9,25},{25,17},{17,1},{2,10},{10... | collective-permute-start | bytes 1572872 | tf_op jit(solution)/shard_map/cond/branch_1_fun/ppermute | solution.py:599
  442.6 15.3 %collective-permute-start.38 = (bf16[2,64,1024]{2,1,0:T(8,128)(2,1)S(1)}, bf16[2,64,1024]{2,1,0:T(8,128)(2,1)S(1)}, u32[]{:S(2)}, u32[]{:S(2)}) collective-permute-start(bf16[2,64,1024]{2,1,0:T(8,128)(2,1)S(1)} %slice_add_fusion.17), channel_id=1, source_target_pairs={{0,8},{8,24},{24,16},{16,0},{1,9},{9,25},{25,17},{17,1},{2,10},{10... | collective-permute-start | bytes 786440 | tf_op jit(solution)/shard_map/cond/branch_1_fun/ppermute | solution.py:607
  443.0 14.9 %collective-permute-start.39 = (bf16[2,64,1024]{2,1,0:T(8,128)(2,1)S(1)}, bf16[2,64,1024]{2,1,0:T(8,128)(2,1)S(1)}, u32[]{:S(2)}, u32[]{:S(2)}) collective-permute-start(bf16[2,64,1024]{2,1,0:T(8,128)(2,1)S(1)} %slice_add_fusion.16), channel_id=1, source_target_pairs={{8,0},{24,8},{16,24},{0,16},{9,1},{25,9},{17,25},{1,17},{10,2},{26... | collective-permute-start | bytes 786440 | tf_op jit(solution)/shard_map/cond/branch_1_fun/ppermute | solution.py:608
  465.2 14.9 %collective-permute-start.3 = (bf16[2,64,1024]{2,1,0:T(8,128)(2,1)}, bf16[2,64,1024]{2,1,0:T(8,128)(2,1)}, u32[]{:S(2)}, u32[]{:S(2)}) collective-permute-start(bf16[2,64,1024]{2,1,0:T(8,128)(2,1)} %get-tuple-element.234), channel_id=1, source_target_pairs={{0,8},{8,24},{24,16},{16,0},{1,9},{9,25},{25,17},{17,1},{2,10},{10... | collective-permute-start | bytes 786440 | tf_op jit(solution)/shard_map/cond/branch_1_fun/ppermute | solution.py:619
  493.2 53.8 %all-to-all-start.2 = ((bf16[4,256,512]{2,1,0:T(8,128)(2,1)}), bf16[4,256,512]{2,1,0:T(8,128)(2,1)}, u32[]{:S(2)}, u32[]{:S(2)}) async-start(bf16[4,256,512]{2,1,0:T(8,128)(2,1)} %bitcast.142), calls=%async_computation.2 | async-start | bytes 2097152 | tf_op jit(solution)/shard_map/cond/branch_1_fun/all_to_all | solution.py:698
  497.5 20.7 %collective-permute-start.62 = (bf16[512,384]{1,0:T(8,128)(2,1)}, bf16[512,384]{1,0:T(8,128)(2,1)S(1)}, u32[]{:S(2)}, u32[]{:S(2)}) collective-permute-start(bf16[512,384]{1,0:T(8,128)(2,1)} %get-tuple-element.237), channel_id=1, source_target_pairs={{0,1},{1,0},{2,3},{3,2},{4,5},{5,4},{6,7},{7,6},{8,9},{9,8},{10,11... | collective-permute-start | bytes 1179656 | tf_op jit(solution)/shard_map/cond/branch_1_fun/ppermute | solution.py:590
  498.3 21.2 %collective-permute-start.63 = (bf16[512,384]{1,0:T(8,128)(2,1)}, bf16[512,384]{1,0:T(8,128)(2,1)S(1)}, u32[]{:S(2)}, u32[]{:S(2)}) collective-permute-start(bf16[512,384]{1,0:T(8,128)(2,1)} %get-tuple-element.238), channel_id=1, source_target_pairs={{0,2},{1,3},{2,0},{3,1},{4,6},{5,7},{6,4},{7,5},{8,10},{9,11},{10,... | collective-permute-start | bytes 1179656 | tf_op jit(solution)/shard_map/cond/branch_1_fun/ppermute | solution.py:590
  499.3 35.1 %collective-permute-start.64 = (bf16[512,384]{1,0:T(8,128)(2,1)}, bf16[512,384]{1,0:T(8,128)(2,1)S(1)}, u32[]{:S(2)}, u32[]{:S(2)}) collective-permute-start(bf16[512,384]{1,0:T(8,128)(2,1)} %get-tuple-element.239), channel_id=1, source_target_pairs={{0,3},{1,2},{2,1},{3,0},{4,7},{5,6},{6,5},{7,4},{8,11},{9,10},{10,... | collective-permute-start | bytes 1179656 | tf_op jit(solution)/shard_map/cond/branch_1_fun/ppermute | solution.py:590
  502.4 33.3 %collective-permute-start.66 = (bf16[2,128,1024]{2,1,0:T(8,128)(2,1)S(1)}, bf16[2,128,1024]{2,1,0:T(8,128)(2,1)S(1)}, u32[]{:S(2)}, u32[]{:S(2)}) collective-permute-start(bf16[2,128,1024]{2,1,0:T(8,128)(2,1)S(1)} %pad_maximum_fusion.8), channel_id=1, source_target_pairs={{8,0},{24,8},{16,24},{0,16},{9,1},{25,9},{17,25},{1,17},{10,2},{26... | collective-permute-start | bytes 1572872 | tf_op jit(solution)/shard_map/cond/branch_1_fun/ppermute | solution.py:635
  505.3 40.1 %collective-permute-start.65 = (bf16[2,128,1024]{2,1,0:T(8,128)(2,1)S(1)}, bf16[2,128,1024]{2,1,0:T(8,128)(2,1)S(1)}, u32[]{:S(2)}, u32[]{:S(2)}) collective-permute-start(bf16[2,128,1024]{2,1,0:T(8,128)(2,1)S(1)} %pad_maximum_fusion.7), channel_id=1, source_target_pairs={{0,8},{8,24},{24,16},{16,0},{1,9},{9,25},{25,17},{17,1},{2,10},{10... | collective-permute-start | bytes 1572872 | tf_op jit(solution)/shard_map/cond/branch_1_fun/ppermute | solution.py:634
  554.7 16.1 %collective-permute-start.72 = (bf16[4,512,384]{2,1,0:T(8,128)(2,1)}, bf16[4,512,384]{2,1,0:T(8,128)(2,1)S(1)}, u32[]{:S(2)}, u32[]{:S(2)}) collective-permute-start(bf16[4,512,384]{2,1,0:T(8,128)(2,1)} %get-tuple-element.253.refs_2_), channel_id=1, source_target_pairs={{0,4},{4,0},{1,5},{5,1},{2,6},{6,2},{3,7},{7,3},{8,12},{12,8},{9,1... | collective-permute-start | bytes 4718600 | tf_op jit(solution)/shard_map/cond/branch_1_fun/ppermute | solution.py:593
  567.7 20.1 %collective-permute-start.67 = (bf16[2,64,1024]{2,1,0:T(8,128)(2,1)S(1)}, bf16[2,64,1024]{2,1,0:T(8,128)(2,1)S(1)}, u32[]{:S(2)}, u32[]{:S(2)}) collective-permute-start(bf16[2,64,1024]{2,1,0:T(8,128)(2,1)S(1)} %get-tuple-element.249), channel_id=1, source_target_pairs={{0,8},{8,24},{24,16},{16,0},{1,9},{9,25},{25,17},{17,1},{2,10},{10... | collective-permute-start | bytes 786440 | tf_op jit(solution)/shard_map/cond/branch_1_fun/ppermute | solution.py:619
  568.4 19.5 %collective-permute-start.70 = (bf16[2,128,1024]{2,1,0:T(8,128)(2,1)S(1)}, bf16[2,128,1024]{2,1,0:T(8,128)(2,1)S(1)}, u32[]{:S(2)}, u32[]{:S(2)}) collective-permute-start(bf16[2,128,1024]{2,1,0:T(8,128)(2,1)S(1)} %pad_maximum_fusion.11), channel_id=1, source_target_pairs={{8,0},{24,8},{16,24},{0,16},{9,1},{25,9},{17,25},{1,17},{10,2},{26... | collective-permute-start | bytes 1572872 | tf_op jit(solution)/shard_map/cond/branch_1_fun/ppermute | solution.py:635
  584.3 24.3 %collective-permute-start.75 = (bf16[2,512,512]{2,1,0:T(8,128)(2,1)S(1)}, bf16[2,512,512]{2,1,0:T(8,128)(2,1)S(1)}, u32[]{:S(2)}, u32[]{:S(2)}) collective-permute-start(bf16[2,512,512]{2,1,0:T(8,128)(2,1)S(1)} %pad_maximum_fusion.9), channel_id=1, source_target_pairs={{0,1},{1,0},{2,3},{3,2},{4,5},{5,4},{6,7},{7,6},{8,9},{9,8},{10,11... | collective-permute-start | bytes 3145736 | tf_op jit(solution)/shard_map/cond/branch_1_fun/ppermute | solution.py:590
  584.4 24.2 %collective-permute-start.76 = (bf16[2,512,512]{2,1,0:T(8,128)(2,1)S(1)}, bf16[2,512,512]{2,1,0:T(8,128)(2,1)S(1)}, u32[]{:S(2)}, u32[]{:S(2)}) collective-permute-start(bf16[2,512,512]{2,1,0:T(8,128)(2,1)S(1)} %stack.133), channel_id=1, source_target_pairs={{0,2},{1,3},{2,0},{3,1},{4,6},{5,7},{6,4},{7,5},{8,10},{9,11},{10,... | collective-permute-start | bytes 3145736 | tf_op jit(solution)/shard_map/cond/branch_1_fun/ppermute | solution.py:590
  623.6 56.1 %all-to-all-start = ((bf16[4,256,1024]{2,1,0:T(8,128)(2,1)}), bf16[4,256,1024]{2,1,0:T(8,128)(2,1)S(1)}, u32[]{:S(2)}, u32[]{:S(2)}) async-start(bf16[4,256,1024]{2,1,0:T(8,128)(2,1)} %bitcast.137), calls=%async_computation | async-start | bytes 4194304 | tf_op jit(solution)/shard_map/cond/branch_1_fun/all_to_all | solution.py:698
  634.1 15.1 %collective-permute-start.49 = (bf16[128,2048]{1,0:T(8,128)(2,1)}, bf16[128,2048]{1,0:T(8,128)(2,1)S(1)}, u32[]{:S(2)}, u32[]{:S(2)}) collective-permute-start(bf16[128,2048]{1,0:T(8,128)(2,1)} %convert_element_type.300), channel_id=1, source_target_pairs={{0,2},{1,3},{2,0},{3,1},{4,6},{5,7},{6,4},{7,5},{8,10},{9,11},{10,... | collective-permute-start | bytes 1572872 | tf_op jit(solution)/shard_map/cond/branch_1_fun/ppermute | solution.py:590
  634.6 15.0 %collective-permute-start.48 = (bf16[128,2048]{1,0:T(8,128)(2,1)}, bf16[128,2048]{1,0:T(8,128)(2,1)S(1)}, u32[]{:S(2)}, u32[]{:S(2)}) collective-permute-start(bf16[128,2048]{1,0:T(8,128)(2,1)} %convert_element_type.300), channel_id=1, source_target_pairs={{0,1},{1,0},{2,3},{3,2},{4,5},{5,4},{6,7},{7,6},{8,9},{9,8},{10,11... | collective-permute-start | bytes 1572872 | tf_op jit(solution)/shard_map/cond/branch_1_fun/ppermute | solution.py:590
  637.6 23.0 %collective-permute-start.44 = (bf16[128,2048]{1,0:T(8,128)(2,1)}, bf16[128,2048]{1,0:T(8,128)(2,1)}, u32[]{:S(2)}, u32[]{:S(2)}) collective-permute-start(bf16[128,2048]{1,0:T(8,128)(2,1)} %convert_element_type.297), channel_id=1, source_target_pairs={{0,2},{1,3},{2,0},{3,1},{4,6},{5,7},{6,4},{7,5},{8,10},{9,11},{10,... | collective-permute-start | bytes 1572872 | tf_op jit(solution)/shard_map/cond/branch_1_fun/ppermute | solution.py:590
  638.8 26.7 %collective-permute-start.43 = (bf16[128,2048]{1,0:T(8,128)(2,1)}, bf16[128,2048]{1,0:T(8,128)(2,1)}, u32[]{:S(2)}, u32[]{:S(2)}) collective-permute-start(bf16[128,2048]{1,0:T(8,128)(2,1)} %convert_element_type.297), channel_id=1, source_target_pairs={{0,1},{1,0},{2,3},{3,2},{4,5},{5,4},{6,7},{7,6},{8,9},{9,8},{10,11... | collective-permute-start | bytes 1572872 | tf_op jit(solution)/shard_map/cond/branch_1_fun/ppermute | solution.py:590
  640.4 31.4 %collective-permute-start.53 = (bf16[512,512]{1,0:T(8,128)(2,1)}, bf16[512,512]{1,0:T(8,128)(2,1)}, u32[]{:S(2)}, u32[]{:S(2)}) collective-permute-start(bf16[512,512]{1,0:T(8,128)(2,1)} %get-tuple-element.267), channel_id=1, source_target_pairs={{0,2},{1,3},{2,0},{3,1},{4,6},{5,7},{6,4},{7,5},{8,10},{9,11},{10,... | collective-permute-start | bytes 1572872 | tf_op jit(solution)/shard_map/cond/branch_1_fun/ppermute | solution.py:590
  649.2 24.3 %collective-permute-start.54 = (bf16[512,512]{1,0:T(8,128)(2,1)}, bf16[512,512]{1,0:T(8,128)(2,1)}, u32[]{:S(2)}, u32[]{:S(2)}) collective-permute-start(bf16[512,512]{1,0:T(8,128)(2,1)} %get-tuple-element.269), channel_id=1, source_target_pairs={{0,1},{1,0},{2,3},{3,2},{4,5},{5,4},{6,7},{7,6},{8,9},{9,8},{10,11... | collective-permute-start | bytes 1572872 | tf_op jit(solution)/shard_map/cond/branch_1_fun/ppermute | solution.py:590
  649.6 28.2 %collective-permute-start.50 = (bf16[64,2048]{1,0:T(8,128)(2,1)S(1)}, bf16[64,2048]{1,0:T(8,128)(2,1)}, u32[]{:S(2)}, u32[]{:S(2)}) collective-permute-start(bf16[64,2048]{1,0:T(8,128)(2,1)S(1)} %slice.402), channel_id=1, source_target_pairs={{0,1},{1,0},{2,3},{3,2},{4,5},{5,4},{6,7},{7,6},{8,9},{9,8},{10,11... | collective-permute-start | bytes 786440 | tf_op jit(solution)/shard_map/cond/branch_1_fun/ppermute | solution.py:590
  660.5 17.3 %collective-permute-start.51 = (bf16[64,2048]{1,0:T(8,128)(2,1)}, bf16[64,2048]{1,0:T(8,128)(2,1)}, u32[]{:S(2)}, u32[]{:S(2)}) collective-permute-start(bf16[64,2048]{1,0:T(8,128)(2,1)} %slice.403), channel_id=1, source_target_pairs={{0,2},{1,3},{2,0},{3,1},{4,6},{5,7},{6,4},{7,5},{8,10},{9,11},{10,... | collective-permute-start | bytes 786440 | tf_op jit(solution)/shard_map/cond/branch_1_fun/ppermute | solution.py:590
  665.5 21.8 %collective-permute-start.45 = (bf16[64,2048]{1,0:T(8,128)(2,1)}, bf16[64,2048]{1,0:T(8,128)(2,1)}, u32[]{:S(2)}, u32[]{:S(2)}) collective-permute-start(bf16[64,2048]{1,0:T(8,128)(2,1)} %slice.400), channel_id=1, source_target_pairs={{0,1},{1,0},{2,3},{3,2},{4,5},{5,4},{6,7},{7,6},{8,9},{9,8},{10,11... | collective-permute-start | bytes 786440 | tf_op jit(solution)/shard_map/cond/branch_1_fun/ppermute | solution.py:590
  671.8 15.5 %collective-permute-start.46 = (bf16[64,2048]{1,0:T(8,128)(2,1)}, bf16[64,2048]{1,0:T(8,128)(2,1)}, u32[]{:S(2)}, u32[]{:S(2)}) collective-permute-start(bf16[64,2048]{1,0:T(8,128)(2,1)} %slice.401), channel_id=1, source_target_pairs={{0,2},{1,3},{2,0},{3,1},{4,6},{5,7},{6,4},{7,5},{8,10},{9,11},{10,... | collective-permute-start | bytes 786440 | tf_op jit(solution)/shard_map/cond/branch_1_fun/ppermute | solution.py:590
  679.7 29.8 %all-to-all-start.1 = ((bf16[4,256,512]{2,1,0:T(8,128)(2,1)}), bf16[4,256,512]{2,1,0:T(8,128)(2,1)}, u32[]{:S(2)}, u32[]{:S(2)}) async-start(bf16[4,256,512]{2,1,0:T(8,128)(2,1)} %bitcast.143), calls=%async_computation.1 | async-start | bytes 2097152 | tf_op jit(solution)/shard_map/cond/branch_1_fun/all_to_all | solution.py:698
  (82 other events, 934.2 us)
Sparse Core Ops, SparseCore 0:
  411.7 50.5 reduce-scatter.6
  465.7 104.1 reduce-scatter.8
